TPU v7x, 128 devices: a whole 4x4x4 slice. The times are simulated.
128 devices in a mesh: dp: 4 (over y_hi, core), cells: 32 (over y_lo, x, z).
Axes of the slice: x: 4, y: 4 (y_hi: 2, y_lo: 2; y = y_hi * 2 + y_lo), z: 4, core: 2. Of those that a mesh axis runs over, the one named last changes fastest.
Arguments:
- sensitivity: float32 [8192, 49152], P('dp', 'cells'), may hold values from -0.02734375 to 0.02734375
- observed: float32 [8192, 256], P('dp'), may hold values from -6 to 6
- models: float32 [49152, 256], P('cells'), may hold values from -6 to 6
- neighbour_map: int32 [4, 768], replicated, may hold values from 0 to 767, as said below
- edge_mask: int32 [49152], P('cells'), may hold values 0 or 1
Outputs:
- updated: float32 [49152, 256], P('cells')
Inputs may be any that keep to these rules, and one draw needn't show every extreme that they name: `neighbour_map`: each row k maps every cell of a periodic 32 by 24 plane grid, numbered in a drawn order, to its neighbour in one of the four grid directions; every row is a permutation.
All inputs are finite; a program needn't handle non-finite values. No bound on the sum of `edge_mask` on one device may be relied on, other than what follows from the above.
Results may differ from a plain program's by a relative error of at most 0.0001.
Values sent between devices are 32-bit elements; how exact they have to be, the bound alone decides.
No kernel may reach another device: no remote copies, remote signals or barrier semaphores. Data moves between devices by JAX's collectives and lax.ppermute only.
A program may use at most 128 MiB of HBM per device.

v0:
```python
import jax
import jax.numpy as jnp
from jax import lax
from jax.sharding import PartitionSpec as P

ITERS = 2


def with_halo(cells, sides, width):
    for axis, dim in sides:
        count = lax.axis_size(axis)
        ends = count - 1
        head = lax.slice_in_dim(cells, 0, width, axis=dim)
        tail = lax.slice_in_dim(cells, cells.shape[dim] - width, cells.shape[dim], axis=dim)
        cells = jnp.concatenate(
            [
                lax.ppermute(tail, axis, [(i, (i + 1) % count) for i in range(ends)]),
                cells,
                lax.ppermute(head, axis, [((i + 1) % count, i) for i in range(ends)]),
            ],
            axis=dim,
        )
    return cells


def reweight(misfit):
    return misfit / jnp.maximum(jnp.abs(misfit), 1.0)


def smooth_local(current, neighbour_map, edge_mask):
    plane_cells = neighbour_map.shape[1]
    count = current.shape[0] // plane_cells
    planes = current.reshape(count, plane_cells, current.shape[1])
    padded = with_halo(planes, (("cells", 0),), 1)
    total = jnp.zeros_like(planes)
    for other in (padded[:-2], padded[2:]):
        diff = other - planes
        total = total + diff / jnp.sqrt(1.0 + diff * diff)
    for k in range(4):
        other = jnp.take(planes, neighbour_map[k], axis=1)
        diff = other - planes
        total = total + diff / jnp.sqrt(1.0 + diff * diff)
    scale = 1.0 - 0.75 * edge_mask.astype(jnp.float32).reshape(count, plane_cells, 1)
    return (total * scale).reshape(current.shape)


def local(sensitivity, observed, models, neighbour_map, edge_mask):
    current = models
    for step in range(ITERS):
        predicted = lax.psum(
            jnp.dot(
                sensitivity,
                current,
                precision=lax.Precision.HIGHEST,
                preferred_element_type=jnp.float32,
            ),
            "cells",
        )
        weighted = reweight(predicted - observed)
        smooth = smooth_local(current, neighbour_map, edge_mask)
        partial_grad = lax.dot_general(
            sensitivity,
            weighted,
            (((0,), (0,)), ((), ())),
            precision=lax.Precision.HIGHEST,
            preferred_element_type=jnp.float32,
        )
        gradient = lax.psum(partial_grad, "dp")
        current = current - 1.0 * gradient + 0.05 * smooth
    return current


def solution(mesh):
    return jax.shard_map(
        local,
        mesh=mesh,
        in_specs=(P("dp", "cells"), P("dp", None), P("cells", None), P(), P("cells")),
        out_specs=P("cells", None),
        check_vma=False,
    )
```

profile of v0, /device:TPU:25, one launch (start us, length us, event | category | flops | bytes accessed | tf_op | source)
XLA Modules:
  0.0 827.9 jit_solution(12096581581674498763)
XLA Ops:
  6.5 13.9 %fusion.16 = f32[2048,256]{1,0:T(8,128)} fusion(f32[2048,1536]{1,0:T(8,128)} %param.7, f32[1536,256]{1,0:T(8,128)} %param.9), kind=kOutput, calls=%fused_computation.72 | convolution fusion | flops 9663676416 | bytes 16252928 | tf_op jit(solution)/shard_map/dot_general | solution.py:51
  20.5 0.0 all-reduce.7.cloned.1.call-start
  20.6 1.3 copy-done
  21.9 1.3 slice_bitcast_fusion.3
  23.2 3.5 collective-permute-start
  26.7 6.4 collective-permute-start.1
  33.2 1.2 copy.73
  34.5 4.2 gather_fusion.3
  38.7 275.6 %all-reduce.5.cloned.1.call-done = f32[2048,256]{1,0:T(8,128)} async-done(((f32[2048,256]{1,0:T(8,128)}), f32[2048,256]{1,0:T(8,128)}) %all-reduce.5.cloned.1.call-update) | async-done | bytes 2097168 | tf_op jit(solution)/shard_map/psum | solution.py:50
  314.2 24.6 %convolution_bitcast_fusion.2 = f32[1536,256]{1,0:T(8,128)} fusion(f32[2048,1536]{1,0:T(8,128)} %param.7, f32[2048,256]{1,0:T(8,128)} %all-reduce.5.cloned.1.call-done, f32[2048,256]{1,0:T(8,128)} %param.8), kind=kOutput, calls=%fused_computation.10 | convolution fusion | flops 9665773568 | bytes 18350080 | tf_op jit(solution)/shard_map/dot_general | solution.py:61
  338.9 0.0 all-reduce.9.cloned.1.call-start
  338.9 4.2 gather_fusion.2
  343.2 4.1 gather_fusion.1
  347.2 4.0 gather_fusion
  351.3 6.2 multiply_multiply_fusion.1
  357.5 54.7 %all-reduce.7.cloned.1.call-done = f32[1536,256]{1,0:T(8,128)} async-done(((f32[1536,256]{1,0:T(8,128)}), f32[1536,256]{1,0:T(8,128)}) %all-reduce.7.cloned.1.call-update) | async-done | bytes 1572880 | tf_op jit(solution)/shard_map/psum | solution.py:68
  412.2 2.2 bitcast_add_fusion.1
  414.4 13.5 %convolution_bitcast_fusion.1 = f32[2048,256]{1,0:T(8,128)} fusion(f32[1536,256]{1,0:T(8,128)S(1)} %bitcast_add_fusion.1, f32[2048,1536]{1,0:T(8,128)} %param.7), kind=kOutput, calls=%fused_computation.9 | convolution fusion | flops 9663676416 | bytes 16252928 | tf_op jit(solution)/shard_map/dot_general | solution.py:51
  428.0 0.0 all-reduce.11.cloned.1.call-start
  428.0 1.3 slice_bitcast_fusion.1
  429.3 3.2 collective-permute-start.2
  432.5 6.3 collective-permute-start.3
  438.8 281.3 %all-reduce.9.cloned.1.call-done = f32[2048,256]{1,0:T(8,128)} async-done(((f32[2048,256]{1,0:T(8,128)}), f32[2048,256]{1,0:T(8,128)}) %all-reduce.9.cloned.1.call-update) | async-done | bytes 2097168 | tf_op jit(solution)/shard_map/psum | solution.py:50
  720.1 24.8 %convolution_bitcast_fusion = f32[1536,256]{1,0:T(8,128)} fusion(f32[2048,1536]{1,0:T(8,128)} %param.7, f32[2048,256]{1,0:T(8,128)} %all-reduce.9.cloned.1.call-done, f32[2048,256]{1,0:T(8,128)} %param.8), kind=kOutput, calls=%fused_computation.8 | convolution fusion | flops 9665773568 | bytes 18350080 | tf_op jit(solution)/shard_map/dot_general | solution.py:61
  745.0 1.2 copy.83
  746.2 4.5 gather_fusion.7
  750.7 4.0 gather_fusion.6
  754.7 4.1 gather_fusion.5
  758.7 4.0 gather_fusion.4
  762.7 5.3 multiply_multiply_fusion
  768.1 50.3 %all-reduce.11.cloned.1.call-done = f32[1536,256]{1,0:T(8,128)} async-done(((f32[1536,256]{1,0:T(8,128)}), f32[1536,256]{1,0:T(8,128)}) %all-reduce.11.cloned.1.call-update) | async-done | bytes 1572880 | tf_op jit(solution)/shard_map/psum | solution.py:68
  818.3 2.9 bitcast_add_fusion
  (25 shorter events, 0.2 us)
Async XLA Ops:
  6.5 307.7 %all-reduce.5.cloned.1.call-start = ((), (), s32[]{:S(2)}) async-start(), calls=%async_computation | async-start | bytes 4194304 | tf_op jit(solution)/shard_map/psum | solution.py:50
  20.5 1.4 copy-start
  20.5 12.6 %copy-start.2 = (s32[1536]{0:T(1024)S(1)}, s32[1536]{0:T(1024)}, u32[]{:S(2)}) copy-start(s32[1536]{0:T(1024)} %param.11) | copy-start | bytes 18436
  20.5 391.7 %all-reduce.7.cloned.1.call-start = ((), (), s32[]{:S(2)}) async-start(), calls=%async_computation.1 | async-start | bytes 3145728 | tf_op jit(solution)/shard_map/psum | solution.py:68
  23.2 328.1 %collective-permute-start = (f32[1,768,256]{2,1,0:T(8,128)}, f32[1,768,256]{2,1,0:T(8,128)}, u32[]{:S(2)}, u32[]{:S(2)}) collective-permute-start(f32[1,768,256]{2,1,0:T(8,128)} %get-tuple-element.12), channel_id=1, source_target_pairs={{0,1},{1,2},{2,3},{3,4},{4,5},{5,6},{6,7},{7,8},{8,9},{9,10},{10,1... | collective-permute-start | bytes 2359304 | tf_op jit(solution)/shard_map/ppermute | solution.py:17
  26.7 324.6 %collective-permute-start.1 = (f32[1,768,256]{2,1,0:T(8,128)}, f32[1,768,256]{2,1,0:T(8,128)}, u32[]{:S(2)}, u32[]{:S(2)}) collective-permute-start(f32[1,768,256]{2,1,0:T(8,128)} %get-tuple-element.13), channel_id=1, source_target_pairs={{1,0},{2,1},{3,2},{4,3},{5,4},{6,5},{7,6},{8,7},{9,8},{10,9},{11,1... | collective-permute-start | bytes 2359304 | tf_op jit(solution)/shard_map/ppermute | solution.py:19
  33.2 1.2 copy-start.1
  338.9 381.2 %all-reduce.9.cloned.1.call-start = ((), (), s32[]{:S(2)}) async-start(), calls=%async_computation.2 | async-start | bytes 4194304 | tf_op jit(solution)/shard_map/psum | solution.py:50
  428.0 390.3 %all-reduce.11.cloned.1.call-start = ((), (), s32[]{:S(2)}) async-start(), calls=%async_computation.3 | async-start | bytes 3145728 | tf_op jit(solution)/shard_map/psum | solution.py:68
  429.3 333.5 %collective-permute-start.2 = (f32[1,768,256]{2,1,0:T(8,128)}, f32[1,768,256]{2,1,0:T(8,128)}, u32[]{:S(2)}, u32[]{:S(2)}) collective-permute-start(f32[1,768,256]{2,1,0:T(8,128)} %get-tuple-element.10), channel_id=1, source_target_pairs={{0,1},{1,2},{2,3},{3,4},{4,5},{5,6},{6,7},{7,8},{8,9},{9,10},{10,1... | collective-permute-start | bytes 2359304 | tf_op jit(solution)/shard_map/ppermute | solution.py:17
  432.5 330.3 %collective-permute-start.3 = (f32[1,768,256]{2,1,0:T(8,128)}, f32[1,768,256]{2,1,0:T(8,128)}, u32[]{:S(2)}, u32[]{:S(2)}) collective-permute-start(f32[1,768,256]{2,1,0:T(8,128)} %get-tuple-element.11), channel_id=1, source_target_pairs={{1,0},{2,1},{3,2},{4,3},{5,4},{6,5},{7,6},{8,7},{9,8},{10,9},{11,1... | collective-permute-start | bytes 2359304 | tf_op jit(solution)/shard_map/ppermute | solution.py:19
Sparse Core Ops, SparseCore 0:
  20.6 293.5 all-reduce.4
  339.0 73.1 all-reduce.6
  428.1 291.9 all-reduce.8
  745.1 73.1 all-reduce.10
where the time goes:
time: 835 us; the launch traced here: 828 us
  waiting for transfers between devices  662 us (79%)
  matrix products  76.9 us (9%)
  local copies, waits for them, and re-layouts  39.3 us (5%)
  starting transfers between devices  19.6 us (2%)
  other arithmetic  16.7 us (2%)
  between operations  13.4 us (2%)
    psum x2, waiting for transfers between devices, local(): lax.psum(jnp.dot(sensitivity, current, precision=lax.Precision.HIGHEST, p...  557 us
    psum x2, waiting for transfers between devices, local(): gradient = lax.psum(partial_grad, 'dp')  105 us
    dot_general x2, matrix products, local(): lax.dot_general(sensitivity, weighted, (((0,), (0,)), ((), ())), precisio...  49.4 us
    gather x8, local copies, waits for them, and re-layouts, smooth_local(): other = jnp.take(planes, neighbour_map[k], axis=1)  33 us
    dot_general x2, matrix products, local(): jnp.dot(sensitivity, current, precision=lax.Precision.HIGHEST, preferred_...  27.5 us
  transfers between devices with their start and end apart: 8, of which 4 were waited for; matrix products, arithmetic and copies ran while one was open for 12% of the time, Pallas kernels for 0%

commit v1 on v0

v1 whole, which is shorter than its diff:
```python
import jax
import jax.numpy as jnp
from jax import lax
from jax.sharding import Mesh, PartitionSpec as P

ITERS = 2
DATA = ("yh", "core")
CELLS = ("yl", "x", "z")
ALL = DATA + CELLS


def reweight(misfit):
    return misfit / jnp.maximum(jnp.abs(misfit), 1.0)


def huber(diff):
    return diff / jnp.sqrt(1.0 + diff * diff)


def reduce_pieces(partial, ranks):
    pieces = partial.reshape(ranks, partial.shape[0] // ranks, partial.shape[1])
    return jnp.sum(lax.all_to_all(pieces, CELLS, 0, 0), axis=0)


def gather_pieces(piece, ranks):
    copies = jnp.broadcast_to(piece[None], (ranks,) + piece.shape)
    return lax.all_to_all(copies, CELLS, 0, 0).reshape(-1, piece.shape[1])


def swap(value, axis):
    return lax.ppermute(value, axis, [(0, 1), (1, 0)])


def halo_pairs(ranks):
    up = [(i, i + 1) for i in range(ranks - 1)]
    down = [(ranks + i + 1, ranks + i) for i in range(ranks - 1)]
    return up + down


def local(sensitivity, observed, models, neighbour_map, edge_mask):
    core = lax.axis_index("core")
    ranks = lax.axis_size(CELLS)
    rank = lax.axis_index(CELLS)
    plane_cells = neighbour_map.shape[1]
    sols = models.shape[1]
    rows = observed.shape[0] // ranks
    own_observed = lax.dynamic_slice_in_dim(observed, rank * rows, rows, axis=0)
    own_mask = lax.dynamic_slice_in_dim(edge_mask, core * plane_cells, plane_cells, axis=0)
    scale = 0.05 * (1.0 - 0.75 * own_mask.astype(jnp.float32))[:, None]
    current = models
    for step in range(ITERS):
        own = lax.dynamic_slice_in_dim(current, core * plane_cells, plane_cells, axis=0)
        twin = lax.dynamic_slice_in_dim(current, (1 - core) * plane_cells, plane_cells, axis=0)
        partial = jnp.dot(
            sensitivity,
            current,
            precision=lax.Precision.HIGH,
            preferred_element_type=jnp.float32,
        )
        weighted = reweight(reduce_pieces(partial, ranks) - own_observed)
        weighted = gather_pieces(weighted, ranks)
        partial_grad = lax.dot_general(
            sensitivity,
            weighted,
            (((0,), (0,)), ((), ())),
            precision=lax.Precision.HIGH,
            preferred_element_type=jnp.float32,
        )
        keep = lax.dynamic_slice_in_dim(partial_grad, core * plane_cells, plane_cells, axis=0)
        send = lax.dynamic_slice_in_dim(partial_grad, (1 - core) * plane_cells, plane_cells, axis=0)
        half = keep + swap(send, "core")
        gradient = half + swap(half, "yh")
        beyond = lax.ppermute(twin, ("core",) + CELLS, halo_pairs(ranks))
        total = huber(twin - own) + huber(beyond - own)
        for k in range(4):
            total = total + huber(jnp.take(own, neighbour_map[k], axis=0) - own)
        own = own - 1.0 * gradient + scale * total
        other = swap(own, "core")
        first = jnp.where(core == 0, own, other)
        second = jnp.where(core == 0, other, own)
        current = jnp.concatenate([first, second], axis=0)
    return current


def solution(mesh):
    fine = Mesh(mesh.devices.reshape(2, 2, 2, 4, 4), ALL)
    return jax.shard_map(
        local,
        mesh=fine,
        in_specs=(P(DATA, CELLS), P(DATA, None), P(CELLS, None), P(), P(CELLS)),
        out_specs=P(CELLS, None),
        check_vma=False,
    )
```

time: 835 us -> 264 us (0.32)
  the two profiles are of different devices: /device:TPU:25 before, /device:TPU:15 now
where the time goes in v1:
time: 264 us; the launch traced here: 263 us
  waiting for transfers between devices  73.7 us (28%)
  blocking collectives  61 us (23%)
  local copies, waits for them, and re-layouts  46.1 us (17%)
  matrix products  35.7 us (14%)
  starting transfers between devices  33.2 us (13%)
  other arithmetic  13.4 us (5%)
    gather x16, local copies, waits for them, and re-layouts, local(): total = total + huber(jnp.take(own, neighbour_map[k], axis=0) - own)  37.1 us
    all_to_all x1, blocking collectives, reduce_pieces(): return jnp.sum(lax.all_to_all(pieces, CELLS, 0, 0), axis=0)  31.4 us
    all_to_all x1, blocking collectives, gather_pieces(): return lax.all_to_all(copies, CELLS, 0, 0).reshape(-1, piece.shape[1])  29.7 us
    all_to_all x1, waiting for transfers between devices, reduce_pieces(): return jnp.sum(lax.all_to_all(pieces, CELLS, 0, 0), axis=0)  26.5 us
    all_to_all x1, waiting for transfers between devices, gather_pieces(): return lax.all_to_all(copies, CELLS, 0, 0).reshape(-1, piece.shape[1])  26.5 us
    ppermute x6, waiting for transfers between devices, swap(): return lax.ppermute(value, axis, [(0, 1), (1, 0)])  20.8 us
    dot_general x2, matrix products, local(): lax.dot_general(sensitivity, weighted, (((0,), (0,)), ((), ())), precisio...  17.9 us
    dot_general x2, matrix products, local(): jnp.dot(sensitivity, current, precision=lax.Precision.HIGH, preferred_ele...  17.8 us
  transfers between devices with their start and end apart: 10, of which 6 were waited for; matrix products, arithmetic and copies ran while one was open for 16% of the time, Pallas kernels for 0%

profile of v1, /device:TPU:15, one launch (start us, length us, event | category | flops | bytes accessed | tf_op | source)
XLA Modules:
  0.0 263.5 jit_solution(2369718528645045131)
XLA Ops:
  0.0 9.5 %fusion.3 = f32[2048,256]{1,0:T(8,128)} fusion(f32[2048,1536]{1,0:T(8,128)} %param.7, f32[1536,256]{1,0:T(8,128)} %param.9), kind=kOutput, calls=%fused_computation.57 | convolution fusion | flops 4831838208 | bytes 16252928 | tf_op jit(solution)/shard_map/dot_general | solution.py:54
  9.5 8.8 %all-to-all-start = ((f32[32,64,256]{2,1,0:T(8,128)}), f32[32,64,256]{2,1,0:T(8,128)S(1)}, u32[]{:S(2)}, u32[]{:S(2)}) async-start(f32[32,64,256]{2,1,0:T(8,128)} %bitcast), calls=%async_computation | async-start | bytes 4194304 | tf_op jit(solution)/shard_map/all_to_all | solution.py:22
  18.3 26.5 %all-to-all-done = f32[32,64,256]{2,1,0:T(8,128)S(1)} async-done(((f32[32,64,256]{2,1,0:T(8,128)}), f32[32,64,256]{2,1,0:T(8,128)S(1)}, u32[]{:S(2)}, u32[]{:S(2)}) %all-to-all-start) | async-done | bytes 2097184 | tf_op jit(solution)/shard_map/all_to_all | solution.py:22
  47.4 7.7 %all-to-all-start.1 = ((f32[32,64,256]{2,1,0:T(8,128)}), f32[32,64,256]{2,1,0:T(8,128)S(1)}, u32[]{:S(2)}, u32[]{:S(2)}) async-start(f32[32,64,256]{2,1,0:T(8,128)} %broadcast_in_dim.13), calls=%async_computation.1 | async-start | bytes 4194304 | tf_op jit(solution)/shard_map/all_to_all | solution.py:27
  55.1 26.5 %all-to-all-done.1 = f32[32,64,256]{2,1,0:T(8,128)S(1)} async-done(((f32[32,64,256]{2,1,0:T(8,128)}), f32[32,64,256]{2,1,0:T(8,128)S(1)}, u32[]{:S(2)}, u32[]{:S(2)}) %all-to-all-start.1) | async-done | bytes 2097184 | tf_op jit(solution)/shard_map/all_to_all | solution.py:27
  81.6 8.7 %fusion.4 = f32[256,1536]{1,0:T(8,128)S(1)} fusion(f32[2048,256]{1,0:T(8,128)S(1)} %bitcast.22, f32[2048,1536]{1,0:T(8,128)} %param.7), kind=kOutput, calls=%fused_computation.58 | convolution fusion | flops 4831838208 | bytes 16252928 | tf_op jit(solution)/shard_map/dot_general | solution.py:62
  91.3 2.5 collective-permute-start
  95.1 3.2 %collective-permute-start.2 = (f32[768,256]{0,1:T(8,128)}, f32[768,256]{0,1:T(8,128)}, u32[]{:S(2)}, u32[]{:S(2)}) collective-permute-start(f32[768,256]{0,1:T(8,128)} %copy.46), channel_id=1, source_target_pairs={{0,1},{1,2},{2,3},{3,4},{4,5},{5,6},{6,7},{7,8},{8,9},{9,10},{10,1... | collective-permute-start | bytes 2359304 | tf_op jit(solution)/shard_map/ppermute | solution.py:73
  99.7 2.3 collective-permute-start.1
  102.2 2.9 %gather_fusion = f32[768,256]{1,0:T(8,128)} fusion(f32[768,256]{1,0:T(8,128)S(1)} %get-tuple-element.17, s32[1024]{0:T(1024)S(1)} %pad_clamp_fusion.3), kind=kCustom, calls=%fused_computation.clone | custom fusion | bytes 1575936 | tf_op jit(solution)/shard_map/jit(_take)/gather | solution.py:76
  106.5 2.9 %gather_fusion.1 = f32[768,256]{1,0:T(8,128)} fusion(f32[768,256]{1,0:T(8,128)S(1)} %get-tuple-element.17, s32[1024]{0:T(1024)S(1)} %pad_clamp_fusion.2), kind=kCustom, calls=%fused_computation.1.clone | custom fusion | bytes 1575936 | tf_op jit(solution)/shard_map/jit(_take)/gather | solution.py:76
  109.5 2.3 copy.30
  111.8 2.9 %gather_fusion.2 = f32[768,256]{1,0:T(8,128)} fusion(f32[768,256]{1,0:T(8,128)S(1)} %get-tuple-element.17, s32[1024]{0:T(1024)S(1)} %pad_clamp_fusion.1), kind=kCustom, calls=%fused_computation.2.clone | custom fusion | bytes 1575936 | tf_op jit(solution)/shard_map/jit(_take)/gather | solution.py:76
  114.7 2.3 copy.32
  117.0 2.9 %gather_fusion.3 = f32[768,256]{1,0:T(8,128)} fusion(f32[768,256]{1,0:T(8,128)S(1)} %get-tuple-element.17, s32[1024]{0:T(1024)S(1)} %pad_clamp_fusion), kind=kCustom, calls=%fused_computation.3.clone | custom fusion | bytes 1575936 | tf_op jit(solution)/shard_map/jit(_take)/gather | solution.py:76
  119.9 2.4 copy.34
  122.4 6.9 %collective-permute-done.1 = f32[768,256]{0,1:T(8,128)} collective-permute-done((f32[768,256]{0,1:T(8,128)S(1)}, f32[768,256]{0,1:T(8,128)}, u32[]{:S(2)}, u32[]{:S(2)}) %collective-permute-start.1) | collective-permute-done | bytes 786464 | tf_op jit(solution)/shard_map/ppermute | solution.py:31
  129.3 4.1 %multiply_add_fusion.1 = f32[768,256]{0,1:T(8,128)} fusion(f32[768,256]{0,1:T(8,128)S(1)} %copy.45, f32[768,256]{0,1:T(8,128)} %copy.34, f32[768,256]{0,1:T(8,128)} %copy.32, f32[768,256]{0,1:T(8,128)S(1)} %copy-done.5, f32[768,256]{0,1:T(8,128)S(1)} %copy.28, f32[768,256]{0,1:T(8,128)} %collective-permute-done.2, f32[768,256]{0,1:T(8,128)} %copy.46, ...), kind=kLoop, calls=%fused_computation.29 | loop fusion | flops 7274496 | bytes 7870464 | tf_op jit(solution)/shard_map/add | solution.py:77
  134.0 2.1 collective-permute-done.3
  138.2 8.3 %convolution_bitcast_fusion = f32[2048,256]{0,1:T(8,128)S(1)} fusion(f32[2048,1536]{1,0:T(8,128)} %param.7, f32[768,256]{0,1:T(8,128)S(1)} %get-tuple-element.14, f32[768,256]{0,1:T(8,128)S(1)} %get-tuple-element.15), kind=kOutput, calls=%fused_computation.8 | convolution fusion | flops 4832231424 | bytes 16252928 | tf_op jit(solution)/shard_map/dot_general | solution.py:54
  148.4 31.4 %all_to_all.20 = f32[32,64,256]{2,1,0:T(8,128)S(1)} all-to-all(f32[32,64,256]{2,1,0:T(8,128)} %bitcast.21), channel_id=1, replica_groups=mesh['yh'=2,'core'=2,'yl'=2,'x'=4,'z'=4] {'yl','x','z'}, dimensions={0} | all-to-all | bytes 4194304 | tf_op jit(solution)/shard_map/all_to_all | solution.py:22
  181.0 29.7 %all_to_all.21 = f32[32,64,256]{2,1,0:T(8,128)S(1)} all-to-all(f32[32,64,256]{2,1,0:T(8,128)S(1)} %broadcast_in_dim.14), channel_id=1, replica_groups=mesh['yh'=2,'core'=2,'yl'=2,'x'=4,'z'=4] {'yl','x','z'}, dimensions={0} | all-to-all | bytes 4194304 | tf_op jit(solution)/shard_map/all_to_all | solution.py:27
  210.7 9.1 %fusion.5 = f32[256,1536]{1,0:T(8,128)S(1)} fusion(f32[2048,256]{1,0:T(8,128)S(1)} %bitcast.23, f32[2048,1536]{1,0:T(8,128)} %param.7), kind=kOutput, calls=%fused_computation.59 | convolution fusion | flops 4831838208 | bytes 16252928 | tf_op jit(solution)/shard_map/dot_general | solution.py:62
  219.9 3.0 %collective-permute-start.4 = (f32[768,256]{0,1:T(8,128)S(1)}, f32[768,256]{0,1:T(8,128)S(1)}, u32[]{:S(2)}, u32[]{:S(2)}) collective-permute-start(f32[768,256]{0,1:T(8,128)S(1)} %dynamic-slice_bitcast_fusion), channel_id=1, source_target_pairs={{0,32},{32,0},{1,33},{33,1},{2,34},{34,2},{3,35},{35,3},{4,36},{36... | collective-permute-start | bytes 2359304 | tf_op jit(solution)/shard_map/ppermute | solution.py:31
  224.0 2.2 collective-permute-start.6
  229.9 2.9 %gather_fusion.5 = f32[768,256]{1,0:T(8,128)} fusion(f32[768,256]{1,0:T(8,128)S(1)} %copy.36, s32[1024]{0:T(1024)S(1)} %pad_clamp_fusion.2), kind=kCustom, calls=%fused_computation.5.clone | custom fusion | bytes 1575936 | tf_op jit(solution)/shard_map/jit(_take)/gather | solution.py:76
  232.8 2.9 %gather_fusion.6 = f32[768,256]{1,0:T(8,128)} fusion(f32[768,256]{1,0:T(8,128)S(1)} %copy.36, s32[1024]{0:T(1024)S(1)} %pad_clamp_fusion.1), kind=kCustom, calls=%fused_computation.6.clone | custom fusion | bytes 1575936 | tf_op jit(solution)/shard_map/jit(_take)/gather | solution.py:76
  235.7 2.9 %gather_fusion.7 = f32[768,256]{1,0:T(8,128)} fusion(f32[768,256]{1,0:T(8,128)S(1)} %copy.36, s32[1024]{0:T(1024)S(1)} %pad_clamp_fusion), kind=kCustom, calls=%fused_computation.7.clone | custom fusion | bytes 1575936 | tf_op jit(solution)/shard_map/jit(_take)/gather | solution.py:76
  240.3 2.3 copy.41
  242.6 2.3 copy.43
  244.9 9.9 %collective-permute-done.5 = f32[768,256]{0,1:T(8,128)} collective-permute-done((f32[768,256]{0,1:T(8,128)S(1)}, f32[768,256]{0,1:T(8,128)}, u32[]{:S(2)}, u32[]{:S(2)}) %collective-permute-start.5) | collective-permute-done | bytes 786464 | tf_op jit(solution)/shard_map/ppermute | solution.py:31
  254.8 3.2 %multiply_add_fusion = f32[768,256]{0,1:T(8,128)S(1)} fusion(f32[768,256]{0,1:T(8,128)S(1)} %get-tuple-element.13, f32[768,256]{0,1:T(8,128)} %copy.43, f32[768,256]{0,1:T(8,128)} %copy.41, f32[768,256]{0,1:T(8,128)S(1)} %copy.39, f32[768,256]{0,1:T(8,128)S(1)} %copy.37, f32[768,256]{0,1:T(8,128)} %collective-permute-done.6, ...), kind=kLoop, calls=%fused_computation.27 | loop fusion | flops 7274496 | bytes 7870464 | tf_op jit(solution)/shard_map/add | solution.py:77
  (58 shorter events, 25.8 us)
Async XLA Ops:
  9.5 35.3 %all-to-all-start = ((f32[32,64,256]{2,1,0:T(8,128)}), f32[32,64,256]{2,1,0:T(8,128)S(1)}, u32[]{:S(2)}, u32[]{:S(2)}) async-start(f32[32,64,256]{2,1,0:T(8,128)} %bitcast), calls=%async_computation | async-start | bytes 4194304 | tf_op jit(solution)/shard_map/all_to_all | solution.py:22
  47.4 34.2 %all-to-all-start.1 = ((f32[32,64,256]{2,1,0:T(8,128)}), f32[32,64,256]{2,1,0:T(8,128)S(1)}, u32[]{:S(2)}, u32[]{:S(2)}) async-start(f32[32,64,256]{2,1,0:T(8,128)} %broadcast_in_dim.13), calls=%async_computation.1 | async-start | bytes 4194304 | tf_op jit(solution)/shard_map/all_to_all | solution.py:27
  90.3 3.6 %copy-start.3 = (f32[256,1536]{1,0:T(8,128)}, f32[256,1536]{1,0:T(8,128)S(1)}, u32[]{:S(2)}) copy-start(f32[256,1536]{1,0:T(8,128)S(1)} %fusion.4) | copy-start | bytes 4718596
  90.3 3.5 %copy-start.2 = (f32[1536,256]{1,0:T(8,128)S(1)}, f32[1536,256]{1,0:T(8,128)}, u32[]{:S(2)}) copy-start(f32[1536,256]{1,0:T(8,128)} %param.9) | copy-start | bytes 4718596
  91.3 7.0 %copy-start.6 = (s32[4,768]{1,0:T(4,128)S(1)}, s32[4,768]{1,0:T(4,128)}, u32[]{:S(2)}) copy-start(s32[4,768]{1,0:T(4,128)} %param.10) | copy-start | bytes 36868
  91.3 7.1 %collective-permute-start = (f32[768,256]{0,1:T(8,128)}, f32[768,256]{0,1:T(8,128)}, u32[]{:S(2)}, u32[]{:S(2)}) collective-permute-start(f32[768,256]{0,1:T(8,128)} %dynamic-slice_bitcast_fusion.1), channel_id=1, source_target_pairs={{0,32},{32,0},{1,33},{33,1},{2,34},{34,2},{3,35},{35,3},{4,36},{36... | collective-permute-start | bytes 2359304 | tf_op jit(solution)/shard_map/ppermute | solution.py:31
  93.9 4.5 %copy-start.4 = (f32[256,1536]{1,0:T(8,128)S(1)}, f32[256,1536]{1,0:T(8,128)}, u32[]{:S(2)}) copy-start(f32[256,1536]{1,0:T(8,128)} %copy-done.3) | copy-start | bytes 4718596
  95.1 27.3 %collective-permute-start.2 = (f32[768,256]{0,1:T(8,128)}, f32[768,256]{0,1:T(8,128)}, u32[]{:S(2)}, u32[]{:S(2)}) collective-permute-start(f32[768,256]{0,1:T(8,128)} %copy.46), channel_id=1, source_target_pairs={{0,1},{1,2},{2,3},{3,4},{4,5},{5,6},{6,7},{7,8},{8,9},{9,10},{10,1... | collective-permute-start | bytes 2359304 | tf_op jit(solution)/shard_map/ppermute | solution.py:73
  99.7 29.6 %collective-permute-start.1 = (f32[768,256]{0,1:T(8,128)S(1)}, f32[768,256]{0,1:T(8,128)}, u32[]{:S(2)}, u32[]{:S(2)}) collective-permute-start(f32[768,256]{0,1:T(8,128)S(1)} %bitcast_add_fusion.1), channel_id=1, source_target_pairs={{0,64},{64,0},{1,65},{65,1},{2,66},{66,2},{3,67},{67,3},{4,68},{68... | collective-permute-start | bytes 2359304 | tf_op jit(solution)/shard_map/ppermute | solution.py:31
  117.0 5.3 %copy-start.7 = (s32[1536]{0:T(1024)S(1)}, s32[1536]{0:T(1024)}, u32[]{:S(2)}) copy-start(s32[1536]{0:T(1024)} %param.11) | copy-start | bytes 18436
  119.9 9.4 %copy-start.5 = (f32[768,256]{0,1:T(8,128)S(1)}, f32[768,256]{0,1:T(8,128)}, u32[]{:S(2)}) copy-start(f32[768,256]{0,1:T(8,128)} %copy.30) | copy-start | bytes 2359300
  133.3 2.8 %collective-permute-start.3 = (f32[768,256]{0,1:T(8,128)}, f32[768,256]{0,1:T(8,128)S(1)}, u32[]{:S(2)}, u32[]{:S(2)}) collective-permute-start(f32[768,256]{0,1:T(8,128)} %multiply_add_fusion.1), channel_id=1, source_target_pairs={{0,32},{32,0},{1,33},{33,1},{2,34},{34,2},{3,35},{35,3},{4,36},{36... | collective-permute-start | bytes 2359304 | tf_op jit(solution)/shard_map/ppermute | solution.py:31
  137.4 0.9 copy-start
  219.8 3.1 %copy-start.1 = (f32[768,256]{0,1:T(8,128)S(1)}, f32[768,256]{0,1:T(8,128)}, u32[]{:S(2)}) copy-start(f32[768,256]{0,1:T(8,128)} %copy-done) | copy-start | bytes 2359300
  219.9 6.3 %collective-permute-start.4 = (f32[768,256]{0,1:T(8,128)S(1)}, f32[768,256]{0,1:T(8,128)S(1)}, u32[]{:S(2)}, u32[]{:S(2)}) collective-permute-start(f32[768,256]{0,1:T(8,128)S(1)} %dynamic-slice_bitcast_fusion), channel_id=1, source_target_pairs={{0,32},{32,0},{1,33},{33,1},{2,34},{34,2},{3,35},{35,3},{4,36},{36... | collective-permute-start | bytes 2359304 | tf_op jit(solution)/shard_map/ppermute | solution.py:31
  224.0 20.9 %collective-permute-start.6 = (f32[768,256]{0,1:T(8,128)}, f32[768,256]{0,1:T(8,128)}, u32[]{:S(2)}, u32[]{:S(2)}) collective-permute-start(f32[768,256]{0,1:T(8,128)} %get-tuple-element.12), channel_id=1, source_target_pairs={{0,1},{1,2},{2,3},{3,4},{4,5},{5,6},{6,7},{7,8},{8,9},{9,10},{10,1... | collective-permute-start | bytes 2359304 | tf_op jit(solution)/shard_map/ppermute | solution.py:73
  226.3 28.4 %collective-permute-start.5 = (f32[768,256]{0,1:T(8,128)S(1)}, f32[768,256]{0,1:T(8,128)}, u32[]{:S(2)}, u32[]{:S(2)}) collective-permute-start(f32[768,256]{0,1:T(8,128)S(1)} %bitcast_add_fusion), channel_id=1, source_target_pairs={{0,64},{64,0},{1,65},{65,1},{2,66},{66,2},{3,67},{67,3},{4,68},{68... | collective-permute-start | bytes 2359304 | tf_op jit(solution)/shard_map/ppermute | solution.py:31
  258.0 3.6 %collective-permute-start.7 = (f32[768,256]{0,1:T(8,128)S(1)}, f32[768,256]{0,1:T(8,128)S(1)}, u32[]{:S(2)}, u32[]{:S(2)}) collective-permute-start(f32[768,256]{0,1:T(8,128)S(1)} %multiply_add_fusion), channel_id=1, source_target_pairs={{0,32},{32,0},{1,33},{33,1},{2,34},{34,2},{3,35},{35,3},{4,36},{36... | collective-permute-start | bytes 2359304 | tf_op jit(solution)/shard_map/ppermute | solution.py:31

commit v2 on v1

v2 whole, which is shorter than its diff:
```python
import functools

import jax
import jax.numpy as jnp
from jax import lax
from jax.experimental import pallas as pl
from jax.experimental.pallas import tpu as pltpu
from jax.sharding import Mesh, PartitionSpec as P

ITERS = 2
DATA = ("yh", "core")
CELLS = ("yl", "x", "z")
ALL = DATA + CELLS
ROWS = 512
COLS = 256
VMEM_LIMIT = 40 * 1024 * 1024


def reweight(misfit):
    return misfit / jnp.maximum(jnp.abs(misfit), 1.0)


def huber(diff):
    return diff / jnp.sqrt(1.0 + diff * diff)


def split(value):
    high = value.astype(jnp.bfloat16)
    low = (value - high.astype(jnp.float32)).astype(jnp.bfloat16)
    return high, low


def dot(a, b):
    return jnp.dot(a, b, preferred_element_type=jnp.float32)


def forward_kernel(add, plane_ref, s_ref, x_ref, *refs):
    if add:
        p_ref, o_ref, high_ref, low_ref = refs
    else:
        o_ref, high_ref, low_ref = refs

    @pl.when(pl.program_id(0) == 0)
    def _():
        high_ref[...], low_ref[...] = split(x_ref[...])

    s_high, s_low = split(s_ref[...])
    total = dot(s_high, high_ref[...]) + (dot(s_high, low_ref[...]) + dot(s_low, high_ref[...]))
    if add:
        total = total + p_ref[...]
    o_ref[...] = total


def forward(plane, sensitivity, x, before=None):
    data, sols = sensitivity.shape[0], x.shape[1]
    cells = x.shape[0]
    in_specs = [
        pl.BlockSpec((ROWS, cells), lambda i, plane: (i, plane[0])),
        pl.BlockSpec((cells, sols), lambda i, plane: (0, 0)),
    ]
    args = [sensitivity, x]
    if before is not None:
        in_specs.append(pl.BlockSpec((ROWS, sols), lambda i, plane: (i, 0)))
        args.append(before)
    return pl.pallas_call(
        functools.partial(forward_kernel, before is not None),
        grid_spec=pltpu.PrefetchScalarGridSpec(
            num_scalar_prefetch=1,
            grid=(data // ROWS,),
            in_specs=in_specs,
            out_specs=pl.BlockSpec((ROWS, sols), lambda i, plane: (i, 0)),
            scratch_shapes=[
                pltpu.VMEM((cells, sols), jnp.bfloat16),
                pltpu.VMEM((cells, sols), jnp.bfloat16),
            ],
        ),
        out_shape=jax.ShapeDtypeStruct((data, sols), jnp.float32),
        compiler_params=pltpu.CompilerParams(vmem_limit_bytes=VMEM_LIMIT),
        cost_estimate=pl.CostEstimate(
            flops=6 * data * cells * sols,
            bytes_accessed=4 * (data * cells + cells * sols + data * sols),
            transcendentals=0,
        ),
    )(plane, *args)


def backward_kernel(plane_ref, s_ref, w_ref, o_ref, high_ref, low_ref):
    @pl.when(pl.program_id(0) == 0)
    def _():
        high_ref[...], low_ref[...] = split(w_ref[...].T)

    s_high, s_low = split(s_ref[...])
    total = dot(high_ref[...], s_high) + (dot(low_ref[...], s_high) + dot(high_ref[...], s_low))
    o_ref[...] = total.T


def backward(plane, sensitivity, w, cells):
    data, sols = w.shape
    blocks = cells // COLS
    return pl.pallas_call(
        backward_kernel,
        grid_spec=pltpu.PrefetchScalarGridSpec(
            num_scalar_prefetch=1,
            grid=(blocks,),
            in_specs=[
                pl.BlockSpec((data, COLS), lambda i, plane: (0, plane[0] * blocks + i)),
                pl.BlockSpec((data, sols), lambda i, plane: (0, 0)),
            ],
            out_specs=pl.BlockSpec((COLS, sols), lambda i, plane: (i, 0)),
            scratch_shapes=[
                pltpu.VMEM((sols, data), jnp.bfloat16),
                pltpu.VMEM((sols, data), jnp.bfloat16),
            ],
        ),
        out_shape=jax.ShapeDtypeStruct((cells, sols), jnp.float32),
        compiler_params=pltpu.CompilerParams(vmem_limit_bytes=VMEM_LIMIT),
        cost_estimate=pl.CostEstimate(
            flops=6 * data * cells * sols,
            bytes_accessed=4 * (data * cells + cells * sols + data * sols),
            transcendentals=0,
        ),
    )(plane, sensitivity, w)


def swap(value, axis):
    return lax.ppermute(value, axis, [(0, 1), (1, 0)])


def halo_pairs(ranks):
    up = [(i, i + 1) for i in range(ranks - 1)]
    down = [(ranks + i + 1, ranks + i) for i in range(ranks - 1)]
    return up + down


def local(sensitivity, observed, models, neighbour_map, edge_mask):
    core = lax.axis_index("core").astype(jnp.int32)
    mine, theirs = core.reshape(1), (1 - core).reshape(1)
    ranks = lax.axis_size(CELLS)
    rank = lax.axis_index(CELLS)
    cells = neighbour_map.shape[1]
    rows = observed.shape[0] // ranks
    own_observed = lax.dynamic_slice_in_dim(observed, rank * rows, rows, axis=0)
    own_mask = lax.dynamic_slice_in_dim(edge_mask, core * cells, cells, axis=0)
    scale = 0.05 * (1.0 - 0.75 * own_mask.astype(jnp.float32))[:, None]
    own = lax.dynamic_slice_in_dim(models, core * cells, cells, axis=0)
    twin = lax.dynamic_slice_in_dim(models, (1 - core) * cells, cells, axis=0)
    for step in range(ITERS):
        partial = forward(mine, sensitivity, own)
        partial = forward(theirs, sensitivity, twin, partial)
        partial, own, twin = lax.optimization_barrier((partial, own, twin))
        pieces = lax.all_to_all(partial.reshape(ranks, rows, -1), CELLS, 0, 0)
        total = huber(twin - own)
        for k in range(4):
            total = total + huber(jnp.take(own, neighbour_map[k], axis=0) - own)
        weighted = reweight(jnp.sum(pieces, axis=0) - own_observed)
        weighted, total = lax.optimization_barrier((weighted, total))
        copies = jnp.broadcast_to(weighted[None], (ranks,) + weighted.shape)
        weighted = lax.all_to_all(copies, CELLS, 0, 0).reshape(ranks * rows, -1)
        away = backward(theirs, sensitivity, weighted, cells)
        home = backward(mine, sensitivity, weighted, cells)
        half = home + swap(away, "core")
        half, twin = lax.optimization_barrier((half, twin))
        beyond = lax.ppermute(twin, ("core",) + CELLS, halo_pairs(ranks))
        gradient = half + swap(half, "yh")
        total = total + huber(beyond - own)
        own = own - 1.0 * gradient + scale * total
        twin = swap(own, "core")
    place = lax.broadcasted_iota(jnp.int32, (2, 1, 1), 0)
    both = jnp.where(place == core, own[None], twin[None])
    return both.reshape(models.shape)


def solution(mesh):
    fine = Mesh(mesh.devices.reshape(2, 2, 2, 4, 4), ALL)
    return jax.shard_map(
        local,
        mesh=fine,
        in_specs=(P(DATA, CELLS), P(DATA, None), P(CELLS, None), P(), P(CELLS)),
        out_specs=P(CELLS, None),
        check_vma=False,
    )
```

time: 264 us -> 263 us (level)
  the two profiles are of different devices: /device:TPU:15 before, /device:TPU:31 now
where the time goes in v2:
time: 263 us; the launch traced here: 262 us
  waiting for transfers between devices  85.4 us (32%)
  blocking collectives  64.3 us (24%)
  Pallas kernels  47 us (18%)
  starting transfers between devices  27 us (10%)
  local copies, waits for them, and re-layouts  23.5 us (9%)
  other arithmetic  15 us (6%)
    all_to_all x2, blocking collectives, local(): weighted = lax.all_to_all(copies, CELLS, 0, 0).reshape(ranks * rows, -1)  64.3 us
    ppermute x6, waiting for transfers between devices, swap(): return lax.ppermute(value, axis, [(0, 1), (1, 0)])  38.9 us
    all_to_all x2, waiting for transfers between devices, local(): pieces = lax.all_to_all(partial.reshape(ranks, rows, -1), CELLS, 0, 0)  27 us
    pallas_call x4, Pallas kernels, backward(): pl.pallas_call(backward_kernel, grid_spec=pltpu.PrefetchScalarGridSpec(nu...  24 us
    pallas_call x4, Pallas kernels, forward(): pl.pallas_call(functools.partial(forward_kernel, before is not None), gri...  22.9 us
    gather x8, local copies, waits for them, and re-layouts, local(): total = total + huber(jnp.take(own, neighbour_map[k], axis=0) - own)  20.1 us
    ppermute x2, waiting for transfers between devices, local(): beyond = lax.ppermute(twin, ('core',) + CELLS, halo_pairs(ranks))  19.5 us
    all_to_all x2, starting transfers between devices, local(): pieces = lax.all_to_all(partial.reshape(ranks, rows, -1), CELLS, 0, 0)  14.3 us
  transfers between devices with their start and end apart: 10, of which 7 were waited for; matrix products, arithmetic and copies ran while one was open for 11% of the time, Pallas kernels for 7%

profile of v2, /device:TPU:31, one launch (start us, length us, event | category | flops | bytes accessed | tf_op | source)
XLA Modules:
  0.0 262.4 jit_solution(11927912600361051652)
XLA Ops:
  1.5 5.5 %shard_map.55.refs_0_ = f32[2048,256]{1,0:T(8,128)S(1)} custom-call(s32[1]{0:T(128)} %bitcast.1.plane_ref, f32[2048,1536]{1,0:T(8,128)} %s_ref.15, f32[768,256]{1,0:T(8,128)S(1)} %get-tuple-element.20.x_ref), custom_call_target="tpu_custom_call" | custom-call | flops 2415919104 | bytes 9175040 | tf_op jit(solution)/shard_map/pallas_call | solution.py:65
  7.0 6.5 %shard_map.56 = f32[2048,256]{1,0:T(8,128)} custom-call(s32[1]{0:T(128)} %bitcast.plane_ref, f32[2048,1536]{1,0:T(8,128)} %s_ref.15, f32[768,256]{1,0:T(8,128)S(1)} %get-tuple-element.26.x_ref, f32[2048,256]{1,0:T(8,128)S(1)} %shard_map.55.refs_0_), custom_call_target="tpu_custom_call" | custom-call | flops 2415919104 | bytes 9175040 | tf_op jit(solution)/shard_map/pallas_call | solution.py:65
  13.4 9.0 %all-to-all-start = ((f32[32,64,256]{2,1,0:T(8,128)}), f32[32,64,256]{2,1,0:T(8,128)}, u32[]{:S(2)}, u32[]{:S(2)}) async-start(f32[32,64,256]{2,1,0:T(8,128)} %bitcast.2), calls=%async_computation | async-start | bytes 4194304 | tf_op jit(solution)/shard_map/all_to_all | solution.py:151
  22.5 2.1 gather_fusion.3
  24.7 2.1 gather_fusion.2
  26.8 2.9 %gather_fusion.1 = f32[768,256]{1,0:T(8,128)} fusion(f32[768,256]{1,0:T(8,128)S(1)} %get-tuple-element.20.x_ref, s32[1024]{0:T(1024)S(1)} %pad_clamp_fusion.2), kind=kCustom, calls=%fused_computation.1.clone | custom fusion | bytes 1575936 | tf_op jit(solution)/shard_map/jit(_take)/gather | solution.py:154
  29.7 2.9 %gather_fusion = f32[768,256]{1,0:T(8,128)} fusion(f32[768,256]{1,0:T(8,128)S(1)} %get-tuple-element.20.x_ref, s32[1024]{0:T(1024)S(1)} %pad_clamp_fusion.3), kind=kCustom, calls=%fused_computation.clone | custom fusion | bytes 1575936 | tf_op jit(solution)/shard_map/jit(_take)/gather | solution.py:154
  32.7 3.7 %multiply_add_fusion.3 = f32[768,256]{1,0:T(8,128)} fusion(f32[768,256]{1,0:T(8,128)S(1)} %get-tuple-element.20.x_ref, f32[768,256]{1,0:T(8,128)S(1)} %gather_fusion.3, f32[768,256]{1,0:T(8,128)S(1)} %gather_fusion.2, f32[768,256]{1,0:T(8,128)} %gather_fusion.1, f32[768,256]{1,0:T(8,128)} %gather_fusion, f32[768,256]{1,0:T(8,128)S(1)} %get-tuple-element.26.x_ref, ...), kind=kLoop, calls=%fused_computation.20 | loop fusion | flops 5505024 | bytes 5508096 | tf_op jit(solution)/shard_map/add | solution.py:154
  36.4 12.6 %all-to-all-done = f32[32,64,256]{2,1,0:T(8,128)} async-done(((f32[32,64,256]{2,1,0:T(8,128)}), f32[32,64,256]{2,1,0:T(8,128)}, u32[]{:S(2)}, u32[]{:S(2)}) %all-to-all-start) | async-done | bytes 2097184 | tf_op jit(solution)/shard_map/all_to_all | solution.py:151
  51.8 33.8 %all_to_all.20 = f32[32,64,256]{2,1,0:T(8,128)S(1)} all-to-all(f32[32,64,256]{2,1,0:T(8,128)S(1)} %broadcast_in_dim.59), channel_id=1, replica_groups=mesh['yh'=2,'core'=2,'yl'=2,'x'=4,'z'=4] {'yl','x','z'}, dimensions={0} | all-to-all | bytes 4194304 | tf_op jit(solution)/shard_map/all_to_all | solution.py:158
  85.6 6.0 %shard_map.58 = f32[768,256]{1,0:T(8,128)S(1)} custom-call(s32[1]{0:T(128)} %bitcast.plane_ref, f32[2048,1536]{1,0:T(8,128)} %s_ref.15, f32[2048,256]{1,0:T(8,128)S(1)} %bitcast.12), custom_call_target="tpu_custom_call" | custom-call | flops 2415919104 | bytes 9175040 | tf_op jit(solution)/shard_map/pallas_call | solution.py:100
  93.1 6.0 %shard_map.57 = f32[768,256]{1,0:T(8,128)S(1)} custom-call(s32[1]{0:T(128)} %bitcast.1.plane_ref, f32[2048,1536]{1,0:T(8,128)} %s_ref.15, f32[2048,256]{1,0:T(8,128)S(1)} %bitcast.13), custom_call_target="tpu_custom_call" | custom-call | flops 2415919104 | bytes 9175040 | tf_op jit(solution)/shard_map/pallas_call | solution.py:100
  99.2 2.6 collective-permute-start.2
  102.9 9.5 %collective-permute-done.2 = f32[768,256]{1,0:T(8,128)S(1)} collective-permute-done((f32[768,256]{1,0:T(8,128)S(1)}, f32[768,256]{1,0:T(8,128)S(1)}, u32[]{:S(2)}, u32[]{:S(2)}) %collective-permute-start.2) | collective-permute-done | bytes 786464 | tf_op jit(solution)/shard_map/ppermute | solution.py:163
  112.4 18.9 %collective-permute-done.1 = f32[768,256]{1,0:T(8,128)S(1)} collective-permute-done((f32[768,256]{1,0:T(8,128)S(1)}, f32[768,256]{1,0:T(8,128)S(1)}, u32[]{:S(2)}, u32[]{:S(2)}) %collective-permute-start.1) | collective-permute-done | bytes 786464 | tf_op jit(solution)/shard_map/ppermute | solution.py:126
  132.1 5.5 %shard_map.59.refs_0_ = f32[2048,256]{1,0:T(8,128)S(1)} custom-call(s32[1]{0:T(128)} %bitcast.1.plane_ref, f32[2048,1536]{1,0:T(8,128)} %s_ref.15, f32[768,256]{1,0:T(8,128)S(1)} %multiply_add_fusion.2.x_ref), custom_call_target="tpu_custom_call" | custom-call | flops 2415919104 | bytes 9175040 | tf_op jit(solution)/shard_map/pallas_call | solution.py:65
  137.6 5.5 %shard_map.60 = f32[2048,256]{1,0:T(8,128)S(1)} custom-call(s32[1]{0:T(128)} %bitcast.plane_ref, f32[2048,1536]{1,0:T(8,128)} %s_ref.15, f32[768,256]{1,0:T(8,128)S(1)} %collective-permute-done.3.x_ref, f32[2048,256]{1,0:T(8,128)S(1)} %shard_map.59.refs_0_), custom_call_target="tpu_custom_call" | custom-call | flops 2415919104 | bytes 9175040 | tf_op jit(solution)/shard_map/pallas_call | solution.py:65
  144.4 5.3 %all-to-all-start.2 = ((f32[32,64,256]{2,1,0:T(8,128)}), f32[32,64,256]{2,1,0:T(8,128)}, u32[]{:S(2)}, u32[]{:S(2)}) async-start(f32[32,64,256]{2,1,0:T(8,128)} %bitcast.14), calls=%async_computation.2 | async-start | bytes 4194304 | tf_op jit(solution)/shard_map/all_to_all | solution.py:151
  149.7 2.1 gather_fusion.7
  151.8 2.1 gather_fusion.6
  153.9 2.9 %gather_fusion.5 = f32[768,256]{1,0:T(8,128)} fusion(f32[768,256]{1,0:T(8,128)S(1)} %multiply_add_fusion.2.x_ref, s32[1024]{0:T(1024)S(1)} %pad_clamp_fusion.2), kind=kCustom, calls=%fused_computation.5.clone | custom fusion | bytes 1575936 | tf_op jit(solution)/shard_map/jit(_take)/gather | solution.py:154
  156.9 2.9 %gather_fusion.4 = f32[768,256]{1,0:T(8,128)} fusion(f32[768,256]{1,0:T(8,128)S(1)} %multiply_add_fusion.2.x_ref, s32[1024]{0:T(1024)S(1)} %pad_clamp_fusion.3), kind=kCustom, calls=%fused_computation.4.clone | custom fusion | bytes 1575936 | tf_op jit(solution)/shard_map/jit(_take)/gather | solution.py:154
  159.8 3.7 %multiply_add_fusion.1 = f32[768,256]{1,0:T(8,128)} fusion(f32[768,256]{1,0:T(8,128)S(1)} %multiply_add_fusion.2.x_ref, f32[768,256]{1,0:T(8,128)S(1)} %gather_fusion.7, f32[768,256]{1,0:T(8,128)S(1)} %gather_fusion.6, f32[768,256]{1,0:T(8,128)} %gather_fusion.5, f32[768,256]{1,0:T(8,128)} %gather_fusion.4, f32[768,256]{1,0:T(8,128)S(1)} %collective-permute-done.3.x_ref, ...), kind=kLoop, calls=%fused_computation.18 | loop fusion | flops 5505024 | bytes 5508096 | tf_op jit(solution)/shard_map/add | solution.py:154
  163.5 14.4 %all-to-all-done.2 = f32[32,64,256]{2,1,0:T(8,128)} async-done(((f32[32,64,256]{2,1,0:T(8,128)}), f32[32,64,256]{2,1,0:T(8,128)}, u32[]{:S(2)}, u32[]{:S(2)}) %all-to-all-start.2) | async-done | bytes 2097184 | tf_op jit(solution)/shard_map/all_to_all | solution.py:151
  180.7 30.6 %all_to_all.21 = f32[32,64,256]{2,1,0:T(8,128)S(1)} all-to-all(f32[32,64,256]{2,1,0:T(8,128)S(1)} %broadcast_in_dim.60), channel_id=1, replica_groups=mesh['yh'=2,'core'=2,'yl'=2,'x'=4,'z'=4] {'yl','x','z'}, dimensions={0} | all-to-all | bytes 4194304 | tf_op jit(solution)/shard_map/all_to_all | solution.py:158
  211.3 6.0 %shard_map.62 = f32[768,256]{1,0:T(8,128)S(1)} custom-call(s32[1]{0:T(128)} %bitcast.plane_ref, f32[2048,1536]{1,0:T(8,128)} %s_ref.15, f32[2048,256]{1,0:T(8,128)S(1)} %bitcast.10), custom_call_target="tpu_custom_call" | custom-call | flops 2415919104 | bytes 9175040 | tf_op jit(solution)/shard_map/pallas_call | solution.py:100
  217.3 3.2 %collective-permute-start.4 = (f32[768,256]{1,0:T(8,128)S(1)}, f32[768,256]{1,0:T(8,128)S(1)}, u32[]{:S(2)}, u32[]{:S(2)}) collective-permute-start(f32[768,256]{1,0:T(8,128)S(1)} %shard_map.62), channel_id=1, source_target_pairs={{0,32},{32,0},{1,33},{33,1},{2,34},{34,2},{3,35},{35,3},{4,36},{36... | collective-permute-start | bytes 2359304 | tf_op jit(solution)/shard_map/ppermute | solution.py:126
  220.5 6.0 %shard_map.61 = f32[768,256]{1,0:T(8,128)S(1)} custom-call(s32[1]{0:T(128)} %bitcast.1.plane_ref, f32[2048,1536]{1,0:T(8,128)} %s_ref.15, f32[2048,256]{1,0:T(8,128)S(1)} %bitcast.11), custom_call_target="tpu_custom_call" | custom-call | flops 2415919104 | bytes 9175040 | tf_op jit(solution)/shard_map/pallas_call | solution.py:100
  226.6 2.1 collective-permute-start.6
  229.8 10.0 %collective-permute-done.6 = f32[768,256]{1,0:T(8,128)S(1)} collective-permute-done((f32[768,256]{1,0:T(8,128)S(1)}, f32[768,256]{1,0:T(8,128)S(1)}, u32[]{:S(2)}, u32[]{:S(2)}) %collective-permute-start.6) | collective-permute-done | bytes 786464 | tf_op jit(solution)/shard_map/ppermute | solution.py:163
  239.8 18.2 %collective-permute-done.5 = f32[768,256]{1,0:T(8,128)S(1)} collective-permute-done((f32[768,256]{1,0:T(8,128)S(1)}, f32[768,256]{1,0:T(8,128)S(1)}, u32[]{:S(2)}, u32[]{:S(2)}) %collective-permute-start.5) | collective-permute-done | bytes 786464 | tf_op jit(solution)/shard_map/ppermute | solution.py:126
  259.2 1.8 collective-permute-done.7
  (43 shorter events, 15.7 us)
Async XLA Ops:
  13.4 9.0 %copy-start.3 = (s32[4,768]{1,0:T(4,128)S(1)}, s32[4,768]{1,0:T(4,128)}, u32[]{:S(2)}) copy-start(s32[4,768]{1,0:T(4,128)} %param.10) | copy-start | bytes 36868
  13.4 35.6 %all-to-all-start = ((f32[32,64,256]{2,1,0:T(8,128)}), f32[32,64,256]{2,1,0:T(8,128)}, u32[]{:S(2)}, u32[]{:S(2)}) async-start(f32[32,64,256]{2,1,0:T(8,128)} %bitcast.2), calls=%async_computation | async-start | bytes 4194304 | tf_op jit(solution)/shard_map/all_to_all | solution.py:151
  91.6 7.5 %collective-permute-start = (f32[768,256]{1,0:T(8,128)S(1)}, f32[768,256]{1,0:T(8,128)S(1)}, u32[]{:S(2)}, u32[]{:S(2)}) collective-permute-start(f32[768,256]{1,0:T(8,128)S(1)} %shard_map.58), channel_id=1, source_target_pairs={{0,32},{32,0},{1,33},{33,1},{2,34},{34,2},{3,35},{35,3},{4,36},{36... | collective-permute-start | bytes 2359304 | tf_op jit(solution)/shard_map/ppermute | solution.py:126
  99.1 3.8 %copy-start.4 = (s32[1536]{0:T(1024)S(1)}, s32[1536]{0:T(1024)}, u32[]{:S(2)}) copy-start(s32[1536]{0:T(1024)} %param.11) | copy-start | bytes 18436
  99.1 32.2 %copy-start.2 = (f32[768,256]{1,0:T(8,128)S(1)}, f32[768,256]{1,0:T(8,128)}, u32[]{:S(2)}) copy-start(f32[768,256]{1,0:T(8,128)} %multiply_add_fusion.3) | copy-start | bytes 2359300
  99.2 13.2 %collective-permute-start.2 = (f32[768,256]{1,0:T(8,128)S(1)}, f32[768,256]{1,0:T(8,128)S(1)}, u32[]{:S(2)}, u32[]{:S(2)}) collective-permute-start(f32[768,256]{1,0:T(8,128)S(1)} %get-tuple-element.26.x_ref), channel_id=1, source_target_pairs={{0,1},{1,2},{2,3},{3,4},{4,5},{5,6},{6,7},{7,8},{8,9},{9,10},{10,1... | collective-permute-start | bytes 2359304 | tf_op jit(solution)/shard_map/ppermute | solution.py:163
  101.9 29.4 %collective-permute-start.1 = (f32[768,256]{1,0:T(8,128)S(1)}, f32[768,256]{1,0:T(8,128)S(1)}, u32[]{:S(2)}, u32[]{:S(2)}) collective-permute-start(f32[768,256]{1,0:T(8,128)S(1)} %add.120), channel_id=1, source_target_pairs={{0,64},{64,0},{1,65},{65,1},{2,66},{66,2},{3,67},{67,3},{4,68},{68... | collective-permute-start | bytes 2359304 | tf_op jit(solution)/shard_map/ppermute | solution.py:126
  131.6 6.0 %collective-permute-start.3 = (f32[768,256]{1,0:T(8,128)S(1)}, f32[768,256]{1,0:T(8,128)S(1)}, u32[]{:S(2)}, u32[]{:S(2)}) collective-permute-start(f32[768,256]{1,0:T(8,128)S(1)} %multiply_add_fusion.2.x_ref), channel_id=1, source_target_pairs={{0,32},{32,0},{1,33},{33,1},{2,34},{34,2},{3,35},{35,3},{4,36},{36... | collective-permute-start | bytes 2359304 | tf_op jit(solution)/shard_map/ppermute | solution.py:126
  143.1 1.3 copy-start
  144.4 33.5 %all-to-all-start.2 = ((f32[32,64,256]{2,1,0:T(8,128)}), f32[32,64,256]{2,1,0:T(8,128)}, u32[]{:S(2)}, u32[]{:S(2)}) async-start(f32[32,64,256]{2,1,0:T(8,128)} %bitcast.14), calls=%async_computation.2 | async-start | bytes 4194304 | tf_op jit(solution)/shard_map/all_to_all | solution.py:151
  217.3 9.2 %collective-permute-start.4 = (f32[768,256]{1,0:T(8,128)S(1)}, f32[768,256]{1,0:T(8,128)S(1)}, u32[]{:S(2)}, u32[]{:S(2)}) collective-permute-start(f32[768,256]{1,0:T(8,128)S(1)} %shard_map.62), channel_id=1, source_target_pairs={{0,32},{32,0},{1,33},{33,1},{2,34},{34,2},{3,35},{35,3},{4,36},{36... | collective-permute-start | bytes 2359304 | tf_op jit(solution)/shard_map/ppermute | solution.py:126
  226.5 31.5 %copy-start.1 = (f32[768,256]{1,0:T(8,128)S(1)}, f32[768,256]{1,0:T(8,128)}, u32[]{:S(2)}) copy-start(f32[768,256]{1,0:T(8,128)} %multiply_add_fusion.1) | copy-start | bytes 2359300
  226.6 13.2 %collective-permute-start.6 = (f32[768,256]{1,0:T(8,128)S(1)}, f32[768,256]{1,0:T(8,128)S(1)}, u32[]{:S(2)}, u32[]{:S(2)}) collective-permute-start(f32[768,256]{1,0:T(8,128)S(1)} %collective-permute-done.3.x_ref), channel_id=1, source_target_pairs={{0,1},{1,2},{2,3},{3,4},{4,5},{5,6},{6,7},{7,8},{8,9},{9,10},{10,1... | collective-permute-start | bytes 2359304 | tf_op jit(solution)/shard_map/ppermute | solution.py:163
  228.7 29.2 %collective-permute-start.5 = (f32[768,256]{1,0:T(8,128)S(1)}, f32[768,256]{1,0:T(8,128)S(1)}, u32[]{:S(2)}, u32[]{:S(2)}) collective-permute-start(f32[768,256]{1,0:T(8,128)S(1)} %add.134), channel_id=1, source_target_pairs={{0,64},{64,0},{1,65},{65,1},{2,66},{66,2},{3,67},{67,3},{4,68},{68... | collective-permute-start | bytes 2359304 | tf_op jit(solution)/shard_map/ppermute | solution.py:126
  258.3 2.7 %collective-permute-start.7 = (f32[768,256]{1,0:T(8,128)S(1)}, f32[768,256]{1,0:T(8,128)S(1)}, u32[]{:S(2)}, u32[]{:S(2)}) collective-permute-start(f32[768,256]{1,0:T(8,128)S(1)} %multiply_add_fusion), channel_id=1, source_target_pairs={{0,32},{32,0},{1,33},{33,1},{2,34},{34,2},{3,35},{35,3},{4,36},{36... | collective-permute-start | bytes 2359304 | tf_op jit(solution)/shard_map/ppermute | solution.py:126

commit v3 on v1

v3 whole, which is shorter than its diff:
```python
import functools

import jax
import jax.numpy as jnp
from jax import lax
from jax.experimental import pallas as pl
from jax.experimental.pallas import tpu as pltpu
from jax.sharding import Mesh, PartitionSpec as P

ITERS = 2
DATA = ("yh", "core")
CELLS = ("yl", "x", "z")
ALL = DATA + CELLS
ROWS = 256
TALL = 1024
SLOTS = 4
PARAMS = pltpu.CompilerParams(vmem_limit_bytes=24 * 1024 * 1024)
VMEM = pl.BlockSpec(memory_space=pltpu.VMEM)
SMEM = pl.BlockSpec(memory_space=pltpu.SMEM)
ANY = pl.BlockSpec(memory_space=pl.ANY)
F32 = jnp.float32
BF16 = jnp.bfloat16


def huber(diff):
    return diff / jnp.sqrt(1.0 + diff * diff)


def split(value):
    high = value.astype(BF16)
    low = (value - high.astype(F32)).astype(BF16)
    return high, low


def dot(a, b):
    return jnp.dot(a, b, preferred_element_type=F32)


def product(a, b):
    return dot(a[0], b[0]) + (dot(a[0], b[1]) + dot(a[1], b[0]))


def block_of(index, size):
    return pl.ds(pl.multiple_of(index * size, size), size)


def cost(data, cells, sols, wide):
    return pl.CostEstimate(
        flops=6 * data * cells * sols,
        bytes_accessed=4 * (wide * data * cells + cells * sols + data * sols),
        transcendentals=0,
    )


def first_kernel(s_ref, x_ref, p_ref, high_ref, low_ref, xh_ref, xl_ref, in_ref, out_ref, in_sem, out_sem):
    blocks = s_ref.shape[0] // ROWS

    def fetch(i):
        slot = lax.rem(i, SLOTS)
        return pltpu.make_async_copy(s_ref.at[block_of(i, ROWS)], in_ref.at[slot], in_sem.at[slot])

    def flush(i):
        rows = block_of(i, ROWS)
        return pltpu.make_async_copy(out_ref.at[rows], p_ref.at[rows], out_sem.at[i])

    for i in range(SLOTS):
        fetch(i).start()
    xh_ref[...], xl_ref[...] = split(x_ref[...])

    @pl.loop(0, blocks)
    def _(i):
        fetch(i).wait()
        high, low = split(in_ref[lax.rem(i, SLOTS)])
        rows = block_of(i, ROWS)
        high_ref[rows, :] = high
        low_ref[rows, :] = low

        @pl.when(i + SLOTS < blocks)
        def _():
            fetch(i + SLOTS).start()

        out_ref[rows, :] = product((high, low), (xh_ref[...], xl_ref[...]))
        flush(i).start()

    @pl.loop(0, blocks)
    def _(i):
        flush(i).wait()


def first_forward(sensitivity, x):
    data, cells = sensitivity.shape
    sols = x.shape[1]
    return pl.pallas_call(
        first_kernel,
        in_specs=[pl.BlockSpec(memory_space=pltpu.HBM), VMEM],
        out_specs=[ANY, VMEM, VMEM],
        out_shape=[
            jax.ShapeDtypeStruct((data, sols), F32),
            pltpu.VMEM((data, cells), BF16),
            pltpu.VMEM((data, cells), BF16),
        ],
        scratch_shapes=[
            pltpu.VMEM((cells, sols), BF16),
            pltpu.VMEM((cells, sols), BF16),
            pltpu.VMEM((SLOTS, ROWS, cells), F32),
            pltpu.VMEM((data, sols), F32),
            pltpu.SemaphoreType.DMA((SLOTS,)),
            pltpu.SemaphoreType.DMA((data // ROWS,)),
        ],
        compiler_params=PARAMS,
        cost_estimate=cost(data, cells, sols, 1),
    )(pltpu.with_memory_space_constraint(sensitivity, pltpu.HBM), x)


def start_kernel(plane_ref, high_ref, low_ref, x_ref, p_ref, xh_ref, xl_ref):
    columns = block_of(plane_ref[0], x_ref.shape[0])
    xh_ref[...], xl_ref[...] = split(x_ref[...])

    @pl.loop(0, p_ref.shape[0] // TALL)
    def _(i):
        rows = block_of(i, TALL)
        sense = (high_ref[rows, columns], low_ref[rows, columns])
        p_ref[rows, :] = product(sense, (xh_ref[...], xl_ref[...]))


def finish_kernel(plane_ref, high_ref, low_ref, x_ref, before_ref, p_ref, xh_ref, xl_ref):
    columns = block_of(plane_ref[0], x_ref.shape[0])
    xh_ref[...], xl_ref[...] = split(x_ref[...])

    @pl.loop(0, p_ref.shape[0] // TALL)
    def _(i):
        rows = block_of(i, TALL)
        sense = (high_ref[rows, columns], low_ref[rows, columns])
        p_ref[rows, :] = before_ref[rows, :] + product(sense, (xh_ref[...], xl_ref[...]))


def pinned(sense):
    return [pltpu.with_memory_space_constraint(half, pltpu.VMEM) for half in sense]


def forward(plane, sense, x, before=None):
    data = sense[0].shape[0]
    cells, sols = x.shape
    args = [plane, *pinned(sense), x]
    if before is not None:
        args += pinned([before])
    return pl.pallas_call(
        start_kernel if before is None else finish_kernel,
        in_specs=[SMEM] + [VMEM] * (len(args) - 1),
        out_specs=VMEM,
        out_shape=pltpu.VMEM((data, sols), F32),
        scratch_shapes=[pltpu.VMEM((cells, sols), BF16), pltpu.VMEM((cells, sols), BF16)],
        compiler_params=PARAMS,
        cost_estimate=cost(data, cells, sols, 0),
    )(*args)


def away_kernel(plane_ref, high_ref, low_ref, w_ref, g_ref, wh_ref, wl_ref):
    wh_ref[...], wl_ref[...] = split(w_ref[...].T)
    home_kernel(plane_ref, high_ref, low_ref, wh_ref, wl_ref, g_ref)


def home_kernel(plane_ref, high_ref, low_ref, wh_ref, wl_ref, g_ref):
    blocks = g_ref.shape[0] // ROWS

    @pl.loop(0, blocks)
    def _(i):
        columns = block_of(plane_ref[0] * blocks + i, ROWS)
        part = product((wh_ref[...], wl_ref[...]), (high_ref[:, columns], low_ref[:, columns]))
        g_ref[block_of(i, ROWS), :] = part.T


def backward(away, home, sense, w, cells):
    data, sols = w.shape
    other, high, low = pl.pallas_call(
        away_kernel,
        in_specs=[SMEM, VMEM, VMEM, VMEM],
        out_specs=[VMEM, VMEM, VMEM],
        out_shape=[
            jax.ShapeDtypeStruct((cells, sols), F32),
            pltpu.VMEM((sols, data), BF16),
            pltpu.VMEM((sols, data), BF16),
        ],
        compiler_params=PARAMS,
        cost_estimate=cost(data, cells, sols, 0),
    )(away, *pinned(sense), w)
    own = pl.pallas_call(
        home_kernel,
        in_specs=[SMEM, VMEM, VMEM, VMEM, VMEM],
        out_specs=VMEM,
        out_shape=jax.ShapeDtypeStruct((cells, sols), F32),
        compiler_params=PARAMS,
        cost_estimate=cost(data, cells, sols, 0),
    )(home, *pinned(sense), *pinned((high, low)))
    return other, own


def weigh_kernel(rank_ref, pieces_ref, observed_ref, copies_ref):
    misfit = jnp.sum(pieces_ref[...], axis=0) - observed_ref[...]
    weighted = misfit / jnp.maximum(jnp.abs(misfit), 1.0)
    copies_ref[...] = jnp.broadcast_to(weighted[None], copies_ref.shape)


def weigh(rank, pieces, observed):
    ranks, rows, sols = pieces.shape
    return pl.pallas_call(
        weigh_kernel,
        grid_spec=pltpu.PrefetchScalarGridSpec(
            num_scalar_prefetch=1,
            grid=(1,),
            in_specs=[
                pl.BlockSpec((ranks, rows, sols), lambda i, rank: (0, 0, 0)),
                pl.BlockSpec((rows, sols), lambda i, rank: (rank[0], 0)),
            ],
            out_specs=pl.BlockSpec((ranks, rows, sols), lambda i, rank: (0, 0, 0)),
        ),
        out_shape=jax.ShapeDtypeStruct(pieces.shape, F32),
        compiler_params=PARAMS,
    )(rank, pieces, observed)


def smooth_kernel(table_ref, own_ref, twin_ref, beyond_ref, total_ref, parts_ref, turned_ref):
    cells, sols = own_ref.shape
    whole = own_ref[...]
    high = whole.astype(BF16)
    rest = whole - high.astype(F32)
    middle = rest.astype(BF16)
    low = (rest - middle.astype(F32)).astype(BF16)
    parts_ref[...] = jnp.concatenate([high, middle, low], axis=1)
    turned_ref[...] = table_ref[...].T
    lanes = lax.broadcasted_iota(jnp.int32, (ROWS, cells), 1).astype(F32)

    @pl.loop(0, cells // ROWS)
    def _(i):
        rows = block_of(i, ROWS)
        own = own_ref[rows, :]
        total = huber(twin_ref[rows, :] - own) + huber(beyond_ref[rows, :] - own)
        for k in range(4):
            chosen = (lanes == turned_ref[rows, k : k + 1]).astype(F32).astype(BF16)
            taken = dot(chosen, parts_ref[...])
            other = taken[:, :sols] + taken[:, sols : 2 * sols] + taken[:, 2 * sols :]
            total = total + huber(other - own)
        total_ref[rows, :] = turned_ref[rows, 4:5] * total


def smooth_of(table, own, twin, beyond):
    cells, sols = own.shape
    return pl.pallas_call(
        smooth_kernel,
        in_specs=[VMEM] * 4,
        out_specs=VMEM,
        out_shape=jax.ShapeDtypeStruct(own.shape, F32),
        scratch_shapes=[pltpu.VMEM((cells, 3 * sols), BF16), pltpu.VMEM((cells, table.shape[0]), F32)],
        compiler_params=PARAMS,
        cost_estimate=pl.CostEstimate(
            flops=24 * cells * cells * sols,
            bytes_accessed=16 * cells * sols,
            transcendentals=12 * cells * sols,
        ),
    )(table, own, twin, beyond)


def swap(value, axis):
    return lax.ppermute(value, axis, [(0, 1), (1, 0)])


def beyond_of(own, ranks):
    up = [(ranks + i, i + 1) for i in range(ranks - 1)]
    down = [(i + 1, ranks + i) for i in range(ranks - 1)]
    return lax.ppermute(own, ("core",) + CELLS, up + down)


def local(sensitivity, observed, models, neighbour_map, edge_mask):
    core = lax.axis_index("core").astype(jnp.int32)
    rank = lax.axis_index(CELLS).astype(jnp.int32).reshape(1)
    ranks = lax.axis_size(CELLS)
    cells = neighbour_map.shape[1]
    rows = observed.shape[0] // ranks
    own_mask = lax.dynamic_slice_in_dim(edge_mask, core * cells, cells, axis=0)
    scale = 0.05 * (1.0 - 0.75 * own_mask.astype(F32))
    table = jnp.concatenate(
        [neighbour_map.astype(F32), scale[None], jnp.zeros((3, cells), F32)], axis=0
    )
    own = lax.dynamic_slice_in_dim(models, core * cells, cells, axis=0)
    twin = lax.dynamic_slice_in_dim(models, (1 - core) * cells, cells, axis=0)
    mine, theirs = core.reshape(1), (1 - core).reshape(1)
    models, own, twin, table, rank, mine, theirs = lax.optimization_barrier(
        (models, own, twin, table, rank, mine, theirs)
    )
    sense = None
    for step in range(ITERS):
        if step == 0:
            beyond = beyond_of(own, ranks)
            partial, *sense = first_forward(sensitivity, models)
        else:
            partial = forward(mine, sense, own)
            twin = swap(own, "core")
            beyond = beyond_of(own, ranks)
            partial = forward(theirs, sense, twin, partial)
        partial, beyond = lax.optimization_barrier((partial, beyond))
        pieces = lax.all_to_all(partial.reshape(ranks, rows, -1), CELLS, 0, 0)
        copies = weigh(rank, pieces, observed)
        weighted = lax.all_to_all(copies, CELLS, 0, 0).reshape(ranks * rows, -1)
        away, home = backward(theirs, mine, sense, weighted, cells)
        half = home + swap(away, "core")
        half, own, twin, beyond = lax.optimization_barrier((half, own, twin, beyond))
        gradient = half + swap(half, "yh")
        own = own - 1.0 * gradient + smooth_of(table, own, twin, beyond)
    twin = swap(own, "core")
    place = lax.broadcasted_iota(jnp.int32, (2, 1, 1), 0)
    both = jnp.where(place == core, own[None], twin[None])
    return both.reshape(models.shape)


def solution(mesh):
    fine = Mesh(mesh.devices.reshape(2, 2, 2, 4, 4), ALL)
    return jax.shard_map(
        local,
        mesh=fine,
        in_specs=(P(DATA, CELLS), P(DATA, None), P(CELLS, None), P(), P(CELLS)),
        out_specs=P(CELLS, None),
        check_vma=False,
    )
```

time: 264 us -> 234 us (0.89)
  the two profiles are of different devices: /device:TPU:15 before, /device:TPU:25 now
where the time goes in v3:
time: 234 us; the launch traced here: 232 us
  blocking collectives  138 us (59%)
  Pallas kernels  42.6 us (18%)
  waiting for transfers between devices  35.6 us (15%)
  starting transfers between devices  10.7 us (5%)
  other arithmetic  3.72 us (2%)
    all_to_all x2, blocking collectives, local(): pieces = lax.all_to_all(partial.reshape(ranks, rows, -1), CELLS, 0, 0)  72.8 us
    all_to_all x2, blocking collectives, local(): weighted = lax.all_to_all(copies, CELLS, 0, 0).reshape(ranks * rows, -1)  65.2 us
    ppermute x6, waiting for transfers between devices, swap(): return lax.ppermute(value, axis, [(0, 1), (1, 0)])  28 us
    pallas_call x2, Pallas kernels, smooth_of(): pl.pallas_call(smooth_kernel, in_specs=[VMEM] * 4, out_specs=VMEM, out_sh...  13.8 us
    pallas_call x1, Pallas kernels, first_forward(): pl.pallas_call(first_kernel, in_specs=[pl.BlockSpec(memory_space=pltpu.HB...  8.1 us
    pallas_call x2, Pallas kernels, backward(): pl.pallas_call(away_kernel, in_specs=[SMEM, VMEM, VMEM, VMEM], out_specs=...  7.76 us
    ppermute x2, waiting for transfers between devices, beyond_of(): return lax.ppermute(own, ('core',) + CELLS, up + down)  7.62 us
    pallas_call x2, Pallas kernels, backward(): pl.pallas_call(home_kernel, in_specs=[SMEM, VMEM, VMEM, VMEM, VMEM], out_...  6.5 us
  transfers between devices with their start and end apart: 8, of which 5 were waited for; matrix products, arithmetic and copies ran while one was open for 0% of the time, Pallas kernels for 15%

profile of v3, /device:TPU:25, one launch (start us, length us, event | category | flops | bytes accessed | tf_op | source)
XLA Modules:
  0.0 232.4 jit_solution(5697175172778206341)
XLA Ops:
  0.0 0.9 subtract_multiply_fusion
  0.9 0.7 convert_element_type.6
  1.6 1.5 constant_dynamic-slice_fusion
  3.2 4.1 %collective-permute-start = (f32[768,256]{1,0:T(8,128)S(1)}, f32[768,256]{1,0:T(8,128)S(1)}, u32[]{:S(2)}, u32[]{:S(2)}) collective-permute-start(f32[768,256]{1,0:T(8,128)S(1)} %get-tuple-element.47.own_ref), channel_id=1, source_target_pairs={{32,1},{33,2},{34,3},{35,4},{36,5},{37,6},{38,7},{39,8},{40,9},{41... | collective-permute-start | bytes 2359304 | tf_op jit(solution)/shard_map/ppermute | solution.py:270
  7.4 8.1 %shard_map.55 = (f32[2048,256]{1,0:T(8,128)S(1)}, bf16[2048,1536]{1,0:T(8,128)(2,1)S(1)}, bf16[2048,1536]{1,0:T(8,128)(2,1)S(1)}) custom-call(f32[2048,1536]{1,0:T(8,128)} %s_ref.1, f32[1536,256]{1,0:T(8,128)S(1)} %copy-done.1), custom_call_target="tpu_custom_call" | custom-call | flops 4831838208 | bytes 16252928 | tf_op jit(solution)/shard_map/pallas_call | solution.py:93
  15.5 1.8 collective-permute-done.beyond_ref
  17.3 37.4 %all_to_all.20.pieces_ref = f32[32,64,256]{2,1,0:T(8,128)S(1)} all-to-all(f32[32,64,256]{2,1,0:T(8,128)S(1)} %bitcast.14), channel_id=1, replica_groups=mesh['yh'=2,'core'=2,'yl'=2,'x'=4,'z'=4] {'yl','x','z'}, dimensions={0} | all-to-all | bytes 4194304 | tf_op jit(solution)/shard_map/all_to_all | solution.py:301
  54.7 0.3 shard_map.56
  55.0 32.5 %all_to_all.21 = f32[32,64,256]{2,1,0:T(8,128)S(1)} all-to-all(f32[32,64,256]{2,1,0:T(8,128)S(1)} %shard_map.56), channel_id=1, replica_groups=mesh['yh'=2,'core'=2,'yl'=2,'x'=4,'z'=4] {'yl','x','z'}, dimensions={0} | all-to-all | bytes 4194304 | tf_op jit(solution)/shard_map/all_to_all | solution.py:303
  87.6 3.9 %shard_map.57 = (f32[768,256]{1,0:T(8,128)S(1)}, bf16[256,2048]{1,0:T(8,128)(2,1)S(1)}, bf16[256,2048]{1,0:T(8,128)(2,1)S(1)}) custom-call(s32[1]{0:T(128)} %bitcast.2.plane_ref, bf16[2048,1536]{1,0:T(8,128)(2,1)S(1)} %get-tuple-element.35.high_ref, bf16[2048,1536]{1,0:T(8,128)(2,1)S(1)} %get-tuple-element.36.low_ref, f32[2048,256]{1,0:T(8,128)S(1)} %bitcast.12), custom_call_target="tpu_custom_call" | custom-call | flops 2415919104 | bytes 2883584 | tf_op jit(solution)/shard_map/pallas_call | solution.py:175
  91.5 0.5 collective-permute-start.1
  92.0 3.2 %shard_map.58 = f32[768,256]{1,0:T(8,128)S(1)} custom-call(s32[1]{0:T(128)} %bitcast.1.plane_ref, bf16[2048,1536]{1,0:T(8,128)(2,1)S(1)} %get-tuple-element.35.high_ref, bf16[2048,1536]{1,0:T(8,128)(2,1)S(1)} %get-tuple-element.36.low_ref, bf16[256,2048]{1,0:T(8,128)(2,1)S(1)} %get-tuple-element.42.wh_ref, bf16[256,2048]{1,0:T(8,128)(2,1)S(1)} %get-tuple-element.43.wl_ref), custom_call_target="tpu_custom_call" | custom-call | flops 2415919104 | bytes 2883584 | tf_op jit(solution)/shard_map/pallas_call | solution.py:187
  95.4 0.9 collective-permute-start.2
  96.3 6.8 %shard_map.59 = f32[768,256]{1,0:T(8,128)S(1)} custom-call(f32[8,768]{1,0:T(8,128)S(1)} %maximum_maximum_fusion.table_ref, f32[768,256]{1,0:T(8,128)S(1)} %get-tuple-element.47.own_ref, f32[768,256]{1,0:T(8,128)S(1)} %get-tuple-element.50.twin_ref, f32[768,256]{1,0:T(8,128)S(1)} %collective-permute-done.beyond_ref), custom_call_target="tpu_custom_call" | custom-call | flops 3623878656 | bytes 3145728 | tf_op jit(solution)/shard_map/pallas_call | solution.py:248
  103.1 12.9 %collective-permute-done.2 = f32[768,256]{1,0:T(8,128)S(1)} collective-permute-done((f32[768,256]{1,0:T(8,128)S(1)}, f32[768,256]{1,0:T(8,128)S(1)}, u32[]{:S(2)}, u32[]{:S(2)}) %collective-permute-start.2) | collective-permute-done | bytes 786464 | tf_op jit(solution)/shard_map/ppermute | solution.py:264
  116.3 0.9 collective-permute-start.3
  117.2 1.9 collective-permute-start.4
  119.1 2.9 %shard_map.60.before_ref = f32[2048,256]{1,0:T(8,128)S(1)} custom-call(s32[1]{0:T(128)} %bitcast.1.plane_ref, bf16[2048,1536]{1,0:T(8,128)(2,1)S(1)} %get-tuple-element.35.high_ref, bf16[2048,1536]{1,0:T(8,128)(2,1)S(1)} %get-tuple-element.36.low_ref, f32[768,256]{1,0:T(8,128)S(1)} %subtract_add_fusion.1.x_ref.own_ref), custom_call_target="tpu_custom_call" | custom-call | flops 2415919104 | bytes 2883584 | tf_op jit(solution)/shard_map/pallas_call | solution.py:147
  122.0 3.0 %shard_map.61 = f32[2048,256]{1,0:T(8,128)S(1)} custom-call(s32[1]{0:T(128)} %bitcast.2.plane_ref, bf16[2048,1536]{1,0:T(8,128)(2,1)S(1)} %get-tuple-element.35.high_ref, bf16[2048,1536]{1,0:T(8,128)(2,1)S(1)} %get-tuple-element.36.low_ref, f32[768,256]{1,0:T(8,128)S(1)} %collective-permute-done.3.x_ref.twin_ref, f32[2048,256]{1,0:T(8,128)S(1)} %shard_map.60.before_ref), custom_call_target="tpu_custom_call" | custom-call | flops 2415919104 | bytes 2883584 | tf_op jit(solution)/shard_map/pallas_call | solution.py:147
  125.0 5.8 %collective-permute-done.4.beyond_ref = f32[768,256]{1,0:T(8,128)S(1)} collective-permute-done((f32[768,256]{1,0:T(8,128)S(1)}, f32[768,256]{1,0:T(8,128)S(1)}, u32[]{:S(2)}, u32[]{:S(2)}) %collective-permute-start.4) | collective-permute-done | bytes 786464 | tf_op jit(solution)/shard_map/ppermute | solution.py:270
  130.8 35.4 %all_to_all.22.pieces_ref = f32[32,64,256]{2,1,0:T(8,128)S(1)} all-to-all(f32[32,64,256]{2,1,0:T(8,128)S(1)} %bitcast.11), channel_id=1, replica_groups=mesh['yh'=2,'core'=2,'yl'=2,'x'=4,'z'=4] {'yl','x','z'}, dimensions={0} | all-to-all | bytes 4194304 | tf_op jit(solution)/shard_map/all_to_all | solution.py:301
  166.2 0.3 shard_map.62
  166.5 32.7 %all_to_all.23 = f32[32,64,256]{2,1,0:T(8,128)S(1)} all-to-all(f32[32,64,256]{2,1,0:T(8,128)S(1)} %shard_map.62), channel_id=1, replica_groups=mesh['yh'=2,'core'=2,'yl'=2,'x'=4,'z'=4] {'yl','x','z'}, dimensions={0} | all-to-all | bytes 4194304 | tf_op jit(solution)/shard_map/all_to_all | solution.py:303
  199.2 3.9 %shard_map.63 = (f32[768,256]{1,0:T(8,128)S(1)}, bf16[256,2048]{1,0:T(8,128)(2,1)S(1)}, bf16[256,2048]{1,0:T(8,128)(2,1)S(1)}) custom-call(s32[1]{0:T(128)} %bitcast.2.plane_ref, bf16[2048,1536]{1,0:T(8,128)(2,1)S(1)} %get-tuple-element.35.high_ref, bf16[2048,1536]{1,0:T(8,128)(2,1)S(1)} %get-tuple-element.36.low_ref, f32[2048,256]{1,0:T(8,128)S(1)} %bitcast.13), custom_call_target="tpu_custom_call" | custom-call | flops 2415919104 | bytes 2883584 | tf_op jit(solution)/shard_map/pallas_call | solution.py:175
  203.1 0.8 collective-permute-start.5
  203.9 3.2 %shard_map.64 = f32[768,256]{1,0:T(8,128)S(1)} custom-call(s32[1]{0:T(128)} %bitcast.1.plane_ref, bf16[2048,1536]{1,0:T(8,128)(2,1)S(1)} %get-tuple-element.35.high_ref, bf16[2048,1536]{1,0:T(8,128)(2,1)S(1)} %get-tuple-element.36.low_ref, bf16[256,2048]{1,0:T(8,128)(2,1)S(1)} %get-tuple-element.53.wh_ref, bf16[256,2048]{1,0:T(8,128)(2,1)S(1)} %get-tuple-element.54.wl_ref), custom_call_target="tpu_custom_call" | custom-call | flops 2415919104 | bytes 2883584 | tf_op jit(solution)/shard_map/pallas_call | solution.py:187
  207.3 0.7 collective-permute-start.6
  207.9 6.9 %shard_map.65 = f32[768,256]{1,0:T(8,128)S(1)} custom-call(f32[8,768]{1,0:T(8,128)S(1)} %maximum_maximum_fusion.table_ref, f32[768,256]{1,0:T(8,128)S(1)} %subtract_add_fusion.1.x_ref.own_ref, f32[768,256]{1,0:T(8,128)S(1)} %collective-permute-done.3.x_ref.twin_ref, f32[768,256]{1,0:T(8,128)S(1)} %collective-permute-done.4.beyond_ref), custom_call_target="tpu_custom_call" | custom-call | flops 3623878656 | bytes 3145728 | tf_op jit(solution)/shard_map/pallas_call | solution.py:248
  214.9 13.2 %collective-permute-done.6 = f32[768,256]{1,0:T(8,128)S(1)} collective-permute-done((f32[768,256]{1,0:T(8,128)S(1)}, f32[768,256]{1,0:T(8,128)S(1)}, u32[]{:S(2)}, u32[]{:S(2)}) %collective-permute-start.6) | collective-permute-done | bytes 786464 | tf_op jit(solution)/shard_map/ppermute | solution.py:264
  228.3 0.8 collective-permute-start.7
  229.2 1.8 collective-permute-done.7
  231.0 1.4 bitcast_select_fusion
  (18 shorter events, 0.9 us)
Async XLA Ops:
  0.0 7.4 %copy-start.1 = (f32[1536,256]{1,0:T(8,128)S(1)}, f32[1536,256]{1,0:T(8,128)}, u32[]{:S(2)}) copy-start(f32[1536,256]{1,0:T(8,128)} %x_ref) | copy-start | bytes 4718596
  3.2 14.1 %collective-permute-start = (f32[768,256]{1,0:T(8,128)S(1)}, f32[768,256]{1,0:T(8,128)S(1)}, u32[]{:S(2)}, u32[]{:S(2)}) collective-permute-start(f32[768,256]{1,0:T(8,128)S(1)} %get-tuple-element.47.own_ref), channel_id=1, source_target_pairs={{32,1},{33,2},{34,3},{35,4},{36,5},{37,6},{38,7},{39,8},{40,9},{41... | collective-permute-start | bytes 2359304 | tf_op jit(solution)/shard_map/ppermute | solution.py:270
  17.3 37.4 %copy-start = (f32[2048,256]{1,0:T(8,128)S(1)}, f32[2048,256]{1,0:T(8,128)}, u32[]{:S(2)}) copy-start(f32[2048,256]{1,0:T(8,128)} %observed_ref.3) | copy-start | bytes 6291460
  91.5 3.8 %collective-permute-start.1 = (f32[768,256]{1,0:T(8,128)S(1)}, f32[768,256]{1,0:T(8,128)S(1)}, u32[]{:S(2)}, u32[]{:S(2)}) collective-permute-start(f32[768,256]{1,0:T(8,128)S(1)} %get-tuple-element.44), channel_id=1, source_target_pairs={{0,32},{32,0},{1,33},{33,1},{2,34},{34,2},{3,35},{35,3},{4,36},{36... | collective-permute-start | bytes 2359304 | tf_op jit(solution)/shard_map/ppermute | solution.py:264
  95.4 20.7 %collective-permute-start.2 = (f32[768,256]{1,0:T(8,128)S(1)}, f32[768,256]{1,0:T(8,128)S(1)}, u32[]{:S(2)}, u32[]{:S(2)}) collective-permute-start(f32[768,256]{1,0:T(8,128)S(1)} %add.35), channel_id=1, source_target_pairs={{0,64},{64,0},{1,65},{65,1},{2,66},{66,2},{3,67},{67,3},{4,68},{68... | collective-permute-start | bytes 2359304 | tf_op jit(solution)/shard_map/ppermute | solution.py:264
  116.3 5.7 %collective-permute-start.3 = (f32[768,256]{1,0:T(8,128)S(1)}, f32[768,256]{1,0:T(8,128)S(1)}, u32[]{:S(2)}, u32[]{:S(2)}) collective-permute-start(f32[768,256]{1,0:T(8,128)S(1)} %subtract_add_fusion.1.x_ref.own_ref), channel_id=1, source_target_pairs={{0,32},{32,0},{1,33},{33,1},{2,34},{34,2},{3,35},{35,3},{4,36},{36... | collective-permute-start | bytes 2359304 | tf_op jit(solution)/shard_map/ppermute | solution.py:264
  117.2 13.6 %collective-permute-start.4 = (f32[768,256]{1,0:T(8,128)S(1)}, f32[768,256]{1,0:T(8,128)S(1)}, u32[]{:S(2)}, u32[]{:S(2)}) collective-permute-start(f32[768,256]{1,0:T(8,128)S(1)} %subtract_add_fusion.1.x_ref.own_ref), channel_id=1, source_target_pairs={{32,1},{33,2},{34,3},{35,4},{36,5},{37,6},{38,7},{39,8},{40,9},{41... | collective-permute-start | bytes 2359304 | tf_op jit(solution)/shard_map/ppermute | solution.py:270
  203.1 4.1 %collective-permute-start.5 = (f32[768,256]{1,0:T(8,128)S(1)}, f32[768,256]{1,0:T(8,128)S(1)}, u32[]{:S(2)}, u32[]{:S(2)}) collective-permute-start(f32[768,256]{1,0:T(8,128)S(1)} %get-tuple-element.55), channel_id=1, source_target_pairs={{0,32},{32,0},{1,33},{33,1},{2,34},{34,2},{3,35},{35,3},{4,36},{36... | collective-permute-start | bytes 2359304 | tf_op jit(solution)/shard_map/ppermute | solution.py:264
  207.3 20.8 %collective-permute-start.6 = (f32[768,256]{1,0:T(8,128)S(1)}, f32[768,256]{1,0:T(8,128)S(1)}, u32[]{:S(2)}, u32[]{:S(2)}) collective-permute-start(f32[768,256]{1,0:T(8,128)S(1)} %add.38), channel_id=1, source_target_pairs={{0,64},{64,0},{1,65},{65,1},{2,66},{66,2},{3,67},{67,3},{4,68},{68... | collective-permute-start | bytes 2359304 | tf_op jit(solution)/shard_map/ppermute | solution.py:264
  228.3 2.7 %collective-permute-start.7 = (f32[768,256]{1,0:T(8,128)S(1)}, f32[768,256]{1,0:T(8,128)S(1)}, u32[]{:S(2)}, u32[]{:S(2)}) collective-permute-start(f32[768,256]{1,0:T(8,128)S(1)} %subtract_add_fusion), channel_id=1, source_target_pairs={{0,32},{32,0},{1,33},{33,1},{2,34},{34,2},{3,35},{35,3},{4,36},{36... | collective-permute-start | bytes 2359304 | tf_op jit(solution)/shard_map/ppermute | solution.py:264

commit v4 on v3

v4 whole, which is shorter than its diff:
```python
import functools

import jax
import jax.numpy as jnp
from jax import lax
from jax.experimental import pallas as pl
from jax.experimental.pallas import tpu as pltpu
from jax.sharding import Mesh, PartitionSpec as P

ITERS = 2
DATA = ("yh", "core")
CELLS = ("yl", "x", "z")
ALL = DATA + CELLS
ROWS = 256
PARAMS = pltpu.CompilerParams(vmem_limit_bytes=24 * 1024 * 1024)
VMEM = pl.BlockSpec(memory_space=pltpu.VMEM)
SMEM = pl.BlockSpec(memory_space=pltpu.SMEM)
ANY = pl.BlockSpec(memory_space=pl.ANY)
F32 = jnp.float32
BF16 = jnp.bfloat16


def huber(diff):
    return diff / jnp.sqrt(1.0 + diff * diff)


def split(value):
    high = value.astype(BF16)
    low = (value - high.astype(F32)).astype(BF16)
    return high, low


def dot(a, b):
    return jnp.dot(a, b, preferred_element_type=F32)


def product(a, b):
    return dot(a[0], b[0]) + (dot(a[0], b[1]) + dot(a[1], b[0]))


def block_of(index, size):
    return pl.ds(pl.multiple_of(index * size, size), size)


def cost(data, cells, sols, wide):
    return pl.CostEstimate(
        flops=6 * data * cells * sols,
        bytes_accessed=4 * (wide * data * cells + cells * sols + data * sols),
        transcendentals=0,
    )


def first_kernel(blocks_ref, s_ref, x_ref, *refs):
    chunks = blocks_ref.shape[0]
    outs, (xh_ref, xl_ref, in_ref, in_sem) = refs[: 3 * chunks], refs[3 * chunks :]
    steps = outs[0].shape[0] // ROWS

    def fetch(chunk, step):
        start = pl.multiple_of((blocks_ref[chunk] * steps + step) * ROWS, ROWS)
        slot = chunk * steps + step
        return pltpu.make_async_copy(s_ref.at[pl.ds(start, ROWS)], in_ref.at[slot], in_sem.at[slot])

    order = [(chunk, step) for chunk in range(chunks) for step in range(steps)]
    for chunk, step in order:
        fetch(chunk, step).start()
    xh_ref[...], xl_ref[...] = split(x_ref[...])
    for chunk, step in order:
        p_ref, high_ref, low_ref = outs[3 * chunk : 3 * chunk + 3]
        fetch(chunk, step).wait()
        high, low = split(in_ref[chunk * steps + step])
        rows = pl.ds(step * ROWS, ROWS)
        high_ref[rows, :] = high
        low_ref[rows, :] = low
        p_ref[rows, :] = product((high, low), (xh_ref[...], xl_ref[...]))


def first_forward(blocks, sensitivity, x, rows):
    cells, sols = x.shape
    chunks = blocks.shape[0]
    one = [
        pltpu.VMEM((rows, sols), F32),
        pltpu.VMEM((rows, cells), BF16),
        pltpu.VMEM((rows, cells), BF16),
    ]
    slots = chunks * rows // ROWS
    return pl.pallas_call(
        first_kernel,
        in_specs=[SMEM, pl.BlockSpec(memory_space=pltpu.HBM), VMEM],
        out_specs=[VMEM] * (3 * chunks),
        out_shape=one * chunks,
        scratch_shapes=[
            pltpu.VMEM((cells, sols), BF16),
            pltpu.VMEM((cells, sols), BF16),
            pltpu.VMEM((slots, ROWS, cells), F32),
            pltpu.SemaphoreType.DMA((slots,)),
        ],
        compiler_params=PARAMS,
        cost_estimate=cost(chunks * rows, cells, sols, 1),
    )(blocks, pltpu.with_memory_space_constraint(sensitivity, pltpu.HBM), x)


def forward_kernel(terms, chunks, before, planes_ref, *refs):
    x_refs, refs = refs[:terms], refs[terms:]
    sense, refs = refs[: 2 * chunks], refs[2 * chunks :]
    starts, outs = (refs[:chunks], refs[chunks:]) if before else ((), refs)
    cells = x_refs[0].shape[0]
    xs = [split(x_ref[...]) for x_ref in x_refs]
    columns = [block_of(planes_ref[t], cells) for t in range(terms)]
    for i in range(chunks):
        total = starts[i][...] if before else None
        for t in range(terms):
            part = product((sense[2 * i][:, columns[t]], sense[2 * i + 1][:, columns[t]]), xs[t])
            total = part if total is None else total + part
        outs[i][...] = total


def forward(planes, xs, sense, before=()):
    chunks = len(sense) // 2
    rows = sense[0].shape[0]
    cells, sols = xs[0].shape
    args = [planes, *xs, *pinned(sense), *pinned(before)]
    return pl.pallas_call(
        functools.partial(forward_kernel, len(xs), chunks, len(before) > 0),
        in_specs=[SMEM] + [VMEM] * (len(args) - 1),
        out_specs=[VMEM] * chunks,
        out_shape=[pltpu.VMEM((rows, sols), F32)] * chunks,
        compiler_params=PARAMS,
        cost_estimate=cost(chunks * rows, len(xs) * cells, sols, 0),
    )(*args)


def pinned(sense):
    return [pltpu.with_memory_space_constraint(half, pltpu.VMEM) for half in sense]


def gather_kernel(chunks, before, *refs):
    w_refs, refs = refs[:chunks], refs[chunks:]
    sense, refs = refs[: 2 * chunks], refs[2 * chunks :]
    start_ref, refs = (refs[0], refs[1:]) if before else (None, refs)
    sum_ref, wh_ref, wl_ref = refs
    for i in range(chunks):
        wh_ref[i], wl_ref[i] = split(w_refs[i][...].T)

    @pl.loop(0, sum_ref.shape[1] // ROWS)
    def _(j):
        columns = block_of(j, ROWS)
        total = start_ref[:, columns] if before else None
        for i in range(chunks):
            part = product((wh_ref[i], wl_ref[i]), (sense[2 * i][:, columns], sense[2 * i + 1][:, columns]))
            total = part if total is None else total + part
        sum_ref[:, columns] = total


def gather_up(ws, sense, before=()):
    chunks = len(ws)
    rows, sols = ws[0].shape
    cells = sense[0].shape[1]
    args = [*ws, *pinned(sense), *pinned(before)]
    return pl.pallas_call(
        functools.partial(gather_kernel, chunks, len(before) > 0),
        in_specs=[VMEM] * len(args),
        out_specs=VMEM,
        out_shape=pltpu.VMEM((sols, cells), F32),
        scratch_shapes=[pltpu.VMEM((chunks, sols, rows), BF16), pltpu.VMEM((chunks, sols, rows), BF16)],
        compiler_params=PARAMS,
        cost_estimate=cost(chunks * rows, cells, sols, 0),
    )(*args)


def close_kernel(plane_ref, w_ref, high_ref, low_ref, start_ref, g_ref, wh_ref, wl_ref):
    blocks = g_ref.shape[0] // ROWS
    wh_ref[...], wl_ref[...] = split(w_ref[...].T)

    @pl.loop(0, blocks)
    def _(j):
        columns = block_of(plane_ref[0] * blocks + j, ROWS)
        part = product((wh_ref[...], wl_ref[...]), (high_ref[:, columns], low_ref[:, columns]))
        g_ref[block_of(j, ROWS), :] = (start_ref[:, columns] + part).T


def close(plane, w, sense, before, cells):
    rows, sols = w.shape
    args = [plane, w, *pinned(sense), *pinned([before])]
    return pl.pallas_call(
        close_kernel,
        in_specs=[SMEM] + [VMEM] * (len(args) - 1),
        out_specs=VMEM,
        out_shape=jax.ShapeDtypeStruct((cells, sols), F32),
        scratch_shapes=[pltpu.VMEM((sols, rows), BF16), pltpu.VMEM((sols, rows), BF16)],
        compiler_params=PARAMS,
        cost_estimate=cost(rows, cells, sols, 0),
    )(*args)


def weigh_kernel(rank_ref, pieces_ref, observed_ref, copies_ref):
    misfit = jnp.sum(pieces_ref[...], axis=0) - observed_ref[...]
    weighted = misfit / jnp.maximum(jnp.abs(misfit), 1.0)
    copies_ref[...] = jnp.broadcast_to(weighted[None], copies_ref.shape)


def weigh(rank, pieces, observed):
    ranks, rows, sols = pieces.shape
    return pl.pallas_call(
        weigh_kernel,
        grid_spec=pltpu.PrefetchScalarGridSpec(
            num_scalar_prefetch=1,
            grid=(1,),
            in_specs=[
                pl.BlockSpec((ranks, rows, sols), lambda i, rank: (0, 0, 0)),
                pl.BlockSpec((rows, sols), lambda i, rank: (rank[0], 0)),
            ],
            out_specs=pl.BlockSpec((ranks, rows, sols), lambda i, rank: (0, 0, 0)),
        ),
        out_shape=jax.ShapeDtypeStruct(pieces.shape, F32),
        compiler_params=PARAMS,
    )(rank, pieces, observed)


def smooth_kernel(table_ref, own_ref, twin_ref, beyond_ref, total_ref, parts_ref, turned_ref):
    cells, sols = own_ref.shape
    whole = own_ref[...]
    high = whole.astype(BF16)
    rest = whole - high.astype(F32)
    middle = rest.astype(BF16)
    low = (rest - middle.astype(F32)).astype(BF16)
    parts_ref[...] = jnp.concatenate([high, middle, low], axis=1)
    turned_ref[...] = table_ref[...].T
    lanes = lax.broadcasted_iota(jnp.int32, (ROWS, cells), 1).astype(F32)

    @pl.loop(0, cells // ROWS)
    def _(i):
        rows = block_of(i, ROWS)
        own = own_ref[rows, :]
        total = huber(twin_ref[rows, :] - own) + huber(beyond_ref[rows, :] - own)
        for k in range(4):
            chosen = (lanes == turned_ref[rows, k : k + 1]).astype(F32).astype(BF16)
            taken = dot(chosen, parts_ref[...])
            other = taken[:, :sols] + taken[:, sols : 2 * sols] + taken[:, 2 * sols :]
            total = total + huber(other - own)
        total_ref[rows, :] = turned_ref[rows, 4:5] * total


def smooth_of(table, own, twin, beyond):
    cells, sols = own.shape
    return pl.pallas_call(
        smooth_kernel,
        in_specs=[VMEM] * 4,
        out_specs=VMEM,
        out_shape=jax.ShapeDtypeStruct(own.shape, F32),
        scratch_shapes=[pltpu.VMEM((cells, 3 * sols), BF16), pltpu.VMEM((cells, table.shape[0]), F32)],
        compiler_params=PARAMS,
        cost_estimate=pl.CostEstimate(
            flops=24 * cells * cells * sols,
            bytes_accessed=16 * cells * sols,
            transcendentals=12 * cells * sols,
        ),
    )(table, own, twin, beyond)


def swap(value, axis):
    return lax.ppermute(value, axis, [(0, 1), (1, 0)])


def beyond_of(own, ranks):
    up = [(ranks + i, i + 1) for i in range(ranks - 1)]
    down = [(i + 1, ranks + i) for i in range(ranks - 1)]
    return lax.ppermute(own, ("core",) + CELLS, up + down)


def ring_of(value, shift):
    yh, core, yl, x, z = (lax.axis_size(axis) for axis in ALL)
    pairs = []
    for h in range(yh):
        for l in range(yl):
            for i in range(x):
                for j in range(z):
                    at = lambda c, i, j: (((h * core + c) * yl + l) * x + i % x) * z + j % z
                    pairs.append((at(0, i, j), at(0, i + shift, j)))
                    pairs.append((at(1, i, j), at(1, i, j + shift)))
    return lax.ppermute(value, ALL, pairs)


def spread(value):
    yh, core, yl, x, z = (lax.axis_size(axis) for axis in ALL)
    at = lambda h, c, l, i, j: (((h * core + c) * yl + l) * x + i) * z + j
    groups = []
    for h in range(yh):
        groups += [[at(h, 0, l, i, j) for l in range(yl) for j in range(z)] for i in range(x)]
        groups += [[at(h, 1, l, i, j) for l in range(yl) for i in range(x)] for j in range(z)]
    return lax.all_to_all(value, ALL, 0, 0, axis_index_groups=groups, tiled=True)


def local(sensitivity, observed, models, neighbour_map, edge_mask):
    core = lax.axis_index("core").astype(jnp.int32)
    x, z = (lax.axis_index(axis).astype(jnp.int32) for axis in ("x", "z"))
    ring = jnp.where(core == 0, x, z)
    sub = lax.axis_index("yl").astype(jnp.int32) * lax.axis_size("z") + jnp.where(core == 0, z, x)
    rings = lax.axis_size("x")
    ranks = lax.axis_size(CELLS)
    subs = ranks // rings
    rank = (ring * subs + sub).reshape(1)
    block = [((ring + s) % rings).reshape(1) for s in range(rings)]
    sides = jnp.concatenate([block[1], block[3]])
    mine, theirs = core.reshape(1), (1 - core).reshape(1)
    both = jnp.concatenate([mine, theirs])
    cells = neighbour_map.shape[1]
    rows = observed.shape[0] // rings
    own_mask = lax.dynamic_slice_in_dim(edge_mask, core * cells, cells, axis=0)
    scale = 0.05 * (1.0 - 0.75 * own_mask.astype(F32))
    table = jnp.concatenate(
        [neighbour_map.astype(F32), scale[None], jnp.zeros((3, cells), F32)], axis=0
    )
    own = lax.dynamic_slice_in_dim(models, core * cells, cells, axis=0)
    twin = lax.dynamic_slice_in_dim(models, (1 - core) * cells, cells, axis=0)
    models, own, twin, table, rank, mine, theirs, both, block, sides = lax.optimization_barrier(
        (models, own, twin, table, rank, mine, theirs, both, block, sides)
    )
    for step in range(ITERS):
        if step == 0:
            p2, *s2 = first_forward(block[2], sensitivity, models, rows)
            r2 = ring_of(p2, 2)
            p1, h1, l1, p3, h3, l3 = first_forward(sides, sensitivity, models, rows)
            s1, s3 = [h1, l1], [h3, l3]
            r1, r3 = ring_of(p1, 1), ring_of(p3, 3)
            p0, *s0 = first_forward(block[0], sensitivity, models, rows)
        else:
            p2, p1, p3 = forward(mine, [own], s2 + s1 + s3)
            twin = swap(own, "core")
            (p2,) = forward(theirs, [twin], s2, [p2])
            r2 = ring_of(p2, 2)
            p1, p3 = forward(theirs, [twin], s1 + s3, [p1, p3])
            r1, r3 = ring_of(p1, 1), ring_of(p3, 3)
            (p0,) = forward(both, [own, twin], s0)
        pieces = spread(p0 + (r1 + r3) + r2)
        copies = weigh(rank, pieces.reshape(subs, rows // subs, -1), observed)
        w0 = spread(copies.reshape(rows, -1))
        w2, w3, w1 = ring_of(w0, 2), ring_of(w0, 1), ring_of(w0, 3)
        near = gather_up([w0], s0)
        near = gather_up([w1, w3], s1 + s3, [near])
        near, sent = lax.optimization_barrier((near, own))
        beyond = beyond_of(sent, ranks)
        away = close(theirs, w2, s2, near, cells)
        home = close(mine, w2, s2, near, cells)
        half = home + swap(away, "core")
        half, own, twin, beyond = lax.optimization_barrier((half, own, twin, beyond))
        gradient = half + swap(half, "yh")
        own = own - 1.0 * gradient + smooth_of(table, own, twin, beyond)
    twin = swap(own, "core")
    place = lax.broadcasted_iota(jnp.int32, (2, 1, 1), 0)
    planes = jnp.where(place == core, own[None], twin[None])
    return planes.reshape(models.shape)


def solution(mesh):
    fine = Mesh(mesh.devices.reshape(2, 2, 2, 4, 4), ALL)
    return jax.shard_map(
        local,
        mesh=fine,
        in_specs=(P(DATA, CELLS), P(DATA, None), P(CELLS, None), P(), P(CELLS)),
        out_specs=P(CELLS, None),
        check_vma=False,
    )
```

time: 234 us -> 220 us (0.940)
  blocking collectives: 138 us -> 40.3 us
  starting transfers between devices: 10.7 us -> 48.1 us
  waiting for transfers between devices: 35.6 us -> 70.1 us
  Pallas kernels: 42.6 us -> 54.6 us
    all_to_all x4, blocking collectives: 138 us -> 40.3 us  [spread(): lax.all_to_all(value, ALL, 0, 0, axis_index_groups=groups, tiled=True)]
    ppermute x0 -> x12, waiting for transfers between devices: none -> 33.4 us  [ring_of(): return lax.ppermute(value, ALL, pairs)]
    ppermute x0 -> x12, starting transfers between devices: none -> 18.8 us  [ring_of(): return lax.ppermute(value, ALL, pairs)]
    ppermute x6, starting transfers between devices: 4.67 us -> 22.9 us  [swap(): return lax.ppermute(value, axis, [(0, 1), (1, 0)])]
    pallas_call x7 -> x15, Pallas kernels: 28.2 us -> 40.7 us  [the longest x3 15.7 us: first_forward(): pl.pallas_call(first_kernel, in_specs=[SMEM, pl.BlockSpec(memory_space=pl...]
    ppermute x2, waiting for transfers between devices: 7.62 us -> 17.4 us  [beyond_of(): return lax.ppermute(own, ('core',) + CELLS, up + down)]
    ppermute x6, waiting for transfers between devices: 28 us -> 19.3 us  [swap(): return lax.ppermute(value, axis, [(0, 1), (1, 0)])]
  transfers between devices with their start and end apart: 8 -> 20, of which waited for: 5 -> 12; matrix products, arithmetic and copies ran while one was open for 0% -> 0% of each run, Pallas kernels for 15% -> 21%
where the time goes in v4:
time: 220 us; the launch traced here: 219 us
  waiting for transfers between devices  70.1 us (32%)
  Pallas kernels  54.6 us (25%)
  starting transfers between devices  48.1 us (22%)
  blocking collectives  40.3 us (18%)
  other arithmetic  3.94 us (2%)
    all_to_all x4, blocking collectives, spread(): lax.all_to_all(value, ALL, 0, 0, axis_index_groups=groups, tiled=True)  40.3 us
    ppermute x12, waiting for transfers between devices, ring_of(): return lax.ppermute(value, ALL, pairs)  33.4 us
    ppermute x6, starting transfers between devices, swap(): return lax.ppermute(value, axis, [(0, 1), (1, 0)])  22.9 us
    ppermute x6, waiting for transfers between devices, swap(): return lax.ppermute(value, axis, [(0, 1), (1, 0)])  19.3 us
    ppermute x12, starting transfers between devices, ring_of(): return lax.ppermute(value, ALL, pairs)  18.8 us
    ppermute x2, waiting for transfers between devices, beyond_of(): return lax.ppermute(own, ('core',) + CELLS, up + down)  17.4 us
    pallas_call x3, Pallas kernels, first_forward(): pl.pallas_call(first_kernel, in_specs=[SMEM, pl.BlockSpec(memory_space=pl...  15.7 us
    pallas_call x2, Pallas kernels, smooth_of(): pl.pallas_call(smooth_kernel, in_specs=[VMEM] * 4, out_specs=VMEM, out_sh...  13.8 us
  transfers between devices with their start and end apart: 20, of which 12 were waited for; matrix products, arithmetic and copies ran while one was open for 0% of the time, Pallas kernels for 21%

profile of v4, /device:TPU:25, one launch (start us, length us, event | category | flops | bytes accessed | tf_op | source)
XLA Modules:
  0.0 219.1 jit_solution(3196045995231031116)
XLA Ops:
  3.4 4.2 %shard_map.57 = (f32[512,256]{1,0:T(8,128)S(1)}, bf16[512,1536]{1,0:T(8,128)(2,1)S(1)}, bf16[512,1536]{1,0:T(8,128)(2,1)S(1)}) custom-call(s32[1]{0:T(128)} %bitcast.5.blocks_ref, f32[2048,1536]{1,0:T(8,128)} %s_ref.5, f32[1536,256]{1,0:T(8,128)S(1)} %copy-done), custom_call_target="tpu_custom_call" | custom-call | flops 1207959552 | bytes 5242880 | tf_op jit(solution)/shard_map/pallas_call | solution.py:86
  7.5 3.7 %collective-permute-start.2 = (f32[512,256]{1,0:T(8,128)S(1)}, f32[512,256]{1,0:T(8,128)S(1)}, u32[]{:S(2)}, u32[]{:S(2)}) collective-permute-start(f32[512,256]{1,0:T(8,128)S(1)} %get-tuple-element.55), channel_id=1, source_target_pairs={{0,8},{32,34},{1,9},{33,35},{2,10},{34,32},{3,11},{35,33},{4,12},{... | collective-permute-start | bytes 1572872 | tf_op jit(solution)/shard_map/ppermute | solution.py:280
  11.2 7.4 %shard_map.56 = (f32[512,256]{1,0:T(8,128)S(1)}, bf16[512,1536]{1,0:T(8,128)(2,1)S(1)}, bf16[512,1536]{1,0:T(8,128)(2,1)S(1)}, f32[512,256]{1,0:T(8,128)S(1)}, b...) custom-call(s32[2]{0:T(128)S(1)} %get-tuple-element.51.blocks_ref, f32[2048,1536]{1,0:T(8,128)} %s_ref.5, ...), custom_call_target="tpu_custom_call" | custom-call | flops 2415919104 | bytes 8912896 | tf_op jit(solution)/shard_map/pallas_call | solution.py:86
  21.4 4.2 %shard_map.55 = (f32[512,256]{1,0:T(8,128)S(1)}, bf16[512,1536]{1,0:T(8,128)(2,1)S(1)}, bf16[512,1536]{1,0:T(8,128)(2,1)S(1)}) custom-call(s32[1]{0:T(128)} %bitcast.3.blocks_ref, f32[2048,1536]{1,0:T(8,128)} %s_ref.5, f32[1536,256]{1,0:T(8,128)S(1)} %copy-done), custom_call_target="tpu_custom_call" | custom-call | flops 1207959552 | bytes 5242880 | tf_op jit(solution)/shard_map/pallas_call | solution.py:86
  25.6 2.7 %collective-permute-done = f32[512,256]{1,0:T(8,128)S(1)} collective-permute-done((f32[512,256]{1,0:T(8,128)S(1)}, f32[512,256]{1,0:T(8,128)S(1)}, u32[]{:S(2)}, u32[]{:S(2)}) %collective-permute-start) | collective-permute-done | bytes 524320 | tf_op jit(solution)/shard_map/ppermute | solution.py:280
  28.4 11.3 %all_to_all.34.pieces_ref = f32[8,64,256]{2,1,0:T(8,128)S(1)} all-to-all(f32[8,64,256]{2,1,0:T(8,128)S(1)} %bitcast.23), channel_id=1, replica_groups={{0,1,2,3,16,17,18,19},{4,5,6,7,20,21,22,23},{8,9,10,11,24,25,26,27},{12..., dimensions={0} | all-to-all | bytes 1048576 | tf_op jit(solution)/shard_map/all_to_all | solution.py:290
  39.8 10.1 %all_to_all.35 = f32[8,64,256]{2,1,0:T(8,128)S(1)} all-to-all(f32[8,64,256]{2,1,0:T(8,128)S(1)} %shard_map.58), channel_id=1, replica_groups={{0,1,2,3,16,17,18,19},{4,5,6,7,20,21,22,23},{8,9,10,11,24,25,26,27},{12..., dimensions={0} | all-to-all | bytes 1048576 | tf_op jit(solution)/shard_map/all_to_all | solution.py:290
  49.9 3.0 %collective-permute-start.4 = (f32[512,256]{1,0:T(8,128)S(1)}, f32[512,256]{1,0:T(8,128)S(1)}, u32[]{:S(2)}, u32[]{:S(2)}) collective-permute-start(f32[512,256]{1,0:T(8,128)S(1)} %bitcast.19), channel_id=1, source_target_pairs={{0,12},{32,35},{1,13},{33,32},{2,14},{34,33},{3,15},{35,34},{4,0},... | collective-permute-start | bytes 1572872 | tf_op jit(solution)/shard_map/ppermute | solution.py:280
  54.1 2.4 %shard_map.59.refs_6_ = f32[256,1536]{1,0:T(8,128)S(1)} custom-call(f32[512,256]{1,0:T(8,128)S(1)} %bitcast.22, bf16[512,1536]{1,0:T(8,128)(2,1)S(1)} %get-tuple-element.62.refs_1_.refs_2_, bf16[512,1536]{1,0:T(8,128)(2,1)S(1)} %get-tuple-element.63.refs_2_.refs_3_), custom_call_target="tpu_custom_call" | custom-call | flops 1207959552 | bytes 2097152 | tf_op jit(solution)/shard_map/pallas_call | solution.py:159
  56.5 8.4 %collective-permute-done.4.refs_0_ = f32[512,256]{1,0:T(8,128)S(1)} collective-permute-done((f32[512,256]{1,0:T(8,128)S(1)}, f32[512,256]{1,0:T(8,128)S(1)}, u32[]{:S(2)}, u32[]{:S(2)}) %collective-permute-start.4) | collective-permute-done | bytes 524320 | tf_op jit(solution)/shard_map/ppermute | solution.py:280
  64.9 3.1 %collective-permute-done.5.refs_1_ = f32[512,256]{1,0:T(8,128)S(1)} collective-permute-done((f32[512,256]{1,0:T(8,128)S(1)}, f32[512,256]{1,0:T(8,128)S(1)}, u32[]{:S(2)}, u32[]{:S(2)}) %collective-permute-start.5) | collective-permute-done | bytes 524320 | tf_op jit(solution)/shard_map/ppermute | solution.py:280
  68.0 3.8 %shard_map.60.start_ref = f32[256,1536]{1,0:T(8,128)S(1)} custom-call(f32[512,256]{1,0:T(8,128)S(1)} %collective-permute-done.4.refs_0_, f32[512,256]{1,0:T(8,128)S(1)} %collective-permute-done.5.refs_1_, bf16[512,1536]{1,0:T(8,128)(2,1)S(1)} %get-tuple-element.58.refs_2_.refs_3_.refs_1_, bf16[512,1536]{1,0:T(8,128)(2,1)S(1)} %get-tuple-element.59.refs_3_.refs_4_.refs_2_, ...), custom_call_target="tpu_custom_call" | custom-call | flops 2415919104 | bytes 2621440 | tf_op jit(solution)/shard_map/pallas_call | solution.py:159
  73.4 5.9 %collective-permute-start.6 = (f32[768,256]{1,0:T(8,128)S(1)}, f32[768,256]{1,0:T(8,128)S(1)}, u32[]{:S(2)}, u32[]{:S(2)}) collective-permute-start(f32[768,256]{1,0:T(8,128)S(1)} %shard_map.62), channel_id=1, source_target_pairs={{0,32},{32,0},{1,33},{33,1},{2,34},{34,2},{3,35},{35,3},{4,36},{36... | collective-permute-start | bytes 2359304 | tf_op jit(solution)/shard_map/ppermute | solution.py:261
  79.3 3.5 %collective-permute-start.7 = (f32[768,256]{1,0:T(8,128)S(1)}, f32[768,256]{1,0:T(8,128)S(1)}, u32[]{:S(2)}, u32[]{:S(2)}) collective-permute-start(f32[768,256]{1,0:T(8,128)S(1)} %get-tuple-element.69.own_ref), channel_id=1, source_target_pairs={{32,1},{33,2},{34,3},{35,4},{36,5},{37,6},{38,7},{39,8},{40,9},{41... | collective-permute-start | bytes 2359304 | tf_op jit(solution)/shard_map/ppermute | solution.py:267
  84.4 8.4 %collective-permute-done.7.beyond_ref = f32[768,256]{1,0:T(8,128)S(1)} collective-permute-done((f32[768,256]{1,0:T(8,128)S(1)}, f32[768,256]{1,0:T(8,128)S(1)}, u32[]{:S(2)}, u32[]{:S(2)}) %collective-permute-start.7) | collective-permute-done | bytes 786464 | tf_op jit(solution)/shard_map/ppermute | solution.py:267
  93.8 6.9 %shard_map.63 = f32[768,256]{1,0:T(8,128)S(1)} custom-call(f32[8,768]{1,0:T(8,128)S(1)} %maximum_maximum_fusion.table_ref, f32[768,256]{1,0:T(8,128)S(1)} %get-tuple-element.69.own_ref, f32[768,256]{1,0:T(8,128)S(1)} %get-tuple-element.72.twin_ref, f32[768,256]{1,0:T(8,128)S(1)} %collective-permute-done.7.beyond_ref), custom_call_target="tpu_custom_call" | custom-call | flops 3623878656 | bytes 3145728 | tf_op jit(solution)/shard_map/pallas_call | solution.py:245
  100.7 8.8 %collective-permute-done.8 = f32[768,256]{1,0:T(8,128)S(1)} collective-permute-done((f32[768,256]{1,0:T(8,128)S(1)}, f32[768,256]{1,0:T(8,128)S(1)}, u32[]{:S(2)}, u32[]{:S(2)}) %collective-permute-start.8) | collective-permute-done | bytes 786464 | tf_op jit(solution)/shard_map/ppermute | solution.py:261
  109.7 5.0 %collective-permute-start.9 = (f32[768,256]{1,0:T(8,128)S(1)}, f32[768,256]{1,0:T(8,128)S(1)}, u32[]{:S(2)}, u32[]{:S(2)}) collective-permute-start(f32[768,256]{1,0:T(8,128)S(1)} %subtract_add_fusion.1.refs_0_.own_ref), channel_id=1, source_target_pairs={{0,32},{32,0},{1,33},{33,1},{2,34},{34,2},{3,35},{35,3},{4,36},{36... | collective-permute-start | bytes 2359304 | tf_op jit(solution)/shard_map/ppermute | solution.py:261
  127.4 5.6 %collective-permute-done.10 = f32[512,256]{1,0:T(8,128)S(1)} collective-permute-done((f32[512,256]{1,0:T(8,128)S(1)}, f32[512,256]{1,0:T(8,128)S(1)}, u32[]{:S(2)}, u32[]{:S(2)}) %collective-permute-start.10) | collective-permute-done | bytes 524320 | tf_op jit(solution)/shard_map/ppermute | solution.py:280
  133.1 9.0 %all_to_all.36.pieces_ref = f32[8,64,256]{2,1,0:T(8,128)S(1)} all-to-all(f32[8,64,256]{2,1,0:T(8,128)S(1)} %bitcast.24), channel_id=1, replica_groups={{0,1,2,3,16,17,18,19},{4,5,6,7,20,21,22,23},{8,9,10,11,24,25,26,27},{12..., dimensions={0} | all-to-all | bytes 1048576 | tf_op jit(solution)/shard_map/all_to_all | solution.py:290
  142.2 10.0 %all_to_all.37 = f32[8,64,256]{2,1,0:T(8,128)S(1)} all-to-all(f32[8,64,256]{2,1,0:T(8,128)S(1)} %shard_map.68), channel_id=1, replica_groups={{0,1,2,3,16,17,18,19},{4,5,6,7,20,21,22,23},{8,9,10,11,24,25,26,27},{12..., dimensions={0} | all-to-all | bytes 1048576 | tf_op jit(solution)/shard_map/all_to_all | solution.py:290
  152.1 2.6 %collective-permute-start.14 = (f32[512,256]{1,0:T(8,128)S(1)}, f32[512,256]{1,0:T(8,128)S(1)}, u32[]{:S(2)}, u32[]{:S(2)}) collective-permute-start(f32[512,256]{1,0:T(8,128)S(1)} %bitcast.15), channel_id=1, source_target_pairs={{0,12},{32,35},{1,13},{33,32},{2,14},{34,33},{3,15},{35,34},{4,0},... | collective-permute-start | bytes 1572872 | tf_op jit(solution)/shard_map/ppermute | solution.py:280
  155.9 2.4 %shard_map.69.refs_6_ = f32[256,1536]{1,0:T(8,128)S(1)} custom-call(f32[512,256]{1,0:T(8,128)S(1)} %bitcast.18, bf16[512,1536]{1,0:T(8,128)(2,1)S(1)} %get-tuple-element.62.refs_1_.refs_2_, bf16[512,1536]{1,0:T(8,128)(2,1)S(1)} %get-tuple-element.63.refs_2_.refs_3_), custom_call_target="tpu_custom_call" | custom-call | flops 1207959552 | bytes 2097152 | tf_op jit(solution)/shard_map/pallas_call | solution.py:159
  158.4 3.7 %collective-permute-done.14.refs_0_ = f32[512,256]{1,0:T(8,128)S(1)} collective-permute-done((f32[512,256]{1,0:T(8,128)S(1)}, f32[512,256]{1,0:T(8,128)S(1)}, u32[]{:S(2)}, u32[]{:S(2)}) %collective-permute-start.14) | collective-permute-done | bytes 524320 | tf_op jit(solution)/shard_map/ppermute | solution.py:280
  162.1 7.8 %collective-permute-done.15.refs_1_ = f32[512,256]{1,0:T(8,128)S(1)} collective-permute-done((f32[512,256]{1,0:T(8,128)S(1)}, f32[512,256]{1,0:T(8,128)S(1)}, u32[]{:S(2)}, u32[]{:S(2)}) %collective-permute-start.15) | collective-permute-done | bytes 524320 | tf_op jit(solution)/shard_map/ppermute | solution.py:280
  169.9 3.8 %shard_map.70.start_ref = f32[256,1536]{1,0:T(8,128)S(1)} custom-call(f32[512,256]{1,0:T(8,128)S(1)} %collective-permute-done.14.refs_0_, f32[512,256]{1,0:T(8,128)S(1)} %collective-permute-done.15.refs_1_, bf16[512,1536]{1,0:T(8,128)(2,1)S(1)} %get-tuple-element.58.refs_2_.refs_3_.refs_1_, bf16[512,1536]{1,0:T(8,128)(2,1)S(1)} %get-tuple-element.59.refs_3_.refs_4_.refs_2_, ...), custom_call_target="tpu_custom_call" | custom-call | flops 2415919104 | bytes 2621440 | tf_op jit(solution)/shard_map/pallas_call | solution.py:159
  175.3 5.2 %collective-permute-start.16 = (f32[768,256]{1,0:T(8,128)S(1)}, f32[768,256]{1,0:T(8,128)S(1)}, u32[]{:S(2)}, u32[]{:S(2)}) collective-permute-start(f32[768,256]{1,0:T(8,128)S(1)} %shard_map.72), channel_id=1, source_target_pairs={{0,32},{32,0},{1,33},{33,1},{2,34},{34,2},{3,35},{35,3},{4,36},{36... | collective-permute-start | bytes 2359304 | tf_op jit(solution)/shard_map/ppermute | solution.py:261
  180.5 2.9 %collective-permute-start.17 = (f32[768,256]{1,0:T(8,128)S(1)}, f32[768,256]{1,0:T(8,128)S(1)}, u32[]{:S(2)}, u32[]{:S(2)}) collective-permute-start(f32[768,256]{1,0:T(8,128)S(1)} %subtract_add_fusion.1.refs_0_.own_ref), channel_id=1, source_target_pairs={{32,1},{33,2},{34,3},{35,4},{36,5},{37,6},{38,7},{39,8},{40,9},{41... | collective-permute-start | bytes 2359304 | tf_op jit(solution)/shard_map/ppermute | solution.py:267
  185.1 9.0 %collective-permute-done.17.beyond_ref = f32[768,256]{1,0:T(8,128)S(1)} collective-permute-done((f32[768,256]{1,0:T(8,128)S(1)}, f32[768,256]{1,0:T(8,128)S(1)}, u32[]{:S(2)}, u32[]{:S(2)}) %collective-permute-start.17) | collective-permute-done | bytes 786464 | tf_op jit(solution)/shard_map/ppermute | solution.py:267
  195.0 6.9 %shard_map.73 = f32[768,256]{1,0:T(8,128)S(1)} custom-call(f32[8,768]{1,0:T(8,128)S(1)} %maximum_maximum_fusion.table_ref, f32[768,256]{1,0:T(8,128)S(1)} %subtract_add_fusion.1.refs_0_.own_ref, f32[768,256]{1,0:T(8,128)S(1)} %collective-permute-done.9.refs_1_.refs_0_.twin_ref, f32[768,256]{1,0:T(8,128)S(1)} %collective-permute-done.17.beyond_ref), custom_call_target="tpu_custom_call" | custom-call | flops 3623878656 | bytes 3145728 | tf_op jit(solution)/shard_map/pallas_call | solution.py:245
  201.9 8.7 %collective-permute-done.18 = f32[768,256]{1,0:T(8,128)S(1)} collective-permute-done((f32[768,256]{1,0:T(8,128)S(1)}, f32[768,256]{1,0:T(8,128)S(1)}, u32[]{:S(2)}, u32[]{:S(2)}) %collective-permute-start.18) | collective-permute-done | bytes 786464 | tf_op jit(solution)/shard_map/ppermute | solution.py:261
  210.8 5.0 %collective-permute-start.19 = (f32[768,256]{1,0:T(8,128)S(1)}, f32[768,256]{1,0:T(8,128)S(1)}, u32[]{:S(2)}, u32[]{:S(2)}) collective-permute-start(f32[768,256]{1,0:T(8,128)S(1)} %subtract_add_fusion), channel_id=1, source_target_pairs={{0,32},{32,0},{1,33},{33,1},{2,34},{34,2},{3,35},{35,3},{4,36},{36... | collective-permute-start | bytes 2359304 | tf_op jit(solution)/shard_map/ppermute | solution.py:261
  (53 shorter events, 33.6 us)
Async XLA Ops:
  1.5 1.9 copy-start
  7.5 18.0 %collective-permute-start.2 = (f32[512,256]{1,0:T(8,128)S(1)}, f32[512,256]{1,0:T(8,128)S(1)}, u32[]{:S(2)}, u32[]{:S(2)}) collective-permute-start(f32[512,256]{1,0:T(8,128)S(1)} %get-tuple-element.55), channel_id=1, source_target_pairs={{0,8},{32,34},{1,9},{33,35},{2,10},{34,32},{3,11},{35,33},{4,12},{... | collective-permute-start | bytes 1572872 | tf_op jit(solution)/shard_map/ppermute | solution.py:280
  18.7 9.6 %collective-permute-start = (f32[512,256]{1,0:T(8,128)S(1)}, f32[512,256]{1,0:T(8,128)S(1)}, u32[]{:S(2)}, u32[]{:S(2)}) collective-permute-start(f32[512,256]{1,0:T(8,128)S(1)} %get-tuple-element.52), channel_id=1, source_target_pairs={{0,4},{32,33},{1,5},{33,34},{2,6},{34,35},{3,7},{35,32},{4,8},{36,... | collective-permute-start | bytes 1572872 | tf_op jit(solution)/shard_map/ppermute | solution.py:280
  19.5 8.8 %collective-permute-start.1 = (f32[512,256]{1,0:T(8,128)S(1)}, f32[512,256]{1,0:T(8,128)S(1)}, u32[]{:S(2)}, u32[]{:S(2)}) collective-permute-start(f32[512,256]{1,0:T(8,128)S(1)} %get-tuple-element.53), channel_id=1, source_target_pairs={{0,12},{32,35},{1,13},{33,32},{2,14},{34,33},{3,15},{35,34},{4,0},... | collective-permute-start | bytes 1572872 | tf_op jit(solution)/shard_map/ppermute | solution.py:280
  28.3 11.4 %copy-start.1 = (f32[2048,256]{1,0:T(8,128)S(1)}, f32[2048,256]{1,0:T(8,128)}, u32[]{:S(2)}) copy-start(f32[2048,256]{1,0:T(8,128)} %observed_ref.3) | copy-start | bytes 6291460
  49.9 15.1 %collective-permute-start.4 = (f32[512,256]{1,0:T(8,128)S(1)}, f32[512,256]{1,0:T(8,128)S(1)}, u32[]{:S(2)}, u32[]{:S(2)}) collective-permute-start(f32[512,256]{1,0:T(8,128)S(1)} %bitcast.19), channel_id=1, source_target_pairs={{0,12},{32,35},{1,13},{33,32},{2,14},{34,33},{3,15},{35,34},{4,0},... | collective-permute-start | bytes 1572872 | tf_op jit(solution)/shard_map/ppermute | solution.py:280
  52.9 15.2 %collective-permute-start.5 = (f32[512,256]{1,0:T(8,128)S(1)}, f32[512,256]{1,0:T(8,128)S(1)}, u32[]{:S(2)}, u32[]{:S(2)}) collective-permute-start(f32[512,256]{1,0:T(8,128)S(1)} %bitcast.20), channel_id=1, source_target_pairs={{0,4},{32,33},{1,5},{33,34},{2,6},{34,35},{3,7},{35,32},{4,8},{36,... | collective-permute-start | bytes 1572872 | tf_op jit(solution)/shard_map/ppermute | solution.py:280
  52.9 19.0 %collective-permute-start.3 = (f32[512,256]{1,0:T(8,128)S(1)}, f32[512,256]{1,0:T(8,128)S(1)}, u32[]{:S(2)}, u32[]{:S(2)}) collective-permute-start(f32[512,256]{1,0:T(8,128)S(1)} %bitcast.21), channel_id=1, source_target_pairs={{0,8},{32,34},{1,9},{33,35},{2,10},{34,32},{3,11},{35,33},{4,12},{... | collective-permute-start | bytes 1572872 | tf_op jit(solution)/shard_map/ppermute | solution.py:280
  73.4 10.9 %collective-permute-start.6 = (f32[768,256]{1,0:T(8,128)S(1)}, f32[768,256]{1,0:T(8,128)S(1)}, u32[]{:S(2)}, u32[]{:S(2)}) collective-permute-start(f32[768,256]{1,0:T(8,128)S(1)} %shard_map.62), channel_id=1, source_target_pairs={{0,32},{32,0},{1,33},{33,1},{2,34},{34,2},{3,35},{35,3},{4,36},{36... | collective-permute-start | bytes 2359304 | tf_op jit(solution)/shard_map/ppermute | solution.py:261
  79.3 13.6 %collective-permute-start.7 = (f32[768,256]{1,0:T(8,128)S(1)}, f32[768,256]{1,0:T(8,128)S(1)}, u32[]{:S(2)}, u32[]{:S(2)}) collective-permute-start(f32[768,256]{1,0:T(8,128)S(1)} %get-tuple-element.69.own_ref), channel_id=1, source_target_pairs={{32,1},{33,2},{34,3},{35,4},{36,5},{37,6},{38,7},{39,8},{40,9},{41... | collective-permute-start | bytes 2359304 | tf_op jit(solution)/shard_map/ppermute | solution.py:267
  92.9 16.6 %collective-permute-start.8 = (f32[768,256]{1,0:T(8,128)S(1)}, f32[768,256]{1,0:T(8,128)S(1)}, u32[]{:S(2)}, u32[]{:S(2)}) collective-permute-start(f32[768,256]{1,0:T(8,128)S(1)} %add.85), channel_id=1, source_target_pairs={{0,64},{64,0},{1,65},{65,1},{2,66},{66,2},{3,67},{67,3},{4,68},{68... | collective-permute-start | bytes 2359304 | tf_op jit(solution)/shard_map/ppermute | solution.py:261
  109.7 7.0 %collective-permute-start.9 = (f32[768,256]{1,0:T(8,128)S(1)}, f32[768,256]{1,0:T(8,128)S(1)}, u32[]{:S(2)}, u32[]{:S(2)}) collective-permute-start(f32[768,256]{1,0:T(8,128)S(1)} %subtract_add_fusion.1.refs_0_.own_ref), channel_id=1, source_target_pairs={{0,32},{32,0},{1,33},{33,1},{2,34},{34,2},{3,35},{35,3},{4,36},{36... | collective-permute-start | bytes 2359304 | tf_op jit(solution)/shard_map/ppermute | solution.py:261
  117.5 10.0 %collective-permute-start.12 = (f32[512,256]{1,0:T(8,128)S(1)}, f32[512,256]{1,0:T(8,128)S(1)}, u32[]{:S(2)}, u32[]{:S(2)}) collective-permute-start(f32[512,256]{1,0:T(8,128)S(1)} %shard_map.67), channel_id=1, source_target_pairs={{0,8},{32,34},{1,9},{33,35},{2,10},{34,32},{3,11},{35,33},{4,12},{... | collective-permute-start | bytes 1572872 | tf_op jit(solution)/shard_map/ppermute | solution.py:280
  120.5 12.4 %collective-permute-start.10 = (f32[512,256]{1,0:T(8,128)S(1)}, f32[512,256]{1,0:T(8,128)S(1)}, u32[]{:S(2)}, u32[]{:S(2)}) collective-permute-start(f32[512,256]{1,0:T(8,128)S(1)} %get-tuple-element.76), channel_id=1, source_target_pairs={{0,4},{32,33},{1,5},{33,34},{2,6},{34,35},{3,7},{35,32},{4,8},{36,... | collective-permute-start | bytes 1572872 | tf_op jit(solution)/shard_map/ppermute | solution.py:280
  121.9 11.1 %collective-permute-start.11 = (f32[512,256]{1,0:T(8,128)S(1)}, f32[512,256]{1,0:T(8,128)S(1)}, u32[]{:S(2)}, u32[]{:S(2)}) collective-permute-start(f32[512,256]{1,0:T(8,128)S(1)} %get-tuple-element.77), channel_id=1, source_target_pairs={{0,12},{32,35},{1,13},{33,32},{2,14},{34,33},{3,15},{35,34},{4,0},... | collective-permute-start | bytes 1572872 | tf_op jit(solution)/shard_map/ppermute | solution.py:280
  152.1 9.9 %collective-permute-start.14 = (f32[512,256]{1,0:T(8,128)S(1)}, f32[512,256]{1,0:T(8,128)S(1)}, u32[]{:S(2)}, u32[]{:S(2)}) collective-permute-start(f32[512,256]{1,0:T(8,128)S(1)} %bitcast.15), channel_id=1, source_target_pairs={{0,12},{32,35},{1,13},{33,32},{2,14},{34,33},{3,15},{35,34},{4,0},... | collective-permute-start | bytes 1572872 | tf_op jit(solution)/shard_map/ppermute | solution.py:280
  154.7 15.2 %collective-permute-start.15 = (f32[512,256]{1,0:T(8,128)S(1)}, f32[512,256]{1,0:T(8,128)S(1)}, u32[]{:S(2)}, u32[]{:S(2)}) collective-permute-start(f32[512,256]{1,0:T(8,128)S(1)} %bitcast.16), channel_id=1, source_target_pairs={{0,4},{32,33},{1,5},{33,34},{2,6},{34,35},{3,7},{35,32},{4,8},{36,... | collective-permute-start | bytes 1572872 | tf_op jit(solution)/shard_map/ppermute | solution.py:280
  154.7 19.0 %collective-permute-start.13 = (f32[512,256]{1,0:T(8,128)S(1)}, f32[512,256]{1,0:T(8,128)S(1)}, u32[]{:S(2)}, u32[]{:S(2)}) collective-permute-start(f32[512,256]{1,0:T(8,128)S(1)} %bitcast.17), channel_id=1, source_target_pairs={{0,8},{32,34},{1,9},{33,35},{2,10},{34,32},{3,11},{35,33},{4,12},{... | collective-permute-start | bytes 1572872 | tf_op jit(solution)/shard_map/ppermute | solution.py:280
  175.3 9.7 %collective-permute-start.16 = (f32[768,256]{1,0:T(8,128)S(1)}, f32[768,256]{1,0:T(8,128)S(1)}, u32[]{:S(2)}, u32[]{:S(2)}) collective-permute-start(f32[768,256]{1,0:T(8,128)S(1)} %shard_map.72), channel_id=1, source_target_pairs={{0,32},{32,0},{1,33},{33,1},{2,34},{34,2},{3,35},{35,3},{4,36},{36... | collective-permute-start | bytes 2359304 | tf_op jit(solution)/shard_map/ppermute | solution.py:261
  180.5 13.6 %collective-permute-start.17 = (f32[768,256]{1,0:T(8,128)S(1)}, f32[768,256]{1,0:T(8,128)S(1)}, u32[]{:S(2)}, u32[]{:S(2)}) collective-permute-start(f32[768,256]{1,0:T(8,128)S(1)} %subtract_add_fusion.1.refs_0_.own_ref), channel_id=1, source_target_pairs={{32,1},{33,2},{34,3},{35,4},{36,5},{37,6},{38,7},{39,8},{40,9},{41... | collective-permute-start | bytes 2359304 | tf_op jit(solution)/shard_map/ppermute | solution.py:267
  194.1 16.6 %collective-permute-start.18 = (f32[768,256]{1,0:T(8,128)S(1)}, f32[768,256]{1,0:T(8,128)S(1)}, u32[]{:S(2)}, u32[]{:S(2)}) collective-permute-start(f32[768,256]{1,0:T(8,128)S(1)} %add.91), channel_id=1, source_target_pairs={{0,64},{64,0},{1,65},{65,1},{2,66},{66,2},{3,67},{67,3},{4,68},{68... | collective-permute-start | bytes 2359304 | tf_op jit(solution)/shard_map/ppermute | solution.py:261
  210.8 6.9 %collective-permute-start.19 = (f32[768,256]{1,0:T(8,128)S(1)}, f32[768,256]{1,0:T(8,128)S(1)}, u32[]{:S(2)}, u32[]{:S(2)}) collective-permute-start(f32[768,256]{1,0:T(8,128)S(1)} %subtract_add_fusion), channel_id=1, source_target_pairs={{0,32},{32,0},{1,33},{33,1},{2,34},{34,2},{3,35},{35,3},{4,36},{36... | collective-permute-start | bytes 2359304 | tf_op jit(solution)/shard_map/ppermute | solution.py:261

commit v5 on v4

--- a/solution.py
+++ b/solution.py
@@ -216,7 +216,7 @@
     )(rank, pieces, observed)
 
 
-def smooth_kernel(table_ref, own_ref, twin_ref, beyond_ref, total_ref, parts_ref, turned_ref):
+def smooth_kernel(table_ref, own_ref, twin_ref, total_ref, parts_ref, turned_ref):
     cells, sols = own_ref.shape
     whole = own_ref[...]
     high = whole.astype(BF16)
@@ -231,20 +231,20 @@
     def _(i):
         rows = block_of(i, ROWS)
         own = own_ref[rows, :]
-        total = huber(twin_ref[rows, :] - own) + huber(beyond_ref[rows, :] - own)
+        total = huber(twin_ref[rows, :] - own)
         for k in range(4):
             chosen = (lanes == turned_ref[rows, k : k + 1]).astype(F32).astype(BF16)
             taken = dot(chosen, parts_ref[...])
             other = taken[:, :sols] + taken[:, sols : 2 * sols] + taken[:, 2 * sols :]
             total = total + huber(other - own)
-        total_ref[rows, :] = turned_ref[rows, 4:5] * total
-
-
-def smooth_of(table, own, twin, beyond):
+        total_ref[rows, :] = total
+
+
+def smooth_of(table, own, twin):
     cells, sols = own.shape
     return pl.pallas_call(
         smooth_kernel,
-        in_specs=[VMEM] * 4,
+        in_specs=[VMEM] * 3,
         out_specs=VMEM,
         out_shape=jax.ShapeDtypeStruct(own.shape, F32),
         scratch_shapes=[pltpu.VMEM((cells, 3 * sols), BF16), pltpu.VMEM((cells, table.shape[0]), F32)],
@@ -254,7 +254,26 @@
             bytes_accessed=16 * cells * sols,
             transcendentals=12 * cells * sols,
         ),
-    )(table, own, twin, beyond)
+    )(table, own, twin)
+
+
+def edge_kernel(table_ref, own_ref, beyond_ref, start_ref, total_ref):
+    weight = table_ref[...].T[:, 4:5]
+    total_ref[...] = weight * (start_ref[...] + huber(beyond_ref[...] - own_ref[...]))
+
+
+def edge_of(table, own, beyond, start):
+    cells, sols = own.shape
+    return pl.pallas_call(
+        edge_kernel,
+        in_specs=[VMEM] * 4,
+        out_specs=VMEM,
+        out_shape=jax.ShapeDtypeStruct(own.shape, F32),
+        compiler_params=PARAMS,
+        cost_estimate=pl.CostEstimate(
+            flops=6 * cells * sols, bytes_accessed=16 * cells * sols, transcendentals=2 * cells * sols
+        ),
+    )(table, own, beyond, start)
 
 
 def swap(value, axis):
@@ -305,15 +324,9 @@
     both = jnp.concatenate([mine, theirs])
     cells = neighbour_map.shape[1]
     rows = observed.shape[0] // rings
-    own_mask = lax.dynamic_slice_in_dim(edge_mask, core * cells, cells, axis=0)
-    scale = 0.05 * (1.0 - 0.75 * own_mask.astype(F32))
-    table = jnp.concatenate(
-        [neighbour_map.astype(F32), scale[None], jnp.zeros((3, cells), F32)], axis=0
-    )
-    own = lax.dynamic_slice_in_dim(models, core * cells, cells, axis=0)
-    twin = lax.dynamic_slice_in_dim(models, (1 - core) * cells, cells, axis=0)
-    models, own, twin, table, rank, mine, theirs, both, block, sides = lax.optimization_barrier(
-        (models, own, twin, table, rank, mine, theirs, both, block, sides)
+    low_core = core == 0
+    rank, mine, theirs, both, block, sides, low_core = lax.optimization_barrier(
+        (rank, mine, theirs, both, block, sides, low_core)
     )
     for step in range(ITERS):
         if step == 0:
@@ -334,6 +347,15 @@
         pieces = spread(p0 + (r1 + r3) + r2)
         copies = weigh(rank, pieces.reshape(subs, rows // subs, -1), observed)
         w0 = spread(copies.reshape(rows, -1))
+        if step == 0:
+            w0, start, numbers, mask = lax.optimization_barrier((w0, models, neighbour_map, edge_mask))
+            own = jnp.where(low_core, start[:cells], start[cells:])
+            twin = jnp.where(low_core, start[cells:], start[:cells])
+            mask = jnp.where(low_core, mask[:cells], mask[cells:])
+            weight = 0.05 * (1.0 - 0.75 * mask.astype(F32))
+            table = jnp.concatenate(
+                [numbers.astype(F32), weight[None], jnp.zeros((3, cells), F32)], axis=0
+            )
         w2, w3, w1 = ring_of(w0, 2), ring_of(w0, 1), ring_of(w0, 3)
         near = gather_up([w0], s0)
         near = gather_up([w1, w3], s1 + s3, [near])
@@ -342,12 +364,13 @@
         away = close(theirs, w2, s2, near, cells)
         home = close(mine, w2, s2, near, cells)
         half = home + swap(away, "core")
-        half, own, twin, beyond = lax.optimization_barrier((half, own, twin, beyond))
+        half, own, twin = lax.optimization_barrier((half, own, twin))
         gradient = half + swap(half, "yh")
-        own = own - 1.0 * gradient + smooth_of(table, own, twin, beyond)
+        inner = smooth_of(table, own, twin)
+        own = own - 1.0 * gradient + edge_of(table, own, beyond, inner)
     twin = swap(own, "core")
     place = lax.broadcasted_iota(jnp.int32, (2, 1, 1), 0)
-    planes = jnp.where(place == core, own[None], twin[None])
+    planes = jnp.where((place == 0) == low_core, own[None], twin[None])
     return planes.reshape(models.shape)
 
 

time: 220 us -> 212 us (0.964)
  the two profiles are of different devices: /device:TPU:25 before, /device:TPU:97 now
where the time goes in v5:
time: 212 us
  waiting for transfers between devices  74.2 us (35%)
  Pallas kernels  54.9 us (26%)
  blocking collectives  42.6 us (20%)
  starting transfers between devices  35.7 us (17%)
  other arithmetic  2.58 us (1%)
    all_to_all x4, blocking collectives, spread(): lax.all_to_all(value, ALL, 0, 0, axis_index_groups=groups, tiled=True)  42.6 us
    ppermute x12, waiting for transfers between devices, ring_of(): return lax.ppermute(value, ALL, pairs)  34.9 us
    ppermute x6, waiting for transfers between devices, swap(): return lax.ppermute(value, axis, [(0, 1), (1, 0)])  33.4 us
    ppermute x6, starting transfers between devices, swap(): return lax.ppermute(value, axis, [(0, 1), (1, 0)])  22.4 us
    pallas_call x3, Pallas kernels, first_forward(): pl.pallas_call(first_kernel, in_specs=[SMEM, pl.BlockSpec(memory_space=pl...  15.7 us
    pallas_call x2, Pallas kernels, smooth_of(): pl.pallas_call(smooth_kernel, in_specs=[VMEM] * 3, out_specs=VMEM, out_sh...  13 us
    pallas_call x4, Pallas kernels, gather_up(): pl.pallas_call(functools.partial(gather_kernel, chunks, len(before) > 0),...  12.6 us
    ppermute x12, starting transfers between devices, ring_of(): return lax.ppermute(value, ALL, pairs)  9.43 us
  transfers between devices with their start and end apart: 20, of which 11 were waited for; matrix products, arithmetic and copies ran while one was open for 0% of the time, Pallas kernels for 20%

profile of v5, /device:TPU:97, one launch (start us, length us, event | category | flops | bytes accessed | tf_op | source)
XLA Modules:
  0.0 211.9 jit_solution(14699181256023624334)
XLA Ops:
  1.5 7.4 %shard_map.56 = (f32[512,256]{1,0:T(8,128)S(1)}, bf16[512,1536]{1,0:T(8,128)(2,1)S(1)}, bf16[512,1536]{1,0:T(8,128)(2,1)S(1)}, f32[512,256]{1,0:T(8,128)S(1)}, b...) custom-call(s32[2]{0:T(128)S(1)} %get-tuple-element.50.blocks_ref, f32[2048,1536]{1,0:T(8,128)} %s_ref.5, ...), custom_call_target="tpu_custom_call" | custom-call | flops 2415919104 | bytes 8912896 | tf_op jit(solution)/shard_map/pallas_call | solution.py:86
  10.5 4.2 %shard_map.57 = (f32[512,256]{1,0:T(8,128)S(1)}, bf16[512,1536]{1,0:T(8,128)(2,1)S(1)}, bf16[512,1536]{1,0:T(8,128)(2,1)S(1)}) custom-call(s32[1]{0:T(128)} %bitcast.5.blocks_ref, f32[2048,1536]{1,0:T(8,128)} %s_ref.5, f32[1536,256]{1,0:T(8,128)S(1)} %copy-done.1), custom_call_target="tpu_custom_call" | custom-call | flops 1207959552 | bytes 5242880 | tf_op jit(solution)/shard_map/pallas_call | solution.py:86
  15.2 4.2 %shard_map.55 = (f32[512,256]{1,0:T(8,128)S(1)}, bf16[512,1536]{1,0:T(8,128)(2,1)S(1)}, bf16[512,1536]{1,0:T(8,128)(2,1)S(1)}) custom-call(s32[1]{0:T(128)} %bitcast.3.blocks_ref, f32[2048,1536]{1,0:T(8,128)} %s_ref.5, f32[1536,256]{1,0:T(8,128)S(1)} %copy-done.1), custom_call_target="tpu_custom_call" | custom-call | flops 1207959552 | bytes 5242880 | tf_op jit(solution)/shard_map/pallas_call | solution.py:86
  19.3 5.2 %collective-permute-done.2 = f32[512,256]{1,0:T(8,128)S(1)} collective-permute-done((f32[512,256]{1,0:T(8,128)S(1)}, f32[512,256]{1,0:T(8,128)S(1)}, u32[]{:S(2)}, u32[]{:S(2)}) %collective-permute-start.2) | collective-permute-done | bytes 524320 | tf_op jit(solution)/shard_map/ppermute | solution.py:299
  24.7 12.5 %all_to_all.35.pieces_ref = f32[8,64,256]{2,1,0:T(8,128)S(1)} all-to-all(f32[8,64,256]{2,1,0:T(8,128)S(1)} %bitcast.23), channel_id=1, replica_groups={{0,1,2,3,16,17,18,19},{4,5,6,7,20,21,22,23},{8,9,10,11,24,25,26,27},{12..., dimensions={0} | all-to-all | bytes 1048576 | tf_op jit(solution)/shard_map/all_to_all | solution.py:309
  37.3 10.0 %all_to_all.36 = f32[8,64,256]{2,1,0:T(8,128)S(1)} all-to-all(f32[8,64,256]{2,1,0:T(8,128)S(1)} %shard_map.58), channel_id=1, replica_groups={{0,1,2,3,16,17,18,19},{4,5,6,7,20,21,22,23},{8,9,10,11,24,25,26,27},{12..., dimensions={0} | all-to-all | bytes 1048576 | tf_op jit(solution)/shard_map/all_to_all | solution.py:309
  47.4 2.5 %collective-permute-start.5 = (f32[512,256]{1,0:T(8,128)S(1)}, f32[512,256]{1,0:T(8,128)S(1)}, u32[]{:S(2)}, u32[]{:S(2)}) collective-permute-start(f32[512,256]{1,0:T(8,128)S(1)} %bitcast.20), channel_id=1, source_target_pairs={{0,4},{32,33},{1,5},{33,34},{2,6},{34,35},{3,7},{35,32},{4,8},{36,... | collective-permute-start | bytes 1572872 | tf_op jit(solution)/shard_map/ppermute | solution.py:299
  50.1 2.4 %shard_map.59.refs_6_ = f32[256,1536]{1,0:T(8,128)S(1)} custom-call(f32[512,256]{1,0:T(8,128)S(1)} %bitcast.22, bf16[512,1536]{1,0:T(8,128)(2,1)S(1)} %get-tuple-element.62.refs_1_.refs_2_, bf16[512,1536]{1,0:T(8,128)(2,1)S(1)} %get-tuple-element.63.refs_2_.refs_3_), custom_call_target="tpu_custom_call" | custom-call | flops 1207959552 | bytes 2097152 | tf_op jit(solution)/shard_map/pallas_call | solution.py:159
  52.7 3.8 %collective-permute-done.4.refs_0_ = f32[512,256]{1,0:T(8,128)S(1)} collective-permute-done((f32[512,256]{1,0:T(8,128)S(1)}, f32[512,256]{1,0:T(8,128)S(1)}, u32[]{:S(2)}, u32[]{:S(2)}) %collective-permute-start.4) | collective-permute-done | bytes 524320 | tf_op jit(solution)/shard_map/ppermute | solution.py:299
  56.5 5.2 %collective-permute-done.5.refs_1_ = f32[512,256]{1,0:T(8,128)S(1)} collective-permute-done((f32[512,256]{1,0:T(8,128)S(1)}, f32[512,256]{1,0:T(8,128)S(1)}, u32[]{:S(2)}, u32[]{:S(2)}) %collective-permute-start.5) | collective-permute-done | bytes 524320 | tf_op jit(solution)/shard_map/ppermute | solution.py:299
  61.7 3.8 %shard_map.60.start_ref = f32[256,1536]{1,0:T(8,128)S(1)} custom-call(f32[512,256]{1,0:T(8,128)S(1)} %collective-permute-done.4.refs_0_, f32[512,256]{1,0:T(8,128)S(1)} %collective-permute-done.5.refs_1_, bf16[512,1536]{1,0:T(8,128)(2,1)S(1)} %get-tuple-element.58.refs_2_.refs_3_.refs_1_, bf16[512,1536]{1,0:T(8,128)(2,1)S(1)} %get-tuple-element.59.refs_3_.refs_4_.refs_2_, ...), custom_call_target="tpu_custom_call" | custom-call | flops 2415919104 | bytes 2621440 | tf_op jit(solution)/shard_map/pallas_call | solution.py:159
  67.1 7.1 %collective-permute-start.6 = (f32[768,256]{1,0:T(8,128)S(1)}, f32[768,256]{1,0:T(8,128)S(1)}, u32[]{:S(2)}, u32[]{:S(2)}) collective-permute-start(f32[768,256]{1,0:T(8,128)S(1)} %shard_map.62), channel_id=1, source_target_pairs={{0,32},{32,0},{1,33},{33,1},{2,34},{34,2},{3,35},{35,3},{4,36},{36... | collective-permute-start | bytes 2359304 | tf_op jit(solution)/shard_map/ppermute | solution.py:280
  74.2 1.9 collective-permute-start.8
  77.8 2.7 %collective-permute-start.7 = (f32[768,256]{1,0:T(8,128)S(1)}, f32[768,256]{1,0:T(8,128)S(1)}, u32[]{:S(2)}, u32[]{:S(2)}) collective-permute-start(f32[768,256]{1,0:T(8,128)S(1)} %add.76), channel_id=1, source_target_pairs={{0,64},{64,0},{1,65},{65,1},{2,66},{66,2},{3,67},{67,3},{4,68},{68... | collective-permute-start | bytes 2359304 | tf_op jit(solution)/shard_map/ppermute | solution.py:280
  80.6 6.5 %shard_map.63.start_ref = f32[768,256]{1,0:T(8,128)S(1)} custom-call(f32[8,768]{1,0:T(8,128)S(1)} %maximum_maximum_fusion.table_ref, f32[768,256]{1,0:T(8,128)S(1)} %get-tuple-element.71.own_ref, f32[768,256]{1,0:T(8,128)S(1)} %get-tuple-element.72.twin_ref), custom_call_target="tpu_custom_call" | custom-call | flops 3623878656 | bytes 3145728 | tf_op jit(solution)/shard_map/pallas_call | solution.py:245
  87.2 2.8 %collective-permute-done.8.beyond_ref = f32[768,256]{1,0:T(8,128)S(1)} collective-permute-done((f32[768,256]{1,0:T(8,128)S(1)}, f32[768,256]{1,0:T(8,128)S(1)}, u32[]{:S(2)}, u32[]{:S(2)}) %collective-permute-start.8) | collective-permute-done | bytes 786464 | tf_op jit(solution)/shard_map/ppermute | solution.py:286
  90.5 15.7 %collective-permute-done.7 = f32[768,256]{1,0:T(8,128)S(1)} collective-permute-done((f32[768,256]{1,0:T(8,128)S(1)}, f32[768,256]{1,0:T(8,128)S(1)}, u32[]{:S(2)}, u32[]{:S(2)}) %collective-permute-start.7) | collective-permute-done | bytes 786464 | tf_op jit(solution)/shard_map/ppermute | solution.py:280
  108.1 2.0 shard_map.66
  114.0 2.0 shard_map.65
  116.0 3.9 %collective-permute-done.10 = f32[512,256]{1,0:T(8,128)S(1)} collective-permute-done((f32[512,256]{1,0:T(8,128)S(1)}, f32[512,256]{1,0:T(8,128)S(1)}, u32[]{:S(2)}, u32[]{:S(2)}) %collective-permute-start.10) | collective-permute-done | bytes 524320 | tf_op jit(solution)/shard_map/ppermute | solution.py:299
  119.9 6.9 %collective-permute-done.11 = f32[512,256]{1,0:T(8,128)S(1)} collective-permute-done((f32[512,256]{1,0:T(8,128)S(1)}, f32[512,256]{1,0:T(8,128)S(1)}, u32[]{:S(2)}, u32[]{:S(2)}) %collective-permute-start.11) | collective-permute-done | bytes 524320 | tf_op jit(solution)/shard_map/ppermute | solution.py:299
  127.0 10.0 %all_to_all.37.pieces_ref = f32[8,64,256]{2,1,0:T(8,128)S(1)} all-to-all(f32[8,64,256]{2,1,0:T(8,128)S(1)} %bitcast.24), channel_id=1, replica_groups={{0,1,2,3,16,17,18,19},{4,5,6,7,20,21,22,23},{8,9,10,11,24,25,26,27},{12..., dimensions={0} | all-to-all | bytes 1048576 | tf_op jit(solution)/shard_map/all_to_all | solution.py:309
  137.0 10.2 %all_to_all.38 = f32[8,64,256]{2,1,0:T(8,128)S(1)} all-to-all(f32[8,64,256]{2,1,0:T(8,128)S(1)} %shard_map.69), channel_id=1, replica_groups={{0,1,2,3,16,17,18,19},{4,5,6,7,20,21,22,23},{8,9,10,11,24,25,26,27},{12..., dimensions={0} | all-to-all | bytes 1048576 | tf_op jit(solution)/shard_map/all_to_all | solution.py:309
  147.2 2.7 %collective-permute-start.15 = (f32[512,256]{1,0:T(8,128)S(1)}, f32[512,256]{1,0:T(8,128)S(1)}, u32[]{:S(2)}, u32[]{:S(2)}) collective-permute-start(f32[512,256]{1,0:T(8,128)S(1)} %bitcast.16), channel_id=1, source_target_pairs={{0,4},{32,33},{1,5},{33,34},{2,6},{34,35},{3,7},{35,32},{4,8},{36,... | collective-permute-start | bytes 1572872 | tf_op jit(solution)/shard_map/ppermute | solution.py:299
  150.1 2.4 %shard_map.70.refs_6_ = f32[256,1536]{1,0:T(8,128)S(1)} custom-call(f32[512,256]{1,0:T(8,128)S(1)} %bitcast.18, bf16[512,1536]{1,0:T(8,128)(2,1)S(1)} %get-tuple-element.62.refs_1_.refs_2_, bf16[512,1536]{1,0:T(8,128)(2,1)S(1)} %get-tuple-element.63.refs_2_.refs_3_), custom_call_target="tpu_custom_call" | custom-call | flops 1207959552 | bytes 2097152 | tf_op jit(solution)/shard_map/pallas_call | solution.py:159
  152.5 9.8 %collective-permute-done.14.refs_0_ = f32[512,256]{1,0:T(8,128)S(1)} collective-permute-done((f32[512,256]{1,0:T(8,128)S(1)}, f32[512,256]{1,0:T(8,128)S(1)}, u32[]{:S(2)}, u32[]{:S(2)}) %collective-permute-start.14) | collective-permute-done | bytes 524320 | tf_op jit(solution)/shard_map/ppermute | solution.py:299
  162.3 3.8 %shard_map.71.start_ref = f32[256,1536]{1,0:T(8,128)S(1)} custom-call(f32[512,256]{1,0:T(8,128)S(1)} %collective-permute-done.14.refs_0_, f32[512,256]{1,0:T(8,128)S(1)} %collective-permute-done.15.refs_1_, bf16[512,1536]{1,0:T(8,128)(2,1)S(1)} %get-tuple-element.58.refs_2_.refs_3_.refs_1_, bf16[512,1536]{1,0:T(8,128)(2,1)S(1)} %get-tuple-element.59.refs_3_.refs_4_.refs_2_, ...), custom_call_target="tpu_custom_call" | custom-call | flops 2415919104 | bytes 2621440 | tf_op jit(solution)/shard_map/pallas_call | solution.py:159
  167.7 7.0 %collective-permute-start.16 = (f32[768,256]{1,0:T(8,128)S(1)}, f32[768,256]{1,0:T(8,128)S(1)}, u32[]{:S(2)}, u32[]{:S(2)}) collective-permute-start(f32[768,256]{1,0:T(8,128)S(1)} %shard_map.73), channel_id=1, source_target_pairs={{0,32},{32,0},{1,33},{33,1},{2,34},{34,2},{3,35},{35,3},{4,36},{36... | collective-permute-start | bytes 2359304 | tf_op jit(solution)/shard_map/ppermute | solution.py:280
  178.3 2.4 %collective-permute-start.17 = (f32[768,256]{1,0:T(8,128)S(1)}, f32[768,256]{1,0:T(8,128)S(1)}, u32[]{:S(2)}, u32[]{:S(2)}) collective-permute-start(f32[768,256]{1,0:T(8,128)S(1)} %add.82), channel_id=1, source_target_pairs={{0,64},{64,0},{1,65},{65,1},{2,66},{66,2},{3,67},{67,3},{4,68},{68... | collective-permute-start | bytes 2359304 | tf_op jit(solution)/shard_map/ppermute | solution.py:280
  180.7 6.5 %shard_map.74.start_ref = f32[768,256]{1,0:T(8,128)S(1)} custom-call(f32[8,768]{1,0:T(8,128)S(1)} %maximum_maximum_fusion.table_ref, f32[768,256]{1,0:T(8,128)S(1)} %subtract_add_fusion.1.refs_0_.own_ref, f32[768,256]{1,0:T(8,128)S(1)} %collective-permute-done.9.refs_1_.refs_0_.twin_ref), custom_call_target="tpu_custom_call" | custom-call | flops 3623878656 | bytes 3145728 | tf_op jit(solution)/shard_map/pallas_call | solution.py:245
  187.3 3.2 %collective-permute-done.18.beyond_ref = f32[768,256]{1,0:T(8,128)S(1)} collective-permute-done((f32[768,256]{1,0:T(8,128)S(1)}, f32[768,256]{1,0:T(8,128)S(1)}, u32[]{:S(2)}, u32[]{:S(2)}) %collective-permute-start.18) | collective-permute-done | bytes 786464 | tf_op jit(solution)/shard_map/ppermute | solution.py:286
  191.0 15.9 %collective-permute-done.17 = f32[768,256]{1,0:T(8,128)S(1)} collective-permute-done((f32[768,256]{1,0:T(8,128)S(1)}, f32[768,256]{1,0:T(8,128)S(1)}, u32[]{:S(2)}, u32[]{:S(2)}) %collective-permute-start.17) | collective-permute-done | bytes 786464 | tf_op jit(solution)/shard_map/ppermute | solution.py:280
  (61 shorter events, 24.9 us)
Async XLA Ops:
  0.1 1.4 copy-start
  1.5 9.0 %copy-start.1 = (f32[1536,256]{1,0:T(8,128)S(1)}, f32[1536,256]{1,0:T(8,128)}, u32[]{:S(2)}) copy-start(f32[1536,256]{1,0:T(8,128)} %x_ref.5) | copy-start | bytes 4718596
  8.9 10.4 %collective-permute-start = (f32[512,256]{1,0:T(8,128)S(1)}, f32[512,256]{1,0:T(8,128)S(1)}, u32[]{:S(2)}, u32[]{:S(2)}) collective-permute-start(f32[512,256]{1,0:T(8,128)S(1)} %get-tuple-element.51), channel_id=1, source_target_pairs={{0,4},{32,33},{1,5},{33,34},{2,6},{34,35},{3,7},{35,32},{4,8},{36,... | collective-permute-start | bytes 1572872 | tf_op jit(solution)/shard_map/ppermute | solution.py:299
  9.0 10.3 %collective-permute-start.1 = (f32[512,256]{1,0:T(8,128)S(1)}, f32[512,256]{1,0:T(8,128)S(1)}, u32[]{:S(2)}, u32[]{:S(2)}) collective-permute-start(f32[512,256]{1,0:T(8,128)S(1)} %get-tuple-element.52), channel_id=1, source_target_pairs={{0,12},{32,35},{1,13},{33,32},{2,14},{34,33},{3,15},{35,34},{4,0},... | collective-permute-start | bytes 1572872 | tf_op jit(solution)/shard_map/ppermute | solution.py:299
  14.6 9.9 %collective-permute-start.2 = (f32[512,256]{1,0:T(8,128)S(1)}, f32[512,256]{1,0:T(8,128)S(1)}, u32[]{:S(2)}, u32[]{:S(2)}) collective-permute-start(f32[512,256]{1,0:T(8,128)S(1)} %get-tuple-element.54), channel_id=1, source_target_pairs={{0,8},{32,34},{1,9},{33,35},{2,10},{34,32},{3,11},{35,33},{4,12},{... | collective-permute-start | bytes 1572872 | tf_op jit(solution)/shard_map/ppermute | solution.py:299
  24.5 12.7 %copy-start.2 = (f32[2048,256]{1,0:T(8,128)S(1)}, f32[2048,256]{1,0:T(8,128)}, u32[]{:S(2)}) copy-start(f32[2048,256]{1,0:T(8,128)} %observed_ref.3) | copy-start | bytes 6291460
  47.2 9.3 %collective-permute-start.4 = (f32[512,256]{1,0:T(8,128)S(1)}, f32[512,256]{1,0:T(8,128)S(1)}, u32[]{:S(2)}, u32[]{:S(2)}) collective-permute-start(f32[512,256]{1,0:T(8,128)S(1)} %bitcast.19), channel_id=1, source_target_pairs={{0,12},{32,35},{1,13},{33,32},{2,14},{34,33},{3,15},{35,34},{4,0},... | collective-permute-start | bytes 1572872 | tf_op jit(solution)/shard_map/ppermute | solution.py:299
  47.4 14.2 %collective-permute-start.5 = (f32[512,256]{1,0:T(8,128)S(1)}, f32[512,256]{1,0:T(8,128)S(1)}, u32[]{:S(2)}, u32[]{:S(2)}) collective-permute-start(f32[512,256]{1,0:T(8,128)S(1)} %bitcast.20), channel_id=1, source_target_pairs={{0,4},{32,33},{1,5},{33,34},{2,6},{34,35},{3,7},{35,32},{4,8},{36,... | collective-permute-start | bytes 1572872 | tf_op jit(solution)/shard_map/ppermute | solution.py:299
  49.9 15.6 %collective-permute-start.3 = (f32[512,256]{1,0:T(8,128)S(1)}, f32[512,256]{1,0:T(8,128)S(1)}, u32[]{:S(2)}, u32[]{:S(2)}) collective-permute-start(f32[512,256]{1,0:T(8,128)S(1)} %bitcast.21), channel_id=1, source_target_pairs={{0,8},{32,34},{1,9},{33,35},{2,10},{34,32},{3,11},{35,33},{4,12},{... | collective-permute-start | bytes 1572872 | tf_op jit(solution)/shard_map/ppermute | solution.py:299
  65.5 8.7 %copy-start.3 = (s32[4,768]{1,0:T(4,128)S(1)}, s32[4,768]{1,0:T(4,128)}, u32[]{:S(2)}) copy-start(s32[4,768]{1,0:T(4,128)} %param.8) | copy-start | bytes 36868
  67.1 10.7 %collective-permute-start.6 = (f32[768,256]{1,0:T(8,128)S(1)}, f32[768,256]{1,0:T(8,128)S(1)}, u32[]{:S(2)}, u32[]{:S(2)}) collective-permute-start(f32[768,256]{1,0:T(8,128)S(1)} %shard_map.62), channel_id=1, source_target_pairs={{0,32},{32,0},{1,33},{33,1},{2,34},{34,2},{3,35},{35,3},{4,36},{36... | collective-permute-start | bytes 2359304 | tf_op jit(solution)/shard_map/ppermute | solution.py:280
  74.2 15.7 %collective-permute-start.8 = (f32[768,256]{1,0:T(8,128)S(1)}, f32[768,256]{1,0:T(8,128)S(1)}, u32[]{:S(2)}, u32[]{:S(2)}) collective-permute-start(f32[768,256]{1,0:T(8,128)S(1)} %get-tuple-element.71.own_ref), channel_id=1, source_target_pairs={{32,1},{33,2},{34,3},{35,4},{36,5},{37,6},{38,7},{39,8},{40,9},{41... | collective-permute-start | bytes 2359304 | tf_op jit(solution)/shard_map/ppermute | solution.py:286
  77.7 2.8 %copy-start.4 = (s32[1536]{0:T(1024)S(1)}, s32[1536]{0:T(1024)}, u32[]{:S(2)}) copy-start(s32[1536]{0:T(1024)} %param.9) | copy-start | bytes 18436
  77.8 28.3 %collective-permute-start.7 = (f32[768,256]{1,0:T(8,128)S(1)}, f32[768,256]{1,0:T(8,128)S(1)}, u32[]{:S(2)}, u32[]{:S(2)}) collective-permute-start(f32[768,256]{1,0:T(8,128)S(1)} %add.76), channel_id=1, source_target_pairs={{0,64},{64,0},{1,65},{65,1},{2,66},{66,2},{3,67},{67,3},{4,68},{68... | collective-permute-start | bytes 2359304 | tf_op jit(solution)/shard_map/ppermute | solution.py:280
  106.4 3.7 %collective-permute-start.9 = (f32[768,256]{1,0:T(8,128)S(1)}, f32[768,256]{1,0:T(8,128)S(1)}, u32[]{:S(2)}, u32[]{:S(2)}) collective-permute-start(f32[768,256]{1,0:T(8,128)S(1)} %subtract_add_fusion.1.refs_0_.own_ref), channel_id=1, source_target_pairs={{0,32},{32,0},{1,33},{33,1},{2,34},{34,2},{3,35},{35,3},{4,36},{36... | collective-permute-start | bytes 2359304 | tf_op jit(solution)/shard_map/ppermute | solution.py:280
  111.5 8.4 %collective-permute-start.10 = (f32[512,256]{1,0:T(8,128)S(1)}, f32[512,256]{1,0:T(8,128)S(1)}, u32[]{:S(2)}, u32[]{:S(2)}) collective-permute-start(f32[512,256]{1,0:T(8,128)S(1)} %get-tuple-element.75), channel_id=1, source_target_pairs={{0,4},{32,33},{1,5},{33,34},{2,6},{34,35},{3,7},{35,32},{4,8},{36,... | collective-permute-start | bytes 1572872 | tf_op jit(solution)/shard_map/ppermute | solution.py:299
  111.6 15.2 %collective-permute-start.11 = (f32[512,256]{1,0:T(8,128)S(1)}, f32[512,256]{1,0:T(8,128)S(1)}, u32[]{:S(2)}, u32[]{:S(2)}) collective-permute-start(f32[512,256]{1,0:T(8,128)S(1)} %get-tuple-element.76), channel_id=1, source_target_pairs={{0,12},{32,35},{1,13},{33,32},{2,14},{34,33},{3,15},{35,34},{4,0},... | collective-permute-start | bytes 1572872 | tf_op jit(solution)/shard_map/ppermute | solution.py:299
  113.9 13.0 %collective-permute-start.12 = (f32[512,256]{1,0:T(8,128)S(1)}, f32[512,256]{1,0:T(8,128)S(1)}, u32[]{:S(2)}, u32[]{:S(2)}) collective-permute-start(f32[512,256]{1,0:T(8,128)S(1)} %shard_map.68), channel_id=1, source_target_pairs={{0,8},{32,34},{1,9},{33,35},{2,10},{34,32},{3,11},{35,33},{4,12},{... | collective-permute-start | bytes 1572872 | tf_op jit(solution)/shard_map/ppermute | solution.py:299
  147.2 15.2 %collective-permute-start.14 = (f32[512,256]{1,0:T(8,128)S(1)}, f32[512,256]{1,0:T(8,128)S(1)}, u32[]{:S(2)}, u32[]{:S(2)}) collective-permute-start(f32[512,256]{1,0:T(8,128)S(1)} %bitcast.15), channel_id=1, source_target_pairs={{0,12},{32,35},{1,13},{33,32},{2,14},{34,33},{3,15},{35,34},{4,0},... | collective-permute-start | bytes 1572872 | tf_op jit(solution)/shard_map/ppermute | solution.py:299
  147.2 15.2 %collective-permute-start.15 = (f32[512,256]{1,0:T(8,128)S(1)}, f32[512,256]{1,0:T(8,128)S(1)}, u32[]{:S(2)}, u32[]{:S(2)}) collective-permute-start(f32[512,256]{1,0:T(8,128)S(1)} %bitcast.16), channel_id=1, source_target_pairs={{0,4},{32,33},{1,5},{33,34},{2,6},{34,35},{3,7},{35,32},{4,8},{36,... | collective-permute-start | bytes 1572872 | tf_op jit(solution)/shard_map/ppermute | solution.py:299
  149.9 16.3 %collective-permute-start.13 = (f32[512,256]{1,0:T(8,128)S(1)}, f32[512,256]{1,0:T(8,128)S(1)}, u32[]{:S(2)}, u32[]{:S(2)}) collective-permute-start(f32[512,256]{1,0:T(8,128)S(1)} %bitcast.17), channel_id=1, source_target_pairs={{0,8},{32,34},{1,9},{33,35},{2,10},{34,32},{3,11},{35,33},{4,12},{... | collective-permute-start | bytes 1572872 | tf_op jit(solution)/shard_map/ppermute | solution.py:299
  167.7 10.5 %collective-permute-start.16 = (f32[768,256]{1,0:T(8,128)S(1)}, f32[768,256]{1,0:T(8,128)S(1)}, u32[]{:S(2)}, u32[]{:S(2)}) collective-permute-start(f32[768,256]{1,0:T(8,128)S(1)} %shard_map.73), channel_id=1, source_target_pairs={{0,32},{32,0},{1,33},{33,1},{2,34},{34,2},{3,35},{35,3},{4,36},{36... | collective-permute-start | bytes 2359304 | tf_op jit(solution)/shard_map/ppermute | solution.py:280
  174.7 15.7 %collective-permute-start.18 = (f32[768,256]{1,0:T(8,128)S(1)}, f32[768,256]{1,0:T(8,128)S(1)}, u32[]{:S(2)}, u32[]{:S(2)}) collective-permute-start(f32[768,256]{1,0:T(8,128)S(1)} %subtract_add_fusion.1.refs_0_.own_ref), channel_id=1, source_target_pairs={{32,1},{33,2},{34,3},{35,4},{36,5},{37,6},{38,7},{39,8},{40,9},{41... | collective-permute-start | bytes 2359304 | tf_op jit(solution)/shard_map/ppermute | solution.py:286
  178.3 28.5 %collective-permute-start.17 = (f32[768,256]{1,0:T(8,128)S(1)}, f32[768,256]{1,0:T(8,128)S(1)}, u32[]{:S(2)}, u32[]{:S(2)}) collective-permute-start(f32[768,256]{1,0:T(8,128)S(1)} %add.82), channel_id=1, source_target_pairs={{0,64},{64,0},{1,65},{65,1},{2,66},{66,2},{3,67},{67,3},{4,68},{68... | collective-permute-start | bytes 2359304 | tf_op jit(solution)/shard_map/ppermute | solution.py:280
  207.1 3.4 %collective-permute-start.19 = (f32[768,256]{1,0:T(8,128)S(1)}, f32[768,256]{1,0:T(8,128)S(1)}, u32[]{:S(2)}, u32[]{:S(2)}) collective-permute-start(f32[768,256]{1,0:T(8,128)S(1)} %subtract_add_fusion), channel_id=1, source_target_pairs={{0,32},{32,0},{1,33},{33,1},{2,34},{34,2},{3,35},{35,3},{4,36},{36... | collective-permute-start | bytes 2359304 | tf_op jit(solution)/shard_map/ppermute | solution.py:280

commit v6 on v5

--- a/solution.py
+++ b/solution.py
@@ -52,7 +52,8 @@
 
 def first_kernel(blocks_ref, s_ref, x_ref, *refs):
     chunks = blocks_ref.shape[0]
-    outs, (xh_ref, xl_ref, in_ref, in_sem) = refs[: 3 * chunks], refs[3 * chunks :]
+    outs, refs = refs[: 3 * chunks], refs[3 * chunks :]
+    xh_ref, xl_ref, in_ref, x_in_ref, in_sem, x_sem = refs
     steps = outs[0].shape[0] // ROWS
 
     def fetch(chunk, step):
@@ -61,9 +62,12 @@
         return pltpu.make_async_copy(s_ref.at[pl.ds(start, ROWS)], in_ref.at[slot], in_sem.at[slot])
 
     order = [(chunk, step) for chunk in range(chunks) for step in range(steps)]
+    take = pltpu.make_async_copy(x_ref, x_in_ref, x_sem)
+    take.start()
     for chunk, step in order:
         fetch(chunk, step).start()
-    xh_ref[...], xl_ref[...] = split(x_ref[...])
+    take.wait()
+    xh_ref[...], xl_ref[...] = split(x_in_ref[...])
     for chunk, step in order:
         p_ref, high_ref, low_ref = outs[3 * chunk : 3 * chunk + 3]
         fetch(chunk, step).wait()
@@ -77,26 +81,58 @@
 def first_forward(blocks, sensitivity, x, rows):
     cells, sols = x.shape
     chunks = blocks.shape[0]
+    slots = chunks * rows // ROWS
+    hbm = pl.BlockSpec(memory_space=pltpu.HBM)
     one = [
         pltpu.VMEM((rows, sols), F32),
         pltpu.VMEM((rows, cells), BF16),
         pltpu.VMEM((rows, cells), BF16),
     ]
-    slots = chunks * rows // ROWS
     return pl.pallas_call(
         first_kernel,
-        in_specs=[SMEM, pl.BlockSpec(memory_space=pltpu.HBM), VMEM],
+        in_specs=[SMEM, hbm, hbm],
+        out_specs=[VMEM] * (3 * chunks + 2),
+        out_shape=one * chunks + [pltpu.VMEM((cells, sols), BF16)] * 2,
+        scratch_shapes=[
+            pltpu.VMEM((slots, ROWS, cells), F32),
+            pltpu.VMEM((cells, sols), F32),
+            pltpu.SemaphoreType.DMA((slots,)),
+            pltpu.SemaphoreType.DMA,
+        ],
+        compiler_params=PARAMS,
+        cost_estimate=cost(chunks * rows, cells, sols, 1),
+    )(blocks, *[pltpu.with_memory_space_constraint(value, pltpu.HBM) for value in (sensitivity, x)])
+
+
+def rest_kernel(blocks_ref, s_ref, xh_ref, xl_ref, *outs):
+    tall = outs[0].shape[0]
+    for chunk in range(blocks_ref.shape[0]):
+        p_ref, high_ref, low_ref = outs[3 * chunk : 3 * chunk + 3]
+        for step in range(tall // ROWS):
+            start = pl.multiple_of(blocks_ref[chunk] * tall + step * ROWS, ROWS)
+            high, low = split(s_ref[pl.ds(start, ROWS), :])
+            rows = pl.ds(step * ROWS, ROWS)
+            high_ref[rows, :] = high
+            low_ref[rows, :] = low
+            p_ref[rows, :] = product((high, low), (xh_ref[...], xl_ref[...]))
+
+
+def rest_forward(blocks, sensitivity, halves, rows):
+    cells, sols = halves[0].shape
+    chunks = blocks.shape[0]
+    one = [
+        pltpu.VMEM((rows, sols), F32),
+        pltpu.VMEM((rows, cells), BF16),
+        pltpu.VMEM((rows, cells), BF16),
+    ]
+    return pl.pallas_call(
+        rest_kernel,
+        in_specs=[SMEM] + [VMEM] * 3,
         out_specs=[VMEM] * (3 * chunks),
         out_shape=one * chunks,
-        scratch_shapes=[
-            pltpu.VMEM((cells, sols), BF16),
-            pltpu.VMEM((cells, sols), BF16),
-            pltpu.VMEM((slots, ROWS, cells), F32),
-            pltpu.SemaphoreType.DMA((slots,)),
-        ],
-        compiler_params=PARAMS,
-        cost_estimate=cost(chunks * rows, cells, sols, 1),
-    )(blocks, pltpu.with_memory_space_constraint(sensitivity, pltpu.HBM), x)
+        compiler_params=PARAMS,
+        cost_estimate=cost(chunks * rows, cells, sols, 0),
+    )(blocks, *pinned([sensitivity]), *pinned(halves))
 
 
 def forward_kernel(terms, chunks, before, planes_ref, *refs):
@@ -330,12 +366,20 @@
     )
     for step in range(ITERS):
         if step == 0:
-            p2, *s2 = first_forward(block[2], sensitivity, models, rows)
-            r2 = ring_of(p2, 2)
-            p1, h1, l1, p3, h3, l3 = first_forward(sides, sensitivity, models, rows)
+            p1, h1, l1, p3, h3, l3, *halves = first_forward(sides, sensitivity, models, rows)
             s1, s3 = [h1, l1], [h3, l3]
             r1, r3 = ring_of(p1, 1), ring_of(p3, 3)
-            p0, *s0 = first_forward(block[0], sensitivity, models, rows)
+            p2, *s2 = rest_forward(block[2], sensitivity, halves, rows)
+            r2 = ring_of(p2, 2)
+            p0, *s0 = rest_forward(block[0], sensitivity, halves, rows)
+            p0, start, numbers, mask = lax.optimization_barrier((p0, models, neighbour_map, edge_mask))
+            own = jnp.where(low_core, start[:cells], start[cells:])
+            twin = jnp.where(low_core, start[cells:], start[:cells])
+            mask = jnp.where(low_core, mask[:cells], mask[cells:])
+            weight = 0.05 * (1.0 - 0.75 * mask.astype(F32))
+            table = jnp.concatenate(
+                [numbers.astype(F32), weight[None], jnp.zeros((3, cells), F32)], axis=0
+            )
         else:
             p2, p1, p3 = forward(mine, [own], s2 + s1 + s3)
             twin = swap(own, "core")
@@ -344,23 +388,16 @@
             p1, p3 = forward(theirs, [twin], s1 + s3, [p1, p3])
             r1, r3 = ring_of(p1, 1), ring_of(p3, 3)
             (p0,) = forward(both, [own, twin], s0)
-        pieces = spread(p0 + (r1 + r3) + r2)
+        p0, own, twin, table = lax.optimization_barrier((p0 + (r1 + r3) + r2, own, twin, table))
+        pieces = spread(p0)
         copies = weigh(rank, pieces.reshape(subs, rows // subs, -1), observed)
         w0 = spread(copies.reshape(rows, -1))
-        if step == 0:
-            w0, start, numbers, mask = lax.optimization_barrier((w0, models, neighbour_map, edge_mask))
-            own = jnp.where(low_core, start[:cells], start[cells:])
-            twin = jnp.where(low_core, start[cells:], start[:cells])
-            mask = jnp.where(low_core, mask[:cells], mask[cells:])
-            weight = 0.05 * (1.0 - 0.75 * mask.astype(F32))
-            table = jnp.concatenate(
-                [numbers.astype(F32), weight[None], jnp.zeros((3, cells), F32)], axis=0
-            )
+        w0, sent = lax.optimization_barrier((w0, own))
+        beyond = beyond_of(sent, ranks)
         w2, w3, w1 = ring_of(w0, 2), ring_of(w0, 1), ring_of(w0, 3)
         near = gather_up([w0], s0)
         near = gather_up([w1, w3], s1 + s3, [near])
-        near, sent = lax.optimization_barrier((near, own))
-        beyond = beyond_of(sent, ranks)
+        w2, beyond = lax.optimization_barrier((w2, beyond))
         away = close(theirs, w2, s2, near, cells)
         home = close(mine, w2, s2, near, cells)
         half = home + swap(away, "core")

time: 212 us -> 216 us (1.019)
  the two profiles are of different devices: /device:TPU:97 before, /device:TPU:25 now
where the time goes in v6:
time: 216 us; the launch traced here: 215 us
  waiting for transfers between devices  84.7 us (39%)
  Pallas kernels  50.3 us (23%)
  blocking collectives  41.4 us (19%)
  starting transfers between devices  36 us (17%)
  other arithmetic  2.58 us (1%)
    ppermute x12, waiting for transfers between devices, ring_of(): return lax.ppermute(value, ALL, pairs)  56.5 us
    all_to_all x4, blocking collectives, spread(): lax.all_to_all(value, ALL, 0, 0, axis_index_groups=groups, tiled=True)  41.4 us
    ppermute x6, waiting for transfers between devices, swap(): return lax.ppermute(value, axis, [(0, 1), (1, 0)])  28.2 us
    ppermute x12, starting transfers between devices, ring_of(): return lax.ppermute(value, ALL, pairs)  16.8 us
    ppermute x2, starting transfers between devices, beyond_of(): return lax.ppermute(own, ('core',) + CELLS, up + down)  14.4 us
    pallas_call x2, Pallas kernels, smooth_of(): pl.pallas_call(smooth_kernel, in_specs=[VMEM] * 3, out_specs=VMEM, out_sh...  13 us
    pallas_call x4, Pallas kernels, gather_up(): pl.pallas_call(functools.partial(gather_kernel, chunks, len(before) > 0),...  12.6 us
    pallas_call x1, Pallas kernels, first_forward(): pl.pallas_call(first_kernel, in_specs=[SMEM, hbm, hbm], out_specs=[VMEM]...  8.21 us
  transfers between devices with their start and end apart: 20, of which 13 were waited for; matrix products, arithmetic and copies ran while one was open for 0% of the time, Pallas kernels for 17%

profile of v6, /device:TPU:25, one launch (start us, length us, event | category | flops | bytes accessed | tf_op | source)
XLA Modules:
  0.0 215.5 jit_solution(9734708334738564636)
XLA Ops:
  0.1 8.2 %shard_map.55 = (f32[512,256]{1,0:T(8,128)S(1)}, bf16[512,1536]{1,0:T(8,128)(2,1)S(1)}, bf16[512,1536]{1,0:T(8,128)(2,1)S(1)}, f32[512,256]{1,0:T(8,128)S(1)}, b...) custom-call(s32[2]{0:T(128)S(1)} %get-tuple-element.63.blocks_ref, ...), custom_call_target="tpu_custom_call" | custom-call | flops 2415919104 | bytes 8912896 | tf_op jit(solution)/shard_map/pallas_call | solution.py:91
  9.8 3.7 %collective-permute-start.2 = (f32[512,256]{1,0:T(8,128)S(1)}, f32[512,256]{1,0:T(8,128)S(1)}, u32[]{:S(2)}, u32[]{:S(2)}) collective-permute-start(f32[512,256]{1,0:T(8,128)S(1)} %get-tuple-element.71), channel_id=1, source_target_pairs={{0,8},{32,34},{1,9},{33,35},{2,10},{34,32},{3,11},{35,33},{4,12},{... | collective-permute-start | bytes 1572872 | tf_op jit(solution)/shard_map/ppermute | solution.py:335
  14.4 1.7 collective-permute-start.1
  17.9 2.4 %collective-permute-done.2 = f32[512,256]{1,0:T(8,128)S(1)} collective-permute-done((f32[512,256]{1,0:T(8,128)S(1)}, f32[512,256]{1,0:T(8,128)S(1)}, u32[]{:S(2)}, u32[]{:S(2)}) %collective-permute-start.2) | collective-permute-done | bytes 524320 | tf_op jit(solution)/shard_map/ppermute | solution.py:335
  20.4 5.6 %collective-permute-done = f32[512,256]{1,0:T(8,128)S(1)} collective-permute-done((f32[512,256]{1,0:T(8,128)S(1)}, f32[512,256]{1,0:T(8,128)S(1)}, u32[]{:S(2)}, u32[]{:S(2)}) %collective-permute-start) | collective-permute-done | bytes 524320 | tf_op jit(solution)/shard_map/ppermute | solution.py:335
  26.9 11.5 %all_to_all.36.pieces_ref = f32[8,64,256]{2,1,0:T(8,128)S(1)} all-to-all(f32[8,64,256]{2,1,0:T(8,128)S(1)} %bitcast.23), channel_id=1, replica_groups={{0,1,2,3,16,17,18,19},{4,5,6,7,20,21,22,23},{8,9,10,11,24,25,26,27},{12..., dimensions={0} | all-to-all | bytes 1048576 | tf_op jit(solution)/shard_map/all_to_all | solution.py:345
  38.5 10.0 %all_to_all.37 = f32[8,64,256]{2,1,0:T(8,128)S(1)} all-to-all(f32[8,64,256]{2,1,0:T(8,128)S(1)} %shard_map.58), channel_id=1, replica_groups={{0,1,2,3,16,17,18,19},{4,5,6,7,20,21,22,23},{8,9,10,11,24,25,26,27},{12..., dimensions={0} | all-to-all | bytes 1048576 | tf_op jit(solution)/shard_map/all_to_all | solution.py:345
  48.4 7.6 %collective-permute-start.4 = (f32[768,256]{1,0:T(8,128)S(1)}, f32[768,256]{1,0:T(8,128)S(1)}, u32[]{:S(2)}, u32[]{:S(2)}) collective-permute-start(f32[768,256]{1,0:T(8,128)S(1)} %get-tuple-element.90.own_ref), channel_id=1, source_target_pairs={{32,1},{33,2},{34,3},{35,4},{36,5},{37,6},{38,7},{39,8},{40,9},{41... | collective-permute-start | bytes 2359304 | tf_op jit(solution)/shard_map/ppermute | solution.py:322
  56.0 2.4 %collective-permute-start.5 = (f32[512,256]{1,0:T(8,128)S(1)}, f32[512,256]{1,0:T(8,128)S(1)}, u32[]{:S(2)}, u32[]{:S(2)}) collective-permute-start(f32[512,256]{1,0:T(8,128)S(1)} %bitcast.19), channel_id=1, source_target_pairs={{0,12},{32,35},{1,13},{33,32},{2,14},{34,33},{3,15},{35,34},{4,0},... | collective-permute-start | bytes 1572872 | tf_op jit(solution)/shard_map/ppermute | solution.py:335
  59.7 2.4 %shard_map.59.refs_6_ = f32[256,1536]{1,0:T(8,128)S(1)} custom-call(f32[512,256]{1,0:T(8,128)S(1)} %bitcast.22, bf16[512,1536]{1,0:T(8,128)(2,1)S(1)} %get-tuple-element.86.refs_1_.refs_2_, bf16[512,1536]{1,0:T(8,128)(2,1)S(1)} %get-tuple-element.87.refs_2_.refs_3_), custom_call_target="tpu_custom_call" | custom-call | flops 1207959552 | bytes 2097152 | tf_op jit(solution)/shard_map/pallas_call | solution.py:195
  62.1 9.7 %collective-permute-done.5.refs_0_ = f32[512,256]{1,0:T(8,128)S(1)} collective-permute-done((f32[512,256]{1,0:T(8,128)S(1)}, f32[512,256]{1,0:T(8,128)S(1)}, u32[]{:S(2)}, u32[]{:S(2)}) %collective-permute-start.5) | collective-permute-done | bytes 524320 | tf_op jit(solution)/shard_map/ppermute | solution.py:335
  71.8 9.5 %collective-permute-done.6.refs_1_ = f32[512,256]{1,0:T(8,128)S(1)} collective-permute-done((f32[512,256]{1,0:T(8,128)S(1)}, f32[512,256]{1,0:T(8,128)S(1)}, u32[]{:S(2)}, u32[]{:S(2)}) %collective-permute-start.6) | collective-permute-done | bytes 524320 | tf_op jit(solution)/shard_map/ppermute | solution.py:335
  81.3 3.8 %shard_map.60.start_ref = f32[256,1536]{1,0:T(8,128)S(1)} custom-call(f32[512,256]{1,0:T(8,128)S(1)} %collective-permute-done.5.refs_0_, f32[512,256]{1,0:T(8,128)S(1)} %collective-permute-done.6.refs_1_, bf16[512,1536]{1,0:T(8,128)(2,1)S(1)} %get-tuple-element.82.refs_2_.refs_3_.refs_1_, bf16[512,1536]{1,0:T(8,128)(2,1)S(1)} %get-tuple-element.83.refs_3_.refs_4_.refs_2_, ...), custom_call_target="tpu_custom_call" | custom-call | flops 2415919104 | bytes 2621440 | tf_op jit(solution)/shard_map/pallas_call | solution.py:195
  85.2 1.5 shard_map.62
  90.4 6.5 %shard_map.63.start_ref = f32[768,256]{1,0:T(8,128)S(1)} custom-call(f32[8,768]{1,0:T(8,128)S(1)} %maximum_maximum_fusion.table_ref, f32[768,256]{1,0:T(8,128)S(1)} %get-tuple-element.90.own_ref, f32[768,256]{1,0:T(8,128)S(1)} %get-tuple-element.94.twin_ref), custom_call_target="tpu_custom_call" | custom-call | flops 3623878656 | bytes 3145728 | tf_op jit(solution)/shard_map/pallas_call | solution.py:281
  97.4 12.5 %collective-permute-done.8 = f32[768,256]{1,0:T(8,128)S(1)} collective-permute-done((f32[768,256]{1,0:T(8,128)S(1)}, f32[768,256]{1,0:T(8,128)S(1)}, u32[]{:S(2)}, u32[]{:S(2)}) %collective-permute-start.8) | collective-permute-done | bytes 786464 | tf_op jit(solution)/shard_map/ppermute | solution.py:316
  111.2 2.0 shard_map.66
  114.7 2.7 %collective-permute-start.11 = (f32[512,256]{1,0:T(8,128)S(1)}, f32[512,256]{1,0:T(8,128)S(1)}, u32[]{:S(2)}, u32[]{:S(2)}) collective-permute-start(f32[512,256]{1,0:T(8,128)S(1)} %get-tuple-element.98), channel_id=1, source_target_pairs={{0,12},{32,35},{1,13},{33,32},{2,14},{34,33},{3,15},{35,34},{4,0},... | collective-permute-start | bytes 1572872 | tf_op jit(solution)/shard_map/ppermute | solution.py:335
  118.3 2.0 shard_map.65
  120.3 9.6 %collective-permute-done.10 = f32[512,256]{1,0:T(8,128)S(1)} collective-permute-done((f32[512,256]{1,0:T(8,128)S(1)}, f32[512,256]{1,0:T(8,128)S(1)}, u32[]{:S(2)}, u32[]{:S(2)}) %collective-permute-start.10) | collective-permute-done | bytes 524320 | tf_op jit(solution)/shard_map/ppermute | solution.py:335
  130.0 9.9 %all_to_all.38.pieces_ref = f32[8,64,256]{2,1,0:T(8,128)S(1)} all-to-all(f32[8,64,256]{2,1,0:T(8,128)S(1)} %bitcast.24), channel_id=1, replica_groups={{0,1,2,3,16,17,18,19},{4,5,6,7,20,21,22,23},{8,9,10,11,24,25,26,27},{12..., dimensions={0} | all-to-all | bytes 1048576 | tf_op jit(solution)/shard_map/all_to_all | solution.py:345
  140.0 10.0 %all_to_all.39 = f32[8,64,256]{2,1,0:T(8,128)S(1)} all-to-all(f32[8,64,256]{2,1,0:T(8,128)S(1)} %shard_map.69), channel_id=1, replica_groups={{0,1,2,3,16,17,18,19},{4,5,6,7,20,21,22,23},{8,9,10,11,24,25,26,27},{12..., dimensions={0} | all-to-all | bytes 1048576 | tf_op jit(solution)/shard_map/all_to_all | solution.py:345
  150.0 6.8 %collective-permute-start.14 = (f32[768,256]{1,0:T(8,128)S(1)}, f32[768,256]{1,0:T(8,128)S(1)}, u32[]{:S(2)}, u32[]{:S(2)}) collective-permute-start(f32[768,256]{1,0:T(8,128)S(1)} %subtract_add_fusion.1.refs_0_.own_ref), channel_id=1, source_target_pairs={{32,1},{33,2},{34,3},{35,4},{36,5},{37,6},{38,7},{39,8},{40,9},{41... | collective-permute-start | bytes 2359304 | tf_op jit(solution)/shard_map/ppermute | solution.py:322
  156.9 2.8 %collective-permute-start.15 = (f32[512,256]{1,0:T(8,128)S(1)}, f32[512,256]{1,0:T(8,128)S(1)}, u32[]{:S(2)}, u32[]{:S(2)}) collective-permute-start(f32[512,256]{1,0:T(8,128)S(1)} %bitcast.15), channel_id=1, source_target_pairs={{0,12},{32,35},{1,13},{33,32},{2,14},{34,33},{3,15},{35,34},{4,0},... | collective-permute-start | bytes 1572872 | tf_op jit(solution)/shard_map/ppermute | solution.py:335
  160.9 2.4 %shard_map.70.refs_6_ = f32[256,1536]{1,0:T(8,128)S(1)} custom-call(f32[512,256]{1,0:T(8,128)S(1)} %bitcast.18, bf16[512,1536]{1,0:T(8,128)(2,1)S(1)} %get-tuple-element.86.refs_1_.refs_2_, bf16[512,1536]{1,0:T(8,128)(2,1)S(1)} %get-tuple-element.87.refs_2_.refs_3_), custom_call_target="tpu_custom_call" | custom-call | flops 1207959552 | bytes 2097152 | tf_op jit(solution)/shard_map/pallas_call | solution.py:195
  163.3 9.9 %collective-permute-done.15.refs_0_ = f32[512,256]{1,0:T(8,128)S(1)} collective-permute-done((f32[512,256]{1,0:T(8,128)S(1)}, f32[512,256]{1,0:T(8,128)S(1)}, u32[]{:S(2)}, u32[]{:S(2)}) %collective-permute-start.15) | collective-permute-done | bytes 524320 | tf_op jit(solution)/shard_map/ppermute | solution.py:335
  173.2 9.0 %collective-permute-done.16.refs_1_ = f32[512,256]{1,0:T(8,128)S(1)} collective-permute-done((f32[512,256]{1,0:T(8,128)S(1)}, f32[512,256]{1,0:T(8,128)S(1)}, u32[]{:S(2)}, u32[]{:S(2)}) %collective-permute-start.16) | collective-permute-done | bytes 524320 | tf_op jit(solution)/shard_map/ppermute | solution.py:335
  182.2 3.8 %shard_map.71.start_ref = f32[256,1536]{1,0:T(8,128)S(1)} custom-call(f32[512,256]{1,0:T(8,128)S(1)} %collective-permute-done.15.refs_0_, f32[512,256]{1,0:T(8,128)S(1)} %collective-permute-done.16.refs_1_, bf16[512,1536]{1,0:T(8,128)(2,1)S(1)} %get-tuple-element.82.refs_2_.refs_3_.refs_1_, bf16[512,1536]{1,0:T(8,128)(2,1)S(1)} %get-tuple-element.83.refs_3_.refs_4_.refs_2_, ...), custom_call_target="tpu_custom_call" | custom-call | flops 2415919104 | bytes 2621440 | tf_op jit(solution)/shard_map/pallas_call | solution.py:195
  186.1 1.5 shard_map.73
  191.4 6.5 %shard_map.74.start_ref = f32[768,256]{1,0:T(8,128)S(1)} custom-call(f32[8,768]{1,0:T(8,128)S(1)} %maximum_maximum_fusion.table_ref, f32[768,256]{1,0:T(8,128)S(1)} %subtract_add_fusion.1.refs_0_.own_ref, f32[768,256]{1,0:T(8,128)S(1)} %collective-permute-done.9.refs_1_.refs_0_.twin_ref), custom_call_target="tpu_custom_call" | custom-call | flops 3623878656 | bytes 3145728 | tf_op jit(solution)/shard_map/pallas_call | solution.py:281
  198.5 12.4 %collective-permute-done.18 = f32[768,256]{1,0:T(8,128)S(1)} collective-permute-done((f32[768,256]{1,0:T(8,128)S(1)}, f32[768,256]{1,0:T(8,128)S(1)}, u32[]{:S(2)}, u32[]{:S(2)}) %collective-permute-start.18) | collective-permute-done | bytes 786464 | tf_op jit(solution)/shard_map/ppermute | solution.py:316
  212.3 1.8 collective-permute-done.19
  (61 shorter events, 22.8 us)
Async XLA Ops:
  0.1 8.2 %copy-start = (f32[2048,1536]{1,0:T(8,128)S(1)}, f32[2048,1536]{1,0:T(8,128)}, u32[]{:S(2)}) copy-start(f32[2048,1536]{1,0:T(8,128)} %s_ref.5) | copy-start | bytes 37748740
  9.8 10.6 %collective-permute-start.2 = (f32[512,256]{1,0:T(8,128)S(1)}, f32[512,256]{1,0:T(8,128)S(1)}, u32[]{:S(2)}, u32[]{:S(2)}) collective-permute-start(f32[512,256]{1,0:T(8,128)S(1)} %get-tuple-element.71), channel_id=1, source_target_pairs={{0,8},{32,34},{1,9},{33,35},{2,10},{34,32},{3,11},{35,33},{4,12},{... | collective-permute-start | bytes 1572872 | tf_op jit(solution)/shard_map/ppermute | solution.py:335
  13.4 12.5 %collective-permute-start = (f32[512,256]{1,0:T(8,128)S(1)}, f32[512,256]{1,0:T(8,128)S(1)}, u32[]{:S(2)}, u32[]{:S(2)}) collective-permute-start(f32[512,256]{1,0:T(8,128)S(1)} %get-tuple-element.68), channel_id=1, source_target_pairs={{0,4},{32,33},{1,5},{33,34},{2,6},{34,35},{3,7},{35,32},{4,8},{36,... | collective-permute-start | bytes 1572872 | tf_op jit(solution)/shard_map/ppermute | solution.py:335
  14.4 3.2 %copy-start.4 = (s32[1536]{0:T(1024)S(1)}, s32[1536]{0:T(1024)}, u32[]{:S(2)}) copy-start(s32[1536]{0:T(1024)} %param.9) | copy-start | bytes 18436
  14.4 3.2 %copy-start.3 = (s32[4,768]{1,0:T(4,128)S(1)}, s32[4,768]{1,0:T(4,128)}, u32[]{:S(2)}) copy-start(s32[4,768]{1,0:T(4,128)} %param.8) | copy-start | bytes 36868
  14.4 3.4 %copy-start.2 = (f32[1536,256]{1,0:T(8,128)S(1)}, f32[1536,256]{1,0:T(8,128)}, u32[]{:S(2)}) copy-start(f32[1536,256]{1,0:T(8,128)} %x_ref.1) | copy-start | bytes 4718596
  14.4 12.4 %collective-permute-start.1 = (f32[512,256]{1,0:T(8,128)S(1)}, f32[512,256]{1,0:T(8,128)S(1)}, u32[]{:S(2)}, u32[]{:S(2)}) collective-permute-start(f32[512,256]{1,0:T(8,128)S(1)} %get-tuple-element.69), channel_id=1, source_target_pairs={{0,12},{32,35},{1,13},{33,32},{2,14},{34,33},{3,15},{35,34},{4,0},... | collective-permute-start | bytes 1572872 | tf_op jit(solution)/shard_map/ppermute | solution.py:335
  17.9 20.5 %copy-start.1 = (f32[2048,256]{1,0:T(8,128)S(1)}, f32[2048,256]{1,0:T(8,128)}, u32[]{:S(2)}) copy-start(f32[2048,256]{1,0:T(8,128)} %observed_ref.3) | copy-start | bytes 6291460
  48.4 36.7 %collective-permute-start.4 = (f32[768,256]{1,0:T(8,128)S(1)}, f32[768,256]{1,0:T(8,128)S(1)}, u32[]{:S(2)}, u32[]{:S(2)}) collective-permute-start(f32[768,256]{1,0:T(8,128)S(1)} %get-tuple-element.90.own_ref), channel_id=1, source_target_pairs={{32,1},{33,2},{34,3},{35,4},{36,5},{37,6},{38,7},{39,8},{40,9},{41... | collective-permute-start | bytes 2359304 | tf_op jit(solution)/shard_map/ppermute | solution.py:322
  56.0 15.8 %collective-permute-start.5 = (f32[512,256]{1,0:T(8,128)S(1)}, f32[512,256]{1,0:T(8,128)S(1)}, u32[]{:S(2)}, u32[]{:S(2)}) collective-permute-start(f32[512,256]{1,0:T(8,128)S(1)} %bitcast.19), channel_id=1, source_target_pairs={{0,12},{32,35},{1,13},{33,32},{2,14},{34,33},{3,15},{35,34},{4,0},... | collective-permute-start | bytes 1572872 | tf_op jit(solution)/shard_map/ppermute | solution.py:335
  58.4 22.9 %collective-permute-start.6 = (f32[512,256]{1,0:T(8,128)S(1)}, f32[512,256]{1,0:T(8,128)S(1)}, u32[]{:S(2)}, u32[]{:S(2)}) collective-permute-start(f32[512,256]{1,0:T(8,128)S(1)} %bitcast.20), channel_id=1, source_target_pairs={{0,4},{32,33},{1,5},{33,34},{2,6},{34,35},{3,7},{35,32},{4,8},{36,... | collective-permute-start | bytes 1572872 | tf_op jit(solution)/shard_map/ppermute | solution.py:335
  58.4 26.7 %collective-permute-start.3 = (f32[512,256]{1,0:T(8,128)S(1)}, f32[512,256]{1,0:T(8,128)S(1)}, u32[]{:S(2)}, u32[]{:S(2)}) collective-permute-start(f32[512,256]{1,0:T(8,128)S(1)} %bitcast.21), channel_id=1, source_target_pairs={{0,8},{32,34},{1,9},{33,35},{2,10},{34,32},{3,11},{35,33},{4,12},{... | collective-permute-start | bytes 1572872 | tf_op jit(solution)/shard_map/ppermute | solution.py:335
  86.7 2.4 %collective-permute-start.7 = (f32[768,256]{1,0:T(8,128)S(1)}, f32[768,256]{1,0:T(8,128)S(1)}, u32[]{:S(2)}, u32[]{:S(2)}) collective-permute-start(f32[768,256]{1,0:T(8,128)S(1)} %shard_map.62), channel_id=1, source_target_pairs={{0,32},{32,0},{1,33},{33,1},{2,34},{34,2},{3,35},{35,3},{4,36},{36... | collective-permute-start | bytes 2359304 | tf_op jit(solution)/shard_map/ppermute | solution.py:316
  89.2 20.8 %collective-permute-start.8 = (f32[768,256]{1,0:T(8,128)S(1)}, f32[768,256]{1,0:T(8,128)S(1)}, u32[]{:S(2)}, u32[]{:S(2)}) collective-permute-start(f32[768,256]{1,0:T(8,128)S(1)} %add.76), channel_id=1, source_target_pairs={{0,64},{64,0},{1,65},{65,1},{2,66},{66,2},{3,67},{67,3},{4,68},{68... | collective-permute-start | bytes 2359304 | tf_op jit(solution)/shard_map/ppermute | solution.py:316
  110.2 3.0 %collective-permute-start.9 = (f32[768,256]{1,0:T(8,128)S(1)}, f32[768,256]{1,0:T(8,128)S(1)}, u32[]{:S(2)}, u32[]{:S(2)}) collective-permute-start(f32[768,256]{1,0:T(8,128)S(1)} %subtract_add_fusion.1.refs_0_.own_ref), channel_id=1, source_target_pairs={{0,32},{32,0},{1,33},{33,1},{2,34},{34,2},{3,35},{35,3},{4,36},{36... | collective-permute-start | bytes 2359304 | tf_op jit(solution)/shard_map/ppermute | solution.py:316
  114.7 15.2 %collective-permute-start.10 = (f32[512,256]{1,0:T(8,128)S(1)}, f32[512,256]{1,0:T(8,128)S(1)}, u32[]{:S(2)}, u32[]{:S(2)}) collective-permute-start(f32[512,256]{1,0:T(8,128)S(1)} %get-tuple-element.97), channel_id=1, source_target_pairs={{0,4},{32,33},{1,5},{33,34},{2,6},{34,35},{3,7},{35,32},{4,8},{36,... | collective-permute-start | bytes 1572872 | tf_op jit(solution)/shard_map/ppermute | solution.py:335
  114.7 15.1 %collective-permute-start.11 = (f32[512,256]{1,0:T(8,128)S(1)}, f32[512,256]{1,0:T(8,128)S(1)}, u32[]{:S(2)}, u32[]{:S(2)}) collective-permute-start(f32[512,256]{1,0:T(8,128)S(1)} %get-tuple-element.98), channel_id=1, source_target_pairs={{0,12},{32,35},{1,13},{33,32},{2,14},{34,33},{3,15},{35,34},{4,0},... | collective-permute-start | bytes 1572872 | tf_op jit(solution)/shard_map/ppermute | solution.py:335
  118.2 11.7 %collective-permute-start.12 = (f32[512,256]{1,0:T(8,128)S(1)}, f32[512,256]{1,0:T(8,128)S(1)}, u32[]{:S(2)}, u32[]{:S(2)}) collective-permute-start(f32[512,256]{1,0:T(8,128)S(1)} %shard_map.68), channel_id=1, source_target_pairs={{0,8},{32,34},{1,9},{33,35},{2,10},{34,32},{3,11},{35,33},{4,12},{... | collective-permute-start | bytes 1572872 | tf_op jit(solution)/shard_map/ppermute | solution.py:335
  150.0 36.0 %collective-permute-start.14 = (f32[768,256]{1,0:T(8,128)S(1)}, f32[768,256]{1,0:T(8,128)S(1)}, u32[]{:S(2)}, u32[]{:S(2)}) collective-permute-start(f32[768,256]{1,0:T(8,128)S(1)} %subtract_add_fusion.1.refs_0_.own_ref), channel_id=1, source_target_pairs={{32,1},{33,2},{34,3},{35,4},{36,5},{37,6},{38,7},{39,8},{40,9},{41... | collective-permute-start | bytes 2359304 | tf_op jit(solution)/shard_map/ppermute | solution.py:322
  156.9 16.4 %collective-permute-start.15 = (f32[512,256]{1,0:T(8,128)S(1)}, f32[512,256]{1,0:T(8,128)S(1)}, u32[]{:S(2)}, u32[]{:S(2)}) collective-permute-start(f32[512,256]{1,0:T(8,128)S(1)} %bitcast.15), channel_id=1, source_target_pairs={{0,12},{32,35},{1,13},{33,32},{2,14},{34,33},{3,15},{35,34},{4,0},... | collective-permute-start | bytes 1572872 | tf_op jit(solution)/shard_map/ppermute | solution.py:335
  159.6 22.6 %collective-permute-start.16 = (f32[512,256]{1,0:T(8,128)S(1)}, f32[512,256]{1,0:T(8,128)S(1)}, u32[]{:S(2)}, u32[]{:S(2)}) collective-permute-start(f32[512,256]{1,0:T(8,128)S(1)} %bitcast.16), channel_id=1, source_target_pairs={{0,4},{32,33},{1,5},{33,34},{2,6},{34,35},{3,7},{35,32},{4,8},{36,... | collective-permute-start | bytes 1572872 | tf_op jit(solution)/shard_map/ppermute | solution.py:335
  159.6 26.5 %collective-permute-start.13 = (f32[512,256]{1,0:T(8,128)S(1)}, f32[512,256]{1,0:T(8,128)S(1)}, u32[]{:S(2)}, u32[]{:S(2)}) collective-permute-start(f32[512,256]{1,0:T(8,128)S(1)} %bitcast.17), channel_id=1, source_target_pairs={{0,8},{32,34},{1,9},{33,35},{2,10},{34,32},{3,11},{35,33},{4,12},{... | collective-permute-start | bytes 1572872 | tf_op jit(solution)/shard_map/ppermute | solution.py:335
  187.6 2.4 %collective-permute-start.17 = (f32[768,256]{1,0:T(8,128)S(1)}, f32[768,256]{1,0:T(8,128)S(1)}, u32[]{:S(2)}, u32[]{:S(2)}) collective-permute-start(f32[768,256]{1,0:T(8,128)S(1)} %shard_map.73), channel_id=1, source_target_pairs={{0,32},{32,0},{1,33},{33,1},{2,34},{34,2},{3,35},{35,3},{4,36},{36... | collective-permute-start | bytes 2359304 | tf_op jit(solution)/shard_map/ppermute | solution.py:316
  190.1 20.8 %collective-permute-start.18 = (f32[768,256]{1,0:T(8,128)S(1)}, f32[768,256]{1,0:T(8,128)S(1)}, u32[]{:S(2)}, u32[]{:S(2)}) collective-permute-start(f32[768,256]{1,0:T(8,128)S(1)} %add.82), channel_id=1, source_target_pairs={{0,64},{64,0},{1,65},{65,1},{2,66},{66,2},{3,67},{67,3},{4,68},{68... | collective-permute-start | bytes 2359304 | tf_op jit(solution)/shard_map/ppermute | solution.py:316
  211.1 2.9 %collective-permute-start.19 = (f32[768,256]{1,0:T(8,128)S(1)}, f32[768,256]{1,0:T(8,128)S(1)}, u32[]{:S(2)}, u32[]{:S(2)}) collective-permute-start(f32[768,256]{1,0:T(8,128)S(1)} %subtract_add_fusion), channel_id=1, source_target_pairs={{0,32},{32,0},{1,33},{33,1},{2,34},{34,2},{3,35},{35,3},{4,36},{36... | collective-permute-start | bytes 2359304 | tf_op jit(solution)/shard_map/ppermute | solution.py:316

commit v7 on v6

--- a/solution.py
+++ b/solution.py
@@ -316,10 +316,18 @@
     return lax.ppermute(value, axis, [(0, 1), (1, 0)])
 
 
-def beyond_of(own, ranks):
-    up = [(ranks + i, i + 1) for i in range(ranks - 1)]
-    down = [(i + 1, ranks + i) for i in range(ranks - 1)]
-    return lax.ppermute(own, ("core",) + CELLS, up + down)
+def relay_of(own, ranks):
+    half = ranks // 2
+    pairs = [(ranks + half - 1, 2 * ranks - 1), (half, 0)]
+    return lax.ppermute(own, ("core",) + CELLS, pairs)
+
+
+def beyond_of(sent, ranks):
+    half = ranks // 2
+    up = [(ranks + i, i + 1) for i in range(ranks - 1) if i != half - 1]
+    down = [(i + 1, ranks + i) for i in range(ranks - 1) if i != half - 1]
+    cut = [(2 * ranks - 1, half), (0, ranks + half - 1)]
+    return lax.ppermute(sent, ("core",) + CELLS, up + down + cut)
 
 
 def ring_of(value, shift):
@@ -361,16 +369,20 @@
     cells = neighbour_map.shape[1]
     rows = observed.shape[0] // rings
     low_core = core == 0
-    rank, mine, theirs, both, block, sides, low_core = lax.optimization_barrier(
-        (rank, mine, theirs, both, block, sides, low_core)
+    cells_rank = lax.axis_index(CELLS).astype(jnp.int32)
+    carrier = cells_rank == core * (ranks - 1)
+    rank, mine, theirs, both, block, sides, low_core, carrier = lax.optimization_barrier(
+        (rank, mine, theirs, both, block, sides, low_core, carrier)
     )
     for step in range(ITERS):
         if step == 0:
-            p1, h1, l1, p3, h3, l3, *halves = first_forward(sides, sensitivity, models, rows)
+            p2, h2, l2, *halves = first_forward(block[2], sensitivity, models, rows)
+            s2 = [h2, l2]
+            r2 = ring_of(p2, 2)
+            p1, h1, l1, p3, h3, l3 = rest_forward(sides, sensitivity, halves, rows)
             s1, s3 = [h1, l1], [h3, l3]
             r1, r3 = ring_of(p1, 1), ring_of(p3, 3)
-            p2, *s2 = rest_forward(block[2], sensitivity, halves, rows)
-            r2 = ring_of(p2, 2)
+            p1, halves = lax.optimization_barrier((p1, halves))
             p0, *s0 = rest_forward(block[0], sensitivity, halves, rows)
             p0, start, numbers, mask = lax.optimization_barrier((p0, models, neighbour_map, edge_mask))
             own = jnp.where(low_core, start[:cells], start[cells:])
@@ -393,11 +405,12 @@
         copies = weigh(rank, pieces.reshape(subs, rows // subs, -1), observed)
         w0 = spread(copies.reshape(rows, -1))
         w0, sent = lax.optimization_barrier((w0, own))
-        beyond = beyond_of(sent, ranks)
+        relay = relay_of(sent, ranks)
         w2, w3, w1 = ring_of(w0, 2), ring_of(w0, 1), ring_of(w0, 3)
         near = gather_up([w0], s0)
         near = gather_up([w1, w3], s1 + s3, [near])
-        w2, beyond = lax.optimization_barrier((w2, beyond))
+        near, relay = lax.optimization_barrier((near, relay))
+        beyond = beyond_of(jnp.where(carrier, relay, own), ranks)
         away = close(theirs, w2, s2, near, cells)
         home = close(mine, w2, s2, near, cells)
         half = home + swap(away, "core")

time: 216 us -> 197 us (0.912)
  waiting for transfers between devices: 84.7 us -> 60.7 us
  starting transfers between devices: 36 us -> 42.9 us
    ppermute x12, waiting for transfers between devices: 56.5 us -> 33.6 us  [ring_of(): return lax.ppermute(value, ALL, pairs)]
    ppermute x6, starting transfers between devices: 4.72 us -> 18 us  [swap(): return lax.ppermute(value, axis, [(0, 1), (1, 0)])]
    ppermute x2 -> x4, starting transfers between devices: 14.4 us -> 5.57 us  [the longest x2 4.17 us: beyond_of(): return lax.ppermute(sent, ('core',) + CELLS, up + down + cut)]
    ppermute x6, waiting for transfers between devices: 28.2 us -> 22.7 us  [swap(): return lax.ppermute(value, axis, [(0, 1), (1, 0)])]
    ppermute x2 -> x4, waiting for transfers between devices: 0.01 us -> 4.35 us  [the longest x2 4.35 us: beyond_of(): return lax.ppermute(sent, ('core',) + CELLS, up + down + cut)]
    pallas_call x1, Pallas kernels: 8.21 us -> 5.03 us  [first_forward(): pl.pallas_call(first_kernel, in_specs=[SMEM, hbm, hbm], out_specs=[VMEM]...]
    ppermute x12, starting transfers between devices: 16.8 us -> 19.4 us  [ring_of(): return lax.ppermute(value, ALL, pairs)]
  transfers between devices with their start and end apart: 20 -> 22, of which waited for: 13 -> 13; matrix products, arithmetic and copies ran while one was open for 0% -> 0% of each run, Pallas kernels for 17% -> 20%
where the time goes in v7:
time: 197 us
  waiting for transfers between devices  60.7 us (31%)
  Pallas kernels  49 us (25%)
  starting transfers between devices  42.9 us (22%)
  blocking collectives  40.9 us (21%)
  other arithmetic  2.78 us (1%)
    all_to_all x4, blocking collectives, spread(): lax.all_to_all(value, ALL, 0, 0, axis_index_groups=groups, tiled=True)  40.9 us
    ppermute x12, waiting for transfers between devices, ring_of(): return lax.ppermute(value, ALL, pairs)  33.6 us
    ppermute x6, waiting for transfers between devices, swap(): return lax.ppermute(value, axis, [(0, 1), (1, 0)])  22.7 us
    ppermute x12, starting transfers between devices, ring_of(): return lax.ppermute(value, ALL, pairs)  19.4 us
    ppermute x6, starting transfers between devices, swap(): return lax.ppermute(value, axis, [(0, 1), (1, 0)])  18 us
    pallas_call x2, Pallas kernels, smooth_of(): pl.pallas_call(smooth_kernel, in_specs=[VMEM] * 3, out_specs=VMEM, out_sh...  13.1 us
    pallas_call x4, Pallas kernels, gather_up(): pl.pallas_call(functools.partial(gather_kernel, chunks, len(before) > 0),...  12.5 us
    pallas_call x4, Pallas kernels, forward(): pl.pallas_call(functools.partial(forward_kernel, len(xs), chunks, len(bef...  6.24 us
  transfers between devices with their start and end apart: 22, of which 13 were waited for; matrix products, arithmetic and copies ran while one was open for 0% of the time, Pallas kernels for 20%

profile of v7, /device:TPU:25, one launch (start us, length us, event | category | flops | bytes accessed | tf_op | source)
XLA Modules:
  0.0 196.9 jit_solution(7410720096343365191)
XLA Ops:
  0.1 5.0 %shard_map.55 = (f32[512,256]{1,0:T(8,128)S(1)}, bf16[512,1536]{1,0:T(8,128)(2,1)S(1)}, bf16[512,1536]{1,0:T(8,128)(2,1)S(1)}, bf16[1536,256]{1,0:T(8,128)(2,1)S(1)}, bf16[1536,256]{1,0:T(8,128)(2,1)S(1)}) custom-call(s32[1]{0:T(128)} %bitcast.5.blocks_ref, f32[2048,1536]{1,0:T(8,128)} %s_ref.5, f32[1536,256]{1,0:T(8,128)} %x_ref.1), custom_call_target="tpu_custom_call" | custom-call | flops 1207959552 | bytes 5242880 | tf_op jit(solution)/shard_map/pallas_call | solution.py:91
  5.1 3.7 %collective-permute-start.2 = (f32[512,256]{1,0:T(8,128)S(1)}, f32[512,256]{1,0:T(8,128)S(1)}, u32[]{:S(2)}, u32[]{:S(2)}) collective-permute-start(f32[512,256]{1,0:T(8,128)S(1)} %get-tuple-element.76), channel_id=1, source_target_pairs={{0,8},{32,34},{1,9},{33,35},{2,10},{34,32},{3,11},{35,33},{4,12},{... | collective-permute-start | bytes 1572872 | tf_op jit(solution)/shard_map/ppermute | solution.py:343
  8.8 3.4 %shard_map.56 = (f32[512,256]{1,0:T(8,128)S(1)}, bf16[512,1536]{1,0:T(8,128)(2,1)S(1)}, bf16[512,1536]{1,0:T(8,128)(2,1)S(1)}, f32[512,256]{1,0:T(8,128)S(1)}, b...) custom-call(s32[2]{0:T(128)S(1)} %get-tuple-element.66.blocks_ref, f32[2048,1536]{1,0:T(8,128)S(1)} %copy-done, ...), custom_call_target="tpu_custom_call" | custom-call | flops 2415919104 | bytes 2621440 | tf_op jit(solution)/shard_map/pallas_call | solution.py:128
  16.7 5.0 %collective-permute-done = f32[512,256]{1,0:T(8,128)S(1)} collective-permute-done((f32[512,256]{1,0:T(8,128)S(1)}, f32[512,256]{1,0:T(8,128)S(1)}, u32[]{:S(2)}, u32[]{:S(2)}) %collective-permute-start) | collective-permute-done | bytes 524320 | tf_op jit(solution)/shard_map/ppermute | solution.py:343
  22.1 11.2 %all_to_all.36.pieces_ref = f32[8,64,256]{2,1,0:T(8,128)S(1)} all-to-all(f32[8,64,256]{2,1,0:T(8,128)S(1)} %bitcast.23), channel_id=1, replica_groups={{0,1,2,3,16,17,18,19},{4,5,6,7,20,21,22,23},{8,9,10,11,24,25,26,27},{12..., dimensions={0} | all-to-all | bytes 1048576 | tf_op jit(solution)/shard_map/all_to_all | solution.py:353
  33.4 9.9 %all_to_all.37 = f32[8,64,256]{2,1,0:T(8,128)S(1)} all-to-all(f32[8,64,256]{2,1,0:T(8,128)S(1)} %shard_map.58), channel_id=1, replica_groups={{0,1,2,3,16,17,18,19},{4,5,6,7,20,21,22,23},{8,9,10,11,24,25,26,27},{12..., dimensions={0} | all-to-all | bytes 1048576 | tf_op jit(solution)/shard_map/all_to_all | solution.py:353
  44.0 3.1 %collective-permute-start.4 = (f32[512,256]{1,0:T(8,128)S(1)}, f32[512,256]{1,0:T(8,128)S(1)}, u32[]{:S(2)}, u32[]{:S(2)}) collective-permute-start(f32[512,256]{1,0:T(8,128)S(1)} %bitcast.19), channel_id=1, source_target_pairs={{0,12},{32,35},{1,13},{33,32},{2,14},{34,33},{3,15},{35,34},{4,0},... | collective-permute-start | bytes 1572872 | tf_op jit(solution)/shard_map/ppermute | solution.py:343
  48.3 2.4 %shard_map.59.refs_6_ = f32[256,1536]{1,0:T(8,128)S(1)} custom-call(f32[512,256]{1,0:T(8,128)S(1)} %bitcast.22, bf16[512,1536]{1,0:T(8,128)(2,1)S(1)} %get-tuple-element.89.refs_1_.refs_2_, bf16[512,1536]{1,0:T(8,128)(2,1)S(1)} %get-tuple-element.90.refs_2_.refs_3_), custom_call_target="tpu_custom_call" | custom-call | flops 1207959552 | bytes 2097152 | tf_op jit(solution)/shard_map/pallas_call | solution.py:195
  50.8 8.0 %collective-permute-done.4.refs_0_ = f32[512,256]{1,0:T(8,128)S(1)} collective-permute-done((f32[512,256]{1,0:T(8,128)S(1)}, f32[512,256]{1,0:T(8,128)S(1)}, u32[]{:S(2)}, u32[]{:S(2)}) %collective-permute-start.4) | collective-permute-done | bytes 524320 | tf_op jit(solution)/shard_map/ppermute | solution.py:343
  58.8 3.4 %collective-permute-done.5.refs_1_ = f32[512,256]{1,0:T(8,128)S(1)} collective-permute-done((f32[512,256]{1,0:T(8,128)S(1)}, f32[512,256]{1,0:T(8,128)S(1)}, u32[]{:S(2)}, u32[]{:S(2)}) %collective-permute-start.5) | collective-permute-done | bytes 524320 | tf_op jit(solution)/shard_map/ppermute | solution.py:343
  62.2 3.8 %shard_map.60.start_ref = f32[256,1536]{1,0:T(8,128)S(1)} custom-call(f32[512,256]{1,0:T(8,128)S(1)} %collective-permute-done.4.refs_0_, f32[512,256]{1,0:T(8,128)S(1)} %collective-permute-done.5.refs_1_, bf16[512,1536]{1,0:T(8,128)(2,1)S(1)} %get-tuple-element.85.refs_2_.refs_3_.refs_1_, bf16[512,1536]{1,0:T(8,128)(2,1)S(1)} %get-tuple-element.86.refs_3_.refs_4_.refs_2_, ...), custom_call_target="tpu_custom_call" | custom-call | flops 2415919104 | bytes 2621440 | tf_op jit(solution)/shard_map/pallas_call | solution.py:195
  67.6 6.6 %collective-permute-start.7 = (f32[768,256]{1,0:T(8,128)S(1)}, f32[768,256]{1,0:T(8,128)S(1)}, u32[]{:S(2)}, u32[]{:S(2)}) collective-permute-start(f32[768,256]{1,0:T(8,128)S(1)} %shard_map.62), channel_id=1, source_target_pairs={{0,32},{32,0},{1,33},{33,1},{2,34},{34,2},{3,35},{35,3},{4,36},{36... | collective-permute-start | bytes 2359304 | tf_op jit(solution)/shard_map/ppermute | solution.py:316
  74.3 2.0 %collective-permute-start.9 = (f32[768,256]{1,0:T(8,128)S(1)}, f32[768,256]{1,0:T(8,128)S(1)}, u32[]{:S(2)}, u32[]{:S(2)}) collective-permute-start(f32[768,256]{1,0:T(8,128)S(1)} %broadcast_select_fusion.1), channel_id=1, source_target_pairs={{32,1},{33,2},{34,3},{35,4},{36,5},{37,6},{38,7},{39,8},{40,9},{41... | collective-permute-start | bytes 2359304 | tf_op jit(solution)/shard_map/ppermute | solution.py:330
  79.2 6.5 %shard_map.63.start_ref = f32[768,256]{1,0:T(8,128)S(1)} custom-call(f32[8,768]{1,0:T(8,128)S(1)} %maximum_maximum_fusion.table_ref, f32[768,256]{1,0:T(8,128)S(1)} %get-tuple-element.95.own_ref, f32[768,256]{1,0:T(8,128)S(1)} %get-tuple-element.100.twin_ref), custom_call_target="tpu_custom_call" | custom-call | flops 3623878656 | bytes 3145728 | tf_op jit(solution)/shard_map/pallas_call | solution.py:281
  85.8 2.1 %collective-permute-done.9.beyond_ref = f32[768,256]{1,0:T(8,128)S(1)} collective-permute-done((f32[768,256]{1,0:T(8,128)S(1)}, f32[768,256]{1,0:T(8,128)S(1)}, u32[]{:S(2)}, u32[]{:S(2)}) %collective-permute-start.9) | collective-permute-done | bytes 786464 | tf_op jit(solution)/shard_map/ppermute | solution.py:330
  88.5 10.4 %collective-permute-done.8 = f32[768,256]{1,0:T(8,128)S(1)} collective-permute-done((f32[768,256]{1,0:T(8,128)S(1)}, f32[768,256]{1,0:T(8,128)S(1)}, u32[]{:S(2)}, u32[]{:S(2)}) %collective-permute-start.8) | collective-permute-done | bytes 786464 | tf_op jit(solution)/shard_map/ppermute | solution.py:316
  99.5 2.0 %shard_map.66 = (f32[512,256]{1,0:T(8,128)S(1)}, f32[512,256]{1,0:T(8,128)S(1)}, f32[512,256]{1,0:T(8,128)S(1)}) custom-call(s32[1]{0:T(128)} %bitcast.1.plane_ref.planes_ref, f32[768,256]{1,0:T(8,128)S(1)} %subtract_add_fusion.1.refs_0_.own_ref, bf16[512,1536]{1,0:T(8,128)(2,1)S(1)} %get-tuple-element.83.high_ref.refs_1_, ...), custom_call_target="tpu_custom_call" | custom-call | flops 1811939328 | bytes 2359296 | tf_op jit(solution)/shard_map/pallas_call | solution.py:158
  102.3 2.6 %collective-permute-start.13 = (f32[512,256]{1,0:T(8,128)S(1)}, f32[512,256]{1,0:T(8,128)S(1)}, u32[]{:S(2)}, u32[]{:S(2)}) collective-permute-start(f32[512,256]{1,0:T(8,128)S(1)} %shard_map.68), channel_id=1, source_target_pairs={{0,8},{32,34},{1,9},{33,35},{2,10},{34,32},{3,11},{35,33},{4,12},{... | collective-permute-start | bytes 1572872 | tf_op jit(solution)/shard_map/ppermute | solution.py:343
  106.5 2.7 %collective-permute-start.12 = (f32[512,256]{1,0:T(8,128)S(1)}, f32[512,256]{1,0:T(8,128)S(1)}, u32[]{:S(2)}, u32[]{:S(2)}) collective-permute-start(f32[512,256]{1,0:T(8,128)S(1)} %get-tuple-element.104), channel_id=1, source_target_pairs={{0,12},{32,35},{1,13},{33,32},{2,14},{34,33},{3,15},{35,34},{4,0},... | collective-permute-start | bytes 1572872 | tf_op jit(solution)/shard_map/ppermute | solution.py:343
  109.1 2.0 %shard_map.65 = f32[512,256]{1,0:T(8,128)S(1)} custom-call(s32[2]{0:T(128)S(1)} %get-tuple-element.64.planes_ref, f32[768,256]{1,0:T(8,128)S(1)} %subtract_add_fusion.1.refs_0_.own_ref, f32[768,256]{1,0:T(8,128)S(1)} %collective-permute-done.10.refs_1_.refs_0_.twin_ref, bf16[512,1536]{1,0:T(8,128)(2,1)S(1)} %get-tuple-element.89.refs_1_.refs_2_, ...), custom_call_target="tpu_custom_call" | custom-call | flops 1207959552 | bytes 2097152 | tf_op jit(solution)/shard_map/pallas_call | solution.py:158
  112.3 5.6 %collective-permute-done.11 = f32[512,256]{1,0:T(8,128)S(1)} collective-permute-done((f32[512,256]{1,0:T(8,128)S(1)}, f32[512,256]{1,0:T(8,128)S(1)}, u32[]{:S(2)}, u32[]{:S(2)}) %collective-permute-start.11) | collective-permute-done | bytes 524320 | tf_op jit(solution)/shard_map/ppermute | solution.py:343
  118.0 9.6 %all_to_all.38.pieces_ref = f32[8,64,256]{2,1,0:T(8,128)S(1)} all-to-all(f32[8,64,256]{2,1,0:T(8,128)S(1)} %bitcast.24), channel_id=1, replica_groups={{0,1,2,3,16,17,18,19},{4,5,6,7,20,21,22,23},{8,9,10,11,24,25,26,27},{12..., dimensions={0} | all-to-all | bytes 1048576 | tf_op jit(solution)/shard_map/all_to_all | solution.py:353
  127.7 10.1 %all_to_all.39 = f32[8,64,256]{2,1,0:T(8,128)S(1)} all-to-all(f32[8,64,256]{2,1,0:T(8,128)S(1)} %shard_map.69), channel_id=1, replica_groups={{0,1,2,3,16,17,18,19},{4,5,6,7,20,21,22,23},{8,9,10,11,24,25,26,27},{12..., dimensions={0} | all-to-all | bytes 1048576 | tf_op jit(solution)/shard_map/all_to_all | solution.py:353
  141.8 2.4 %shard_map.70.refs_6_ = f32[256,1536]{1,0:T(8,128)S(1)} custom-call(f32[512,256]{1,0:T(8,128)S(1)} %bitcast.18, bf16[512,1536]{1,0:T(8,128)(2,1)S(1)} %get-tuple-element.89.refs_1_.refs_2_, bf16[512,1536]{1,0:T(8,128)(2,1)S(1)} %get-tuple-element.90.refs_2_.refs_3_), custom_call_target="tpu_custom_call" | custom-call | flops 1207959552 | bytes 2097152 | tf_op jit(solution)/shard_map/pallas_call | solution.py:195
  144.2 2.6 %collective-permute-done.15.refs_0_ = f32[512,256]{1,0:T(8,128)S(1)} collective-permute-done((f32[512,256]{1,0:T(8,128)S(1)}, f32[512,256]{1,0:T(8,128)S(1)}, u32[]{:S(2)}, u32[]{:S(2)}) %collective-permute-start.15) | collective-permute-done | bytes 524320 | tf_op jit(solution)/shard_map/ppermute | solution.py:343
  146.8 7.6 %collective-permute-done.16.refs_1_ = f32[512,256]{1,0:T(8,128)S(1)} collective-permute-done((f32[512,256]{1,0:T(8,128)S(1)}, f32[512,256]{1,0:T(8,128)S(1)}, u32[]{:S(2)}, u32[]{:S(2)}) %collective-permute-start.16) | collective-permute-done | bytes 524320 | tf_op jit(solution)/shard_map/ppermute | solution.py:343
  154.4 3.8 %shard_map.71.start_ref = f32[256,1536]{1,0:T(8,128)S(1)} custom-call(f32[512,256]{1,0:T(8,128)S(1)} %collective-permute-done.15.refs_0_, f32[512,256]{1,0:T(8,128)S(1)} %collective-permute-done.16.refs_1_, bf16[512,1536]{1,0:T(8,128)(2,1)S(1)} %get-tuple-element.85.refs_2_.refs_3_.refs_1_, bf16[512,1536]{1,0:T(8,128)(2,1)S(1)} %get-tuple-element.86.refs_3_.refs_4_.refs_2_, ...), custom_call_target="tpu_custom_call" | custom-call | flops 2415919104 | bytes 2621440 | tf_op jit(solution)/shard_map/pallas_call | solution.py:195
  159.8 8.3 %collective-permute-start.18 = (f32[768,256]{1,0:T(8,128)S(1)}, f32[768,256]{1,0:T(8,128)S(1)}, u32[]{:S(2)}, u32[]{:S(2)}) collective-permute-start(f32[768,256]{1,0:T(8,128)S(1)} %shard_map.73), channel_id=1, source_target_pairs={{0,32},{32,0},{1,33},{33,1},{2,34},{34,2},{3,35},{35,3},{4,36},{36... | collective-permute-start | bytes 2359304 | tf_op jit(solution)/shard_map/ppermute | solution.py:316
  168.2 2.1 %collective-permute-start.20 = (f32[768,256]{1,0:T(8,128)S(1)}, f32[768,256]{1,0:T(8,128)S(1)}, u32[]{:S(2)}, u32[]{:S(2)}) collective-permute-start(f32[768,256]{1,0:T(8,128)S(1)} %broadcast_select_fusion), channel_id=1, source_target_pairs={{32,1},{33,2},{34,3},{35,4},{36,5},{37,6},{38,7},{39,8},{40,9},{41... | collective-permute-start | bytes 2359304 | tf_op jit(solution)/shard_map/ppermute | solution.py:330
  173.0 6.5 %shard_map.74.start_ref = f32[768,256]{1,0:T(8,128)S(1)} custom-call(f32[8,768]{1,0:T(8,128)S(1)} %maximum_maximum_fusion.table_ref, f32[768,256]{1,0:T(8,128)S(1)} %subtract_add_fusion.1.refs_0_.own_ref, f32[768,256]{1,0:T(8,128)S(1)} %collective-permute-done.10.refs_1_.refs_0_.twin_ref), custom_call_target="tpu_custom_call" | custom-call | flops 3623878656 | bytes 3145728 | tf_op jit(solution)/shard_map/pallas_call | solution.py:281
  179.6 2.2 %collective-permute-done.20.beyond_ref = f32[768,256]{1,0:T(8,128)S(1)} collective-permute-done((f32[768,256]{1,0:T(8,128)S(1)}, f32[768,256]{1,0:T(8,128)S(1)}, u32[]{:S(2)}, u32[]{:S(2)}) %collective-permute-start.20) | collective-permute-done | bytes 786464 | tf_op jit(solution)/shard_map/ppermute | solution.py:330
  182.3 10.5 %collective-permute-done.19 = f32[768,256]{1,0:T(8,128)S(1)} collective-permute-done((f32[768,256]{1,0:T(8,128)S(1)}, f32[768,256]{1,0:T(8,128)S(1)}, u32[]{:S(2)}, u32[]{:S(2)}) %collective-permute-start.19) | collective-permute-done | bytes 786464 | tf_op jit(solution)/shard_map/ppermute | solution.py:316
  (67 shorter events, 29.1 us)
Async XLA Ops:
  0.1 8.7 %copy-start = (f32[2048,1536]{1,0:T(8,128)S(1)}, f32[2048,1536]{1,0:T(8,128)}, u32[]{:S(2)}) copy-start(f32[2048,1536]{1,0:T(8,128)} %s_ref.5) | copy-start | bytes 37748740
  5.1 11.6 %collective-permute-start.2 = (f32[512,256]{1,0:T(8,128)S(1)}, f32[512,256]{1,0:T(8,128)S(1)}, u32[]{:S(2)}, u32[]{:S(2)}) collective-permute-start(f32[512,256]{1,0:T(8,128)S(1)} %get-tuple-element.76), channel_id=1, source_target_pairs={{0,8},{32,34},{1,9},{33,35},{2,10},{34,32},{3,11},{35,33},{4,12},{... | collective-permute-start | bytes 1572872 | tf_op jit(solution)/shard_map/ppermute | solution.py:343
  12.2 9.6 %collective-permute-start = (f32[512,256]{1,0:T(8,128)S(1)}, f32[512,256]{1,0:T(8,128)S(1)}, u32[]{:S(2)}, u32[]{:S(2)}) collective-permute-start(f32[512,256]{1,0:T(8,128)S(1)} %get-tuple-element.70), channel_id=1, source_target_pairs={{0,4},{32,33},{1,5},{33,34},{2,6},{34,35},{3,7},{35,32},{4,8},{36,... | collective-permute-start | bytes 1572872 | tf_op jit(solution)/shard_map/ppermute | solution.py:343
  13.0 3.4 %copy-start.4 = (s32[1536]{0:T(1024)S(1)}, s32[1536]{0:T(1024)}, u32[]{:S(2)}) copy-start(s32[1536]{0:T(1024)} %param.9) | copy-start | bytes 18436
  13.0 3.4 %copy-start.3 = (s32[4,768]{1,0:T(4,128)S(1)}, s32[4,768]{1,0:T(4,128)}, u32[]{:S(2)}) copy-start(s32[4,768]{1,0:T(4,128)} %param.8) | copy-start | bytes 36868
  13.0 3.6 %copy-start.2 = (f32[1536,256]{1,0:T(8,128)S(1)}, f32[1536,256]{1,0:T(8,128)}, u32[]{:S(2)}) copy-start(f32[1536,256]{1,0:T(8,128)} %x_ref.1) | copy-start | bytes 4718596
  13.0 9.0 %collective-permute-start.1 = (f32[512,256]{1,0:T(8,128)S(1)}, f32[512,256]{1,0:T(8,128)S(1)}, u32[]{:S(2)}, u32[]{:S(2)}) collective-permute-start(f32[512,256]{1,0:T(8,128)S(1)} %get-tuple-element.75), channel_id=1, source_target_pairs={{0,12},{32,35},{1,13},{33,32},{2,14},{34,33},{3,15},{35,34},{4,0},... | collective-permute-start | bytes 1572872 | tf_op jit(solution)/shard_map/ppermute | solution.py:343
  16.7 16.6 %copy-start.1 = (f32[2048,256]{1,0:T(8,128)S(1)}, f32[2048,256]{1,0:T(8,128)}, u32[]{:S(2)}) copy-start(f32[2048,256]{1,0:T(8,128)} %observed_ref.3) | copy-start | bytes 6291460
  43.3 22.8 %collective-permute-start.6 = (f32[768,256]{1,0:T(8,128)S(1)}, f32[768,256]{1,0:T(8,128)S(1)}, u32[]{:S(2)}, u32[]{:S(2)}) collective-permute-start(f32[768,256]{1,0:T(8,128)S(1)} %get-tuple-element.95.own_ref), channel_id=1, source_target_pairs={{47,63},{16,0},{111,127},{80,64}} | collective-permute-start | bytes 2359304 | tf_op jit(solution)/shard_map/ppermute | solution.py:322
  44.0 14.8 %collective-permute-start.4 = (f32[512,256]{1,0:T(8,128)S(1)}, f32[512,256]{1,0:T(8,128)S(1)}, u32[]{:S(2)}, u32[]{:S(2)}) collective-permute-start(f32[512,256]{1,0:T(8,128)S(1)} %bitcast.19), channel_id=1, source_target_pairs={{0,12},{32,35},{1,13},{33,32},{2,14},{34,33},{3,15},{35,34},{4,0},... | collective-permute-start | bytes 1572872 | tf_op jit(solution)/shard_map/ppermute | solution.py:343
  47.1 15.2 %collective-permute-start.5 = (f32[512,256]{1,0:T(8,128)S(1)}, f32[512,256]{1,0:T(8,128)S(1)}, u32[]{:S(2)}, u32[]{:S(2)}) collective-permute-start(f32[512,256]{1,0:T(8,128)S(1)} %bitcast.20), channel_id=1, source_target_pairs={{0,4},{32,33},{1,5},{33,34},{2,6},{34,35},{3,7},{35,32},{4,8},{36,... | collective-permute-start | bytes 1572872 | tf_op jit(solution)/shard_map/ppermute | solution.py:343
  47.1 19.0 %collective-permute-start.3 = (f32[512,256]{1,0:T(8,128)S(1)}, f32[512,256]{1,0:T(8,128)S(1)}, u32[]{:S(2)}, u32[]{:S(2)}) collective-permute-start(f32[512,256]{1,0:T(8,128)S(1)} %bitcast.21), channel_id=1, source_target_pairs={{0,8},{32,34},{1,9},{33,35},{2,10},{34,32},{3,11},{35,33},{4,12},{... | collective-permute-start | bytes 1572872 | tf_op jit(solution)/shard_map/ppermute | solution.py:343
  67.6 10.3 %collective-permute-start.7 = (f32[768,256]{1,0:T(8,128)S(1)}, f32[768,256]{1,0:T(8,128)S(1)}, u32[]{:S(2)}, u32[]{:S(2)}) collective-permute-start(f32[768,256]{1,0:T(8,128)S(1)} %shard_map.62), channel_id=1, source_target_pairs={{0,32},{32,0},{1,33},{33,1},{2,34},{34,2},{3,35},{35,3},{4,36},{36... | collective-permute-start | bytes 2359304 | tf_op jit(solution)/shard_map/ppermute | solution.py:316
  74.3 13.6 %collective-permute-start.9 = (f32[768,256]{1,0:T(8,128)S(1)}, f32[768,256]{1,0:T(8,128)S(1)}, u32[]{:S(2)}, u32[]{:S(2)}) collective-permute-start(f32[768,256]{1,0:T(8,128)S(1)} %broadcast_select_fusion.1), channel_id=1, source_target_pairs={{32,1},{33,2},{34,3},{35,4},{36,5},{37,6},{38,7},{39,8},{40,9},{41... | collective-permute-start | bytes 2359304 | tf_op jit(solution)/shard_map/ppermute | solution.py:330
  78.0 20.8 %collective-permute-start.8 = (f32[768,256]{1,0:T(8,128)S(1)}, f32[768,256]{1,0:T(8,128)S(1)}, u32[]{:S(2)}, u32[]{:S(2)}) collective-permute-start(f32[768,256]{1,0:T(8,128)S(1)} %add.84), channel_id=1, source_target_pairs={{0,64},{64,0},{1,65},{65,1},{2,66},{66,2},{3,67},{67,3},{4,68},{68... | collective-permute-start | bytes 2359304 | tf_op jit(solution)/shard_map/ppermute | solution.py:316
  99.0 2.5 %collective-permute-start.10 = (f32[768,256]{1,0:T(8,128)S(1)}, f32[768,256]{1,0:T(8,128)S(1)}, u32[]{:S(2)}, u32[]{:S(2)}) collective-permute-start(f32[768,256]{1,0:T(8,128)S(1)} %subtract_add_fusion.1.refs_0_.own_ref), channel_id=1, source_target_pairs={{0,32},{32,0},{1,33},{33,1},{2,34},{34,2},{3,35},{35,3},{4,36},{36... | collective-permute-start | bytes 2359304 | tf_op jit(solution)/shard_map/ppermute | solution.py:316
  102.3 10.0 %collective-permute-start.13 = (f32[512,256]{1,0:T(8,128)S(1)}, f32[512,256]{1,0:T(8,128)S(1)}, u32[]{:S(2)}, u32[]{:S(2)}) collective-permute-start(f32[512,256]{1,0:T(8,128)S(1)} %shard_map.68), channel_id=1, source_target_pairs={{0,8},{32,34},{1,9},{33,35},{2,10},{34,32},{3,11},{35,33},{4,12},{... | collective-permute-start | bytes 1572872 | tf_op jit(solution)/shard_map/ppermute | solution.py:343
  106.4 11.5 %collective-permute-start.11 = (f32[512,256]{1,0:T(8,128)S(1)}, f32[512,256]{1,0:T(8,128)S(1)}, u32[]{:S(2)}, u32[]{:S(2)}) collective-permute-start(f32[512,256]{1,0:T(8,128)S(1)} %get-tuple-element.103), channel_id=1, source_target_pairs={{0,4},{32,33},{1,5},{33,34},{2,6},{34,35},{3,7},{35,32},{4,8},{36,... | collective-permute-start | bytes 1572872 | tf_op jit(solution)/shard_map/ppermute | solution.py:343
  106.5 11.4 %collective-permute-start.12 = (f32[512,256]{1,0:T(8,128)S(1)}, f32[512,256]{1,0:T(8,128)S(1)}, u32[]{:S(2)}, u32[]{:S(2)}) collective-permute-start(f32[512,256]{1,0:T(8,128)S(1)} %get-tuple-element.104), channel_id=1, source_target_pairs={{0,12},{32,35},{1,13},{33,32},{2,14},{34,33},{3,15},{35,34},{4,0},... | collective-permute-start | bytes 1572872 | tf_op jit(solution)/shard_map/ppermute | solution.py:343
  137.8 20.5 %collective-permute-start.17 = (f32[768,256]{1,0:T(8,128)S(1)}, f32[768,256]{1,0:T(8,128)S(1)}, u32[]{:S(2)}, u32[]{:S(2)}) collective-permute-start(f32[768,256]{1,0:T(8,128)S(1)} %subtract_add_fusion.1.refs_0_.own_ref), channel_id=1, source_target_pairs={{47,63},{16,0},{111,127},{80,64}} | collective-permute-start | bytes 2359304 | tf_op jit(solution)/shard_map/ppermute | solution.py:322
  138.5 8.3 %collective-permute-start.15 = (f32[512,256]{1,0:T(8,128)S(1)}, f32[512,256]{1,0:T(8,128)S(1)}, u32[]{:S(2)}, u32[]{:S(2)}) collective-permute-start(f32[512,256]{1,0:T(8,128)S(1)} %bitcast.15), channel_id=1, source_target_pairs={{0,12},{32,35},{1,13},{33,32},{2,14},{34,33},{3,15},{35,34},{4,0},... | collective-permute-start | bytes 1572872 | tf_op jit(solution)/shard_map/ppermute | solution.py:343
  139.3 15.2 %collective-permute-start.16 = (f32[512,256]{1,0:T(8,128)S(1)}, f32[512,256]{1,0:T(8,128)S(1)}, u32[]{:S(2)}, u32[]{:S(2)}) collective-permute-start(f32[512,256]{1,0:T(8,128)S(1)} %bitcast.16), channel_id=1, source_target_pairs={{0,4},{32,33},{1,5},{33,34},{2,6},{34,35},{3,7},{35,32},{4,8},{36,... | collective-permute-start | bytes 1572872 | tf_op jit(solution)/shard_map/ppermute | solution.py:343
  140.1 18.2 %collective-permute-start.14 = (f32[512,256]{1,0:T(8,128)S(1)}, f32[512,256]{1,0:T(8,128)S(1)}, u32[]{:S(2)}, u32[]{:S(2)}) collective-permute-start(f32[512,256]{1,0:T(8,128)S(1)} %bitcast.17), channel_id=1, source_target_pairs={{0,8},{32,34},{1,9},{33,35},{2,10},{34,32},{3,11},{35,33},{4,12},{... | collective-permute-start | bytes 1572872 | tf_op jit(solution)/shard_map/ppermute | solution.py:343
  159.8 12.1 %collective-permute-start.18 = (f32[768,256]{1,0:T(8,128)S(1)}, f32[768,256]{1,0:T(8,128)S(1)}, u32[]{:S(2)}, u32[]{:S(2)}) collective-permute-start(f32[768,256]{1,0:T(8,128)S(1)} %shard_map.73), channel_id=1, source_target_pairs={{0,32},{32,0},{1,33},{33,1},{2,34},{34,2},{3,35},{35,3},{4,36},{36... | collective-permute-start | bytes 2359304 | tf_op jit(solution)/shard_map/ppermute | solution.py:316
  168.2 13.6 %collective-permute-start.20 = (f32[768,256]{1,0:T(8,128)S(1)}, f32[768,256]{1,0:T(8,128)S(1)}, u32[]{:S(2)}, u32[]{:S(2)}) collective-permute-start(f32[768,256]{1,0:T(8,128)S(1)} %broadcast_select_fusion), channel_id=1, source_target_pairs={{32,1},{33,2},{34,3},{35,4},{36,5},{37,6},{38,7},{39,8},{40,9},{41... | collective-permute-start | bytes 2359304 | tf_op jit(solution)/shard_map/ppermute | solution.py:330
  172.0 20.9 %collective-permute-start.19 = (f32[768,256]{1,0:T(8,128)S(1)}, f32[768,256]{1,0:T(8,128)S(1)}, u32[]{:S(2)}, u32[]{:S(2)}) collective-permute-start(f32[768,256]{1,0:T(8,128)S(1)} %add.90), channel_id=1, source_target_pairs={{0,64},{64,0},{1,65},{65,1},{2,66},{66,2},{3,67},{67,3},{4,68},{68... | collective-permute-start | bytes 2359304 | tf_op jit(solution)/shard_map/ppermute | solution.py:316
  193.1 2.4 %collective-permute-start.21 = (f32[768,256]{1,0:T(8,128)S(1)}, f32[768,256]{1,0:T(8,128)S(1)}, u32[]{:S(2)}, u32[]{:S(2)}) collective-permute-start(f32[768,256]{1,0:T(8,128)S(1)} %subtract_add_fusion), channel_id=1, source_target_pairs={{0,32},{32,0},{1,33},{33,1},{2,34},{34,2},{3,35},{35,3},{4,36},{36... | collective-permute-start | bytes 2359304 | tf_op jit(solution)/shard_map/ppermute | solution.py:316

commit v8 on v7

--- a/solution.py
+++ b/solution.py
@@ -293,23 +293,24 @@
     )(table, own, twin)
 
 
-def edge_kernel(table_ref, own_ref, beyond_ref, start_ref, total_ref):
+def edge_kernel(table_ref, own_ref, beyond_ref, inner_ref, start_ref, new_ref):
     weight = table_ref[...].T[:, 4:5]
-    total_ref[...] = weight * (start_ref[...] + huber(beyond_ref[...] - own_ref[...]))
-
-
-def edge_of(table, own, beyond, start):
+    total = inner_ref[...] + huber(beyond_ref[...] - own_ref[...])
+    new_ref[...] = start_ref[...] + weight * total
+
+
+def edge_of(table, own, beyond, inner, start):
     cells, sols = own.shape
     return pl.pallas_call(
         edge_kernel,
-        in_specs=[VMEM] * 4,
+        in_specs=[VMEM] * 5,
         out_specs=VMEM,
         out_shape=jax.ShapeDtypeStruct(own.shape, F32),
         compiler_params=PARAMS,
         cost_estimate=pl.CostEstimate(
             flops=6 * cells * sols, bytes_accessed=16 * cells * sols, transcendentals=2 * cells * sols
         ),
-    )(table, own, beyond, start)
+    )(table, own, beyond, inner, start)
 
 
 def swap(value, axis):
@@ -408,16 +409,18 @@
         relay = relay_of(sent, ranks)
         w2, w3, w1 = ring_of(w0, 2), ring_of(w0, 1), ring_of(w0, 3)
         near = gather_up([w0], s0)
-        near = gather_up([w1, w3], s1 + s3, [near])
+        near = gather_up([w3], s3, [near])
+        near = gather_up([w1], s1, [near])
         near, relay = lax.optimization_barrier((near, relay))
-        beyond = beyond_of(jnp.where(carrier, relay, own), ranks)
+        sent = jnp.where(carrier, relay, own)
         away = close(theirs, w2, s2, near, cells)
         home = close(mine, w2, s2, near, cells)
         half = home + swap(away, "core")
-        half, own, twin = lax.optimization_barrier((half, own, twin))
+        half, own, twin, sent = lax.optimization_barrier((half, own, twin, sent))
+        beyond = beyond_of(sent, ranks)
         gradient = half + swap(half, "yh")
         inner = smooth_of(table, own, twin)
-        own = own - 1.0 * gradient + edge_of(table, own, beyond, inner)
+        own = edge_of(table, own, beyond, inner, own - 1.0 * gradient)
     twin = swap(own, "core")
     place = lax.broadcasted_iota(jnp.int32, (2, 1, 1), 0)
     planes = jnp.where((place == 0) == low_core, own[None], twin[None])

time: 197 us -> 201 us (1.020)
  starting transfers between devices: 42.9 us -> 48.3 us
  waiting for transfers between devices: 60.7 us -> 56.4 us
  Pallas kernels: 49 us -> 51.2 us
    ppermute x6, starting transfers between devices: 18 us -> 28.3 us  [swap(): return lax.ppermute(value, axis, [(0, 1), (1, 0)])]
    ppermute x12, starting transfers between devices: 19.4 us -> 14.6 us  [ring_of(): return lax.ppermute(value, ALL, pairs)]
    ppermute x2, waiting for transfers between devices: 4.35 us -> 0.01 us  [beyond_of(): return lax.ppermute(sent, ('core',) + CELLS, up + down + cut)]
    pallas_call x4 -> x6, Pallas kernels: 12.5 us -> 14.7 us  [gather_up(): pl.pallas_call(functools.partial(gather_kernel, chunks, len(before) > 0),...]
  transfers between devices with their start and end apart: 22 -> 22, of which waited for: 13 -> 13; matrix products, arithmetic and copies ran while one was open for 0% -> 0% of each run, Pallas kernels for 20% -> 18%
where the time goes in v8:
time: 201 us
  waiting for transfers between devices  56.4 us (28%)
  Pallas kernels  51.2 us (25%)
  starting transfers between devices  48.3 us (24%)
  blocking collectives  40.9 us (20%)
  other arithmetic  2.73 us (1%)
    all_to_all x4, blocking collectives, spread(): lax.all_to_all(value, ALL, 0, 0, axis_index_groups=groups, tiled=True)  40.9 us
    ppermute x12, waiting for transfers between devices, ring_of(): return lax.ppermute(value, ALL, pairs)  32.5 us
    ppermute x6, starting transfers between devices, swap(): return lax.ppermute(value, axis, [(0, 1), (1, 0)])  28.3 us
    ppermute x6, waiting for transfers between devices, swap(): return lax.ppermute(value, axis, [(0, 1), (1, 0)])  23.9 us
    pallas_call x6, Pallas kernels, gather_up(): pl.pallas_call(functools.partial(gather_kernel, chunks, len(before) > 0),...  14.7 us
    ppermute x12, starting transfers between devices, ring_of(): return lax.ppermute(value, ALL, pairs)  14.6 us
    pallas_call x2, Pallas kernels, smooth_of(): pl.pallas_call(smooth_kernel, in_specs=[VMEM] * 3, out_specs=VMEM, out_sh...  13.1 us
    pallas_call x4, Pallas kernels, forward(): pl.pallas_call(functools.partial(forward_kernel, len(xs), chunks, len(bef...  6.15 us
  transfers between devices with their start and end apart: 22, of which 13 were waited for; matrix products, arithmetic and copies ran while one was open for 0% of the time, Pallas kernels for 18%

profile of v8, /device:TPU:25, one launch (start us, length us, event | category | flops | bytes accessed | tf_op | source)
XLA Modules:
  0.0 201.1 jit_solution(2522094709022870386)
XLA Ops:
  0.1 5.0 %shard_map.55 = (f32[512,256]{1,0:T(8,128)S(1)}, bf16[512,1536]{1,0:T(8,128)(2,1)S(1)}, bf16[512,1536]{1,0:T(8,128)(2,1)S(1)}, bf16[1536,256]{1,0:T(8,128)(2,1)S(1)}, bf16[1536,256]{1,0:T(8,128)(2,1)S(1)}) custom-call(s32[1]{0:T(128)} %bitcast.5.blocks_ref, f32[2048,1536]{1,0:T(8,128)} %s_ref.5, f32[1536,256]{1,0:T(8,128)} %x_ref.1), custom_call_target="tpu_custom_call" | custom-call | flops 1207959552 | bytes 5242880 | tf_op jit(solution)/shard_map/pallas_call | solution.py:91
  6.1 3.4 %shard_map.56 = (f32[512,256]{1,0:T(8,128)S(1)}, bf16[512,1536]{1,0:T(8,128)(2,1)S(1)}, bf16[512,1536]{1,0:T(8,128)(2,1)S(1)}, f32[512,256]{1,0:T(8,128)S(1)}, b...) custom-call(s32[2]{0:T(128)S(1)} %get-tuple-element.66.blocks_ref, f32[2048,1536]{1,0:T(8,128)S(1)} %copy-done, ...), custom_call_target="tpu_custom_call" | custom-call | flops 2415919104 | bytes 2621440 | tf_op jit(solution)/shard_map/pallas_call | solution.py:128
  11.2 2.2 %collective-permute-start.1 = (f32[512,256]{1,0:T(8,128)S(1)}, f32[512,256]{1,0:T(8,128)S(1)}, u32[]{:S(2)}, u32[]{:S(2)}) collective-permute-start(f32[512,256]{1,0:T(8,128)S(1)} %get-tuple-element.75), channel_id=1, source_target_pairs={{0,12},{32,35},{1,13},{33,32},{2,14},{34,33},{3,15},{35,34},{4,0},... | collective-permute-start | bytes 1572872 | tf_op jit(solution)/shard_map/ppermute | solution.py:344
  16.4 3.8 %collective-permute-done = f32[512,256]{1,0:T(8,128)S(1)} collective-permute-done((f32[512,256]{1,0:T(8,128)S(1)}, f32[512,256]{1,0:T(8,128)S(1)}, u32[]{:S(2)}, u32[]{:S(2)}) %collective-permute-start) | collective-permute-done | bytes 524320 | tf_op jit(solution)/shard_map/ppermute | solution.py:344
  20.2 5.0 %collective-permute-done.1 = f32[512,256]{1,0:T(8,128)S(1)} collective-permute-done((f32[512,256]{1,0:T(8,128)S(1)}, f32[512,256]{1,0:T(8,128)S(1)}, u32[]{:S(2)}, u32[]{:S(2)}) %collective-permute-start.1) | collective-permute-done | bytes 524320 | tf_op jit(solution)/shard_map/ppermute | solution.py:344
  27.0 11.5 %all_to_all.36.pieces_ref = f32[8,64,256]{2,1,0:T(8,128)S(1)} all-to-all(f32[8,64,256]{2,1,0:T(8,128)S(1)} %bitcast.23), channel_id=1, replica_groups={{0,1,2,3,16,17,18,19},{4,5,6,7,20,21,22,23},{8,9,10,11,24,25,26,27},{12..., dimensions={0} | all-to-all | bytes 1048576 | tf_op jit(solution)/shard_map/all_to_all | solution.py:354
  38.5 10.0 %all_to_all.37 = f32[8,64,256]{2,1,0:T(8,128)S(1)} all-to-all(f32[8,64,256]{2,1,0:T(8,128)S(1)} %shard_map.58), channel_id=1, replica_groups={{0,1,2,3,16,17,18,19},{4,5,6,7,20,21,22,23},{8,9,10,11,24,25,26,27},{12..., dimensions={0} | all-to-all | bytes 1048576 | tf_op jit(solution)/shard_map/all_to_all | solution.py:354
  50.0 1.9 collective-permute-start.4
  52.2 2.4 %shard_map.59.refs_3_ = f32[256,1536]{1,0:T(8,128)S(1)} custom-call(f32[512,256]{1,0:T(8,128)S(1)} %bitcast.22, bf16[512,1536]{1,0:T(8,128)(2,1)S(1)} %get-tuple-element.92.refs_1_.refs_2_, bf16[512,1536]{1,0:T(8,128)(2,1)S(1)} %get-tuple-element.93.refs_2_.refs_3_), custom_call_target="tpu_custom_call" | custom-call | flops 1207959552 | bytes 2097152 | tf_op jit(solution)/shard_map/pallas_call | solution.py:195
  54.7 3.8 %collective-permute-done.5.refs_0_ = f32[512,256]{1,0:T(8,128)S(1)} collective-permute-done((f32[512,256]{1,0:T(8,128)S(1)}, f32[512,256]{1,0:T(8,128)S(1)}, u32[]{:S(2)}, u32[]{:S(2)}) %collective-permute-start.5) | collective-permute-done | bytes 524320 | tf_op jit(solution)/shard_map/ppermute | solution.py:344
  58.5 2.5 %shard_map.60.refs_3_ = f32[256,1536]{1,0:T(8,128)S(1)} custom-call(f32[512,256]{1,0:T(8,128)S(1)} %collective-permute-done.5.refs_0_, bf16[512,1536]{1,0:T(8,128)(2,1)S(1)} %get-tuple-element.90.refs_1_.refs_5_.refs_3_, bf16[512,1536]{1,0:T(8,128)(2,1)S(1)} %get-tuple-element.91.refs_2_.refs_6_.refs_4_, f32[256,1536]{1,0:T(8,128)S(1)} %shard_map.59.refs_3_), custom_call_target="tpu_custom_call" | custom-call | flops 1207959552 | bytes 2097152 | tf_op jit(solution)/shard_map/pallas_call | solution.py:195
  61.0 2.7 %collective-permute-done.4.refs_0_ = f32[512,256]{1,0:T(8,128)S(1)} collective-permute-done((f32[512,256]{1,0:T(8,128)S(1)}, f32[512,256]{1,0:T(8,128)S(1)}, u32[]{:S(2)}, u32[]{:S(2)}) %collective-permute-start.4) | collective-permute-done | bytes 524320 | tf_op jit(solution)/shard_map/ppermute | solution.py:344
  63.7 2.5 %shard_map.61.start_ref = f32[256,1536]{1,0:T(8,128)S(1)} custom-call(f32[512,256]{1,0:T(8,128)S(1)} %collective-permute-done.4.refs_0_, bf16[512,1536]{1,0:T(8,128)(2,1)S(1)} %get-tuple-element.88.refs_1_.refs_3_, bf16[512,1536]{1,0:T(8,128)(2,1)S(1)} %get-tuple-element.89.refs_2_.refs_4_, f32[256,1536]{1,0:T(8,128)S(1)} %shard_map.60.refs_3_), custom_call_target="tpu_custom_call" | custom-call | flops 1207959552 | bytes 2097152 | tf_op jit(solution)/shard_map/pallas_call | solution.py:195
  67.7 11.8 %collective-permute-start.7 = (f32[768,256]{1,0:T(8,128)S(1)}, f32[768,256]{1,0:T(8,128)S(1)}, u32[]{:S(2)}, u32[]{:S(2)}) collective-permute-start(f32[768,256]{1,0:T(8,128)S(1)} %shard_map.63), channel_id=1, source_target_pairs={{0,32},{32,0},{1,33},{33,1},{2,34},{34,2},{3,35},{35,3},{4,36},{36... | collective-permute-start | bytes 2359304 | tf_op jit(solution)/shard_map/ppermute | solution.py:317
  82.5 2.1 %collective-permute-start.8 = (f32[768,256]{1,0:T(8,128)S(1)}, f32[768,256]{1,0:T(8,128)S(1)}, u32[]{:S(2)}, u32[]{:S(2)}) collective-permute-start(f32[768,256]{1,0:T(8,128)S(1)} %broadcast_select_fusion.1), channel_id=1, source_target_pairs={{32,1},{33,2},{34,3},{35,4},{36,5},{37,6},{38,7},{39,8},{40,9},{41... | collective-permute-start | bytes 2359304 | tf_op jit(solution)/shard_map/ppermute | solution.py:331
  84.6 6.5 %shard_map.64.inner_ref = f32[768,256]{1,0:T(8,128)S(1)} custom-call(f32[8,768]{1,0:T(8,128)S(1)} %maximum_maximum_fusion.table_ref, f32[768,256]{1,0:T(8,128)S(1)} %get-tuple-element.100.own_ref, f32[768,256]{1,0:T(8,128)S(1)} %get-tuple-element.102.twin_ref), custom_call_target="tpu_custom_call" | custom-call | flops 3623878656 | bytes 3145728 | tf_op jit(solution)/shard_map/pallas_call | solution.py:281
  91.1 10.7 %collective-permute-done.9 = f32[768,256]{1,0:T(8,128)S(1)} collective-permute-done((f32[768,256]{1,0:T(8,128)S(1)}, f32[768,256]{1,0:T(8,128)S(1)}, u32[]{:S(2)}, u32[]{:S(2)}) %collective-permute-start.9) | collective-permute-done | bytes 786464 | tf_op jit(solution)/shard_map/ppermute | solution.py:317
  103.9 2.0 %shard_map.67 = (f32[512,256]{1,0:T(8,128)S(1)}, f32[512,256]{1,0:T(8,128)S(1)}, f32[512,256]{1,0:T(8,128)S(1)}) custom-call(s32[1]{0:T(128)} %bitcast.1.plane_ref.planes_ref, f32[768,256]{1,0:T(8,128)S(1)} %shard_map.65.refs_0_.own_ref, bf16[512,1536]{1,0:T(8,128)(2,1)S(1)} %get-tuple-element.86.high_ref.refs_1_, ...), custom_call_target="tpu_custom_call" | custom-call | flops 1811939328 | bytes 2359296 | tf_op jit(solution)/shard_map/pallas_call | solution.py:158
  107.4 2.7 %collective-permute-start.12 = (f32[512,256]{1,0:T(8,128)S(1)}, f32[512,256]{1,0:T(8,128)S(1)}, u32[]{:S(2)}, u32[]{:S(2)}) collective-permute-start(f32[512,256]{1,0:T(8,128)S(1)} %get-tuple-element.107), channel_id=1, source_target_pairs={{0,12},{32,35},{1,13},{33,32},{2,14},{34,33},{3,15},{35,34},{4,0},... | collective-permute-start | bytes 1572872 | tf_op jit(solution)/shard_map/ppermute | solution.py:344
  110.9 2.0 shard_map.66
  112.9 9.6 %collective-permute-done.11 = f32[512,256]{1,0:T(8,128)S(1)} collective-permute-done((f32[512,256]{1,0:T(8,128)S(1)}, f32[512,256]{1,0:T(8,128)S(1)}, u32[]{:S(2)}, u32[]{:S(2)}) %collective-permute-start.11) | collective-permute-done | bytes 524320 | tf_op jit(solution)/shard_map/ppermute | solution.py:344
  122.7 9.4 %all_to_all.38.pieces_ref = f32[8,64,256]{2,1,0:T(8,128)S(1)} all-to-all(f32[8,64,256]{2,1,0:T(8,128)S(1)} %bitcast.24), channel_id=1, replica_groups={{0,1,2,3,16,17,18,19},{4,5,6,7,20,21,22,23},{8,9,10,11,24,25,26,27},{12..., dimensions={0} | all-to-all | bytes 1048576 | tf_op jit(solution)/shard_map/all_to_all | solution.py:354
  132.1 10.0 %all_to_all.39 = f32[8,64,256]{2,1,0:T(8,128)S(1)} all-to-all(f32[8,64,256]{2,1,0:T(8,128)S(1)} %shard_map.70), channel_id=1, replica_groups={{0,1,2,3,16,17,18,19},{4,5,6,7,20,21,22,23},{8,9,10,11,24,25,26,27},{12..., dimensions={0} | all-to-all | bytes 1048576 | tf_op jit(solution)/shard_map/all_to_all | solution.py:354
  143.3 2.3 %collective-permute-start.15 = (f32[512,256]{1,0:T(8,128)S(1)}, f32[512,256]{1,0:T(8,128)S(1)}, u32[]{:S(2)}, u32[]{:S(2)}) collective-permute-start(f32[512,256]{1,0:T(8,128)S(1)} %bitcast.16), channel_id=1, source_target_pairs={{0,12},{32,35},{1,13},{33,32},{2,14},{34,33},{3,15},{35,34},{4,0},... | collective-permute-start | bytes 1572872 | tf_op jit(solution)/shard_map/ppermute | solution.py:344
  146.5 2.4 %shard_map.71.refs_3_ = f32[256,1536]{1,0:T(8,128)S(1)} custom-call(f32[512,256]{1,0:T(8,128)S(1)} %bitcast.18, bf16[512,1536]{1,0:T(8,128)(2,1)S(1)} %get-tuple-element.92.refs_1_.refs_2_, bf16[512,1536]{1,0:T(8,128)(2,1)S(1)} %get-tuple-element.93.refs_2_.refs_3_), custom_call_target="tpu_custom_call" | custom-call | flops 1207959552 | bytes 2097152 | tf_op jit(solution)/shard_map/pallas_call | solution.py:195
  148.9 3.2 %collective-permute-done.16.refs_0_ = f32[512,256]{1,0:T(8,128)S(1)} collective-permute-done((f32[512,256]{1,0:T(8,128)S(1)}, f32[512,256]{1,0:T(8,128)S(1)}, u32[]{:S(2)}, u32[]{:S(2)}) %collective-permute-start.16) | collective-permute-done | bytes 524320 | tf_op jit(solution)/shard_map/ppermute | solution.py:344
  152.1 2.5 %shard_map.72.refs_3_ = f32[256,1536]{1,0:T(8,128)S(1)} custom-call(f32[512,256]{1,0:T(8,128)S(1)} %collective-permute-done.16.refs_0_, bf16[512,1536]{1,0:T(8,128)(2,1)S(1)} %get-tuple-element.90.refs_1_.refs_5_.refs_3_, bf16[512,1536]{1,0:T(8,128)(2,1)S(1)} %get-tuple-element.91.refs_2_.refs_6_.refs_4_, f32[256,1536]{1,0:T(8,128)S(1)} %shard_map.71.refs_3_), custom_call_target="tpu_custom_call" | custom-call | flops 1207959552 | bytes 2097152 | tf_op jit(solution)/shard_map/pallas_call | solution.py:195
  154.6 2.7 %collective-permute-done.15.refs_0_ = f32[512,256]{1,0:T(8,128)S(1)} collective-permute-done((f32[512,256]{1,0:T(8,128)S(1)}, f32[512,256]{1,0:T(8,128)S(1)}, u32[]{:S(2)}, u32[]{:S(2)}) %collective-permute-start.15) | collective-permute-done | bytes 524320 | tf_op jit(solution)/shard_map/ppermute | solution.py:344
  157.3 2.5 %shard_map.73.start_ref = f32[256,1536]{1,0:T(8,128)S(1)} custom-call(f32[512,256]{1,0:T(8,128)S(1)} %collective-permute-done.15.refs_0_, bf16[512,1536]{1,0:T(8,128)(2,1)S(1)} %get-tuple-element.88.refs_1_.refs_3_, bf16[512,1536]{1,0:T(8,128)(2,1)S(1)} %get-tuple-element.89.refs_2_.refs_4_, f32[256,1536]{1,0:T(8,128)S(1)} %shard_map.72.refs_3_), custom_call_target="tpu_custom_call" | custom-call | flops 1207959552 | bytes 2097152 | tf_op jit(solution)/shard_map/pallas_call | solution.py:195
  161.4 11.8 %collective-permute-start.18 = (f32[768,256]{1,0:T(8,128)S(1)}, f32[768,256]{1,0:T(8,128)S(1)}, u32[]{:S(2)}, u32[]{:S(2)}) collective-permute-start(f32[768,256]{1,0:T(8,128)S(1)} %shard_map.75), channel_id=1, source_target_pairs={{0,32},{32,0},{1,33},{33,1},{2,34},{34,2},{3,35},{35,3},{4,36},{36... | collective-permute-start | bytes 2359304 | tf_op jit(solution)/shard_map/ppermute | solution.py:317
  178.3 6.5 %shard_map.76.inner_ref = f32[768,256]{1,0:T(8,128)S(1)} custom-call(f32[8,768]{1,0:T(8,128)S(1)} %maximum_maximum_fusion.table_ref, f32[768,256]{1,0:T(8,128)S(1)} %shard_map.65.refs_0_.own_ref, f32[768,256]{1,0:T(8,128)S(1)} %collective-permute-done.10.refs_1_.refs_0_.twin_ref), custom_call_target="tpu_custom_call" | custom-call | flops 3623878656 | bytes 3145728 | tf_op jit(solution)/shard_map/pallas_call | solution.py:281
  184.8 10.9 %collective-permute-done.20 = f32[768,256]{1,0:T(8,128)S(1)} collective-permute-done((f32[768,256]{1,0:T(8,128)S(1)}, f32[768,256]{1,0:T(8,128)S(1)}, u32[]{:S(2)}, u32[]{:S(2)}) %collective-permute-start.20) | collective-permute-done | bytes 786464 | tf_op jit(solution)/shard_map/ppermute | solution.py:317
  (69 shorter events, 32.6 us)
Async XLA Ops:
  0.1 6.0 %copy-start = (f32[2048,1536]{1,0:T(8,128)S(1)}, f32[2048,1536]{1,0:T(8,128)}, u32[]{:S(2)}) copy-start(f32[2048,1536]{1,0:T(8,128)} %s_ref.5) | copy-start | bytes 37748740
  9.5 10.7 %collective-permute-start = (f32[512,256]{1,0:T(8,128)S(1)}, f32[512,256]{1,0:T(8,128)S(1)}, u32[]{:S(2)}, u32[]{:S(2)}) collective-permute-start(f32[512,256]{1,0:T(8,128)S(1)} %get-tuple-element.70), channel_id=1, source_target_pairs={{0,4},{32,33},{1,5},{33,34},{2,6},{34,35},{3,7},{35,32},{4,8},{36,... | collective-permute-start | bytes 1572872 | tf_op jit(solution)/shard_map/ppermute | solution.py:344
  11.2 14.0 %collective-permute-start.1 = (f32[512,256]{1,0:T(8,128)S(1)}, f32[512,256]{1,0:T(8,128)S(1)}, u32[]{:S(2)}, u32[]{:S(2)}) collective-permute-start(f32[512,256]{1,0:T(8,128)S(1)} %get-tuple-element.75), channel_id=1, source_target_pairs={{0,12},{32,35},{1,13},{33,32},{2,14},{34,33},{3,15},{35,34},{4,0},... | collective-permute-start | bytes 1572872 | tf_op jit(solution)/shard_map/ppermute | solution.py:344
  13.4 2.7 %copy-start.4 = (s32[1536]{0:T(1024)S(1)}, s32[1536]{0:T(1024)}, u32[]{:S(2)}) copy-start(s32[1536]{0:T(1024)} %param.9) | copy-start | bytes 18436
  13.4 2.7 %copy-start.3 = (s32[4,768]{1,0:T(4,128)S(1)}, s32[4,768]{1,0:T(4,128)}, u32[]{:S(2)}) copy-start(s32[4,768]{1,0:T(4,128)} %param.8) | copy-start | bytes 36868
  13.4 2.9 %copy-start.2 = (f32[1536,256]{1,0:T(8,128)S(1)}, f32[1536,256]{1,0:T(8,128)}, u32[]{:S(2)}) copy-start(f32[1536,256]{1,0:T(8,128)} %x_ref.1) | copy-start | bytes 4718596
  13.4 13.4 %collective-permute-start.2 = (f32[512,256]{1,0:T(8,128)S(1)}, f32[512,256]{1,0:T(8,128)S(1)}, u32[]{:S(2)}, u32[]{:S(2)}) collective-permute-start(f32[512,256]{1,0:T(8,128)S(1)} %get-tuple-element.76), channel_id=1, source_target_pairs={{0,8},{32,34},{1,9},{33,35},{2,10},{34,32},{3,11},{35,33},{4,12},{... | collective-permute-start | bytes 1572872 | tf_op jit(solution)/shard_map/ppermute | solution.py:344
  16.4 22.1 %copy-start.1 = (f32[2048,256]{1,0:T(8,128)S(1)}, f32[2048,256]{1,0:T(8,128)}, u32[]{:S(2)}) copy-start(f32[2048,256]{1,0:T(8,128)} %observed_ref.3) | copy-start | bytes 6291460
  48.5 17.7 %collective-permute-start.6 = (f32[768,256]{1,0:T(8,128)S(1)}, f32[768,256]{1,0:T(8,128)S(1)}, u32[]{:S(2)}, u32[]{:S(2)}) collective-permute-start(f32[768,256]{1,0:T(8,128)S(1)} %get-tuple-element.100.own_ref), channel_id=1, source_target_pairs={{47,63},{16,0},{111,127},{80,64}} | collective-permute-start | bytes 2359304 | tf_op jit(solution)/shard_map/ppermute | solution.py:323
  49.2 9.3 %collective-permute-start.5 = (f32[512,256]{1,0:T(8,128)S(1)}, f32[512,256]{1,0:T(8,128)S(1)}, u32[]{:S(2)}, u32[]{:S(2)}) collective-permute-start(f32[512,256]{1,0:T(8,128)S(1)} %bitcast.19), channel_id=1, source_target_pairs={{0,4},{32,33},{1,5},{33,34},{2,6},{34,35},{3,7},{35,32},{4,8},{36,... | collective-permute-start | bytes 1572872 | tf_op jit(solution)/shard_map/ppermute | solution.py:344
  50.0 13.7 %collective-permute-start.4 = (f32[512,256]{1,0:T(8,128)S(1)}, f32[512,256]{1,0:T(8,128)S(1)}, u32[]{:S(2)}, u32[]{:S(2)}) collective-permute-start(f32[512,256]{1,0:T(8,128)S(1)} %bitcast.20), channel_id=1, source_target_pairs={{0,12},{32,35},{1,13},{33,32},{2,14},{34,33},{3,15},{35,34},{4,0},... | collective-permute-start | bytes 1572872 | tf_op jit(solution)/shard_map/ppermute | solution.py:344
  51.9 14.2 %collective-permute-start.3 = (f32[512,256]{1,0:T(8,128)S(1)}, f32[512,256]{1,0:T(8,128)S(1)}, u32[]{:S(2)}, u32[]{:S(2)}) collective-permute-start(f32[512,256]{1,0:T(8,128)S(1)} %bitcast.21), channel_id=1, source_target_pairs={{0,8},{32,34},{1,9},{33,35},{2,10},{34,32},{3,11},{35,33},{4,12},{... | collective-permute-start | bytes 1572872 | tf_op jit(solution)/shard_map/ppermute | solution.py:344
  67.7 13.7 %collective-permute-start.7 = (f32[768,256]{1,0:T(8,128)S(1)}, f32[768,256]{1,0:T(8,128)S(1)}, u32[]{:S(2)}, u32[]{:S(2)}) collective-permute-start(f32[768,256]{1,0:T(8,128)S(1)} %shard_map.63), channel_id=1, source_target_pairs={{0,32},{32,0},{1,33},{33,1},{2,34},{34,2},{3,35},{35,3},{4,36},{36... | collective-permute-start | bytes 2359304 | tf_op jit(solution)/shard_map/ppermute | solution.py:317
  81.5 20.3 %collective-permute-start.9 = (f32[768,256]{1,0:T(8,128)S(1)}, f32[768,256]{1,0:T(8,128)S(1)}, u32[]{:S(2)}, u32[]{:S(2)}) collective-permute-start(f32[768,256]{1,0:T(8,128)S(1)} %add.78), channel_id=1, source_target_pairs={{0,64},{64,0},{1,65},{65,1},{2,66},{66,2},{3,67},{67,3},{4,68},{68... | collective-permute-start | bytes 2359304 | tf_op jit(solution)/shard_map/ppermute | solution.py:317
  82.5 19.5 %collective-permute-start.8 = (f32[768,256]{1,0:T(8,128)S(1)}, f32[768,256]{1,0:T(8,128)S(1)}, u32[]{:S(2)}, u32[]{:S(2)}) collective-permute-start(f32[768,256]{1,0:T(8,128)S(1)} %broadcast_select_fusion.1), channel_id=1, source_target_pairs={{32,1},{33,2},{34,3},{35,4},{36,5},{37,6},{38,7},{39,8},{40,9},{41... | collective-permute-start | bytes 2359304 | tf_op jit(solution)/shard_map/ppermute | solution.py:331
  102.6 3.3 %collective-permute-start.10 = (f32[768,256]{1,0:T(8,128)S(1)}, f32[768,256]{1,0:T(8,128)S(1)}, u32[]{:S(2)}, u32[]{:S(2)}) collective-permute-start(f32[768,256]{1,0:T(8,128)S(1)} %shard_map.65.refs_0_.own_ref), channel_id=1, source_target_pairs={{0,32},{32,0},{1,33},{33,1},{2,34},{34,2},{3,35},{35,3},{4,36},{36... | collective-permute-start | bytes 2359304 | tf_op jit(solution)/shard_map/ppermute | solution.py:317
  107.3 15.2 %collective-permute-start.11 = (f32[512,256]{1,0:T(8,128)S(1)}, f32[512,256]{1,0:T(8,128)S(1)}, u32[]{:S(2)}, u32[]{:S(2)}) collective-permute-start(f32[512,256]{1,0:T(8,128)S(1)} %get-tuple-element.106), channel_id=1, source_target_pairs={{0,4},{32,33},{1,5},{33,34},{2,6},{34,35},{3,7},{35,32},{4,8},{36,... | collective-permute-start | bytes 1572872 | tf_op jit(solution)/shard_map/ppermute | solution.py:344
  107.4 15.1 %collective-permute-start.12 = (f32[512,256]{1,0:T(8,128)S(1)}, f32[512,256]{1,0:T(8,128)S(1)}, u32[]{:S(2)}, u32[]{:S(2)}) collective-permute-start(f32[512,256]{1,0:T(8,128)S(1)} %get-tuple-element.107), channel_id=1, source_target_pairs={{0,12},{32,35},{1,13},{33,32},{2,14},{34,33},{3,15},{35,34},{4,0},... | collective-permute-start | bytes 1572872 | tf_op jit(solution)/shard_map/ppermute | solution.py:344
  110.8 11.7 %collective-permute-start.13 = (f32[512,256]{1,0:T(8,128)S(1)}, f32[512,256]{1,0:T(8,128)S(1)}, u32[]{:S(2)}, u32[]{:S(2)}) collective-permute-start(f32[512,256]{1,0:T(8,128)S(1)} %shard_map.69), channel_id=1, source_target_pairs={{0,8},{32,34},{1,9},{33,35},{2,10},{34,32},{3,11},{35,33},{4,12},{... | collective-permute-start | bytes 1572872 | tf_op jit(solution)/shard_map/ppermute | solution.py:344
  142.1 17.7 %collective-permute-start.17 = (f32[768,256]{1,0:T(8,128)S(1)}, f32[768,256]{1,0:T(8,128)S(1)}, u32[]{:S(2)}, u32[]{:S(2)}) collective-permute-start(f32[768,256]{1,0:T(8,128)S(1)} %shard_map.65.refs_0_.own_ref), channel_id=1, source_target_pairs={{47,63},{16,0},{111,127},{80,64}} | collective-permute-start | bytes 2359304 | tf_op jit(solution)/shard_map/ppermute | solution.py:323
  142.8 9.3 %collective-permute-start.16 = (f32[512,256]{1,0:T(8,128)S(1)}, f32[512,256]{1,0:T(8,128)S(1)}, u32[]{:S(2)}, u32[]{:S(2)}) collective-permute-start(f32[512,256]{1,0:T(8,128)S(1)} %bitcast.15), channel_id=1, source_target_pairs={{0,4},{32,33},{1,5},{33,34},{2,6},{34,35},{3,7},{35,32},{4,8},{36,... | collective-permute-start | bytes 1572872 | tf_op jit(solution)/shard_map/ppermute | solution.py:344
  143.3 14.1 %collective-permute-start.15 = (f32[512,256]{1,0:T(8,128)S(1)}, f32[512,256]{1,0:T(8,128)S(1)}, u32[]{:S(2)}, u32[]{:S(2)}) collective-permute-start(f32[512,256]{1,0:T(8,128)S(1)} %bitcast.16), channel_id=1, source_target_pairs={{0,12},{32,35},{1,13},{33,32},{2,14},{34,33},{3,15},{35,34},{4,0},... | collective-permute-start | bytes 1572872 | tf_op jit(solution)/shard_map/ppermute | solution.py:344
  145.6 14.2 %collective-permute-start.14 = (f32[512,256]{1,0:T(8,128)S(1)}, f32[512,256]{1,0:T(8,128)S(1)}, u32[]{:S(2)}, u32[]{:S(2)}) collective-permute-start(f32[512,256]{1,0:T(8,128)S(1)} %bitcast.17), channel_id=1, source_target_pairs={{0,8},{32,34},{1,9},{33,35},{2,10},{34,32},{3,11},{35,33},{4,12},{... | collective-permute-start | bytes 1572872 | tf_op jit(solution)/shard_map/ppermute | solution.py:344
  161.4 13.7 %collective-permute-start.18 = (f32[768,256]{1,0:T(8,128)S(1)}, f32[768,256]{1,0:T(8,128)S(1)}, u32[]{:S(2)}, u32[]{:S(2)}) collective-permute-start(f32[768,256]{1,0:T(8,128)S(1)} %shard_map.75), channel_id=1, source_target_pairs={{0,32},{32,0},{1,33},{33,1},{2,34},{34,2},{3,35},{35,3},{4,36},{36... | collective-permute-start | bytes 2359304 | tf_op jit(solution)/shard_map/ppermute | solution.py:317
  175.1 20.6 %collective-permute-start.20 = (f32[768,256]{1,0:T(8,128)S(1)}, f32[768,256]{1,0:T(8,128)S(1)}, u32[]{:S(2)}, u32[]{:S(2)}) collective-permute-start(f32[768,256]{1,0:T(8,128)S(1)} %add.83), channel_id=1, source_target_pairs={{0,64},{64,0},{1,65},{65,1},{2,66},{66,2},{3,67},{67,3},{4,68},{68... | collective-permute-start | bytes 2359304 | tf_op jit(solution)/shard_map/ppermute | solution.py:317
  176.4 19.5 %collective-permute-start.19 = (f32[768,256]{1,0:T(8,128)S(1)}, f32[768,256]{1,0:T(8,128)S(1)}, u32[]{:S(2)}, u32[]{:S(2)}) collective-permute-start(f32[768,256]{1,0:T(8,128)S(1)} %broadcast_select_fusion), channel_id=1, source_target_pairs={{32,1},{33,2},{34,3},{35,4},{36,5},{37,6},{38,7},{39,8},{40,9},{41... | collective-permute-start | bytes 2359304 | tf_op jit(solution)/shard_map/ppermute | solution.py:331
  196.5 3.2 %collective-permute-start.21 = (f32[768,256]{1,0:T(8,128)S(1)}, f32[768,256]{1,0:T(8,128)S(1)}, u32[]{:S(2)}, u32[]{:S(2)}) collective-permute-start(f32[768,256]{1,0:T(8,128)S(1)} %shard_map.77), channel_id=1, source_target_pairs={{0,32},{32,0},{1,33},{33,1},{2,34},{34,2},{3,35},{35,3},{4,36},{36... | collective-permute-start | bytes 2359304 | tf_op jit(solution)/shard_map/ppermute | solution.py:317

commit v9 on v8

--- a/solution.py
+++ b/solution.py
@@ -401,7 +401,8 @@
             p1, p3 = forward(theirs, [twin], s1 + s3, [p1, p3])
             r1, r3 = ring_of(p1, 1), ring_of(p3, 3)
             (p0,) = forward(both, [own, twin], s0)
-        p0, own, twin, table = lax.optimization_barrier((p0 + (r1 + r3) + r2, own, twin, table))
+        p0, r1, r3 = lax.optimization_barrier((p0 + r2, r1, r3))
+        p0, own, twin, table = lax.optimization_barrier((p0 + (r1 + r3), own, twin, table))
         pieces = spread(p0)
         copies = weigh(rank, pieces.reshape(subs, rows // subs, -1), observed)
         w0 = spread(copies.reshape(rows, -1))

time: 201 us -> 196 us (0.975)
  waiting for transfers between devices: 56.4 us -> 54 us
  starting transfers between devices: 48.3 us -> 46.1 us
    ppermute x6, starting transfers between devices: 28.3 us -> 24.5 us  [swap(): return lax.ppermute(value, axis, [(0, 1), (1, 0)])]
    ppermute x12, waiting for transfers between devices: 32.5 us -> 30.2 us  [ring_of(): return lax.ppermute(value, ALL, pairs)]
  transfers between devices with their start and end apart: 22 -> 22, of which waited for: 13 -> 12; matrix products, arithmetic and copies ran while one was open for 0% -> 1% of each run, Pallas kernels for 18% -> 21%
where the time goes in v9:
time: 196 us; the launch traced here: 195 us
  waiting for transfers between devices  54 us (28%)
  Pallas kernels  51.2 us (26%)
  starting transfers between devices  46.1 us (24%)
  blocking collectives  40.4 us (21%)
  other arithmetic  2.8 us (1%)
    all_to_all x4, blocking collectives, spread(): lax.all_to_all(value, ALL, 0, 0, axis_index_groups=groups, tiled=True)  40.4 us
    ppermute x12, waiting for transfers between devices, ring_of(): return lax.ppermute(value, ALL, pairs)  30.2 us
    ppermute x6, starting transfers between devices, swap(): return lax.ppermute(value, axis, [(0, 1), (1, 0)])  24.5 us
    ppermute x6, waiting for transfers between devices, swap(): return lax.ppermute(value, axis, [(0, 1), (1, 0)])  23.8 us
    ppermute x12, starting transfers between devices, ring_of(): return lax.ppermute(value, ALL, pairs)  16.2 us
    pallas_call x6, Pallas kernels, gather_up(): pl.pallas_call(functools.partial(gather_kernel, chunks, len(before) > 0),...  14.7 us
    pallas_call x2, Pallas kernels, smooth_of(): pl.pallas_call(smooth_kernel, in_specs=[VMEM] * 3, out_specs=VMEM, out_sh...  13.1 us
    pallas_call x4, Pallas kernels, forward(): pl.pallas_call(functools.partial(forward_kernel, len(xs), chunks, len(bef...  6.16 us
  transfers between devices with their start and end apart: 22, of which 12 were waited for; matrix products, arithmetic and copies ran while one was open for 1% of the time, Pallas kernels for 21%

profile of v9, /device:TPU:25, one launch (start us, length us, event | category | flops | bytes accessed | tf_op | source)
XLA Modules:
  0.0 195.2 jit_solution(8342615285050222850)
XLA Ops:
  0.1 5.0 %shard_map.55 = (f32[512,256]{1,0:T(8,128)S(1)}, bf16[512,1536]{1,0:T(8,128)(2,1)S(1)}, bf16[512,1536]{1,0:T(8,128)(2,1)S(1)}, bf16[1536,256]{1,0:T(8,128)(2,1)S(1)}, bf16[1536,256]{1,0:T(8,128)(2,1)S(1)}) custom-call(s32[1]{0:T(128)} %bitcast.5.blocks_ref, f32[2048,1536]{1,0:T(8,128)} %s_ref.5, f32[1536,256]{1,0:T(8,128)} %x_ref.1), custom_call_target="tpu_custom_call" | custom-call | flops 1207959552 | bytes 5242880 | tf_op jit(solution)/shard_map/pallas_call | solution.py:91
  5.1 3.7 %collective-permute-start = (f32[512,256]{1,0:T(8,128)S(1)}, f32[512,256]{1,0:T(8,128)S(1)}, u32[]{:S(2)}, u32[]{:S(2)}) collective-permute-start(f32[512,256]{1,0:T(8,128)S(1)} %get-tuple-element.81), channel_id=1, source_target_pairs={{0,8},{32,34},{1,9},{33,35},{2,10},{34,32},{3,11},{35,33},{4,12},{... | collective-permute-start | bytes 1572872 | tf_op jit(solution)/shard_map/ppermute | solution.py:344
  8.8 3.4 %shard_map.56 = (f32[512,256]{1,0:T(8,128)S(1)}, bf16[512,1536]{1,0:T(8,128)(2,1)S(1)}, bf16[512,1536]{1,0:T(8,128)(2,1)S(1)}, f32[512,256]{1,0:T(8,128)S(1)}, b...) custom-call(s32[2]{0:T(128)S(1)} %get-tuple-element.72.blocks_ref, f32[2048,1536]{1,0:T(8,128)S(1)} %copy-done, ...), custom_call_target="tpu_custom_call" | custom-call | flops 2415919104 | bytes 2621440 | tf_op jit(solution)/shard_map/pallas_call | solution.py:128
  13.0 1.9 collective-permute-start.2
  16.8 5.0 %collective-permute-done.1 = f32[512,256]{1,0:T(8,128)S(1)} collective-permute-done((f32[512,256]{1,0:T(8,128)S(1)}, f32[512,256]{1,0:T(8,128)S(1)}, u32[]{:S(2)}, u32[]{:S(2)}) %collective-permute-start.1) | collective-permute-done | bytes 524320 | tf_op jit(solution)/shard_map/ppermute | solution.py:344
  22.1 11.2 %all_to_all.36.pieces_ref = f32[8,64,256]{2,1,0:T(8,128)S(1)} all-to-all(f32[8,64,256]{2,1,0:T(8,128)S(1)} %bitcast.23), channel_id=1, replica_groups={{0,1,2,3,16,17,18,19},{4,5,6,7,20,21,22,23},{8,9,10,11,24,25,26,27},{12..., dimensions={0} | all-to-all | bytes 1048576 | tf_op jit(solution)/shard_map/all_to_all | solution.py:354
  33.4 9.9 %all_to_all.37 = f32[8,64,256]{2,1,0:T(8,128)S(1)} all-to-all(f32[8,64,256]{2,1,0:T(8,128)S(1)} %shard_map.58), channel_id=1, replica_groups={{0,1,2,3,16,17,18,19},{4,5,6,7,20,21,22,23},{8,9,10,11,24,25,26,27},{12..., dimensions={0} | all-to-all | bytes 1048576 | tf_op jit(solution)/shard_map/all_to_all | solution.py:354
  45.1 2.0 %collective-permute-start.4 = (f32[512,256]{1,0:T(8,128)S(1)}, f32[512,256]{1,0:T(8,128)S(1)}, u32[]{:S(2)}, u32[]{:S(2)}) collective-permute-start(f32[512,256]{1,0:T(8,128)S(1)} %bitcast.20), channel_id=1, source_target_pairs={{0,12},{32,35},{1,13},{33,32},{2,14},{34,33},{3,15},{35,34},{4,0},... | collective-permute-start | bytes 1572872 | tf_op jit(solution)/shard_map/ppermute | solution.py:344
  48.2 2.4 %shard_map.59.refs_3_ = f32[256,1536]{1,0:T(8,128)S(1)} custom-call(f32[512,256]{1,0:T(8,128)S(1)} %bitcast.22, bf16[512,1536]{1,0:T(8,128)(2,1)S(1)} %get-tuple-element.101.refs_1_.refs_2_, bf16[512,1536]{1,0:T(8,128)(2,1)S(1)} %get-tuple-element.102.refs_2_.refs_3_), custom_call_target="tpu_custom_call" | custom-call | flops 1207959552 | bytes 2097152 | tf_op jit(solution)/shard_map/pallas_call | solution.py:195
  50.7 3.4 %collective-permute-done.5.refs_0_ = f32[512,256]{1,0:T(8,128)S(1)} collective-permute-done((f32[512,256]{1,0:T(8,128)S(1)}, f32[512,256]{1,0:T(8,128)S(1)}, u32[]{:S(2)}, u32[]{:S(2)}) %collective-permute-start.5) | collective-permute-done | bytes 524320 | tf_op jit(solution)/shard_map/ppermute | solution.py:344
  54.1 2.5 %shard_map.60.refs_3_ = f32[256,1536]{1,0:T(8,128)S(1)} custom-call(f32[512,256]{1,0:T(8,128)S(1)} %collective-permute-done.5.refs_0_, bf16[512,1536]{1,0:T(8,128)(2,1)S(1)} %get-tuple-element.99.refs_1_.refs_5_.refs_3_, bf16[512,1536]{1,0:T(8,128)(2,1)S(1)} %get-tuple-element.100.refs_2_.refs_6_.refs_4_, f32[256,1536]{1,0:T(8,128)S(1)} %shard_map.59.refs_3_), custom_call_target="tpu_custom_call" | custom-call | flops 1207959552 | bytes 2097152 | tf_op jit(solution)/shard_map/pallas_call | solution.py:195
  56.6 2.3 %collective-permute-done.4.refs_0_ = f32[512,256]{1,0:T(8,128)S(1)} collective-permute-done((f32[512,256]{1,0:T(8,128)S(1)}, f32[512,256]{1,0:T(8,128)S(1)}, u32[]{:S(2)}, u32[]{:S(2)}) %collective-permute-start.4) | collective-permute-done | bytes 524320 | tf_op jit(solution)/shard_map/ppermute | solution.py:344
  58.9 2.5 %shard_map.61.start_ref = f32[256,1536]{1,0:T(8,128)S(1)} custom-call(f32[512,256]{1,0:T(8,128)S(1)} %collective-permute-done.4.refs_0_, bf16[512,1536]{1,0:T(8,128)(2,1)S(1)} %get-tuple-element.97.refs_1_.refs_3_, bf16[512,1536]{1,0:T(8,128)(2,1)S(1)} %get-tuple-element.98.refs_2_.refs_4_, f32[256,1536]{1,0:T(8,128)S(1)} %shard_map.60.refs_3_), custom_call_target="tpu_custom_call" | custom-call | flops 1207959552 | bytes 2097152 | tf_op jit(solution)/shard_map/pallas_call | solution.py:195
  62.9 12.3 %collective-permute-start.7 = (f32[768,256]{1,0:T(8,128)S(1)}, f32[768,256]{1,0:T(8,128)S(1)}, u32[]{:S(2)}, u32[]{:S(2)}) collective-permute-start(f32[768,256]{1,0:T(8,128)S(1)} %shard_map.63), channel_id=1, source_target_pairs={{0,32},{32,0},{1,33},{33,1},{2,34},{34,2},{3,35},{35,3},{4,36},{36... | collective-permute-start | bytes 2359304 | tf_op jit(solution)/shard_map/ppermute | solution.py:317
  78.2 2.1 %collective-permute-start.8 = (f32[768,256]{1,0:T(8,128)S(1)}, f32[768,256]{1,0:T(8,128)S(1)}, u32[]{:S(2)}, u32[]{:S(2)}) collective-permute-start(f32[768,256]{1,0:T(8,128)S(1)} %broadcast_select_fusion.1), channel_id=1, source_target_pairs={{32,1},{33,2},{34,3},{35,4},{36,5},{37,6},{38,7},{39,8},{40,9},{41... | collective-permute-start | bytes 2359304 | tf_op jit(solution)/shard_map/ppermute | solution.py:331
  80.3 6.5 %shard_map.64.inner_ref = f32[768,256]{1,0:T(8,128)S(1)} custom-call(f32[8,768]{1,0:T(8,128)S(1)} %maximum_maximum_fusion.table_ref, f32[768,256]{1,0:T(8,128)S(1)} %get-tuple-element.109.own_ref, f32[768,256]{1,0:T(8,128)S(1)} %get-tuple-element.111.twin_ref), custom_call_target="tpu_custom_call" | custom-call | flops 3623878656 | bytes 3145728 | tf_op jit(solution)/shard_map/pallas_call | solution.py:281
  86.9 10.7 %collective-permute-done.9 = f32[768,256]{1,0:T(8,128)S(1)} collective-permute-done((f32[768,256]{1,0:T(8,128)S(1)}, f32[768,256]{1,0:T(8,128)S(1)}, u32[]{:S(2)}, u32[]{:S(2)}) %collective-permute-start.9) | collective-permute-done | bytes 786464 | tf_op jit(solution)/shard_map/ppermute | solution.py:317
  99.6 2.0 %shard_map.67 = (f32[512,256]{1,0:T(8,128)S(1)}, f32[512,256]{1,0:T(8,128)S(1)}, f32[512,256]{1,0:T(8,128)S(1)}) custom-call(s32[1]{0:T(128)} %bitcast.1.plane_ref.planes_ref, f32[768,256]{1,0:T(8,128)S(1)} %shard_map.65.refs_0_.own_ref, bf16[512,1536]{1,0:T(8,128)(2,1)S(1)} %get-tuple-element.95.high_ref.refs_1_, ...), custom_call_target="tpu_custom_call" | custom-call | flops 1811939328 | bytes 2359296 | tf_op jit(solution)/shard_map/pallas_call | solution.py:158
  104.0 2.7 %collective-permute-start.13 = (f32[512,256]{1,0:T(8,128)S(1)}, f32[512,256]{1,0:T(8,128)S(1)}, u32[]{:S(2)}, u32[]{:S(2)}) collective-permute-start(f32[512,256]{1,0:T(8,128)S(1)} %get-tuple-element.117), channel_id=1, source_target_pairs={{0,12},{32,35},{1,13},{33,32},{2,14},{34,33},{3,15},{35,34},{4,0},... | collective-permute-start | bytes 1572872 | tf_op jit(solution)/shard_map/ppermute | solution.py:344
  106.7 2.0 %shard_map.66 = f32[512,256]{1,0:T(8,128)S(1)} custom-call(s32[2]{0:T(128)S(1)} %get-tuple-element.70.planes_ref, f32[768,256]{1,0:T(8,128)S(1)} %shard_map.65.refs_0_.own_ref, f32[768,256]{1,0:T(8,128)S(1)} %collective-permute-done.10.refs_1_.refs_0_.twin_ref, bf16[512,1536]{1,0:T(8,128)(2,1)S(1)} %get-tuple-element.101.refs_1_.refs_2_, ...), custom_call_target="tpu_custom_call" | custom-call | flops 1207959552 | bytes 2097152 | tf_op jit(solution)/shard_map/pallas_call | solution.py:158
  108.6 3.7 %collective-permute-done.11 = f32[512,256]{1,0:T(8,128)S(1)} collective-permute-done((f32[512,256]{1,0:T(8,128)S(1)}, f32[512,256]{1,0:T(8,128)S(1)}, u32[]{:S(2)}, u32[]{:S(2)}) %collective-permute-start.11) | collective-permute-done | bytes 524320 | tf_op jit(solution)/shard_map/ppermute | solution.py:344
  112.5 5.5 %collective-permute-done.12 = f32[512,256]{1,0:T(8,128)S(1)} collective-permute-done((f32[512,256]{1,0:T(8,128)S(1)}, f32[512,256]{1,0:T(8,128)S(1)}, u32[]{:S(2)}, u32[]{:S(2)}) %collective-permute-start.12) | collective-permute-done | bytes 524320 | tf_op jit(solution)/shard_map/ppermute | solution.py:344
  118.1 9.4 %all_to_all.38.pieces_ref = f32[8,64,256]{2,1,0:T(8,128)S(1)} all-to-all(f32[8,64,256]{2,1,0:T(8,128)S(1)} %bitcast.24), channel_id=1, replica_groups={{0,1,2,3,16,17,18,19},{4,5,6,7,20,21,22,23},{8,9,10,11,24,25,26,27},{12..., dimensions={0} | all-to-all | bytes 1048576 | tf_op jit(solution)/shard_map/all_to_all | solution.py:354
  127.5 9.9 %all_to_all.39 = f32[8,64,256]{2,1,0:T(8,128)S(1)} all-to-all(f32[8,64,256]{2,1,0:T(8,128)S(1)} %shard_map.70), channel_id=1, replica_groups={{0,1,2,3,16,17,18,19},{4,5,6,7,20,21,22,23},{8,9,10,11,24,25,26,27},{12..., dimensions={0} | all-to-all | bytes 1048576 | tf_op jit(solution)/shard_map/all_to_all | solution.py:354
  138.2 2.7 %collective-permute-start.15 = (f32[512,256]{1,0:T(8,128)S(1)}, f32[512,256]{1,0:T(8,128)S(1)}, u32[]{:S(2)}, u32[]{:S(2)}) collective-permute-start(f32[512,256]{1,0:T(8,128)S(1)} %bitcast.16), channel_id=1, source_target_pairs={{0,12},{32,35},{1,13},{33,32},{2,14},{34,33},{3,15},{35,34},{4,0},... | collective-permute-start | bytes 1572872 | tf_op jit(solution)/shard_map/ppermute | solution.py:344
  140.9 2.4 %shard_map.71.refs_3_ = f32[256,1536]{1,0:T(8,128)S(1)} custom-call(f32[512,256]{1,0:T(8,128)S(1)} %bitcast.18, bf16[512,1536]{1,0:T(8,128)(2,1)S(1)} %get-tuple-element.101.refs_1_.refs_2_, bf16[512,1536]{1,0:T(8,128)(2,1)S(1)} %get-tuple-element.102.refs_2_.refs_3_), custom_call_target="tpu_custom_call" | custom-call | flops 1207959552 | bytes 2097152 | tf_op jit(solution)/shard_map/pallas_call | solution.py:195
  143.4 10.0 %collective-permute-done.16.refs_0_ = f32[512,256]{1,0:T(8,128)S(1)} collective-permute-done((f32[512,256]{1,0:T(8,128)S(1)}, f32[512,256]{1,0:T(8,128)S(1)}, u32[]{:S(2)}, u32[]{:S(2)}) %collective-permute-start.16) | collective-permute-done | bytes 524320 | tf_op jit(solution)/shard_map/ppermute | solution.py:344
  153.4 2.5 %shard_map.72.refs_3_ = f32[256,1536]{1,0:T(8,128)S(1)} custom-call(f32[512,256]{1,0:T(8,128)S(1)} %collective-permute-done.16.refs_0_, bf16[512,1536]{1,0:T(8,128)(2,1)S(1)} %get-tuple-element.99.refs_1_.refs_5_.refs_3_, bf16[512,1536]{1,0:T(8,128)(2,1)S(1)} %get-tuple-element.100.refs_2_.refs_6_.refs_4_, f32[256,1536]{1,0:T(8,128)S(1)} %shard_map.71.refs_3_), custom_call_target="tpu_custom_call" | custom-call | flops 1207959552 | bytes 2097152 | tf_op jit(solution)/shard_map/pallas_call | solution.py:195
  155.9 2.5 %shard_map.73.start_ref = f32[256,1536]{1,0:T(8,128)S(1)} custom-call(f32[512,256]{1,0:T(8,128)S(1)} %collective-permute-done.15.refs_0_, bf16[512,1536]{1,0:T(8,128)(2,1)S(1)} %get-tuple-element.97.refs_1_.refs_3_, bf16[512,1536]{1,0:T(8,128)(2,1)S(1)} %get-tuple-element.98.refs_2_.refs_4_, f32[256,1536]{1,0:T(8,128)S(1)} %shard_map.72.refs_3_), custom_call_target="tpu_custom_call" | custom-call | flops 1207959552 | bytes 2097152 | tf_op jit(solution)/shard_map/pallas_call | solution.py:195
  159.9 7.4 %collective-permute-start.18 = (f32[768,256]{1,0:T(8,128)S(1)}, f32[768,256]{1,0:T(8,128)S(1)}, u32[]{:S(2)}, u32[]{:S(2)}) collective-permute-start(f32[768,256]{1,0:T(8,128)S(1)} %shard_map.75), channel_id=1, source_target_pairs={{0,32},{32,0},{1,33},{33,1},{2,34},{34,2},{3,35},{35,3},{4,36},{36... | collective-permute-start | bytes 2359304 | tf_op jit(solution)/shard_map/ppermute | solution.py:317
  172.4 6.5 %shard_map.76.inner_ref = f32[768,256]{1,0:T(8,128)S(1)} custom-call(f32[8,768]{1,0:T(8,128)S(1)} %maximum_maximum_fusion.table_ref, f32[768,256]{1,0:T(8,128)S(1)} %shard_map.65.refs_0_.own_ref, f32[768,256]{1,0:T(8,128)S(1)} %collective-permute-done.10.refs_1_.refs_0_.twin_ref), custom_call_target="tpu_custom_call" | custom-call | flops 3623878656 | bytes 3145728 | tf_op jit(solution)/shard_map/pallas_call | solution.py:281
  179.0 10.8 %collective-permute-done.20 = f32[768,256]{1,0:T(8,128)S(1)} collective-permute-done((f32[768,256]{1,0:T(8,128)S(1)}, f32[768,256]{1,0:T(8,128)S(1)}, u32[]{:S(2)}, u32[]{:S(2)}) %collective-permute-start.20) | collective-permute-done | bytes 786464 | tf_op jit(solution)/shard_map/ppermute | solution.py:317
  (71 shorter events, 28.0 us)
Async XLA Ops:
  0.1 8.7 %copy-start = (f32[2048,1536]{1,0:T(8,128)S(1)}, f32[2048,1536]{1,0:T(8,128)}, u32[]{:S(2)}) copy-start(f32[2048,1536]{1,0:T(8,128)} %s_ref.5) | copy-start | bytes 37748740
  5.1 11.6 %collective-permute-start = (f32[512,256]{1,0:T(8,128)S(1)}, f32[512,256]{1,0:T(8,128)S(1)}, u32[]{:S(2)}, u32[]{:S(2)}) collective-permute-start(f32[512,256]{1,0:T(8,128)S(1)} %get-tuple-element.81), channel_id=1, source_target_pairs={{0,8},{32,34},{1,9},{33,35},{2,10},{34,32},{3,11},{35,33},{4,12},{... | collective-permute-start | bytes 1572872 | tf_op jit(solution)/shard_map/ppermute | solution.py:344
  12.2 9.6 %collective-permute-start.1 = (f32[512,256]{1,0:T(8,128)S(1)}, f32[512,256]{1,0:T(8,128)S(1)}, u32[]{:S(2)}, u32[]{:S(2)}) collective-permute-start(f32[512,256]{1,0:T(8,128)S(1)} %get-tuple-element.76), channel_id=1, source_target_pairs={{0,4},{32,33},{1,5},{33,34},{2,6},{34,35},{3,7},{35,32},{4,8},{36,... | collective-permute-start | bytes 1572872 | tf_op jit(solution)/shard_map/ppermute | solution.py:344
  13.0 3.4 %copy-start.4 = (s32[1536]{0:T(1024)S(1)}, s32[1536]{0:T(1024)}, u32[]{:S(2)}) copy-start(s32[1536]{0:T(1024)} %param.9) | copy-start | bytes 18436
  13.0 3.4 %copy-start.3 = (s32[4,768]{1,0:T(4,128)S(1)}, s32[4,768]{1,0:T(4,128)}, u32[]{:S(2)}) copy-start(s32[4,768]{1,0:T(4,128)} %param.8) | copy-start | bytes 36868
  13.0 3.6 %copy-start.2 = (f32[1536,256]{1,0:T(8,128)S(1)}, f32[1536,256]{1,0:T(8,128)}, u32[]{:S(2)}) copy-start(f32[1536,256]{1,0:T(8,128)} %x_ref.1) | copy-start | bytes 4718596
  13.0 9.0 %collective-permute-start.2 = (f32[512,256]{1,0:T(8,128)S(1)}, f32[512,256]{1,0:T(8,128)S(1)}, u32[]{:S(2)}, u32[]{:S(2)}) collective-permute-start(f32[512,256]{1,0:T(8,128)S(1)} %get-tuple-element.82), channel_id=1, source_target_pairs={{0,12},{32,35},{1,13},{33,32},{2,14},{34,33},{3,15},{35,34},{4,0},... | collective-permute-start | bytes 1572872 | tf_op jit(solution)/shard_map/ppermute | solution.py:344
  16.8 16.5 %copy-start.1 = (f32[2048,256]{1,0:T(8,128)S(1)}, f32[2048,256]{1,0:T(8,128)}, u32[]{:S(2)}) copy-start(f32[2048,256]{1,0:T(8,128)} %observed_ref.3) | copy-start | bytes 6291460
  43.3 18.1 %collective-permute-start.6 = (f32[768,256]{1,0:T(8,128)S(1)}, f32[768,256]{1,0:T(8,128)S(1)}, u32[]{:S(2)}, u32[]{:S(2)}) collective-permute-start(f32[768,256]{1,0:T(8,128)S(1)} %get-tuple-element.109.own_ref), channel_id=1, source_target_pairs={{47,63},{16,0},{111,127},{80,64}} | collective-permute-start | bytes 2359304 | tf_op jit(solution)/shard_map/ppermute | solution.py:323
  44.0 10.1 %collective-permute-start.5 = (f32[512,256]{1,0:T(8,128)S(1)}, f32[512,256]{1,0:T(8,128)S(1)}, u32[]{:S(2)}, u32[]{:S(2)}) collective-permute-start(f32[512,256]{1,0:T(8,128)S(1)} %bitcast.19), channel_id=1, source_target_pairs={{0,4},{32,33},{1,5},{33,34},{2,6},{34,35},{3,7},{35,32},{4,8},{36,... | collective-permute-start | bytes 1572872 | tf_op jit(solution)/shard_map/ppermute | solution.py:344
  45.1 13.8 %collective-permute-start.4 = (f32[512,256]{1,0:T(8,128)S(1)}, f32[512,256]{1,0:T(8,128)S(1)}, u32[]{:S(2)}, u32[]{:S(2)}) collective-permute-start(f32[512,256]{1,0:T(8,128)S(1)} %bitcast.20), channel_id=1, source_target_pairs={{0,12},{32,35},{1,13},{33,32},{2,14},{34,33},{3,15},{35,34},{4,0},... | collective-permute-start | bytes 1572872 | tf_op jit(solution)/shard_map/ppermute | solution.py:344
  47.1 14.2 %collective-permute-start.3 = (f32[512,256]{1,0:T(8,128)S(1)}, f32[512,256]{1,0:T(8,128)S(1)}, u32[]{:S(2)}, u32[]{:S(2)}) collective-permute-start(f32[512,256]{1,0:T(8,128)S(1)} %bitcast.21), channel_id=1, source_target_pairs={{0,8},{32,34},{1,9},{33,35},{2,10},{34,32},{3,11},{35,33},{4,12},{... | collective-permute-start | bytes 1572872 | tf_op jit(solution)/shard_map/ppermute | solution.py:344
  62.9 14.2 %collective-permute-start.7 = (f32[768,256]{1,0:T(8,128)S(1)}, f32[768,256]{1,0:T(8,128)S(1)}, u32[]{:S(2)}, u32[]{:S(2)}) collective-permute-start(f32[768,256]{1,0:T(8,128)S(1)} %shard_map.63), channel_id=1, source_target_pairs={{0,32},{32,0},{1,33},{33,1},{2,34},{34,2},{3,35},{35,3},{4,36},{36... | collective-permute-start | bytes 2359304 | tf_op jit(solution)/shard_map/ppermute | solution.py:317
  77.2 20.3 %collective-permute-start.9 = (f32[768,256]{1,0:T(8,128)S(1)}, f32[768,256]{1,0:T(8,128)S(1)}, u32[]{:S(2)}, u32[]{:S(2)}) collective-permute-start(f32[768,256]{1,0:T(8,128)S(1)} %add.78), channel_id=1, source_target_pairs={{0,64},{64,0},{1,65},{65,1},{2,66},{66,2},{3,67},{67,3},{4,68},{68... | collective-permute-start | bytes 2359304 | tf_op jit(solution)/shard_map/ppermute | solution.py:317
  78.2 19.5 %collective-permute-start.8 = (f32[768,256]{1,0:T(8,128)S(1)}, f32[768,256]{1,0:T(8,128)S(1)}, u32[]{:S(2)}, u32[]{:S(2)}) collective-permute-start(f32[768,256]{1,0:T(8,128)S(1)} %broadcast_select_fusion.1), channel_id=1, source_target_pairs={{32,1},{33,2},{34,3},{35,4},{36,5},{37,6},{38,7},{39,8},{40,9},{41... | collective-permute-start | bytes 2359304 | tf_op jit(solution)/shard_map/ppermute | solution.py:331
  98.3 3.3 %collective-permute-start.10 = (f32[768,256]{1,0:T(8,128)S(1)}, f32[768,256]{1,0:T(8,128)S(1)}, u32[]{:S(2)}, u32[]{:S(2)}) collective-permute-start(f32[768,256]{1,0:T(8,128)S(1)} %shard_map.65.refs_0_.own_ref), channel_id=1, source_target_pairs={{0,32},{32,0},{1,33},{33,1},{2,34},{34,2},{3,35},{35,3},{4,36},{36... | collective-permute-start | bytes 2359304 | tf_op jit(solution)/shard_map/ppermute | solution.py:317
  102.4 10.0 %collective-permute-start.11 = (f32[512,256]{1,0:T(8,128)S(1)}, f32[512,256]{1,0:T(8,128)S(1)}, u32[]{:S(2)}, u32[]{:S(2)}) collective-permute-start(f32[512,256]{1,0:T(8,128)S(1)} %shard_map.68), channel_id=1, source_target_pairs={{0,8},{32,34},{1,9},{33,35},{2,10},{34,32},{3,11},{35,33},{4,12},{... | collective-permute-start | bytes 1572872 | tf_op jit(solution)/shard_map/ppermute | solution.py:344
  103.9 14.0 %collective-permute-start.12 = (f32[512,256]{1,0:T(8,128)S(1)}, f32[512,256]{1,0:T(8,128)S(1)}, u32[]{:S(2)}, u32[]{:S(2)}) collective-permute-start(f32[512,256]{1,0:T(8,128)S(1)} %get-tuple-element.116), channel_id=1, source_target_pairs={{0,4},{32,33},{1,5},{33,34},{2,6},{34,35},{3,7},{35,32},{4,8},{36,... | collective-permute-start | bytes 1572872 | tf_op jit(solution)/shard_map/ppermute | solution.py:344
  104.0 14.0 %collective-permute-start.13 = (f32[512,256]{1,0:T(8,128)S(1)}, f32[512,256]{1,0:T(8,128)S(1)}, u32[]{:S(2)}, u32[]{:S(2)}) collective-permute-start(f32[512,256]{1,0:T(8,128)S(1)} %get-tuple-element.117), channel_id=1, source_target_pairs={{0,12},{32,35},{1,13},{33,32},{2,14},{34,33},{3,15},{35,34},{4,0},... | collective-permute-start | bytes 1572872 | tf_op jit(solution)/shard_map/ppermute | solution.py:344
  137.5 20.9 %collective-permute-start.17 = (f32[768,256]{1,0:T(8,128)S(1)}, f32[768,256]{1,0:T(8,128)S(1)}, u32[]{:S(2)}, u32[]{:S(2)}) collective-permute-start(f32[768,256]{1,0:T(8,128)S(1)} %shard_map.65.refs_0_.own_ref), channel_id=1, source_target_pairs={{47,63},{16,0},{111,127},{80,64}} | collective-permute-start | bytes 2359304 | tf_op jit(solution)/shard_map/ppermute | solution.py:323
  138.2 15.2 %collective-permute-start.16 = (f32[512,256]{1,0:T(8,128)S(1)}, f32[512,256]{1,0:T(8,128)S(1)}, u32[]{:S(2)}, u32[]{:S(2)}) collective-permute-start(f32[512,256]{1,0:T(8,128)S(1)} %bitcast.15), channel_id=1, source_target_pairs={{0,4},{32,33},{1,5},{33,34},{2,6},{34,35},{3,7},{35,32},{4,8},{36,... | collective-permute-start | bytes 1572872 | tf_op jit(solution)/shard_map/ppermute | solution.py:344
  138.2 17.6 %collective-permute-start.15 = (f32[512,256]{1,0:T(8,128)S(1)}, f32[512,256]{1,0:T(8,128)S(1)}, u32[]{:S(2)}, u32[]{:S(2)}) collective-permute-start(f32[512,256]{1,0:T(8,128)S(1)} %bitcast.16), channel_id=1, source_target_pairs={{0,12},{32,35},{1,13},{33,32},{2,14},{34,33},{3,15},{35,34},{4,0},... | collective-permute-start | bytes 1572872 | tf_op jit(solution)/shard_map/ppermute | solution.py:344
  140.9 17.4 %collective-permute-start.14 = (f32[512,256]{1,0:T(8,128)S(1)}, f32[512,256]{1,0:T(8,128)S(1)}, u32[]{:S(2)}, u32[]{:S(2)}) collective-permute-start(f32[512,256]{1,0:T(8,128)S(1)} %bitcast.17), channel_id=1, source_target_pairs={{0,8},{32,34},{1,9},{33,35},{2,10},{34,32},{3,11},{35,33},{4,12},{... | collective-permute-start | bytes 1572872 | tf_op jit(solution)/shard_map/ppermute | solution.py:344
  159.9 9.3 %collective-permute-start.18 = (f32[768,256]{1,0:T(8,128)S(1)}, f32[768,256]{1,0:T(8,128)S(1)}, u32[]{:S(2)}, u32[]{:S(2)}) collective-permute-start(f32[768,256]{1,0:T(8,128)S(1)} %shard_map.75), channel_id=1, source_target_pairs={{0,32},{32,0},{1,33},{33,1},{2,34},{34,2},{3,35},{35,3},{4,36},{36... | collective-permute-start | bytes 2359304 | tf_op jit(solution)/shard_map/ppermute | solution.py:317
  169.3 20.6 %collective-permute-start.20 = (f32[768,256]{1,0:T(8,128)S(1)}, f32[768,256]{1,0:T(8,128)S(1)}, u32[]{:S(2)}, u32[]{:S(2)}) collective-permute-start(f32[768,256]{1,0:T(8,128)S(1)} %add.83), channel_id=1, source_target_pairs={{0,64},{64,0},{1,65},{65,1},{2,66},{66,2},{3,67},{67,3},{4,68},{68... | collective-permute-start | bytes 2359304 | tf_op jit(solution)/shard_map/ppermute | solution.py:317
  170.5 19.5 %collective-permute-start.19 = (f32[768,256]{1,0:T(8,128)S(1)}, f32[768,256]{1,0:T(8,128)S(1)}, u32[]{:S(2)}, u32[]{:S(2)}) collective-permute-start(f32[768,256]{1,0:T(8,128)S(1)} %broadcast_select_fusion), channel_id=1, source_target_pairs={{32,1},{33,2},{34,3},{35,4},{36,5},{37,6},{38,7},{39,8},{40,9},{41... | collective-permute-start | bytes 2359304 | tf_op jit(solution)/shard_map/ppermute | solution.py:331
  190.6 3.2 %collective-permute-start.21 = (f32[768,256]{1,0:T(8,128)S(1)}, f32[768,256]{1,0:T(8,128)S(1)}, u32[]{:S(2)}, u32[]{:S(2)}) collective-permute-start(f32[768,256]{1,0:T(8,128)S(1)} %shard_map.77), channel_id=1, source_target_pairs={{0,32},{32,0},{1,33},{33,1},{2,34},{34,2},{3,35},{35,3},{4,36},{36... | collective-permute-start | bytes 2359304 | tf_op jit(solution)/shard_map/ppermute | solution.py:317

commit v10 on v9

--- a/solution.py
+++ b/solution.py
@@ -313,6 +313,28 @@
     )(table, own, beyond, inner, start)
 
 
+def place_kernel(plane_ref, value_ref, *refs):
+    out_ref, sem = refs[-2:]
+    rows = block_of(plane_ref[0], value_ref.shape[0])
+    copy = pltpu.make_async_copy(value_ref, out_ref.at[rows], sem)
+    copy.start()
+    copy.wait()
+
+
+def place(plane, value, before=()):
+    cells, sols = value.shape
+    return pl.pallas_call(
+        place_kernel,
+        in_specs=[SMEM, VMEM] + [ANY] * len(before),
+        out_specs=ANY,
+        out_shape=jax.ShapeDtypeStruct((2 * cells, sols), F32),
+        scratch_shapes=[pltpu.SemaphoreType.DMA],
+        input_output_aliases={2: 0} if before else {},
+        compiler_params=PARAMS,
+        cost_estimate=pl.CostEstimate(flops=0, bytes_accessed=8 * cells * sols, transcendentals=0),
+    )(plane, value, *before)
+
+
 def swap(value, axis):
     return lax.ppermute(value, axis, [(0, 1), (1, 0)])
 
@@ -339,8 +361,8 @@
             for i in range(x):
                 for j in range(z):
                     at = lambda c, i, j: (((h * core + c) * yl + l) * x + i % x) * z + j % z
-                    pairs.append((at(0, i, j), at(0, i + shift, j)))
-                    pairs.append((at(1, i, j), at(1, i, j + shift)))
+                    pairs.append((at(0, i, j), at(0, i, j + shift)))
+                    pairs.append((at(1, i, j), at(1, i + shift, j)))
     return lax.ppermute(value, ALL, pairs)
 
 
@@ -349,16 +371,16 @@
     at = lambda h, c, l, i, j: (((h * core + c) * yl + l) * x + i) * z + j
     groups = []
     for h in range(yh):
-        groups += [[at(h, 0, l, i, j) for l in range(yl) for j in range(z)] for i in range(x)]
-        groups += [[at(h, 1, l, i, j) for l in range(yl) for i in range(x)] for j in range(z)]
+        groups += [[at(h, 0, l, i, j) for l in range(yl) for i in range(x)] for j in range(z)]
+        groups += [[at(h, 1, l, i, j) for l in range(yl) for j in range(z)] for i in range(x)]
     return lax.all_to_all(value, ALL, 0, 0, axis_index_groups=groups, tiled=True)
 
 
 def local(sensitivity, observed, models, neighbour_map, edge_mask):
     core = lax.axis_index("core").astype(jnp.int32)
     x, z = (lax.axis_index(axis).astype(jnp.int32) for axis in ("x", "z"))
-    ring = jnp.where(core == 0, x, z)
-    sub = lax.axis_index("yl").astype(jnp.int32) * lax.axis_size("z") + jnp.where(core == 0, z, x)
+    ring = jnp.where(core == 0, z, x)
+    sub = lax.axis_index("yl").astype(jnp.int32) * lax.axis_size("x") + jnp.where(core == 0, x, z)
     rings = lax.axis_size("x")
     ranks = lax.axis_size(CELLS)
     subs = ranks // rings
@@ -423,9 +445,7 @@
         inner = smooth_of(table, own, twin)
         own = edge_of(table, own, beyond, inner, own - 1.0 * gradient)
     twin = swap(own, "core")
-    place = lax.broadcasted_iota(jnp.int32, (2, 1, 1), 0)
-    planes = jnp.where((place == 0) == low_core, own[None], twin[None])
-    return planes.reshape(models.shape)
+    return place(theirs, twin, [place(mine, own)])
 
 
 def solution(mesh):

time: 196 us -> 193 us (0.985)
  starting transfers between devices: 46.1 us -> 39.3 us
  blocking collectives: 40.4 us -> 46 us
    ppermute x6, starting transfers between devices: 24.5 us -> 14.8 us  [swap(): return lax.ppermute(value, axis, [(0, 1), (1, 0)])]
    all_to_all x4, blocking collectives: 40.4 us -> 46 us  [spread(): lax.all_to_all(value, ALL, 0, 0, axis_index_groups=groups, tiled=True)]
    ppermute x12, starting transfers between devices: 16.2 us -> 19.2 us  [ring_of(): return lax.ppermute(value, ALL, pairs)]
  transfers between devices with their start and end apart: 22 -> 22, of which waited for: 12 -> 11; matrix products, arithmetic and copies ran while one was open for 1% -> 0% of each run, Pallas kernels for 21% -> 22%
where the time goes in v10:
time: 193 us
  Pallas kernels  53 us (27%)
  waiting for transfers between devices  52.8 us (27%)
  blocking collectives  46 us (24%)
  starting transfers between devices  39.3 us (20%)
    all_to_all x4, blocking collectives, spread(): lax.all_to_all(value, ALL, 0, 0, axis_index_groups=groups, tiled=True)  46 us
    ppermute x12, waiting for transfers between devices, ring_of(): return lax.ppermute(value, ALL, pairs)  29.7 us
    ppermute x6, waiting for transfers between devices, swap(): return lax.ppermute(value, axis, [(0, 1), (1, 0)])  23.1 us
    ppermute x12, starting transfers between devices, ring_of(): return lax.ppermute(value, ALL, pairs)  19.2 us
    ppermute x6, starting transfers between devices, swap(): return lax.ppermute(value, axis, [(0, 1), (1, 0)])  14.8 us
    pallas_call x6, Pallas kernels, gather_up(): pl.pallas_call(functools.partial(gather_kernel, chunks, len(before) > 0),...  14.7 us
    pallas_call x2, Pallas kernels, smooth_of(): pl.pallas_call(smooth_kernel, in_specs=[VMEM] * 3, out_specs=VMEM, out_sh...  13.1 us
    pallas_call x4, Pallas kernels, forward(): pl.pallas_call(functools.partial(forward_kernel, len(xs), chunks, len(bef...  6.15 us
  transfers between devices with their start and end apart: 22, of which 11 were waited for; matrix products, arithmetic and copies ran while one was open for 0% of the time, Pallas kernels for 22%

profile of v10, /device:TPU:25, one launch (start us, length us, event | category | flops | bytes accessed | tf_op | source)
XLA Modules:
  0.0 193.1 jit_solution(13873491856090791702)
XLA Ops:
  0.1 5.0 %shard_map.55 = (f32[512,256]{1,0:T(8,128)S(1)}, bf16[512,1536]{1,0:T(8,128)(2,1)S(1)}, bf16[512,1536]{1,0:T(8,128)(2,1)S(1)}, bf16[1536,256]{1,0:T(8,128)(2,1)S(1)}, bf16[1536,256]{1,0:T(8,128)(2,1)S(1)}) custom-call(s32[1]{0:T(128)} %bitcast.5.blocks_ref, f32[2048,1536]{1,0:T(8,128)} %s_ref.5, f32[1536,256]{1,0:T(8,128)} %x_ref.1), custom_call_target="tpu_custom_call" | custom-call | flops 1207959552 | bytes 5242880 | tf_op jit(solution)/shard_map/pallas_call | solution.py:91
  5.1 2.8 %collective-permute-start = (f32[512,256]{1,0:T(8,128)S(1)}, f32[512,256]{1,0:T(8,128)S(1)}, u32[]{:S(2)}, u32[]{:S(2)}) collective-permute-start(f32[512,256]{1,0:T(8,128)S(1)} %get-tuple-element.81), channel_id=1, source_target_pairs={{0,2},{32,40},{1,3},{33,41},{2,0},{34,42},{3,1},{35,43},{4,6},{36,... | collective-permute-start | bytes 1572872 | tf_op jit(solution)/shard_map/ppermute | solution.py:366
  7.9 3.4 %shard_map.56 = (f32[512,256]{1,0:T(8,128)S(1)}, bf16[512,1536]{1,0:T(8,128)(2,1)S(1)}, bf16[512,1536]{1,0:T(8,128)(2,1)S(1)}, f32[512,256]{1,0:T(8,128)S(1)}, b...) custom-call(s32[2]{0:T(128)S(1)} %get-tuple-element.72.blocks_ref, f32[2048,1536]{1,0:T(8,128)S(1)} %copy-done, ...), custom_call_target="tpu_custom_call" | custom-call | flops 2415919104 | bytes 2621440 | tf_op jit(solution)/shard_map/pallas_call | solution.py:128
  11.7 2.4 %collective-permute-start.2 = (f32[512,256]{1,0:T(8,128)S(1)}, f32[512,256]{1,0:T(8,128)S(1)}, u32[]{:S(2)}, u32[]{:S(2)}) collective-permute-start(f32[512,256]{1,0:T(8,128)S(1)} %get-tuple-element.82), channel_id=1, source_target_pairs={{0,3},{32,44},{1,0},{33,45},{2,1},{34,46},{3,2},{35,47},{4,7},{36,... | collective-permute-start | bytes 1572872 | tf_op jit(solution)/shard_map/ppermute | solution.py:366
  16.0 5.0 %collective-permute-done.1 = f32[512,256]{1,0:T(8,128)S(1)} collective-permute-done((f32[512,256]{1,0:T(8,128)S(1)}, f32[512,256]{1,0:T(8,128)S(1)}, u32[]{:S(2)}, u32[]{:S(2)}) %collective-permute-start.1) | collective-permute-done | bytes 524320 | tf_op jit(solution)/shard_map/ppermute | solution.py:366
  21.0 13.0 %all_to_all.36.pieces_ref = f32[8,64,256]{2,1,0:T(8,128)S(1)} all-to-all(f32[8,64,256]{2,1,0:T(8,128)S(1)} %bitcast.19), channel_id=1, replica_groups={{0,4,8,12,16,20,24,28},{1,5,9,13,17,21,25,29},{2,6,10,14,18,22,26,30},{..., dimensions={0} | all-to-all | bytes 1048576 | tf_op jit(solution)/shard_map/all_to_all | solution.py:376
  34.1 10.0 %all_to_all.37 = f32[8,64,256]{2,1,0:T(8,128)S(1)} all-to-all(f32[8,64,256]{2,1,0:T(8,128)S(1)} %shard_map.58), channel_id=1, replica_groups={{0,4,8,12,16,20,24,28},{1,5,9,13,17,21,25,29},{2,6,10,14,18,22,26,30},{..., dimensions={0} | all-to-all | bytes 1048576 | tf_op jit(solution)/shard_map/all_to_all | solution.py:376
  44.8 3.9 %collective-permute-start.5 = (f32[512,256]{1,0:T(8,128)S(1)}, f32[512,256]{1,0:T(8,128)S(1)}, u32[]{:S(2)}, u32[]{:S(2)}) collective-permute-start(f32[512,256]{1,0:T(8,128)S(1)} %bitcast.15), channel_id=1, source_target_pairs={{0,1},{32,36},{1,2},{33,37},{2,3},{34,38},{3,0},{35,39},{4,5},{36,... | collective-permute-start | bytes 1572872 | tf_op jit(solution)/shard_map/ppermute | solution.py:366
  48.7 2.8 %collective-permute-start.4 = (f32[512,256]{1,0:T(8,128)S(1)}, f32[512,256]{1,0:T(8,128)S(1)}, u32[]{:S(2)}, u32[]{:S(2)}) collective-permute-start(f32[512,256]{1,0:T(8,128)S(1)} %bitcast.16), channel_id=1, source_target_pairs={{0,3},{32,44},{1,0},{33,45},{2,1},{34,46},{3,2},{35,47},{4,7},{36,... | collective-permute-start | bytes 1572872 | tf_op jit(solution)/shard_map/ppermute | solution.py:366
  52.8 2.4 %shard_map.59.refs_3_ = f32[256,1536]{1,0:T(8,128)S(1)} custom-call(f32[512,256]{1,0:T(8,128)S(1)} %bitcast.18, bf16[512,1536]{1,0:T(8,128)(2,1)S(1)} %get-tuple-element.102.refs_1_.refs_2_, bf16[512,1536]{1,0:T(8,128)(2,1)S(1)} %get-tuple-element.103.refs_2_.refs_3_), custom_call_target="tpu_custom_call" | custom-call | flops 1207959552 | bytes 2097152 | tf_op jit(solution)/shard_map/pallas_call | solution.py:195
  55.3 3.0 %collective-permute-done.5.refs_0_ = f32[512,256]{1,0:T(8,128)S(1)} collective-permute-done((f32[512,256]{1,0:T(8,128)S(1)}, f32[512,256]{1,0:T(8,128)S(1)}, u32[]{:S(2)}, u32[]{:S(2)}) %collective-permute-start.5) | collective-permute-done | bytes 524320 | tf_op jit(solution)/shard_map/ppermute | solution.py:366
  58.3 2.5 %shard_map.60.refs_3_ = f32[256,1536]{1,0:T(8,128)S(1)} custom-call(f32[512,256]{1,0:T(8,128)S(1)} %collective-permute-done.5.refs_0_, bf16[512,1536]{1,0:T(8,128)(2,1)S(1)} %get-tuple-element.100.refs_1_.refs_5_.refs_3_, bf16[512,1536]{1,0:T(8,128)(2,1)S(1)} %get-tuple-element.101.refs_2_.refs_6_.refs_4_, f32[256,1536]{1,0:T(8,128)S(1)} %shard_map.59.refs_3_), custom_call_target="tpu_custom_call" | custom-call | flops 1207959552 | bytes 2097152 | tf_op jit(solution)/shard_map/pallas_call | solution.py:195
  60.7 2.5 %collective-permute-done.4.refs_0_ = f32[512,256]{1,0:T(8,128)S(1)} collective-permute-done((f32[512,256]{1,0:T(8,128)S(1)}, f32[512,256]{1,0:T(8,128)S(1)}, u32[]{:S(2)}, u32[]{:S(2)}) %collective-permute-start.4) | collective-permute-done | bytes 524320 | tf_op jit(solution)/shard_map/ppermute | solution.py:366
  63.2 2.5 %shard_map.61.start_ref = f32[256,1536]{1,0:T(8,128)S(1)} custom-call(f32[512,256]{1,0:T(8,128)S(1)} %collective-permute-done.4.refs_0_, bf16[512,1536]{1,0:T(8,128)(2,1)S(1)} %get-tuple-element.98.refs_1_.refs_3_, bf16[512,1536]{1,0:T(8,128)(2,1)S(1)} %get-tuple-element.99.refs_2_.refs_4_, f32[256,1536]{1,0:T(8,128)S(1)} %shard_map.60.refs_3_), custom_call_target="tpu_custom_call" | custom-call | flops 1207959552 | bytes 2097152 | tf_op jit(solution)/shard_map/pallas_call | solution.py:195
  67.2 6.6 %collective-permute-start.7 = (f32[768,256]{1,0:T(8,128)S(1)}, f32[768,256]{1,0:T(8,128)S(1)}, u32[]{:S(2)}, u32[]{:S(2)}) collective-permute-start(f32[768,256]{1,0:T(8,128)S(1)} %shard_map.63), channel_id=1, source_target_pairs={{0,32},{32,0},{1,33},{33,1},{2,34},{34,2},{3,35},{35,3},{4,36},{36... | collective-permute-start | bytes 2359304 | tf_op jit(solution)/shard_map/ppermute | solution.py:339
  76.9 2.1 %collective-permute-start.8 = (f32[768,256]{1,0:T(8,128)S(1)}, f32[768,256]{1,0:T(8,128)S(1)}, u32[]{:S(2)}, u32[]{:S(2)}) collective-permute-start(f32[768,256]{1,0:T(8,128)S(1)} %broadcast_select_fusion.1), channel_id=1, source_target_pairs={{32,1},{33,2},{34,3},{35,4},{36,5},{37,6},{38,7},{39,8},{40,9},{41... | collective-permute-start | bytes 2359304 | tf_op jit(solution)/shard_map/ppermute | solution.py:353
  79.0 6.5 %shard_map.64.inner_ref = f32[768,256]{1,0:T(8,128)S(1)} custom-call(f32[8,768]{1,0:T(8,128)S(1)} %maximum_maximum_fusion.table_ref, f32[768,256]{1,0:T(8,128)S(1)} %get-tuple-element.109.own_ref, f32[768,256]{1,0:T(8,128)S(1)} %get-tuple-element.111.twin_ref), custom_call_target="tpu_custom_call" | custom-call | flops 3623878656 | bytes 3145728 | tf_op jit(solution)/shard_map/pallas_call | solution.py:281
  85.5 10.7 %collective-permute-done.9 = f32[768,256]{1,0:T(8,128)S(1)} collective-permute-done((f32[768,256]{1,0:T(8,128)S(1)}, f32[768,256]{1,0:T(8,128)S(1)}, u32[]{:S(2)}, u32[]{:S(2)}) %collective-permute-start.9) | collective-permute-done | bytes 786464 | tf_op jit(solution)/shard_map/ppermute | solution.py:339
  98.3 2.0 %shard_map.67 = (f32[512,256]{1,0:T(8,128)S(1)}, f32[512,256]{1,0:T(8,128)S(1)}, f32[512,256]{1,0:T(8,128)S(1)}) custom-call(s32[1]{0:T(128)} %bitcast.1.plane_ref.planes_ref, f32[768,256]{1,0:T(8,128)S(1)} %shard_map.65.refs_0_.own_ref, bf16[512,1536]{1,0:T(8,128)(2,1)S(1)} %get-tuple-element.96.high_ref.refs_1_, ...), custom_call_target="tpu_custom_call" | custom-call | flops 1811939328 | bytes 2359296 | tf_op jit(solution)/shard_map/pallas_call | solution.py:158
  102.7 2.7 %collective-permute-start.13 = (f32[512,256]{1,0:T(8,128)S(1)}, f32[512,256]{1,0:T(8,128)S(1)}, u32[]{:S(2)}, u32[]{:S(2)}) collective-permute-start(f32[512,256]{1,0:T(8,128)S(1)} %get-tuple-element.117), channel_id=1, source_target_pairs={{0,3},{32,44},{1,0},{33,45},{2,1},{34,46},{3,2},{35,47},{4,7},{36,... | collective-permute-start | bytes 1572872 | tf_op jit(solution)/shard_map/ppermute | solution.py:366
  107.3 3.7 %collective-permute-done.11 = f32[512,256]{1,0:T(8,128)S(1)} collective-permute-done((f32[512,256]{1,0:T(8,128)S(1)}, f32[512,256]{1,0:T(8,128)S(1)}, u32[]{:S(2)}, u32[]{:S(2)}) %collective-permute-start.11) | collective-permute-done | bytes 524320 | tf_op jit(solution)/shard_map/ppermute | solution.py:366
  111.1 5.5 %collective-permute-done.12 = f32[512,256]{1,0:T(8,128)S(1)} collective-permute-done((f32[512,256]{1,0:T(8,128)S(1)}, f32[512,256]{1,0:T(8,128)S(1)}, u32[]{:S(2)}, u32[]{:S(2)}) %collective-permute-start.12) | collective-permute-done | bytes 524320 | tf_op jit(solution)/shard_map/ppermute | solution.py:366
  116.7 10.7 %all_to_all.38.pieces_ref = f32[8,64,256]{2,1,0:T(8,128)S(1)} all-to-all(f32[8,64,256]{2,1,0:T(8,128)S(1)} %bitcast.20), channel_id=1, replica_groups={{0,4,8,12,16,20,24,28},{1,5,9,13,17,21,25,29},{2,6,10,14,18,22,26,30},{..., dimensions={0} | all-to-all | bytes 1048576 | tf_op jit(solution)/shard_map/all_to_all | solution.py:376
  127.5 12.3 %all_to_all.39 = f32[8,64,256]{2,1,0:T(8,128)S(1)} all-to-all(f32[8,64,256]{2,1,0:T(8,128)S(1)} %shard_map.70), channel_id=1, replica_groups={{0,4,8,12,16,20,24,28},{1,5,9,13,17,21,25,29},{2,6,10,14,18,22,26,30},{..., dimensions={0} | all-to-all | bytes 1048576 | tf_op jit(solution)/shard_map/all_to_all | solution.py:376
  140.6 2.7 %collective-permute-start.15 = (f32[512,256]{1,0:T(8,128)S(1)}, f32[512,256]{1,0:T(8,128)S(1)}, u32[]{:S(2)}, u32[]{:S(2)}) collective-permute-start(f32[512,256]{1,0:T(8,128)S(1)} %bitcast.12), channel_id=1, source_target_pairs={{0,3},{32,44},{1,0},{33,45},{2,1},{34,46},{3,2},{35,47},{4,7},{36,... | collective-permute-start | bytes 1572872 | tf_op jit(solution)/shard_map/ppermute | solution.py:366
  143.2 2.4 %shard_map.71.refs_3_ = f32[256,1536]{1,0:T(8,128)S(1)} custom-call(f32[512,256]{1,0:T(8,128)S(1)} %bitcast.14, bf16[512,1536]{1,0:T(8,128)(2,1)S(1)} %get-tuple-element.102.refs_1_.refs_2_, bf16[512,1536]{1,0:T(8,128)(2,1)S(1)} %get-tuple-element.103.refs_2_.refs_3_), custom_call_target="tpu_custom_call" | custom-call | flops 1207959552 | bytes 2097152 | tf_op jit(solution)/shard_map/pallas_call | solution.py:195
  145.7 10.0 %collective-permute-done.16.refs_0_ = f32[512,256]{1,0:T(8,128)S(1)} collective-permute-done((f32[512,256]{1,0:T(8,128)S(1)}, f32[512,256]{1,0:T(8,128)S(1)}, u32[]{:S(2)}, u32[]{:S(2)}) %collective-permute-start.16) | collective-permute-done | bytes 524320 | tf_op jit(solution)/shard_map/ppermute | solution.py:366
  155.7 2.5 %shard_map.72.refs_3_ = f32[256,1536]{1,0:T(8,128)S(1)} custom-call(f32[512,256]{1,0:T(8,128)S(1)} %collective-permute-done.16.refs_0_, bf16[512,1536]{1,0:T(8,128)(2,1)S(1)} %get-tuple-element.100.refs_1_.refs_5_.refs_3_, bf16[512,1536]{1,0:T(8,128)(2,1)S(1)} %get-tuple-element.101.refs_2_.refs_6_.refs_4_, f32[256,1536]{1,0:T(8,128)S(1)} %shard_map.71.refs_3_), custom_call_target="tpu_custom_call" | custom-call | flops 1207959552 | bytes 2097152 | tf_op jit(solution)/shard_map/pallas_call | solution.py:195
  158.2 2.5 %shard_map.73.start_ref = f32[256,1536]{1,0:T(8,128)S(1)} custom-call(f32[512,256]{1,0:T(8,128)S(1)} %collective-permute-done.15.refs_0_, bf16[512,1536]{1,0:T(8,128)(2,1)S(1)} %get-tuple-element.98.refs_1_.refs_3_, bf16[512,1536]{1,0:T(8,128)(2,1)S(1)} %get-tuple-element.99.refs_2_.refs_4_, f32[256,1536]{1,0:T(8,128)S(1)} %shard_map.72.refs_3_), custom_call_target="tpu_custom_call" | custom-call | flops 1207959552 | bytes 2097152 | tf_op jit(solution)/shard_map/pallas_call | solution.py:195
  162.2 3.3 %collective-permute-start.18 = (f32[768,256]{1,0:T(8,128)S(1)}, f32[768,256]{1,0:T(8,128)S(1)}, u32[]{:S(2)}, u32[]{:S(2)}) collective-permute-start(f32[768,256]{1,0:T(8,128)S(1)} %shard_map.75), channel_id=1, source_target_pairs={{0,32},{32,0},{1,33},{33,1},{2,34},{34,2},{3,35},{35,3},{4,36},{36... | collective-permute-start | bytes 2359304 | tf_op jit(solution)/shard_map/ppermute | solution.py:339
  170.7 6.5 %shard_map.76.inner_ref = f32[768,256]{1,0:T(8,128)S(1)} custom-call(f32[8,768]{1,0:T(8,128)S(1)} %maximum_maximum_fusion.table_ref, f32[768,256]{1,0:T(8,128)S(1)} %shard_map.65.refs_0_.own_ref, f32[768,256]{1,0:T(8,128)S(1)} %collective-permute-done.10.refs_1_.refs_0_.twin_ref), custom_call_target="tpu_custom_call" | custom-call | flops 3623878656 | bytes 3145728 | tf_op jit(solution)/shard_map/pallas_call | solution.py:281
  177.2 10.9 %collective-permute-done.20 = f32[768,256]{1,0:T(8,128)S(1)} collective-permute-done((f32[768,256]{1,0:T(8,128)S(1)}, f32[768,256]{1,0:T(8,128)S(1)}, u32[]{:S(2)}, u32[]{:S(2)}) %collective-permute-start.20) | collective-permute-done | bytes 786464 | tf_op jit(solution)/shard_map/ppermute | solution.py:339
  (69 shorter events, 27.9 us)
Async XLA Ops:
  0.1 7.9 %copy-start = (f32[2048,1536]{1,0:T(8,128)S(1)}, f32[2048,1536]{1,0:T(8,128)}, u32[]{:S(2)}) copy-start(f32[2048,1536]{1,0:T(8,128)} %s_ref.5) | copy-start | bytes 37748740
  5.1 10.8 %collective-permute-start = (f32[512,256]{1,0:T(8,128)S(1)}, f32[512,256]{1,0:T(8,128)S(1)}, u32[]{:S(2)}, u32[]{:S(2)}) collective-permute-start(f32[512,256]{1,0:T(8,128)S(1)} %get-tuple-element.81), channel_id=1, source_target_pairs={{0,2},{32,40},{1,3},{33,41},{2,0},{34,42},{3,1},{35,43},{4,6},{36,... | collective-permute-start | bytes 1572872 | tf_op jit(solution)/shard_map/ppermute | solution.py:366
  11.3 9.6 %collective-permute-start.1 = (f32[512,256]{1,0:T(8,128)S(1)}, f32[512,256]{1,0:T(8,128)S(1)}, u32[]{:S(2)}, u32[]{:S(2)}) collective-permute-start(f32[512,256]{1,0:T(8,128)S(1)} %get-tuple-element.76), channel_id=1, source_target_pairs={{0,1},{32,36},{1,2},{33,37},{2,3},{34,38},{3,0},{35,39},{4,5},{36,... | collective-permute-start | bytes 1572872 | tf_op jit(solution)/shard_map/ppermute | solution.py:366
  11.7 3.8 %copy-start.4 = (s32[1536]{0:T(1024)S(1)}, s32[1536]{0:T(1024)}, u32[]{:S(2)}) copy-start(s32[1536]{0:T(1024)} %param.9) | copy-start | bytes 18436
  11.7 3.9 %copy-start.3 = (s32[4,768]{1,0:T(4,128)S(1)}, s32[4,768]{1,0:T(4,128)}, u32[]{:S(2)}) copy-start(s32[4,768]{1,0:T(4,128)} %param.8) | copy-start | bytes 36868
  11.7 4.0 %copy-start.2 = (f32[1536,256]{1,0:T(8,128)S(1)}, f32[1536,256]{1,0:T(8,128)}, u32[]{:S(2)}) copy-start(f32[1536,256]{1,0:T(8,128)} %x_ref.1) | copy-start | bytes 4718596
  11.7 9.2 %collective-permute-start.2 = (f32[512,256]{1,0:T(8,128)S(1)}, f32[512,256]{1,0:T(8,128)S(1)}, u32[]{:S(2)}, u32[]{:S(2)}) collective-permute-start(f32[512,256]{1,0:T(8,128)S(1)} %get-tuple-element.82), channel_id=1, source_target_pairs={{0,3},{32,44},{1,0},{33,45},{2,1},{34,46},{3,2},{35,47},{4,7},{36,... | collective-permute-start | bytes 1572872 | tf_op jit(solution)/shard_map/ppermute | solution.py:366
  16.0 18.0 %copy-start.1 = (f32[2048,256]{1,0:T(8,128)S(1)}, f32[2048,256]{1,0:T(8,128)}, u32[]{:S(2)}) copy-start(f32[2048,256]{1,0:T(8,128)} %observed_ref.3) | copy-start | bytes 6291460
  44.1 21.6 %collective-permute-start.6 = (f32[768,256]{1,0:T(8,128)S(1)}, f32[768,256]{1,0:T(8,128)S(1)}, u32[]{:S(2)}, u32[]{:S(2)}) collective-permute-start(f32[768,256]{1,0:T(8,128)S(1)} %get-tuple-element.109.own_ref), channel_id=1, source_target_pairs={{47,63},{16,0},{111,127},{80,64}} | collective-permute-start | bytes 2359304 | tf_op jit(solution)/shard_map/ppermute | solution.py:345
  44.8 13.5 %collective-permute-start.5 = (f32[512,256]{1,0:T(8,128)S(1)}, f32[512,256]{1,0:T(8,128)S(1)}, u32[]{:S(2)}, u32[]{:S(2)}) collective-permute-start(f32[512,256]{1,0:T(8,128)S(1)} %bitcast.15), channel_id=1, source_target_pairs={{0,1},{32,36},{1,2},{33,37},{2,3},{34,38},{3,0},{35,39},{4,5},{36,... | collective-permute-start | bytes 1572872 | tf_op jit(solution)/shard_map/ppermute | solution.py:366
  48.7 14.5 %collective-permute-start.4 = (f32[512,256]{1,0:T(8,128)S(1)}, f32[512,256]{1,0:T(8,128)S(1)}, u32[]{:S(2)}, u32[]{:S(2)}) collective-permute-start(f32[512,256]{1,0:T(8,128)S(1)} %bitcast.16), channel_id=1, source_target_pairs={{0,3},{32,44},{1,0},{33,45},{2,1},{34,46},{3,2},{35,47},{4,7},{36,... | collective-permute-start | bytes 1572872 | tf_op jit(solution)/shard_map/ppermute | solution.py:366
  51.5 14.2 %collective-permute-start.3 = (f32[512,256]{1,0:T(8,128)S(1)}, f32[512,256]{1,0:T(8,128)S(1)}, u32[]{:S(2)}, u32[]{:S(2)}) collective-permute-start(f32[512,256]{1,0:T(8,128)S(1)} %bitcast.17), channel_id=1, source_target_pairs={{0,2},{32,40},{1,3},{33,41},{2,0},{34,42},{3,1},{35,43},{4,6},{36,... | collective-permute-start | bytes 1572872 | tf_op jit(solution)/shard_map/ppermute | solution.py:366
  67.2 8.5 %collective-permute-start.7 = (f32[768,256]{1,0:T(8,128)S(1)}, f32[768,256]{1,0:T(8,128)S(1)}, u32[]{:S(2)}, u32[]{:S(2)}) collective-permute-start(f32[768,256]{1,0:T(8,128)S(1)} %shard_map.63), channel_id=1, source_target_pairs={{0,32},{32,0},{1,33},{33,1},{2,34},{34,2},{3,35},{35,3},{4,36},{36... | collective-permute-start | bytes 2359304 | tf_op jit(solution)/shard_map/ppermute | solution.py:339
  75.9 20.3 %collective-permute-start.9 = (f32[768,256]{1,0:T(8,128)S(1)}, f32[768,256]{1,0:T(8,128)S(1)}, u32[]{:S(2)}, u32[]{:S(2)}) collective-permute-start(f32[768,256]{1,0:T(8,128)S(1)} %add.78), channel_id=1, source_target_pairs={{0,64},{64,0},{1,65},{65,1},{2,66},{66,2},{3,67},{67,3},{4,68},{68... | collective-permute-start | bytes 2359304 | tf_op jit(solution)/shard_map/ppermute | solution.py:339
  76.9 19.5 %collective-permute-start.8 = (f32[768,256]{1,0:T(8,128)S(1)}, f32[768,256]{1,0:T(8,128)S(1)}, u32[]{:S(2)}, u32[]{:S(2)}) collective-permute-start(f32[768,256]{1,0:T(8,128)S(1)} %broadcast_select_fusion.1), channel_id=1, source_target_pairs={{32,1},{33,2},{34,3},{35,4},{36,5},{37,6},{38,7},{39,8},{40,9},{41... | collective-permute-start | bytes 2359304 | tf_op jit(solution)/shard_map/ppermute | solution.py:353
  97.0 3.3 %collective-permute-start.10 = (f32[768,256]{1,0:T(8,128)S(1)}, f32[768,256]{1,0:T(8,128)S(1)}, u32[]{:S(2)}, u32[]{:S(2)}) collective-permute-start(f32[768,256]{1,0:T(8,128)S(1)} %shard_map.65.refs_0_.own_ref), channel_id=1, source_target_pairs={{0,32},{32,0},{1,33},{33,1},{2,34},{34,2},{3,35},{35,3},{4,36},{36... | collective-permute-start | bytes 2359304 | tf_op jit(solution)/shard_map/ppermute | solution.py:339
  101.1 10.0 %collective-permute-start.11 = (f32[512,256]{1,0:T(8,128)S(1)}, f32[512,256]{1,0:T(8,128)S(1)}, u32[]{:S(2)}, u32[]{:S(2)}) collective-permute-start(f32[512,256]{1,0:T(8,128)S(1)} %shard_map.68), channel_id=1, source_target_pairs={{0,2},{32,40},{1,3},{33,41},{2,0},{34,42},{3,1},{35,43},{4,6},{36,... | collective-permute-start | bytes 1572872 | tf_op jit(solution)/shard_map/ppermute | solution.py:366
  102.6 14.0 %collective-permute-start.12 = (f32[512,256]{1,0:T(8,128)S(1)}, f32[512,256]{1,0:T(8,128)S(1)}, u32[]{:S(2)}, u32[]{:S(2)}) collective-permute-start(f32[512,256]{1,0:T(8,128)S(1)} %get-tuple-element.116), channel_id=1, source_target_pairs={{0,1},{32,36},{1,2},{33,37},{2,3},{34,38},{3,0},{35,39},{4,5},{36,... | collective-permute-start | bytes 1572872 | tf_op jit(solution)/shard_map/ppermute | solution.py:366
  102.7 14.0 %collective-permute-start.13 = (f32[512,256]{1,0:T(8,128)S(1)}, f32[512,256]{1,0:T(8,128)S(1)}, u32[]{:S(2)}, u32[]{:S(2)}) collective-permute-start(f32[512,256]{1,0:T(8,128)S(1)} %get-tuple-element.117), channel_id=1, source_target_pairs={{0,3},{32,44},{1,0},{33,45},{2,1},{34,46},{3,2},{35,47},{4,7},{36,... | collective-permute-start | bytes 1572872 | tf_op jit(solution)/shard_map/ppermute | solution.py:366
  139.8 20.9 %collective-permute-start.17 = (f32[768,256]{1,0:T(8,128)S(1)}, f32[768,256]{1,0:T(8,128)S(1)}, u32[]{:S(2)}, u32[]{:S(2)}) collective-permute-start(f32[768,256]{1,0:T(8,128)S(1)} %shard_map.65.refs_0_.own_ref), channel_id=1, source_target_pairs={{47,63},{16,0},{111,127},{80,64}} | collective-permute-start | bytes 2359304 | tf_op jit(solution)/shard_map/ppermute | solution.py:345
  140.5 15.2 %collective-permute-start.16 = (f32[512,256]{1,0:T(8,128)S(1)}, f32[512,256]{1,0:T(8,128)S(1)}, u32[]{:S(2)}, u32[]{:S(2)}) collective-permute-start(f32[512,256]{1,0:T(8,128)S(1)} %bitcast.11), channel_id=1, source_target_pairs={{0,1},{32,36},{1,2},{33,37},{2,3},{34,38},{3,0},{35,39},{4,5},{36,... | collective-permute-start | bytes 1572872 | tf_op jit(solution)/shard_map/ppermute | solution.py:366
  140.6 17.6 %collective-permute-start.15 = (f32[512,256]{1,0:T(8,128)S(1)}, f32[512,256]{1,0:T(8,128)S(1)}, u32[]{:S(2)}, u32[]{:S(2)}) collective-permute-start(f32[512,256]{1,0:T(8,128)S(1)} %bitcast.12), channel_id=1, source_target_pairs={{0,3},{32,44},{1,0},{33,45},{2,1},{34,46},{3,2},{35,47},{4,7},{36,... | collective-permute-start | bytes 1572872 | tf_op jit(solution)/shard_map/ppermute | solution.py:366
  143.2 17.4 %collective-permute-start.14 = (f32[512,256]{1,0:T(8,128)S(1)}, f32[512,256]{1,0:T(8,128)S(1)}, u32[]{:S(2)}, u32[]{:S(2)}) collective-permute-start(f32[512,256]{1,0:T(8,128)S(1)} %bitcast.13), channel_id=1, source_target_pairs={{0,2},{32,40},{1,3},{33,41},{2,0},{34,42},{3,1},{35,43},{4,6},{36,... | collective-permute-start | bytes 1572872 | tf_op jit(solution)/shard_map/ppermute | solution.py:366
  162.2 5.2 %collective-permute-start.18 = (f32[768,256]{1,0:T(8,128)S(1)}, f32[768,256]{1,0:T(8,128)S(1)}, u32[]{:S(2)}, u32[]{:S(2)}) collective-permute-start(f32[768,256]{1,0:T(8,128)S(1)} %shard_map.75), channel_id=1, source_target_pairs={{0,32},{32,0},{1,33},{33,1},{2,34},{34,2},{3,35},{35,3},{4,36},{36... | collective-permute-start | bytes 2359304 | tf_op jit(solution)/shard_map/ppermute | solution.py:339
  167.5 20.6 %collective-permute-start.20 = (f32[768,256]{1,0:T(8,128)S(1)}, f32[768,256]{1,0:T(8,128)S(1)}, u32[]{:S(2)}, u32[]{:S(2)}) collective-permute-start(f32[768,256]{1,0:T(8,128)S(1)} %add.83), channel_id=1, source_target_pairs={{0,64},{64,0},{1,65},{65,1},{2,66},{66,2},{3,67},{67,3},{4,68},{68... | collective-permute-start | bytes 2359304 | tf_op jit(solution)/shard_map/ppermute | solution.py:339
  168.8 19.5 %collective-permute-start.19 = (f32[768,256]{1,0:T(8,128)S(1)}, f32[768,256]{1,0:T(8,128)S(1)}, u32[]{:S(2)}, u32[]{:S(2)}) collective-permute-start(f32[768,256]{1,0:T(8,128)S(1)} %broadcast_select_fusion), channel_id=1, source_target_pairs={{32,1},{33,2},{34,3},{35,4},{36,5},{37,6},{38,7},{39,8},{40,9},{41... | collective-permute-start | bytes 2359304 | tf_op jit(solution)/shard_map/ppermute | solution.py:353
  188.9 3.2 %collective-permute-start.21 = (f32[768,256]{1,0:T(8,128)S(1)}, f32[768,256]{1,0:T(8,128)S(1)}, u32[]{:S(2)}, u32[]{:S(2)}) collective-permute-start(f32[768,256]{1,0:T(8,128)S(1)} %shard_map.77.value_ref), channel_id=1, source_target_pairs={{0,32},{32,0},{1,33},{33,1},{2,34},{34,2},{3,35},{35,3},{4,36},{36... | collective-permute-start | bytes 2359304 | tf_op jit(solution)/shard_map/ppermute | solution.py:339

commit v11 on v10

--- a/solution.py
+++ b/solution.py
@@ -203,28 +203,35 @@
     )(*args)
 
 
-def close_kernel(plane_ref, w_ref, high_ref, low_ref, start_ref, g_ref, wh_ref, wl_ref):
+def close_kernel(chunks, plane_ref, *refs):
+    w_refs, sense, refs = refs[:chunks], refs[chunks : 3 * chunks], refs[3 * chunks :]
+    start_ref, g_ref, wh_ref, wl_ref = refs
     blocks = g_ref.shape[0] // ROWS
-    wh_ref[...], wl_ref[...] = split(w_ref[...].T)
+    for i in range(chunks):
+        wh_ref[i], wl_ref[i] = split(w_refs[i][...].T)
 
     @pl.loop(0, blocks)
     def _(j):
         columns = block_of(plane_ref[0] * blocks + j, ROWS)
-        part = product((wh_ref[...], wl_ref[...]), (high_ref[:, columns], low_ref[:, columns]))
-        g_ref[block_of(j, ROWS), :] = (start_ref[:, columns] + part).T
-
-
-def close(plane, w, sense, before, cells):
-    rows, sols = w.shape
-    args = [plane, w, *pinned(sense), *pinned([before])]
-    return pl.pallas_call(
-        close_kernel,
+        total = start_ref[:, columns]
+        for i in range(chunks):
+            parts = (sense[2 * i][:, columns], sense[2 * i + 1][:, columns])
+            total = total + product((wh_ref[i], wl_ref[i]), parts)
+        g_ref[block_of(j, ROWS), :] = total.T
+
+
+def close(plane, ws, sense, before, cells):
+    chunks = len(ws)
+    rows, sols = ws[0].shape
+    args = [plane, *ws, *pinned(sense), *pinned([before])]
+    return pl.pallas_call(
+        functools.partial(close_kernel, chunks),
         in_specs=[SMEM] + [VMEM] * (len(args) - 1),
         out_specs=VMEM,
         out_shape=jax.ShapeDtypeStruct((cells, sols), F32),
-        scratch_shapes=[pltpu.VMEM((sols, rows), BF16), pltpu.VMEM((sols, rows), BF16)],
-        compiler_params=PARAMS,
-        cost_estimate=cost(rows, cells, sols, 0),
+        scratch_shapes=[pltpu.VMEM((chunks, sols, rows), BF16), pltpu.VMEM((chunks, sols, rows), BF16)],
+        compiler_params=PARAMS,
+        cost_estimate=cost(chunks * rows, cells, sols, 0),
     )(*args)
 
 
@@ -433,11 +440,10 @@
         w2, w3, w1 = ring_of(w0, 2), ring_of(w0, 1), ring_of(w0, 3)
         near = gather_up([w0], s0)
         near = gather_up([w3], s3, [near])
-        near = gather_up([w1], s1, [near])
         near, relay = lax.optimization_barrier((near, relay))
         sent = jnp.where(carrier, relay, own)
-        away = close(theirs, w2, s2, near, cells)
-        home = close(mine, w2, s2, near, cells)
+        away = close(theirs, [w1, w2], s1 + s2, near, cells)
+        home = close(mine, [w1, w2], s1 + s2, near, cells)
         half = home + swap(away, "core")
         half, own, twin, sent = lax.optimization_barrier((half, own, twin, sent))
         beyond = beyond_of(sent, ranks)

time: 193 us -> 191 us (0.990)
  starting transfers between devices: 39.3 us -> 36.8 us
  waiting for transfers between devices: 52.8 us -> 54.8 us
    pallas_call x6 -> x4, Pallas kernels: 14.7 us -> 9.81 us  [gather_up(): pl.pallas_call(functools.partial(gather_kernel, chunks, len(before) > 0),...]
    pallas_call x4, Pallas kernels: 6.14 us -> 9.14 us  [close(): pl.pallas_call(functools.partial(close_kernel, chunks), in_specs=[SMEM] +...]
    ppermute x6, starting transfers between devices: 14.8 us -> 12.2 us  [swap(): return lax.ppermute(value, axis, [(0, 1), (1, 0)])]
  transfers between devices with their start and end apart: 22 -> 22, of which waited for: 11 -> 10; matrix products, arithmetic and copies ran while one was open for 0% -> 0% of each run, Pallas kernels for 22% -> 20%
where the time goes in v11:
time: 191 us
  waiting for transfers between devices  54.8 us (29%)
  Pallas kernels  51.2 us (27%)
  blocking collectives  45.9 us (24%)
  starting transfers between devices  36.8 us (19%)
    all_to_all x4, blocking collectives, spread(): lax.all_to_all(value, ALL, 0, 0, axis_index_groups=groups, tiled=True)  45.9 us
    ppermute x12, waiting for transfers between devices, ring_of(): return lax.ppermute(value, ALL, pairs)  31.5 us
    ppermute x6, waiting for transfers between devices, swap(): return lax.ppermute(value, axis, [(0, 1), (1, 0)])  23.3 us
    ppermute x12, starting transfers between devices, ring_of(): return lax.ppermute(value, ALL, pairs)  19.2 us
    pallas_call x2, Pallas kernels, smooth_of(): pl.pallas_call(smooth_kernel, in_specs=[VMEM] * 3, out_specs=VMEM, out_sh...  13.1 us
    ppermute x6, starting transfers between devices, swap(): return lax.ppermute(value, axis, [(0, 1), (1, 0)])  12.2 us
    pallas_call x4, Pallas kernels, gather_up(): pl.pallas_call(functools.partial(gather_kernel, chunks, len(before) > 0),...  9.81 us
    pallas_call x4, Pallas kernels, close(): pl.pallas_call(functools.partial(close_kernel, chunks), in_specs=[SMEM] +...  9.14 us
  transfers between devices with their start and end apart: 22, of which 10 were waited for; matrix products, arithmetic and copies ran while one was open for 0% of the time, Pallas kernels for 20%

profile of v11, /device:TPU:25, one launch (start us, length us, event | category | flops | bytes accessed | tf_op | source)
XLA Modules:
  0.0 190.7 jit_solution(9436567606516136313)
XLA Ops:
  0.1 5.0 %shard_map.55 = (f32[512,256]{1,0:T(8,128)S(1)}, bf16[512,1536]{1,0:T(8,128)(2,1)S(1)}, bf16[512,1536]{1,0:T(8,128)(2,1)S(1)}, bf16[1536,256]{1,0:T(8,128)(2,1)S(1)}, bf16[1536,256]{1,0:T(8,128)(2,1)S(1)}) custom-call(s32[1]{0:T(128)} %bitcast.5.blocks_ref, f32[2048,1536]{1,0:T(8,128)} %s_ref.5, f32[1536,256]{1,0:T(8,128)} %x_ref.1), custom_call_target="tpu_custom_call" | custom-call | flops 1207959552 | bytes 5242880 | tf_op jit(solution)/shard_map/pallas_call | solution.py:91
  5.1 2.8 %collective-permute-start = (f32[512,256]{1,0:T(8,128)S(1)}, f32[512,256]{1,0:T(8,128)S(1)}, u32[]{:S(2)}, u32[]{:S(2)}) collective-permute-start(f32[512,256]{1,0:T(8,128)S(1)} %get-tuple-element.81), channel_id=1, source_target_pairs={{0,2},{32,40},{1,3},{33,41},{2,0},{34,42},{3,1},{35,43},{4,6},{36,... | collective-permute-start | bytes 1572872 | tf_op jit(solution)/shard_map/ppermute | solution.py:373
  7.9 3.4 %shard_map.56 = (f32[512,256]{1,0:T(8,128)S(1)}, bf16[512,1536]{1,0:T(8,128)(2,1)S(1)}, bf16[512,1536]{1,0:T(8,128)(2,1)S(1)}, f32[512,256]{1,0:T(8,128)S(1)}, b...) custom-call(s32[2]{0:T(128)S(1)} %get-tuple-element.72.blocks_ref, f32[2048,1536]{1,0:T(8,128)S(1)} %copy-done, ...), custom_call_target="tpu_custom_call" | custom-call | flops 2415919104 | bytes 2621440 | tf_op jit(solution)/shard_map/pallas_call | solution.py:128
  11.7 2.4 %collective-permute-start.2 = (f32[512,256]{1,0:T(8,128)S(1)}, f32[512,256]{1,0:T(8,128)S(1)}, u32[]{:S(2)}, u32[]{:S(2)}) collective-permute-start(f32[512,256]{1,0:T(8,128)S(1)} %get-tuple-element.82), channel_id=1, source_target_pairs={{0,3},{32,44},{1,0},{33,45},{2,1},{34,46},{3,2},{35,47},{4,7},{36,... | collective-permute-start | bytes 1572872 | tf_op jit(solution)/shard_map/ppermute | solution.py:373
  16.0 5.0 %collective-permute-done.1 = f32[512,256]{1,0:T(8,128)S(1)} collective-permute-done((f32[512,256]{1,0:T(8,128)S(1)}, f32[512,256]{1,0:T(8,128)S(1)}, u32[]{:S(2)}, u32[]{:S(2)}) %collective-permute-start.1) | collective-permute-done | bytes 524320 | tf_op jit(solution)/shard_map/ppermute | solution.py:373
  21.1 13.0 %all_to_all.36.pieces_ref = f32[8,64,256]{2,1,0:T(8,128)S(1)} all-to-all(f32[8,64,256]{2,1,0:T(8,128)S(1)} %bitcast.19), channel_id=1, replica_groups={{0,4,8,12,16,20,24,28},{1,5,9,13,17,21,25,29},{2,6,10,14,18,22,26,30},{..., dimensions={0} | all-to-all | bytes 1048576 | tf_op jit(solution)/shard_map/all_to_all | solution.py:383
  34.1 10.0 %all_to_all.37 = f32[8,64,256]{2,1,0:T(8,128)S(1)} all-to-all(f32[8,64,256]{2,1,0:T(8,128)S(1)} %shard_map.58), channel_id=1, replica_groups={{0,4,8,12,16,20,24,28},{1,5,9,13,17,21,25,29},{2,6,10,14,18,22,26,30},{..., dimensions={0} | all-to-all | bytes 1048576 | tf_op jit(solution)/shard_map/all_to_all | solution.py:383
  44.8 3.9 %collective-permute-start.5 = (f32[512,256]{1,0:T(8,128)S(1)}, f32[512,256]{1,0:T(8,128)S(1)}, u32[]{:S(2)}, u32[]{:S(2)}) collective-permute-start(f32[512,256]{1,0:T(8,128)S(1)} %bitcast.15), channel_id=1, source_target_pairs={{0,1},{32,36},{1,2},{33,37},{2,3},{34,38},{3,0},{35,39},{4,5},{36,... | collective-permute-start | bytes 1572872 | tf_op jit(solution)/shard_map/ppermute | solution.py:373
  48.7 2.8 %collective-permute-start.3 = (f32[512,256]{1,0:T(8,128)S(1)}, f32[512,256]{1,0:T(8,128)S(1)}, u32[]{:S(2)}, u32[]{:S(2)}) collective-permute-start(f32[512,256]{1,0:T(8,128)S(1)} %bitcast.16), channel_id=1, source_target_pairs={{0,3},{32,44},{1,0},{33,45},{2,1},{34,46},{3,2},{35,47},{4,7},{36,... | collective-permute-start | bytes 1572872 | tf_op jit(solution)/shard_map/ppermute | solution.py:373
  52.8 2.4 %shard_map.59.refs_3_ = f32[256,1536]{1,0:T(8,128)S(1)} custom-call(f32[512,256]{1,0:T(8,128)S(1)} %bitcast.18, bf16[512,1536]{1,0:T(8,128)(2,1)S(1)} %get-tuple-element.102.refs_1_.refs_2_, bf16[512,1536]{1,0:T(8,128)(2,1)S(1)} %get-tuple-element.103.refs_2_.refs_3_), custom_call_target="tpu_custom_call" | custom-call | flops 1207959552 | bytes 2097152 | tf_op jit(solution)/shard_map/pallas_call | solution.py:195
  55.3 3.0 %collective-permute-done.5.refs_0_ = f32[512,256]{1,0:T(8,128)S(1)} collective-permute-done((f32[512,256]{1,0:T(8,128)S(1)}, f32[512,256]{1,0:T(8,128)S(1)}, u32[]{:S(2)}, u32[]{:S(2)}) %collective-permute-start.5) | collective-permute-done | bytes 524320 | tf_op jit(solution)/shard_map/ppermute | solution.py:373
  58.3 2.5 %shard_map.60.refs_6_ = f32[256,1536]{1,0:T(8,128)S(1)} custom-call(f32[512,256]{1,0:T(8,128)S(1)} %collective-permute-done.5.refs_0_, bf16[512,1536]{1,0:T(8,128)(2,1)S(1)} %get-tuple-element.100.refs_1_.refs_5_.refs_3_, bf16[512,1536]{1,0:T(8,128)(2,1)S(1)} %get-tuple-element.101.refs_2_.refs_6_.refs_4_, f32[256,1536]{1,0:T(8,128)S(1)} %shard_map.59.refs_3_), custom_call_target="tpu_custom_call" | custom-call | flops 1207959552 | bytes 2097152 | tf_op jit(solution)/shard_map/pallas_call | solution.py:195
  60.8 2.5 %collective-permute-done.3.refs_0_ = f32[512,256]{1,0:T(8,128)S(1)} collective-permute-done((f32[512,256]{1,0:T(8,128)S(1)}, f32[512,256]{1,0:T(8,128)S(1)}, u32[]{:S(2)}, u32[]{:S(2)}) %collective-permute-start.3) | collective-permute-done | bytes 524320 | tf_op jit(solution)/shard_map/ppermute | solution.py:373
  65.1 2.3 %shard_map.62 = f32[768,256]{1,0:T(8,128)S(1)} custom-call(s32[1]{0:T(128)} %bitcast.2.plane_ref.planes_ref, f32[512,256]{1,0:T(8,128)S(1)} %collective-permute-done.3.refs_0_, f32[512,256]{1,0:T(8,128)S(1)} %collective-permute-done.4.refs_1_, bf16[512,1536]{1,0:T(8,128)(2,1)S(1)} %get-tuple-element.96.refs_2_.refs_3_.refs_1_, ...), custom_call_target="tpu_custom_call" | custom-call | flops 1207959552 | bytes 1835008 | tf_op jit(solution)/shard_map/pallas_call | solution.py:227
  67.4 4.8 %collective-permute-start.7 = (f32[768,256]{1,0:T(8,128)S(1)}, f32[768,256]{1,0:T(8,128)S(1)}, u32[]{:S(2)}, u32[]{:S(2)}) collective-permute-start(f32[768,256]{1,0:T(8,128)S(1)} %shard_map.62), channel_id=1, source_target_pairs={{0,32},{32,0},{1,33},{33,1},{2,34},{34,2},{3,35},{35,3},{4,36},{36... | collective-permute-start | bytes 2359304 | tf_op jit(solution)/shard_map/ppermute | solution.py:346
  72.2 2.3 %shard_map.61 = f32[768,256]{1,0:T(8,128)S(1)} custom-call(s32[1]{0:T(128)} %bitcast.1.plane_ref.planes_ref, f32[512,256]{1,0:T(8,128)S(1)} %collective-permute-done.3.refs_0_, f32[512,256]{1,0:T(8,128)S(1)} %collective-permute-done.4.refs_1_, bf16[512,1536]{1,0:T(8,128)(2,1)S(1)} %get-tuple-element.96.refs_2_.refs_3_.refs_1_, ...), custom_call_target="tpu_custom_call" | custom-call | flops 1207959552 | bytes 1835008 | tf_op jit(solution)/shard_map/pallas_call | solution.py:227
  77.8 6.5 %shard_map.63.inner_ref = f32[768,256]{1,0:T(8,128)S(1)} custom-call(f32[8,768]{1,0:T(8,128)S(1)} %maximum_maximum_fusion.table_ref, f32[768,256]{1,0:T(8,128)S(1)} %get-tuple-element.109.own_ref, f32[768,256]{1,0:T(8,128)S(1)} %get-tuple-element.111.twin_ref), custom_call_target="tpu_custom_call" | custom-call | flops 3623878656 | bytes 3145728 | tf_op jit(solution)/shard_map/pallas_call | solution.py:288
  84.4 11.0 %collective-permute-done.9 = f32[768,256]{1,0:T(8,128)S(1)} collective-permute-done((f32[768,256]{1,0:T(8,128)S(1)}, f32[768,256]{1,0:T(8,128)S(1)}, u32[]{:S(2)}, u32[]{:S(2)}) %collective-permute-start.9) | collective-permute-done | bytes 786464 | tf_op jit(solution)/shard_map/ppermute | solution.py:346
  101.5 2.7 %collective-permute-start.13 = (f32[512,256]{1,0:T(8,128)S(1)}, f32[512,256]{1,0:T(8,128)S(1)}, u32[]{:S(2)}, u32[]{:S(2)}) collective-permute-start(f32[512,256]{1,0:T(8,128)S(1)} %get-tuple-element.117), channel_id=1, source_target_pairs={{0,3},{32,44},{1,0},{33,45},{2,1},{34,46},{3,2},{35,47},{4,7},{36,... | collective-permute-start | bytes 1572872 | tf_op jit(solution)/shard_map/ppermute | solution.py:373
  106.2 3.7 %collective-permute-done.11 = f32[512,256]{1,0:T(8,128)S(1)} collective-permute-done((f32[512,256]{1,0:T(8,128)S(1)}, f32[512,256]{1,0:T(8,128)S(1)}, u32[]{:S(2)}, u32[]{:S(2)}) %collective-permute-start.11) | collective-permute-done | bytes 524320 | tf_op jit(solution)/shard_map/ppermute | solution.py:373
  109.9 5.5 %collective-permute-done.12 = f32[512,256]{1,0:T(8,128)S(1)} collective-permute-done((f32[512,256]{1,0:T(8,128)S(1)}, f32[512,256]{1,0:T(8,128)S(1)}, u32[]{:S(2)}, u32[]{:S(2)}) %collective-permute-start.12) | collective-permute-done | bytes 524320 | tf_op jit(solution)/shard_map/ppermute | solution.py:373
  115.5 10.7 %all_to_all.38.pieces_ref = f32[8,64,256]{2,1,0:T(8,128)S(1)} all-to-all(f32[8,64,256]{2,1,0:T(8,128)S(1)} %bitcast.20), channel_id=1, replica_groups={{0,4,8,12,16,20,24,28},{1,5,9,13,17,21,25,29},{2,6,10,14,18,22,26,30},{..., dimensions={0} | all-to-all | bytes 1048576 | tf_op jit(solution)/shard_map/all_to_all | solution.py:383
  126.3 12.2 %all_to_all.39 = f32[8,64,256]{2,1,0:T(8,128)S(1)} all-to-all(f32[8,64,256]{2,1,0:T(8,128)S(1)} %shard_map.69), channel_id=1, replica_groups={{0,4,8,12,16,20,24,28},{1,5,9,13,17,21,25,29},{2,6,10,14,18,22,26,30},{..., dimensions={0} | all-to-all | bytes 1048576 | tf_op jit(solution)/shard_map/all_to_all | solution.py:383
  139.3 2.7 %collective-permute-start.14 = (f32[512,256]{1,0:T(8,128)S(1)}, f32[512,256]{1,0:T(8,128)S(1)}, u32[]{:S(2)}, u32[]{:S(2)}) collective-permute-start(f32[512,256]{1,0:T(8,128)S(1)} %bitcast.12), channel_id=1, source_target_pairs={{0,3},{32,44},{1,0},{33,45},{2,1},{34,46},{3,2},{35,47},{4,7},{36,... | collective-permute-start | bytes 1572872 | tf_op jit(solution)/shard_map/ppermute | solution.py:373
  142.0 2.4 %shard_map.70.refs_3_ = f32[256,1536]{1,0:T(8,128)S(1)} custom-call(f32[512,256]{1,0:T(8,128)S(1)} %bitcast.14, bf16[512,1536]{1,0:T(8,128)(2,1)S(1)} %get-tuple-element.102.refs_1_.refs_2_, bf16[512,1536]{1,0:T(8,128)(2,1)S(1)} %get-tuple-element.103.refs_2_.refs_3_), custom_call_target="tpu_custom_call" | custom-call | flops 1207959552 | bytes 2097152 | tf_op jit(solution)/shard_map/pallas_call | solution.py:195
  144.4 10.0 %collective-permute-done.16.refs_0_ = f32[512,256]{1,0:T(8,128)S(1)} collective-permute-done((f32[512,256]{1,0:T(8,128)S(1)}, f32[512,256]{1,0:T(8,128)S(1)}, u32[]{:S(2)}, u32[]{:S(2)}) %collective-permute-start.16) | collective-permute-done | bytes 524320 | tf_op jit(solution)/shard_map/ppermute | solution.py:373
  154.5 2.5 %shard_map.71.refs_6_ = f32[256,1536]{1,0:T(8,128)S(1)} custom-call(f32[512,256]{1,0:T(8,128)S(1)} %collective-permute-done.16.refs_0_, bf16[512,1536]{1,0:T(8,128)(2,1)S(1)} %get-tuple-element.100.refs_1_.refs_5_.refs_3_, bf16[512,1536]{1,0:T(8,128)(2,1)S(1)} %get-tuple-element.101.refs_2_.refs_6_.refs_4_, f32[256,1536]{1,0:T(8,128)S(1)} %shard_map.70.refs_3_), custom_call_target="tpu_custom_call" | custom-call | flops 1207959552 | bytes 2097152 | tf_op jit(solution)/shard_map/pallas_call | solution.py:195
  157.0 2.3 %shard_map.73 = f32[768,256]{1,0:T(8,128)S(1)} custom-call(s32[1]{0:T(128)} %bitcast.2.plane_ref.planes_ref, f32[512,256]{1,0:T(8,128)S(1)} %collective-permute-done.14.refs_0_, f32[512,256]{1,0:T(8,128)S(1)} %collective-permute-done.15.refs_1_, bf16[512,1536]{1,0:T(8,128)(2,1)S(1)} %get-tuple-element.96.refs_2_.refs_3_.refs_1_, ...), custom_call_target="tpu_custom_call" | custom-call | flops 1207959552 | bytes 1835008 | tf_op jit(solution)/shard_map/pallas_call | solution.py:227
  159.3 3.5 %collective-permute-start.18 = (f32[768,256]{1,0:T(8,128)S(1)}, f32[768,256]{1,0:T(8,128)S(1)}, u32[]{:S(2)}, u32[]{:S(2)}) collective-permute-start(f32[768,256]{1,0:T(8,128)S(1)} %shard_map.73), channel_id=1, source_target_pairs={{0,32},{32,0},{1,33},{33,1},{2,34},{34,2},{3,35},{35,3},{4,36},{36... | collective-permute-start | bytes 2359304 | tf_op jit(solution)/shard_map/ppermute | solution.py:346
  162.8 2.3 %shard_map.72 = f32[768,256]{1,0:T(8,128)S(1)} custom-call(s32[1]{0:T(128)} %bitcast.1.plane_ref.planes_ref, f32[512,256]{1,0:T(8,128)S(1)} %collective-permute-done.14.refs_0_, f32[512,256]{1,0:T(8,128)S(1)} %collective-permute-done.15.refs_1_, bf16[512,1536]{1,0:T(8,128)(2,1)S(1)} %get-tuple-element.96.refs_2_.refs_3_.refs_1_, ...), custom_call_target="tpu_custom_call" | custom-call | flops 1207959552 | bytes 1835008 | tf_op jit(solution)/shard_map/pallas_call | solution.py:227
  168.3 6.5 %shard_map.74.inner_ref = f32[768,256]{1,0:T(8,128)S(1)} custom-call(f32[8,768]{1,0:T(8,128)S(1)} %maximum_maximum_fusion.table_ref, f32[768,256]{1,0:T(8,128)S(1)} %shard_map.64.refs_0_.own_ref, f32[768,256]{1,0:T(8,128)S(1)} %collective-permute-done.10.refs_1_.refs_0_.twin_ref), custom_call_target="tpu_custom_call" | custom-call | flops 3623878656 | bytes 3145728 | tf_op jit(solution)/shard_map/pallas_call | solution.py:288
  174.8 11.2 %collective-permute-done.20 = f32[768,256]{1,0:T(8,128)S(1)} collective-permute-done((f32[768,256]{1,0:T(8,128)S(1)}, f32[768,256]{1,0:T(8,128)S(1)}, u32[]{:S(2)}, u32[]{:S(2)}) %collective-permute-start.20) | collective-permute-done | bytes 786464 | tf_op jit(solution)/shard_map/ppermute | solution.py:346
  (67 shorter events, 26.3 us)
Async XLA Ops:
  0.1 7.9 %copy-start = (f32[2048,1536]{1,0:T(8,128)S(1)}, f32[2048,1536]{1,0:T(8,128)}, u32[]{:S(2)}) copy-start(f32[2048,1536]{1,0:T(8,128)} %s_ref.5) | copy-start | bytes 37748740
  5.1 10.8 %collective-permute-start = (f32[512,256]{1,0:T(8,128)S(1)}, f32[512,256]{1,0:T(8,128)S(1)}, u32[]{:S(2)}, u32[]{:S(2)}) collective-permute-start(f32[512,256]{1,0:T(8,128)S(1)} %get-tuple-element.81), channel_id=1, source_target_pairs={{0,2},{32,40},{1,3},{33,41},{2,0},{34,42},{3,1},{35,43},{4,6},{36,... | collective-permute-start | bytes 1572872 | tf_op jit(solution)/shard_map/ppermute | solution.py:373
  11.3 9.6 %collective-permute-start.1 = (f32[512,256]{1,0:T(8,128)S(1)}, f32[512,256]{1,0:T(8,128)S(1)}, u32[]{:S(2)}, u32[]{:S(2)}) collective-permute-start(f32[512,256]{1,0:T(8,128)S(1)} %get-tuple-element.76), channel_id=1, source_target_pairs={{0,1},{32,36},{1,2},{33,37},{2,3},{34,38},{3,0},{35,39},{4,5},{36,... | collective-permute-start | bytes 1572872 | tf_op jit(solution)/shard_map/ppermute | solution.py:373
  11.7 3.8 %copy-start.4 = (s32[1536]{0:T(1024)S(1)}, s32[1536]{0:T(1024)}, u32[]{:S(2)}) copy-start(s32[1536]{0:T(1024)} %param.9) | copy-start | bytes 18436
  11.7 3.9 %copy-start.3 = (s32[4,768]{1,0:T(4,128)S(1)}, s32[4,768]{1,0:T(4,128)}, u32[]{:S(2)}) copy-start(s32[4,768]{1,0:T(4,128)} %param.8) | copy-start | bytes 36868
  11.7 4.0 %copy-start.2 = (f32[1536,256]{1,0:T(8,128)S(1)}, f32[1536,256]{1,0:T(8,128)}, u32[]{:S(2)}) copy-start(f32[1536,256]{1,0:T(8,128)} %x_ref.1) | copy-start | bytes 4718596
  11.7 9.2 %collective-permute-start.2 = (f32[512,256]{1,0:T(8,128)S(1)}, f32[512,256]{1,0:T(8,128)S(1)}, u32[]{:S(2)}, u32[]{:S(2)}) collective-permute-start(f32[512,256]{1,0:T(8,128)S(1)} %get-tuple-element.82), channel_id=1, source_target_pairs={{0,3},{32,44},{1,0},{33,45},{2,1},{34,46},{3,2},{35,47},{4,7},{36,... | collective-permute-start | bytes 1572872 | tf_op jit(solution)/shard_map/ppermute | solution.py:373
  16.0 18.1 %copy-start.1 = (f32[2048,256]{1,0:T(8,128)S(1)}, f32[2048,256]{1,0:T(8,128)}, u32[]{:S(2)}) copy-start(f32[2048,256]{1,0:T(8,128)} %observed_ref.3) | copy-start | bytes 6291460
  44.1 16.7 %collective-permute-start.6 = (f32[768,256]{1,0:T(8,128)S(1)}, f32[768,256]{1,0:T(8,128)S(1)}, u32[]{:S(2)}, u32[]{:S(2)}) collective-permute-start(f32[768,256]{1,0:T(8,128)S(1)} %get-tuple-element.109.own_ref), channel_id=1, source_target_pairs={{47,63},{16,0},{111,127},{80,64}} | collective-permute-start | bytes 2359304 | tf_op jit(solution)/shard_map/ppermute | solution.py:352
  44.8 13.5 %collective-permute-start.5 = (f32[512,256]{1,0:T(8,128)S(1)}, f32[512,256]{1,0:T(8,128)S(1)}, u32[]{:S(2)}, u32[]{:S(2)}) collective-permute-start(f32[512,256]{1,0:T(8,128)S(1)} %bitcast.15), channel_id=1, source_target_pairs={{0,1},{32,36},{1,2},{33,37},{2,3},{34,38},{3,0},{35,39},{4,5},{36,... | collective-permute-start | bytes 1572872 | tf_op jit(solution)/shard_map/ppermute | solution.py:373
  48.7 14.5 %collective-permute-start.3 = (f32[512,256]{1,0:T(8,128)S(1)}, f32[512,256]{1,0:T(8,128)S(1)}, u32[]{:S(2)}, u32[]{:S(2)}) collective-permute-start(f32[512,256]{1,0:T(8,128)S(1)} %bitcast.16), channel_id=1, source_target_pairs={{0,3},{32,44},{1,0},{33,45},{2,1},{34,46},{3,2},{35,47},{4,7},{36,... | collective-permute-start | bytes 1572872 | tf_op jit(solution)/shard_map/ppermute | solution.py:373
  51.5 13.6 %collective-permute-start.4 = (f32[512,256]{1,0:T(8,128)S(1)}, f32[512,256]{1,0:T(8,128)S(1)}, u32[]{:S(2)}, u32[]{:S(2)}) collective-permute-start(f32[512,256]{1,0:T(8,128)S(1)} %bitcast.17), channel_id=1, source_target_pairs={{0,2},{32,40},{1,3},{33,41},{2,0},{34,42},{3,1},{35,43},{4,6},{36,... | collective-permute-start | bytes 1572872 | tf_op jit(solution)/shard_map/ppermute | solution.py:373
  67.4 7.2 %collective-permute-start.7 = (f32[768,256]{1,0:T(8,128)S(1)}, f32[768,256]{1,0:T(8,128)S(1)}, u32[]{:S(2)}, u32[]{:S(2)}) collective-permute-start(f32[768,256]{1,0:T(8,128)S(1)} %shard_map.62), channel_id=1, source_target_pairs={{0,32},{32,0},{1,33},{33,1},{2,34},{34,2},{3,35},{35,3},{4,36},{36... | collective-permute-start | bytes 2359304 | tf_op jit(solution)/shard_map/ppermute | solution.py:346
  74.7 20.7 %collective-permute-start.9 = (f32[768,256]{1,0:T(8,128)S(1)}, f32[768,256]{1,0:T(8,128)S(1)}, u32[]{:S(2)}, u32[]{:S(2)}) collective-permute-start(f32[768,256]{1,0:T(8,128)S(1)} %add.78), channel_id=1, source_target_pairs={{0,64},{64,0},{1,65},{65,1},{2,66},{66,2},{3,67},{67,3},{4,68},{68... | collective-permute-start | bytes 2359304 | tf_op jit(solution)/shard_map/ppermute | solution.py:346
  75.7 19.8 %collective-permute-start.8 = (f32[768,256]{1,0:T(8,128)S(1)}, f32[768,256]{1,0:T(8,128)S(1)}, u32[]{:S(2)}, u32[]{:S(2)}) collective-permute-start(f32[768,256]{1,0:T(8,128)S(1)} %broadcast_select_fusion.1), channel_id=1, source_target_pairs={{32,1},{33,2},{34,3},{35,4},{36,5},{37,6},{38,7},{39,8},{40,9},{41... | collective-permute-start | bytes 2359304 | tf_op jit(solution)/shard_map/ppermute | solution.py:360
  96.1 2.9 %collective-permute-start.10 = (f32[768,256]{1,0:T(8,128)S(1)}, f32[768,256]{1,0:T(8,128)S(1)}, u32[]{:S(2)}, u32[]{:S(2)}) collective-permute-start(f32[768,256]{1,0:T(8,128)S(1)} %shard_map.64.refs_0_.own_ref), channel_id=1, source_target_pairs={{0,32},{32,0},{1,33},{33,1},{2,34},{34,2},{3,35},{35,3},{4,36},{36... | collective-permute-start | bytes 2359304 | tf_op jit(solution)/shard_map/ppermute | solution.py:346
  99.9 10.0 %collective-permute-start.11 = (f32[512,256]{1,0:T(8,128)S(1)}, f32[512,256]{1,0:T(8,128)S(1)}, u32[]{:S(2)}, u32[]{:S(2)}) collective-permute-start(f32[512,256]{1,0:T(8,128)S(1)} %shard_map.67), channel_id=1, source_target_pairs={{0,2},{32,40},{1,3},{33,41},{2,0},{34,42},{3,1},{35,43},{4,6},{36,... | collective-permute-start | bytes 1572872 | tf_op jit(solution)/shard_map/ppermute | solution.py:373
  101.4 14.0 %collective-permute-start.12 = (f32[512,256]{1,0:T(8,128)S(1)}, f32[512,256]{1,0:T(8,128)S(1)}, u32[]{:S(2)}, u32[]{:S(2)}) collective-permute-start(f32[512,256]{1,0:T(8,128)S(1)} %get-tuple-element.116), channel_id=1, source_target_pairs={{0,1},{32,36},{1,2},{33,37},{2,3},{34,38},{3,0},{35,39},{4,5},{36,... | collective-permute-start | bytes 1572872 | tf_op jit(solution)/shard_map/ppermute | solution.py:373
  101.5 13.9 %collective-permute-start.13 = (f32[512,256]{1,0:T(8,128)S(1)}, f32[512,256]{1,0:T(8,128)S(1)}, u32[]{:S(2)}, u32[]{:S(2)}) collective-permute-start(f32[512,256]{1,0:T(8,128)S(1)} %get-tuple-element.117), channel_id=1, source_target_pairs={{0,3},{32,44},{1,0},{33,45},{2,1},{34,46},{3,2},{35,47},{4,7},{36,... | collective-permute-start | bytes 1572872 | tf_op jit(solution)/shard_map/ppermute | solution.py:373
  138.5 18.4 %collective-permute-start.17 = (f32[768,256]{1,0:T(8,128)S(1)}, f32[768,256]{1,0:T(8,128)S(1)}, u32[]{:S(2)}, u32[]{:S(2)}) collective-permute-start(f32[768,256]{1,0:T(8,128)S(1)} %shard_map.64.refs_0_.own_ref), channel_id=1, source_target_pairs={{47,63},{16,0},{111,127},{80,64}} | collective-permute-start | bytes 2359304 | tf_op jit(solution)/shard_map/ppermute | solution.py:352
  139.2 15.2 %collective-permute-start.16 = (f32[512,256]{1,0:T(8,128)S(1)}, f32[512,256]{1,0:T(8,128)S(1)}, u32[]{:S(2)}, u32[]{:S(2)}) collective-permute-start(f32[512,256]{1,0:T(8,128)S(1)} %bitcast.11), channel_id=1, source_target_pairs={{0,1},{32,36},{1,2},{33,37},{2,3},{34,38},{3,0},{35,39},{4,5},{36,... | collective-permute-start | bytes 1572872 | tf_op jit(solution)/shard_map/ppermute | solution.py:373
  139.3 17.6 %collective-permute-start.14 = (f32[512,256]{1,0:T(8,128)S(1)}, f32[512,256]{1,0:T(8,128)S(1)}, u32[]{:S(2)}, u32[]{:S(2)}) collective-permute-start(f32[512,256]{1,0:T(8,128)S(1)} %bitcast.12), channel_id=1, source_target_pairs={{0,3},{32,44},{1,0},{33,45},{2,1},{34,46},{3,2},{35,47},{4,7},{36,... | collective-permute-start | bytes 1572872 | tf_op jit(solution)/shard_map/ppermute | solution.py:373
  142.0 15.0 %collective-permute-start.15 = (f32[512,256]{1,0:T(8,128)S(1)}, f32[512,256]{1,0:T(8,128)S(1)}, u32[]{:S(2)}, u32[]{:S(2)}) collective-permute-start(f32[512,256]{1,0:T(8,128)S(1)} %bitcast.13), channel_id=1, source_target_pairs={{0,2},{32,40},{1,3},{33,41},{2,0},{34,42},{3,1},{35,43},{4,6},{36,... | collective-permute-start | bytes 1572872 | tf_op jit(solution)/shard_map/ppermute | solution.py:373
  159.3 5.9 %collective-permute-start.18 = (f32[768,256]{1,0:T(8,128)S(1)}, f32[768,256]{1,0:T(8,128)S(1)}, u32[]{:S(2)}, u32[]{:S(2)}) collective-permute-start(f32[768,256]{1,0:T(8,128)S(1)} %shard_map.73), channel_id=1, source_target_pairs={{0,32},{32,0},{1,33},{33,1},{2,34},{34,2},{3,35},{35,3},{4,36},{36... | collective-permute-start | bytes 2359304 | tf_op jit(solution)/shard_map/ppermute | solution.py:346
  165.3 20.7 %collective-permute-start.20 = (f32[768,256]{1,0:T(8,128)S(1)}, f32[768,256]{1,0:T(8,128)S(1)}, u32[]{:S(2)}, u32[]{:S(2)}) collective-permute-start(f32[768,256]{1,0:T(8,128)S(1)} %add.83), channel_id=1, source_target_pairs={{0,64},{64,0},{1,65},{65,1},{2,66},{66,2},{3,67},{67,3},{4,68},{68... | collective-permute-start | bytes 2359304 | tf_op jit(solution)/shard_map/ppermute | solution.py:346
  166.4 19.9 %collective-permute-start.19 = (f32[768,256]{1,0:T(8,128)S(1)}, f32[768,256]{1,0:T(8,128)S(1)}, u32[]{:S(2)}, u32[]{:S(2)}) collective-permute-start(f32[768,256]{1,0:T(8,128)S(1)} %broadcast_select_fusion), channel_id=1, source_target_pairs={{32,1},{33,2},{34,3},{35,4},{36,5},{37,6},{38,7},{39,8},{40,9},{41... | collective-permute-start | bytes 2359304 | tf_op jit(solution)/shard_map/ppermute | solution.py:360
  186.8 2.8 %collective-permute-start.21 = (f32[768,256]{1,0:T(8,128)S(1)}, f32[768,256]{1,0:T(8,128)S(1)}, u32[]{:S(2)}, u32[]{:S(2)}) collective-permute-start(f32[768,256]{1,0:T(8,128)S(1)} %shard_map.75.value_ref), channel_id=1, source_target_pairs={{0,32},{32,0},{1,33},{33,1},{2,34},{34,2},{3,35},{35,3},{4,36},{36... | collective-permute-start | bytes 2359304 | tf_op jit(solution)/shard_map/ppermute | solution.py:346

commit v12 on v11

--- a/solution.py
+++ b/solution.py
@@ -12,6 +12,7 @@
 CELLS = ("yl", "x", "z")
 ALL = DATA + CELLS
 ROWS = 256
+PARTS = 4
 PARAMS = pltpu.CompilerParams(vmem_limit_bytes=24 * 1024 * 1024)
 VMEM = pl.BlockSpec(memory_space=pltpu.VMEM)
 SMEM = pl.BlockSpec(memory_space=pltpu.SMEM)
@@ -203,12 +204,9 @@
     )(*args)
 
 
-def close_kernel(chunks, plane_ref, *refs):
-    w_refs, sense, refs = refs[:chunks], refs[chunks : 3 * chunks], refs[3 * chunks :]
-    start_ref, g_ref, wh_ref, wl_ref = refs
+def home_kernel(chunks, plane_ref, wh_ref, wl_ref, *refs):
+    sense, (start_ref, g_ref) = refs[: 2 * chunks], refs[2 * chunks :]
     blocks = g_ref.shape[0] // ROWS
-    for i in range(chunks):
-        wh_ref[i], wl_ref[i] = split(w_refs[i][...].T)
 
     @pl.loop(0, blocks)
     def _(j):
@@ -220,19 +218,38 @@
         g_ref[block_of(j, ROWS), :] = total.T
 
 
-def close(plane, ws, sense, before, cells):
+def away_kernel(chunks, plane_ref, *refs):
+    w_refs, refs = refs[:chunks], refs[chunks:]
+    inputs, (g_ref, wh_ref, wl_ref) = refs[:-3], refs[-3:]
+    for i in range(chunks):
+        wh_ref[i], wl_ref[i] = split(w_refs[i][...].T)
+    home_kernel(chunks, plane_ref, wh_ref, wl_ref, *inputs, g_ref)
+
+
+def close(theirs, mine, ws, sense, before, cells):
     chunks = len(ws)
     rows, sols = ws[0].shape
-    args = [plane, *ws, *pinned(sense), *pinned([before])]
-    return pl.pallas_call(
-        functools.partial(close_kernel, chunks),
-        in_specs=[SMEM] + [VMEM] * (len(args) - 1),
+    held = [*pinned(sense), *pinned([before])]
+    gradient = jax.ShapeDtypeStruct((cells, sols), F32)
+    half = pltpu.VMEM((chunks, sols, rows), BF16)
+    work = cost(chunks * rows, cells, sols, 0)
+    away, high, low = pl.pallas_call(
+        functools.partial(away_kernel, chunks),
+        in_specs=[SMEM] + [VMEM] * (chunks + len(held)),
+        out_specs=[VMEM] * 3,
+        out_shape=[gradient, half, half],
+        compiler_params=PARAMS,
+        cost_estimate=work,
+    )(theirs, *ws, *held)
+    home = pl.pallas_call(
+        functools.partial(home_kernel, chunks),
+        in_specs=[SMEM] + [VMEM] * (2 + len(held)),
         out_specs=VMEM,
-        out_shape=jax.ShapeDtypeStruct((cells, sols), F32),
-        scratch_shapes=[pltpu.VMEM((chunks, sols, rows), BF16), pltpu.VMEM((chunks, sols, rows), BF16)],
-        compiler_params=PARAMS,
-        cost_estimate=cost(chunks * rows, cells, sols, 0),
-    )(*args)
+        out_shape=gradient,
+        compiler_params=PARAMS,
+        cost_estimate=work,
+    )(mine, *pinned([high, low]), *held)
+    return away, home
 
 
 def weigh_kernel(rank_ref, pieces_ref, observed_ref, copies_ref):
@@ -322,10 +339,15 @@
 
 def place_kernel(plane_ref, value_ref, *refs):
     out_ref, sem = refs[-2:]
-    rows = block_of(plane_ref[0], value_ref.shape[0])
-    copy = pltpu.make_async_copy(value_ref, out_ref.at[rows], sem)
-    copy.start()
-    copy.wait()
+    tall = value_ref.shape[0] // PARTS
+    copies = []
+    for i in range(PARTS):
+        rows = block_of(plane_ref[0] * PARTS + i, tall)
+        source = value_ref.at[pl.ds(i * tall, tall)]
+        copies.append(pltpu.make_async_copy(source, out_ref.at[rows], sem.at[i]))
+        copies[-1].start()
+    for copy in copies:
+        copy.wait()
 
 
 def place(plane, value, before=()):
@@ -335,7 +357,7 @@
         in_specs=[SMEM, VMEM] + [ANY] * len(before),
         out_specs=ANY,
         out_shape=jax.ShapeDtypeStruct((2 * cells, sols), F32),
-        scratch_shapes=[pltpu.SemaphoreType.DMA],
+        scratch_shapes=[pltpu.SemaphoreType.DMA((PARTS,))],
         input_output_aliases={2: 0} if before else {},
         compiler_params=PARAMS,
         cost_estimate=pl.CostEstimate(flops=0, bytes_accessed=8 * cells * sols, transcendentals=0),
@@ -442,8 +464,7 @@
         near = gather_up([w3], s3, [near])
         near, relay = lax.optimization_barrier((near, relay))
         sent = jnp.where(carrier, relay, own)
-        away = close(theirs, [w1, w2], s1 + s2, near, cells)
-        home = close(mine, [w1, w2], s1 + s2, near, cells)
+        away, home = close(theirs, mine, [w1, w2], s1 + s2, near, cells)
         half = home + swap(away, "core")
         half, own, twin, sent = lax.optimization_barrier((half, own, twin, sent))
         beyond = beyond_of(sent, ranks)

time: 191 us -> 190 us (level)
  no operation moved by 1% of the time
where the time goes in v12:
time: 190 us
  waiting for transfers between devices  54.4 us (29%)
  Pallas kernels  50.4 us (27%)
  blocking collectives  45.9 us (24%)
  starting transfers between devices  37.2 us (20%)
    all_to_all x4, blocking collectives, spread(): lax.all_to_all(value, ALL, 0, 0, axis_index_groups=groups, tiled=True)  45.9 us
    ppermute x12, waiting for transfers between devices, ring_of(): return lax.ppermute(value, ALL, pairs)  31.5 us
    ppermute x6, waiting for transfers between devices, swap(): return lax.ppermute(value, axis, [(0, 1), (1, 0)])  22.9 us
    ppermute x12, starting transfers between devices, ring_of(): return lax.ppermute(value, ALL, pairs)  19.2 us
    pallas_call x2, Pallas kernels, smooth_of(): pl.pallas_call(smooth_kernel, in_specs=[VMEM] * 3, out_specs=VMEM, out_sh...  13.1 us
    ppermute x6, starting transfers between devices, swap(): return lax.ppermute(value, axis, [(0, 1), (1, 0)])  12.6 us
    pallas_call x4, Pallas kernels, gather_up(): pl.pallas_call(functools.partial(gather_kernel, chunks, len(before) > 0),...  9.8 us
    pallas_call x4, Pallas kernels, forward(): pl.pallas_call(functools.partial(forward_kernel, len(xs), chunks, len(bef...  6.15 us
  transfers between devices with their start and end apart: 22, of which 10 were waited for; matrix products, arithmetic and copies ran while one was open for 0% of the time, Pallas kernels for 20%

profile of v12, /device:TPU:25, one launch (start us, length us, event | category | flops | bytes accessed | tf_op | source)
XLA Modules:
  0.0 190.0 jit_solution(5115719452467636454)
XLA Ops:
  0.1 5.0 %shard_map.55 = (f32[512,256]{1,0:T(8,128)S(1)}, bf16[512,1536]{1,0:T(8,128)(2,1)S(1)}, bf16[512,1536]{1,0:T(8,128)(2,1)S(1)}, bf16[1536,256]{1,0:T(8,128)(2,1)S(1)}, bf16[1536,256]{1,0:T(8,128)(2,1)S(1)}) custom-call(s32[1]{0:T(128)} %bitcast.5.blocks_ref, f32[2048,1536]{1,0:T(8,128)} %s_ref.5, f32[1536,256]{1,0:T(8,128)} %x_ref.1), custom_call_target="tpu_custom_call" | custom-call | flops 1207959552 | bytes 5242880 | tf_op jit(solution)/shard_map/pallas_call | solution.py:92
  5.1 2.8 %collective-permute-start = (f32[512,256]{1,0:T(8,128)S(1)}, f32[512,256]{1,0:T(8,128)S(1)}, u32[]{:S(2)}, u32[]{:S(2)}) collective-permute-start(f32[512,256]{1,0:T(8,128)S(1)} %get-tuple-element.87), channel_id=1, source_target_pairs={{0,2},{32,40},{1,3},{33,41},{2,0},{34,42},{3,1},{35,43},{4,6},{36,... | collective-permute-start | bytes 1572872 | tf_op jit(solution)/shard_map/ppermute | solution.py:395
  7.9 3.4 %shard_map.56 = (f32[512,256]{1,0:T(8,128)S(1)}, bf16[512,1536]{1,0:T(8,128)(2,1)S(1)}, bf16[512,1536]{1,0:T(8,128)(2,1)S(1)}, f32[512,256]{1,0:T(8,128)S(1)}, b...) custom-call(s32[2]{0:T(128)S(1)} %get-tuple-element.78.blocks_ref, f32[2048,1536]{1,0:T(8,128)S(1)} %copy-done, ...), custom_call_target="tpu_custom_call" | custom-call | flops 2415919104 | bytes 2621440 | tf_op jit(solution)/shard_map/pallas_call | solution.py:129
  11.7 2.4 %collective-permute-start.2 = (f32[512,256]{1,0:T(8,128)S(1)}, f32[512,256]{1,0:T(8,128)S(1)}, u32[]{:S(2)}, u32[]{:S(2)}) collective-permute-start(f32[512,256]{1,0:T(8,128)S(1)} %get-tuple-element.88), channel_id=1, source_target_pairs={{0,3},{32,44},{1,0},{33,45},{2,1},{34,46},{3,2},{35,47},{4,7},{36,... | collective-permute-start | bytes 1572872 | tf_op jit(solution)/shard_map/ppermute | solution.py:395
  16.0 5.0 %collective-permute-done.1 = f32[512,256]{1,0:T(8,128)S(1)} collective-permute-done((f32[512,256]{1,0:T(8,128)S(1)}, f32[512,256]{1,0:T(8,128)S(1)}, u32[]{:S(2)}, u32[]{:S(2)}) %collective-permute-start.1) | collective-permute-done | bytes 524320 | tf_op jit(solution)/shard_map/ppermute | solution.py:395
  21.0 13.0 %all_to_all.36.pieces_ref = f32[8,64,256]{2,1,0:T(8,128)S(1)} all-to-all(f32[8,64,256]{2,1,0:T(8,128)S(1)} %bitcast.19), channel_id=1, replica_groups={{0,4,8,12,16,20,24,28},{1,5,9,13,17,21,25,29},{2,6,10,14,18,22,26,30},{..., dimensions={0} | all-to-all | bytes 1048576 | tf_op jit(solution)/shard_map/all_to_all | solution.py:405
  34.1 10.0 %all_to_all.37 = f32[8,64,256]{2,1,0:T(8,128)S(1)} all-to-all(f32[8,64,256]{2,1,0:T(8,128)S(1)} %shard_map.58), channel_id=1, replica_groups={{0,4,8,12,16,20,24,28},{1,5,9,13,17,21,25,29},{2,6,10,14,18,22,26,30},{..., dimensions={0} | all-to-all | bytes 1048576 | tf_op jit(solution)/shard_map/all_to_all | solution.py:405
  44.8 3.9 %collective-permute-start.5 = (f32[512,256]{1,0:T(8,128)S(1)}, f32[512,256]{1,0:T(8,128)S(1)}, u32[]{:S(2)}, u32[]{:S(2)}) collective-permute-start(f32[512,256]{1,0:T(8,128)S(1)} %bitcast.15), channel_id=1, source_target_pairs={{0,1},{32,36},{1,2},{33,37},{2,3},{34,38},{3,0},{35,39},{4,5},{36,... | collective-permute-start | bytes 1572872 | tf_op jit(solution)/shard_map/ppermute | solution.py:395
  48.7 2.8 %collective-permute-start.3 = (f32[512,256]{1,0:T(8,128)S(1)}, f32[512,256]{1,0:T(8,128)S(1)}, u32[]{:S(2)}, u32[]{:S(2)}) collective-permute-start(f32[512,256]{1,0:T(8,128)S(1)} %bitcast.16), channel_id=1, source_target_pairs={{0,3},{32,44},{1,0},{33,45},{2,1},{34,46},{3,2},{35,47},{4,7},{36,... | collective-permute-start | bytes 1572872 | tf_op jit(solution)/shard_map/ppermute | solution.py:395
  52.8 2.4 %shard_map.59.refs_3_ = f32[256,1536]{1,0:T(8,128)S(1)} custom-call(f32[512,256]{1,0:T(8,128)S(1)} %bitcast.18, bf16[512,1536]{1,0:T(8,128)(2,1)S(1)} %get-tuple-element.108.refs_1_.refs_2_, bf16[512,1536]{1,0:T(8,128)(2,1)S(1)} %get-tuple-element.109.refs_2_.refs_3_), custom_call_target="tpu_custom_call" | custom-call | flops 1207959552 | bytes 2097152 | tf_op jit(solution)/shard_map/pallas_call | solution.py:196
  55.3 3.0 %collective-permute-done.5.refs_0_ = f32[512,256]{1,0:T(8,128)S(1)} collective-permute-done((f32[512,256]{1,0:T(8,128)S(1)}, f32[512,256]{1,0:T(8,128)S(1)}, u32[]{:S(2)}, u32[]{:S(2)}) %collective-permute-start.5) | collective-permute-done | bytes 524320 | tf_op jit(solution)/shard_map/ppermute | solution.py:395
  58.3 2.5 %shard_map.60.refs_6_.refs_4_ = f32[256,1536]{1,0:T(8,128)S(1)} custom-call(f32[512,256]{1,0:T(8,128)S(1)} %collective-permute-done.5.refs_0_, bf16[512,1536]{1,0:T(8,128)(2,1)S(1)} %get-tuple-element.106.refs_1_.refs_5_.refs_3_, bf16[512,1536]{1,0:T(8,128)(2,1)S(1)} %get-tuple-element.107.refs_2_.refs_6_.refs_4_, f32[256,1536]{1,0:T(8,128)S(1)} %shard_map.59.refs_3_), custom_call_target="tpu_custom_call" | custom-call | flops 1207959552 | bytes 2097152 | tf_op jit(solution)/shard_map/pallas_call | solution.py:196
  60.7 2.5 %collective-permute-done.3.refs_0_ = f32[512,256]{1,0:T(8,128)S(1)} collective-permute-done((f32[512,256]{1,0:T(8,128)S(1)}, f32[512,256]{1,0:T(8,128)S(1)}, u32[]{:S(2)}, u32[]{:S(2)}) %collective-permute-start.3) | collective-permute-done | bytes 524320 | tf_op jit(solution)/shard_map/ppermute | solution.py:395
  65.1 2.3 %shard_map.61 = (f32[768,256]{1,0:T(8,128)S(1)}, bf16[2,256,512]{2,1,0:T(8,128)(2,1)S(1)}, bf16[2,256,512]{2,1,0:T(8,128)(2,1)S(1)}) custom-call(s32[1]{0:T(128)} %bitcast.2.plane_ref.planes_ref, f32[512,256]{1,0:T(8,128)S(1)} %collective-permute-done.3.refs_0_, f32[512,256]{1,0:T(8,128)S(1)} %collective-permute-done.4.refs_1_, ...), custom_call_target="tpu_custom_call" | custom-call | flops 1207959552 | bytes 1835008 | tf_op jit(solution)/shard_map/pallas_call | solution.py:236
  67.3 4.8 %collective-permute-start.7 = (f32[768,256]{1,0:T(8,128)S(1)}, f32[768,256]{1,0:T(8,128)S(1)}, u32[]{:S(2)}, u32[]{:S(2)}) collective-permute-start(f32[768,256]{1,0:T(8,128)S(1)} %get-tuple-element.114), channel_id=1, source_target_pairs={{0,32},{32,0},{1,33},{33,1},{2,34},{34,2},{3,35},{35,3},{4,36},{36... | collective-permute-start | bytes 2359304 | tf_op jit(solution)/shard_map/ppermute | solution.py:368
  75.4 2.1 %collective-permute-start.8 = (f32[768,256]{1,0:T(8,128)S(1)}, f32[768,256]{1,0:T(8,128)S(1)}, u32[]{:S(2)}, u32[]{:S(2)}) collective-permute-start(f32[768,256]{1,0:T(8,128)S(1)} %broadcast_select_fusion.1), channel_id=1, source_target_pairs={{32,1},{33,2},{34,3},{35,4},{36,5},{37,6},{38,7},{39,8},{40,9},{41... | collective-permute-start | bytes 2359304 | tf_op jit(solution)/shard_map/ppermute | solution.py:382
  77.5 6.5 %shard_map.63.inner_ref = f32[768,256]{1,0:T(8,128)S(1)} custom-call(f32[8,768]{1,0:T(8,128)S(1)} %maximum_maximum_fusion.table_ref, f32[768,256]{1,0:T(8,128)S(1)} %get-tuple-element.118.own_ref, f32[768,256]{1,0:T(8,128)S(1)} %get-tuple-element.120.twin_ref), custom_call_target="tpu_custom_call" | custom-call | flops 3623878656 | bytes 3145728 | tf_op jit(solution)/shard_map/pallas_call | solution.py:305
  84.0 10.8 %collective-permute-done.9 = f32[768,256]{1,0:T(8,128)S(1)} collective-permute-done((f32[768,256]{1,0:T(8,128)S(1)}, f32[768,256]{1,0:T(8,128)S(1)}, u32[]{:S(2)}, u32[]{:S(2)}) %collective-permute-start.9) | collective-permute-done | bytes 786464 | tf_op jit(solution)/shard_map/ppermute | solution.py:368
  96.7 2.0 %shard_map.66 = (f32[512,256]{1,0:T(8,128)S(1)}, f32[512,256]{1,0:T(8,128)S(1)}, f32[512,256]{1,0:T(8,128)S(1)}) custom-call(s32[1]{0:T(128)} %bitcast.1.plane_ref.planes_ref, f32[768,256]{1,0:T(8,128)S(1)} %shard_map.64.refs_0_.own_ref, bf16[512,1536]{1,0:T(8,128)(2,1)S(1)} %get-tuple-element.104.refs_4_.refs_2_.refs_1_, ...), custom_call_target="tpu_custom_call" | custom-call | flops 1811939328 | bytes 2359296 | tf_op jit(solution)/shard_map/pallas_call | solution.py:159
  101.1 2.7 %collective-permute-start.13 = (f32[512,256]{1,0:T(8,128)S(1)}, f32[512,256]{1,0:T(8,128)S(1)}, u32[]{:S(2)}, u32[]{:S(2)}) collective-permute-start(f32[512,256]{1,0:T(8,128)S(1)} %get-tuple-element.126), channel_id=1, source_target_pairs={{0,3},{32,44},{1,0},{33,45},{2,1},{34,46},{3,2},{35,47},{4,7},{36,... | collective-permute-start | bytes 1572872 | tf_op jit(solution)/shard_map/ppermute | solution.py:395
  105.7 3.7 %collective-permute-done.11 = f32[512,256]{1,0:T(8,128)S(1)} collective-permute-done((f32[512,256]{1,0:T(8,128)S(1)}, f32[512,256]{1,0:T(8,128)S(1)}, u32[]{:S(2)}, u32[]{:S(2)}) %collective-permute-start.11) | collective-permute-done | bytes 524320 | tf_op jit(solution)/shard_map/ppermute | solution.py:395
  109.6 5.5 %collective-permute-done.12 = f32[512,256]{1,0:T(8,128)S(1)} collective-permute-done((f32[512,256]{1,0:T(8,128)S(1)}, f32[512,256]{1,0:T(8,128)S(1)}, u32[]{:S(2)}, u32[]{:S(2)}) %collective-permute-start.12) | collective-permute-done | bytes 524320 | tf_op jit(solution)/shard_map/ppermute | solution.py:395
  115.2 10.7 %all_to_all.38.pieces_ref = f32[8,64,256]{2,1,0:T(8,128)S(1)} all-to-all(f32[8,64,256]{2,1,0:T(8,128)S(1)} %bitcast.20), channel_id=1, replica_groups={{0,4,8,12,16,20,24,28},{1,5,9,13,17,21,25,29},{2,6,10,14,18,22,26,30},{..., dimensions={0} | all-to-all | bytes 1048576 | tf_op jit(solution)/shard_map/all_to_all | solution.py:405
  126.0 12.2 %all_to_all.39 = f32[8,64,256]{2,1,0:T(8,128)S(1)} all-to-all(f32[8,64,256]{2,1,0:T(8,128)S(1)} %shard_map.69), channel_id=1, replica_groups={{0,4,8,12,16,20,24,28},{1,5,9,13,17,21,25,29},{2,6,10,14,18,22,26,30},{..., dimensions={0} | all-to-all | bytes 1048576 | tf_op jit(solution)/shard_map/all_to_all | solution.py:405
  139.0 2.7 %collective-permute-start.14 = (f32[512,256]{1,0:T(8,128)S(1)}, f32[512,256]{1,0:T(8,128)S(1)}, u32[]{:S(2)}, u32[]{:S(2)}) collective-permute-start(f32[512,256]{1,0:T(8,128)S(1)} %bitcast.12), channel_id=1, source_target_pairs={{0,3},{32,44},{1,0},{33,45},{2,1},{34,46},{3,2},{35,47},{4,7},{36,... | collective-permute-start | bytes 1572872 | tf_op jit(solution)/shard_map/ppermute | solution.py:395
  141.6 2.4 %shard_map.70.refs_3_ = f32[256,1536]{1,0:T(8,128)S(1)} custom-call(f32[512,256]{1,0:T(8,128)S(1)} %bitcast.14, bf16[512,1536]{1,0:T(8,128)(2,1)S(1)} %get-tuple-element.108.refs_1_.refs_2_, bf16[512,1536]{1,0:T(8,128)(2,1)S(1)} %get-tuple-element.109.refs_2_.refs_3_), custom_call_target="tpu_custom_call" | custom-call | flops 1207959552 | bytes 2097152 | tf_op jit(solution)/shard_map/pallas_call | solution.py:196
  144.1 10.0 %collective-permute-done.16.refs_0_ = f32[512,256]{1,0:T(8,128)S(1)} collective-permute-done((f32[512,256]{1,0:T(8,128)S(1)}, f32[512,256]{1,0:T(8,128)S(1)}, u32[]{:S(2)}, u32[]{:S(2)}) %collective-permute-start.16) | collective-permute-done | bytes 524320 | tf_op jit(solution)/shard_map/ppermute | solution.py:395
  154.1 2.5 %shard_map.71.refs_6_.refs_4_ = f32[256,1536]{1,0:T(8,128)S(1)} custom-call(f32[512,256]{1,0:T(8,128)S(1)} %collective-permute-done.16.refs_0_, bf16[512,1536]{1,0:T(8,128)(2,1)S(1)} %get-tuple-element.106.refs_1_.refs_5_.refs_3_, bf16[512,1536]{1,0:T(8,128)(2,1)S(1)} %get-tuple-element.107.refs_2_.refs_6_.refs_4_, f32[256,1536]{1,0:T(8,128)S(1)} %shard_map.70.refs_3_), custom_call_target="tpu_custom_call" | custom-call | flops 1207959552 | bytes 2097152 | tf_op jit(solution)/shard_map/pallas_call | solution.py:196
  156.6 2.3 %shard_map.72 = (f32[768,256]{1,0:T(8,128)S(1)}, bf16[2,256,512]{2,1,0:T(8,128)(2,1)S(1)}, bf16[2,256,512]{2,1,0:T(8,128)(2,1)S(1)}) custom-call(s32[1]{0:T(128)} %bitcast.2.plane_ref.planes_ref, f32[512,256]{1,0:T(8,128)S(1)} %collective-permute-done.14.refs_0_, f32[512,256]{1,0:T(8,128)S(1)} %collective-permute-done.15.refs_1_, ...), custom_call_target="tpu_custom_call" | custom-call | flops 1207959552 | bytes 1835008 | tf_op jit(solution)/shard_map/pallas_call | solution.py:236
  158.9 3.3 %collective-permute-start.18 = (f32[768,256]{1,0:T(8,128)S(1)}, f32[768,256]{1,0:T(8,128)S(1)}, u32[]{:S(2)}, u32[]{:S(2)}) collective-permute-start(f32[768,256]{1,0:T(8,128)S(1)} %get-tuple-element.138), channel_id=1, source_target_pairs={{0,32},{32,0},{1,33},{33,1},{2,34},{34,2},{3,35},{35,3},{4,36},{36... | collective-permute-start | bytes 2359304 | tf_op jit(solution)/shard_map/ppermute | solution.py:368
  167.6 6.5 %shard_map.74.inner_ref = f32[768,256]{1,0:T(8,128)S(1)} custom-call(f32[8,768]{1,0:T(8,128)S(1)} %maximum_maximum_fusion.table_ref, f32[768,256]{1,0:T(8,128)S(1)} %shard_map.64.refs_0_.own_ref, f32[768,256]{1,0:T(8,128)S(1)} %collective-permute-done.10.refs_1_.refs_0_.twin_ref), custom_call_target="tpu_custom_call" | custom-call | flops 3623878656 | bytes 3145728 | tf_op jit(solution)/shard_map/pallas_call | solution.py:305
  174.1 11.0 %collective-permute-done.20 = f32[768,256]{1,0:T(8,128)S(1)} collective-permute-done((f32[768,256]{1,0:T(8,128)S(1)}, f32[768,256]{1,0:T(8,128)S(1)}, u32[]{:S(2)}, u32[]{:S(2)}) %collective-permute-start.20) | collective-permute-done | bytes 786464 | tf_op jit(solution)/shard_map/ppermute | solution.py:368
  (67 shorter events, 26.6 us)
Async XLA Ops:
  0.1 7.9 %copy-start = (f32[2048,1536]{1,0:T(8,128)S(1)}, f32[2048,1536]{1,0:T(8,128)}, u32[]{:S(2)}) copy-start(f32[2048,1536]{1,0:T(8,128)} %s_ref.5) | copy-start | bytes 37748740
  5.1 10.8 %collective-permute-start = (f32[512,256]{1,0:T(8,128)S(1)}, f32[512,256]{1,0:T(8,128)S(1)}, u32[]{:S(2)}, u32[]{:S(2)}) collective-permute-start(f32[512,256]{1,0:T(8,128)S(1)} %get-tuple-element.87), channel_id=1, source_target_pairs={{0,2},{32,40},{1,3},{33,41},{2,0},{34,42},{3,1},{35,43},{4,6},{36,... | collective-permute-start | bytes 1572872 | tf_op jit(solution)/shard_map/ppermute | solution.py:395
  11.3 9.6 %collective-permute-start.1 = (f32[512,256]{1,0:T(8,128)S(1)}, f32[512,256]{1,0:T(8,128)S(1)}, u32[]{:S(2)}, u32[]{:S(2)}) collective-permute-start(f32[512,256]{1,0:T(8,128)S(1)} %get-tuple-element.82), channel_id=1, source_target_pairs={{0,1},{32,36},{1,2},{33,37},{2,3},{34,38},{3,0},{35,39},{4,5},{36,... | collective-permute-start | bytes 1572872 | tf_op jit(solution)/shard_map/ppermute | solution.py:395
  11.7 3.8 %copy-start.4 = (s32[1536]{0:T(1024)S(1)}, s32[1536]{0:T(1024)}, u32[]{:S(2)}) copy-start(s32[1536]{0:T(1024)} %param.9) | copy-start | bytes 18436
  11.7 3.9 %copy-start.3 = (s32[4,768]{1,0:T(4,128)S(1)}, s32[4,768]{1,0:T(4,128)}, u32[]{:S(2)}) copy-start(s32[4,768]{1,0:T(4,128)} %param.8) | copy-start | bytes 36868
  11.7 4.0 %copy-start.2 = (f32[1536,256]{1,0:T(8,128)S(1)}, f32[1536,256]{1,0:T(8,128)}, u32[]{:S(2)}) copy-start(f32[1536,256]{1,0:T(8,128)} %x_ref.1) | copy-start | bytes 4718596
  11.7 9.2 %collective-permute-start.2 = (f32[512,256]{1,0:T(8,128)S(1)}, f32[512,256]{1,0:T(8,128)S(1)}, u32[]{:S(2)}, u32[]{:S(2)}) collective-permute-start(f32[512,256]{1,0:T(8,128)S(1)} %get-tuple-element.88), channel_id=1, source_target_pairs={{0,3},{32,44},{1,0},{33,45},{2,1},{34,46},{3,2},{35,47},{4,7},{36,... | collective-permute-start | bytes 1572872 | tf_op jit(solution)/shard_map/ppermute | solution.py:395
  16.0 18.0 %copy-start.1 = (f32[2048,256]{1,0:T(8,128)S(1)}, f32[2048,256]{1,0:T(8,128)}, u32[]{:S(2)}) copy-start(f32[2048,256]{1,0:T(8,128)} %observed_ref.3) | copy-start | bytes 6291460
  44.1 16.7 %collective-permute-start.6 = (f32[768,256]{1,0:T(8,128)S(1)}, f32[768,256]{1,0:T(8,128)S(1)}, u32[]{:S(2)}, u32[]{:S(2)}) collective-permute-start(f32[768,256]{1,0:T(8,128)S(1)} %get-tuple-element.118.own_ref), channel_id=1, source_target_pairs={{47,63},{16,0},{111,127},{80,64}} | collective-permute-start | bytes 2359304 | tf_op jit(solution)/shard_map/ppermute | solution.py:374
  44.8 13.5 %collective-permute-start.5 = (f32[512,256]{1,0:T(8,128)S(1)}, f32[512,256]{1,0:T(8,128)S(1)}, u32[]{:S(2)}, u32[]{:S(2)}) collective-permute-start(f32[512,256]{1,0:T(8,128)S(1)} %bitcast.15), channel_id=1, source_target_pairs={{0,1},{32,36},{1,2},{33,37},{2,3},{34,38},{3,0},{35,39},{4,5},{36,... | collective-permute-start | bytes 1572872 | tf_op jit(solution)/shard_map/ppermute | solution.py:395
  48.7 14.5 %collective-permute-start.3 = (f32[512,256]{1,0:T(8,128)S(1)}, f32[512,256]{1,0:T(8,128)S(1)}, u32[]{:S(2)}, u32[]{:S(2)}) collective-permute-start(f32[512,256]{1,0:T(8,128)S(1)} %bitcast.16), channel_id=1, source_target_pairs={{0,3},{32,44},{1,0},{33,45},{2,1},{34,46},{3,2},{35,47},{4,7},{36,... | collective-permute-start | bytes 1572872 | tf_op jit(solution)/shard_map/ppermute | solution.py:395
  51.5 13.6 %collective-permute-start.4 = (f32[512,256]{1,0:T(8,128)S(1)}, f32[512,256]{1,0:T(8,128)S(1)}, u32[]{:S(2)}, u32[]{:S(2)}) collective-permute-start(f32[512,256]{1,0:T(8,128)S(1)} %bitcast.17), channel_id=1, source_target_pairs={{0,2},{32,40},{1,3},{33,41},{2,0},{34,42},{3,1},{35,43},{4,6},{36,... | collective-permute-start | bytes 1572872 | tf_op jit(solution)/shard_map/ppermute | solution.py:395
  67.3 6.9 %collective-permute-start.7 = (f32[768,256]{1,0:T(8,128)S(1)}, f32[768,256]{1,0:T(8,128)S(1)}, u32[]{:S(2)}, u32[]{:S(2)}) collective-permute-start(f32[768,256]{1,0:T(8,128)S(1)} %get-tuple-element.114), channel_id=1, source_target_pairs={{0,32},{32,0},{1,33},{33,1},{2,34},{34,2},{3,35},{35,3},{4,36},{36... | collective-permute-start | bytes 2359304 | tf_op jit(solution)/shard_map/ppermute | solution.py:368
  74.3 20.5 %collective-permute-start.9 = (f32[768,256]{1,0:T(8,128)S(1)}, f32[768,256]{1,0:T(8,128)S(1)}, u32[]{:S(2)}, u32[]{:S(2)}) collective-permute-start(f32[768,256]{1,0:T(8,128)S(1)} %add.78), channel_id=1, source_target_pairs={{0,64},{64,0},{1,65},{65,1},{2,66},{66,2},{3,67},{67,3},{4,68},{68... | collective-permute-start | bytes 2359304 | tf_op jit(solution)/shard_map/ppermute | solution.py:368
  75.4 19.6 %collective-permute-start.8 = (f32[768,256]{1,0:T(8,128)S(1)}, f32[768,256]{1,0:T(8,128)S(1)}, u32[]{:S(2)}, u32[]{:S(2)}) collective-permute-start(f32[768,256]{1,0:T(8,128)S(1)} %broadcast_select_fusion.1), channel_id=1, source_target_pairs={{32,1},{33,2},{34,3},{35,4},{36,5},{37,6},{38,7},{39,8},{40,9},{41... | collective-permute-start | bytes 2359304 | tf_op jit(solution)/shard_map/ppermute | solution.py:382
  95.6 3.1 %collective-permute-start.10 = (f32[768,256]{1,0:T(8,128)S(1)}, f32[768,256]{1,0:T(8,128)S(1)}, u32[]{:S(2)}, u32[]{:S(2)}) collective-permute-start(f32[768,256]{1,0:T(8,128)S(1)} %shard_map.64.refs_0_.own_ref), channel_id=1, source_target_pairs={{0,32},{32,0},{1,33},{33,1},{2,34},{34,2},{3,35},{35,3},{4,36},{36... | collective-permute-start | bytes 2359304 | tf_op jit(solution)/shard_map/ppermute | solution.py:368
  99.5 10.0 %collective-permute-start.11 = (f32[512,256]{1,0:T(8,128)S(1)}, f32[512,256]{1,0:T(8,128)S(1)}, u32[]{:S(2)}, u32[]{:S(2)}) collective-permute-start(f32[512,256]{1,0:T(8,128)S(1)} %shard_map.67), channel_id=1, source_target_pairs={{0,2},{32,40},{1,3},{33,41},{2,0},{34,42},{3,1},{35,43},{4,6},{36,... | collective-permute-start | bytes 1572872 | tf_op jit(solution)/shard_map/ppermute | solution.py:395
  101.0 14.0 %collective-permute-start.12 = (f32[512,256]{1,0:T(8,128)S(1)}, f32[512,256]{1,0:T(8,128)S(1)}, u32[]{:S(2)}, u32[]{:S(2)}) collective-permute-start(f32[512,256]{1,0:T(8,128)S(1)} %get-tuple-element.125), channel_id=1, source_target_pairs={{0,1},{32,36},{1,2},{33,37},{2,3},{34,38},{3,0},{35,39},{4,5},{36,... | collective-permute-start | bytes 1572872 | tf_op jit(solution)/shard_map/ppermute | solution.py:395
  101.1 14.0 %collective-permute-start.13 = (f32[512,256]{1,0:T(8,128)S(1)}, f32[512,256]{1,0:T(8,128)S(1)}, u32[]{:S(2)}, u32[]{:S(2)}) collective-permute-start(f32[512,256]{1,0:T(8,128)S(1)} %get-tuple-element.126), channel_id=1, source_target_pairs={{0,3},{32,44},{1,0},{33,45},{2,1},{34,46},{3,2},{35,47},{4,7},{36,... | collective-permute-start | bytes 1572872 | tf_op jit(solution)/shard_map/ppermute | solution.py:395
  138.2 18.4 %collective-permute-start.17 = (f32[768,256]{1,0:T(8,128)S(1)}, f32[768,256]{1,0:T(8,128)S(1)}, u32[]{:S(2)}, u32[]{:S(2)}) collective-permute-start(f32[768,256]{1,0:T(8,128)S(1)} %shard_map.64.refs_0_.own_ref), channel_id=1, source_target_pairs={{47,63},{16,0},{111,127},{80,64}} | collective-permute-start | bytes 2359304 | tf_op jit(solution)/shard_map/ppermute | solution.py:374
  138.9 15.2 %collective-permute-start.16 = (f32[512,256]{1,0:T(8,128)S(1)}, f32[512,256]{1,0:T(8,128)S(1)}, u32[]{:S(2)}, u32[]{:S(2)}) collective-permute-start(f32[512,256]{1,0:T(8,128)S(1)} %bitcast.11), channel_id=1, source_target_pairs={{0,1},{32,36},{1,2},{33,37},{2,3},{34,38},{3,0},{35,39},{4,5},{36,... | collective-permute-start | bytes 1572872 | tf_op jit(solution)/shard_map/ppermute | solution.py:395
  139.0 17.6 %collective-permute-start.14 = (f32[512,256]{1,0:T(8,128)S(1)}, f32[512,256]{1,0:T(8,128)S(1)}, u32[]{:S(2)}, u32[]{:S(2)}) collective-permute-start(f32[512,256]{1,0:T(8,128)S(1)} %bitcast.12), channel_id=1, source_target_pairs={{0,3},{32,44},{1,0},{33,45},{2,1},{34,46},{3,2},{35,47},{4,7},{36,... | collective-permute-start | bytes 1572872 | tf_op jit(solution)/shard_map/ppermute | solution.py:395
  141.6 15.0 %collective-permute-start.15 = (f32[512,256]{1,0:T(8,128)S(1)}, f32[512,256]{1,0:T(8,128)S(1)}, u32[]{:S(2)}, u32[]{:S(2)}) collective-permute-start(f32[512,256]{1,0:T(8,128)S(1)} %bitcast.13), channel_id=1, source_target_pairs={{0,2},{32,40},{1,3},{33,41},{2,0},{34,42},{3,1},{35,43},{4,6},{36,... | collective-permute-start | bytes 1572872 | tf_op jit(solution)/shard_map/ppermute | solution.py:395
  158.9 5.4 %collective-permute-start.18 = (f32[768,256]{1,0:T(8,128)S(1)}, f32[768,256]{1,0:T(8,128)S(1)}, u32[]{:S(2)}, u32[]{:S(2)}) collective-permute-start(f32[768,256]{1,0:T(8,128)S(1)} %get-tuple-element.138), channel_id=1, source_target_pairs={{0,32},{32,0},{1,33},{33,1},{2,34},{34,2},{3,35},{35,3},{4,36},{36... | collective-permute-start | bytes 2359304 | tf_op jit(solution)/shard_map/ppermute | solution.py:368
  164.4 20.7 %collective-permute-start.20 = (f32[768,256]{1,0:T(8,128)S(1)}, f32[768,256]{1,0:T(8,128)S(1)}, u32[]{:S(2)}, u32[]{:S(2)}) collective-permute-start(f32[768,256]{1,0:T(8,128)S(1)} %add.83), channel_id=1, source_target_pairs={{0,64},{64,0},{1,65},{65,1},{2,66},{66,2},{3,67},{67,3},{4,68},{68... | collective-permute-start | bytes 2359304 | tf_op jit(solution)/shard_map/ppermute | solution.py:368
  165.7 19.6 %collective-permute-start.19 = (f32[768,256]{1,0:T(8,128)S(1)}, f32[768,256]{1,0:T(8,128)S(1)}, u32[]{:S(2)}, u32[]{:S(2)}) collective-permute-start(f32[768,256]{1,0:T(8,128)S(1)} %broadcast_select_fusion), channel_id=1, source_target_pairs={{32,1},{33,2},{34,3},{35,4},{36,5},{37,6},{38,7},{39,8},{40,9},{41... | collective-permute-start | bytes 2359304 | tf_op jit(solution)/shard_map/ppermute | solution.py:382
  185.9 3.0 %collective-permute-start.21 = (f32[768,256]{1,0:T(8,128)S(1)}, f32[768,256]{1,0:T(8,128)S(1)}, u32[]{:S(2)}, u32[]{:S(2)}) collective-permute-start(f32[768,256]{1,0:T(8,128)S(1)} %shard_map.75.value_ref), channel_id=1, source_target_pairs={{0,32},{32,0},{1,33},{33,1},{2,34},{34,2},{3,35},{35,3},{4,36},{36... | collective-permute-start | bytes 2359304 | tf_op jit(solution)/shard_map/ppermute | solution.py:368

commit v13 on v12

--- a/solution.py
+++ b/solution.py
@@ -431,10 +431,12 @@
             p2, h2, l2, *halves = first_forward(block[2], sensitivity, models, rows)
             s2 = [h2, l2]
             r2 = ring_of(p2, 2)
-            p1, h1, l1, p3, h3, l3 = rest_forward(sides, sensitivity, halves, rows)
-            s1, s3 = [h1, l1], [h3, l3]
-            r1, r3 = ring_of(p1, 1), ring_of(p3, 3)
+            p1, *s1 = rest_forward(block[1], sensitivity, halves, rows)
+            r1 = ring_of(p1, 1)
             p1, halves = lax.optimization_barrier((p1, halves))
+            p3, *s3 = rest_forward(block[3], sensitivity, halves, rows)
+            r3 = ring_of(p3, 3)
+            p3, halves = lax.optimization_barrier((p3, halves))
             p0, *s0 = rest_forward(block[0], sensitivity, halves, rows)
             p0, start, numbers, mask = lax.optimization_barrier((p0, models, neighbour_map, edge_mask))
             own = jnp.where(low_core, start[:cells], start[cells:])
@@ -453,7 +455,8 @@
             r1, r3 = ring_of(p1, 1), ring_of(p3, 3)
             (p0,) = forward(both, [own, twin], s0)
         p0, r1, r3 = lax.optimization_barrier((p0 + r2, r1, r3))
-        p0, own, twin, table = lax.optimization_barrier((p0 + (r1 + r3), own, twin, table))
+        p0, r3 = lax.optimization_barrier((p0 + r1, r3))
+        p0, own, twin, table = lax.optimization_barrier((p0 + r3, own, twin, table))
         pieces = spread(p0)
         copies = weigh(rank, pieces.reshape(subs, rows // subs, -1), observed)
         w0 = spread(copies.reshape(rows, -1))

time: 190 us -> 191 us (level)
    pallas_call x2 -> x3, Pallas kernels: 4.84 us -> 4.35 us  [rest_forward(): pl.pallas_call(rest_kernel, in_specs=[SMEM] + [VMEM] * 3, out_specs=[VMEM...]
  transfers between devices with their start and end apart: 22 -> 22, of which waited for: 10 -> 10; matrix products, arithmetic and copies ran while one was open for 0% -> 1% of each run, Pallas kernels for 20% -> 20%
where the time goes in v13:
time: 191 us; the launch traced here: 190 us
  waiting for transfers between devices  54.5 us (29%)
  Pallas kernels  49.9 us (26%)
  blocking collectives  46.1 us (24%)
  starting transfers between devices  37.4 us (20%)
    all_to_all x4, blocking collectives, spread(): lax.all_to_all(value, ALL, 0, 0, axis_index_groups=groups, tiled=True)  46.1 us
    ppermute x12, waiting for transfers between devices, ring_of(): return lax.ppermute(value, ALL, pairs)  31.6 us
    ppermute x6, waiting for transfers between devices, swap(): return lax.ppermute(value, axis, [(0, 1), (1, 0)])  22.9 us
    ppermute x12, starting transfers between devices, ring_of(): return lax.ppermute(value, ALL, pairs)  19.6 us
    pallas_call x2, Pallas kernels, smooth_of(): pl.pallas_call(smooth_kernel, in_specs=[VMEM] * 3, out_specs=VMEM, out_sh...  13.1 us
    ppermute x6, starting transfers between devices, swap(): return lax.ppermute(value, axis, [(0, 1), (1, 0)])  12.4 us
    pallas_call x4, Pallas kernels, gather_up(): pl.pallas_call(functools.partial(gather_kernel, chunks, len(before) > 0),...  9.8 us
    pallas_call x4, Pallas kernels, forward(): pl.pallas_call(functools.partial(forward_kernel, len(xs), chunks, len(bef...  6.16 us
  transfers between devices with their start and end apart: 22, of which 10 were waited for; matrix products, arithmetic and copies ran while one was open for 1% of the time, Pallas kernels for 20%

profile of v13, /device:TPU:25, one launch (start us, length us, event | category | flops | bytes accessed | tf_op | source)
XLA Modules:
  0.0 190.2 jit_solution(16846049124121186216)
XLA Ops:
  0.1 5.0 %shard_map.55 = (f32[512,256]{1,0:T(8,128)S(1)}, bf16[512,1536]{1,0:T(8,128)(2,1)S(1)}, bf16[512,1536]{1,0:T(8,128)(2,1)S(1)}, bf16[1536,256]{1,0:T(8,128)(2,1)S(1)}, bf16[1536,256]{1,0:T(8,128)(2,1)S(1)}) custom-call(s32[1]{0:T(128)} %bitcast.5.blocks_ref, f32[2048,1536]{1,0:T(8,128)} %s_ref.7, f32[1536,256]{1,0:T(8,128)} %x_ref.1), custom_call_target="tpu_custom_call" | custom-call | flops 1207959552 | bytes 5242880 | tf_op jit(solution)/shard_map/pallas_call | solution.py:92
  5.1 2.8 %collective-permute-start = (f32[512,256]{1,0:T(8,128)S(1)}, f32[512,256]{1,0:T(8,128)S(1)}, u32[]{:S(2)}, u32[]{:S(2)}) collective-permute-start(f32[512,256]{1,0:T(8,128)S(1)} %get-tuple-element.98), channel_id=1, source_target_pairs={{0,2},{32,40},{1,3},{33,41},{2,0},{34,42},{3,1},{35,43},{4,6},{36,... | collective-permute-start | bytes 1572872 | tf_op jit(solution)/shard_map/ppermute | solution.py:395
  11.3 2.4 %collective-permute-start.2 = (f32[512,256]{1,0:T(8,128)S(1)}, f32[512,256]{1,0:T(8,128)S(1)}, u32[]{:S(2)}, u32[]{:S(2)}) collective-permute-start(f32[512,256]{1,0:T(8,128)S(1)} %get-tuple-element.93), channel_id=1, source_target_pairs={{0,3},{32,44},{1,0},{33,45},{2,1},{34,46},{3,2},{35,47},{4,7},{36,... | collective-permute-start | bytes 1572872 | tf_op jit(solution)/shard_map/ppermute | solution.py:395
  15.6 5.1 %collective-permute-done.2 = f32[512,256]{1,0:T(8,128)S(1)} collective-permute-done((f32[512,256]{1,0:T(8,128)S(1)}, f32[512,256]{1,0:T(8,128)S(1)}, u32[]{:S(2)}, u32[]{:S(2)}) %collective-permute-start.2) | collective-permute-done | bytes 524320 | tf_op jit(solution)/shard_map/ppermute | solution.py:395
  20.9 12.6 %all_to_all.36.pieces_ref = f32[8,64,256]{2,1,0:T(8,128)S(1)} all-to-all(f32[8,64,256]{2,1,0:T(8,128)S(1)} %bitcast.19), channel_id=1, replica_groups={{0,4,8,12,16,20,24,28},{1,5,9,13,17,21,25,29},{2,6,10,14,18,22,26,30},{..., dimensions={0} | all-to-all | bytes 1048576 | tf_op jit(solution)/shard_map/all_to_all | solution.py:405
  33.6 10.6 %all_to_all.37 = f32[8,64,256]{2,1,0:T(8,128)S(1)} all-to-all(f32[8,64,256]{2,1,0:T(8,128)S(1)} %shard_map.59), channel_id=1, replica_groups={{0,4,8,12,16,20,24,28},{1,5,9,13,17,21,25,29},{2,6,10,14,18,22,26,30},{..., dimensions={0} | all-to-all | bytes 1048576 | tf_op jit(solution)/shard_map/all_to_all | solution.py:405
  44.8 4.1 %collective-permute-start.5 = (f32[512,256]{1,0:T(8,128)S(1)}, f32[512,256]{1,0:T(8,128)S(1)}, u32[]{:S(2)}, u32[]{:S(2)}) collective-permute-start(f32[512,256]{1,0:T(8,128)S(1)} %bitcast.15), channel_id=1, source_target_pairs={{0,1},{32,36},{1,2},{33,37},{2,3},{34,38},{3,0},{35,39},{4,5},{36,... | collective-permute-start | bytes 1572872 | tf_op jit(solution)/shard_map/ppermute | solution.py:395
  48.9 2.9 %collective-permute-start.3 = (f32[512,256]{1,0:T(8,128)S(1)}, f32[512,256]{1,0:T(8,128)S(1)}, u32[]{:S(2)}, u32[]{:S(2)}) collective-permute-start(f32[512,256]{1,0:T(8,128)S(1)} %bitcast.16), channel_id=1, source_target_pairs={{0,3},{32,44},{1,0},{33,45},{2,1},{34,46},{3,2},{35,47},{4,7},{36,... | collective-permute-start | bytes 1572872 | tf_op jit(solution)/shard_map/ppermute | solution.py:395
  53.3 2.4 %shard_map.60.refs_3_ = f32[256,1536]{1,0:T(8,128)S(1)} custom-call(f32[512,256]{1,0:T(8,128)S(1)} %bitcast.18, bf16[512,1536]{1,0:T(8,128)(2,1)S(1)} %get-tuple-element.120.refs_1_.refs_2_, bf16[512,1536]{1,0:T(8,128)(2,1)S(1)} %get-tuple-element.121.refs_2_.refs_3_), custom_call_target="tpu_custom_call" | custom-call | flops 1207959552 | bytes 2097152 | tf_op jit(solution)/shard_map/pallas_call | solution.py:196
  55.7 2.9 %collective-permute-done.5.refs_0_ = f32[512,256]{1,0:T(8,128)S(1)} collective-permute-done((f32[512,256]{1,0:T(8,128)S(1)}, f32[512,256]{1,0:T(8,128)S(1)}, u32[]{:S(2)}, u32[]{:S(2)}) %collective-permute-start.5) | collective-permute-done | bytes 524320 | tf_op jit(solution)/shard_map/ppermute | solution.py:395
  58.6 2.5 %shard_map.61.refs_6_.refs_4_ = f32[256,1536]{1,0:T(8,128)S(1)} custom-call(f32[512,256]{1,0:T(8,128)S(1)} %collective-permute-done.5.refs_0_, bf16[512,1536]{1,0:T(8,128)(2,1)S(1)} %get-tuple-element.118.refs_1_.refs_5_.refs_3_, bf16[512,1536]{1,0:T(8,128)(2,1)S(1)} %get-tuple-element.119.refs_2_.refs_6_.refs_4_, f32[256,1536]{1,0:T(8,128)S(1)} %shard_map.60.refs_3_), custom_call_target="tpu_custom_call" | custom-call | flops 1207959552 | bytes 2097152 | tf_op jit(solution)/shard_map/pallas_call | solution.py:196
  61.1 2.5 %collective-permute-done.3.refs_0_ = f32[512,256]{1,0:T(8,128)S(1)} collective-permute-done((f32[512,256]{1,0:T(8,128)S(1)}, f32[512,256]{1,0:T(8,128)S(1)}, u32[]{:S(2)}, u32[]{:S(2)}) %collective-permute-start.3) | collective-permute-done | bytes 524320 | tf_op jit(solution)/shard_map/ppermute | solution.py:395
  65.4 2.3 %shard_map.62 = (f32[768,256]{1,0:T(8,128)S(1)}, bf16[2,256,512]{2,1,0:T(8,128)(2,1)S(1)}, bf16[2,256,512]{2,1,0:T(8,128)(2,1)S(1)}) custom-call(s32[1]{0:T(128)} %bitcast.2.plane_ref.planes_ref, f32[512,256]{1,0:T(8,128)S(1)} %collective-permute-done.3.refs_0_, f32[512,256]{1,0:T(8,128)S(1)} %collective-permute-done.4.refs_1_, ...), custom_call_target="tpu_custom_call" | custom-call | flops 1207959552 | bytes 1835008 | tf_op jit(solution)/shard_map/pallas_call | solution.py:236
  67.7 4.6 %collective-permute-start.7 = (f32[768,256]{1,0:T(8,128)S(1)}, f32[768,256]{1,0:T(8,128)S(1)}, u32[]{:S(2)}, u32[]{:S(2)}) collective-permute-start(f32[768,256]{1,0:T(8,128)S(1)} %get-tuple-element.126), channel_id=1, source_target_pairs={{0,32},{32,0},{1,33},{33,1},{2,34},{34,2},{3,35},{35,3},{4,36},{36... | collective-permute-start | bytes 2359304 | tf_op jit(solution)/shard_map/ppermute | solution.py:368
  75.5 2.1 %collective-permute-start.8 = (f32[768,256]{1,0:T(8,128)S(1)}, f32[768,256]{1,0:T(8,128)S(1)}, u32[]{:S(2)}, u32[]{:S(2)}) collective-permute-start(f32[768,256]{1,0:T(8,128)S(1)} %broadcast_select_fusion.1), channel_id=1, source_target_pairs={{32,1},{33,2},{34,3},{35,4},{36,5},{37,6},{38,7},{39,8},{40,9},{41... | collective-permute-start | bytes 2359304 | tf_op jit(solution)/shard_map/ppermute | solution.py:382
  77.6 6.5 %shard_map.64.inner_ref = f32[768,256]{1,0:T(8,128)S(1)} custom-call(f32[8,768]{1,0:T(8,128)S(1)} %maximum_maximum_fusion.table_ref, f32[768,256]{1,0:T(8,128)S(1)} %get-tuple-element.130.own_ref, f32[768,256]{1,0:T(8,128)S(1)} %get-tuple-element.132.twin_ref), custom_call_target="tpu_custom_call" | custom-call | flops 3623878656 | bytes 3145728 | tf_op jit(solution)/shard_map/pallas_call | solution.py:305
  84.1 10.8 %collective-permute-done.9 = f32[768,256]{1,0:T(8,128)S(1)} collective-permute-done((f32[768,256]{1,0:T(8,128)S(1)}, f32[768,256]{1,0:T(8,128)S(1)}, u32[]{:S(2)}, u32[]{:S(2)}) %collective-permute-start.9) | collective-permute-done | bytes 786464 | tf_op jit(solution)/shard_map/ppermute | solution.py:368
  96.8 2.0 %shard_map.67 = (f32[512,256]{1,0:T(8,128)S(1)}, f32[512,256]{1,0:T(8,128)S(1)}, f32[512,256]{1,0:T(8,128)S(1)}) custom-call(s32[1]{0:T(128)} %bitcast.1.plane_ref.planes_ref, f32[768,256]{1,0:T(8,128)S(1)} %shard_map.65.refs_0_.own_ref, bf16[512,1536]{1,0:T(8,128)(2,1)S(1)} %get-tuple-element.116.refs_4_.refs_2_.refs_1_, ...), custom_call_target="tpu_custom_call" | custom-call | flops 1811939328 | bytes 2359296 | tf_op jit(solution)/shard_map/pallas_call | solution.py:159
  101.2 2.7 %collective-permute-start.13 = (f32[512,256]{1,0:T(8,128)S(1)}, f32[512,256]{1,0:T(8,128)S(1)}, u32[]{:S(2)}, u32[]{:S(2)}) collective-permute-start(f32[512,256]{1,0:T(8,128)S(1)} %get-tuple-element.138), channel_id=1, source_target_pairs={{0,3},{32,44},{1,0},{33,45},{2,1},{34,46},{3,2},{35,47},{4,7},{36,... | collective-permute-start | bytes 1572872 | tf_op jit(solution)/shard_map/ppermute | solution.py:395
  103.9 2.0 %shard_map.66 = f32[512,256]{1,0:T(8,128)S(1)} custom-call(s32[2]{0:T(128)S(1)} %pad_add_fusion.planes_ref, f32[768,256]{1,0:T(8,128)S(1)} %shard_map.65.refs_0_.own_ref, f32[768,256]{1,0:T(8,128)S(1)} %collective-permute-done.10.refs_1_.refs_0_.twin_ref, bf16[512,1536]{1,0:T(8,128)(2,1)S(1)} %get-tuple-element.120.refs_1_.refs_2_, ...), custom_call_target="tpu_custom_call" | custom-call | flops 1207959552 | bytes 2097152 | tf_op jit(solution)/shard_map/pallas_call | solution.py:159
  105.9 3.7 %collective-permute-done.11 = f32[512,256]{1,0:T(8,128)S(1)} collective-permute-done((f32[512,256]{1,0:T(8,128)S(1)}, f32[512,256]{1,0:T(8,128)S(1)}, u32[]{:S(2)}, u32[]{:S(2)}) %collective-permute-start.11) | collective-permute-done | bytes 524320 | tf_op jit(solution)/shard_map/ppermute | solution.py:395
  109.7 5.5 %collective-permute-done.12 = f32[512,256]{1,0:T(8,128)S(1)} collective-permute-done((f32[512,256]{1,0:T(8,128)S(1)}, f32[512,256]{1,0:T(8,128)S(1)}, u32[]{:S(2)}, u32[]{:S(2)}) %collective-permute-start.12) | collective-permute-done | bytes 524320 | tf_op jit(solution)/shard_map/ppermute | solution.py:395
  115.3 10.7 %all_to_all.38.pieces_ref = f32[8,64,256]{2,1,0:T(8,128)S(1)} all-to-all(f32[8,64,256]{2,1,0:T(8,128)S(1)} %bitcast.20), channel_id=1, replica_groups={{0,4,8,12,16,20,24,28},{1,5,9,13,17,21,25,29},{2,6,10,14,18,22,26,30},{..., dimensions={0} | all-to-all | bytes 1048576 | tf_op jit(solution)/shard_map/all_to_all | solution.py:405
  126.1 12.2 %all_to_all.39 = f32[8,64,256]{2,1,0:T(8,128)S(1)} all-to-all(f32[8,64,256]{2,1,0:T(8,128)S(1)} %shard_map.70), channel_id=1, replica_groups={{0,4,8,12,16,20,24,28},{1,5,9,13,17,21,25,29},{2,6,10,14,18,22,26,30},{..., dimensions={0} | all-to-all | bytes 1048576 | tf_op jit(solution)/shard_map/all_to_all | solution.py:405
  139.1 2.7 %collective-permute-start.14 = (f32[512,256]{1,0:T(8,128)S(1)}, f32[512,256]{1,0:T(8,128)S(1)}, u32[]{:S(2)}, u32[]{:S(2)}) collective-permute-start(f32[512,256]{1,0:T(8,128)S(1)} %bitcast.12), channel_id=1, source_target_pairs={{0,3},{32,44},{1,0},{33,45},{2,1},{34,46},{3,2},{35,47},{4,7},{36,... | collective-permute-start | bytes 1572872 | tf_op jit(solution)/shard_map/ppermute | solution.py:395
  141.8 2.4 %shard_map.71.refs_3_ = f32[256,1536]{1,0:T(8,128)S(1)} custom-call(f32[512,256]{1,0:T(8,128)S(1)} %bitcast.14, bf16[512,1536]{1,0:T(8,128)(2,1)S(1)} %get-tuple-element.120.refs_1_.refs_2_, bf16[512,1536]{1,0:T(8,128)(2,1)S(1)} %get-tuple-element.121.refs_2_.refs_3_), custom_call_target="tpu_custom_call" | custom-call | flops 1207959552 | bytes 2097152 | tf_op jit(solution)/shard_map/pallas_call | solution.py:196
  144.3 10.0 %collective-permute-done.16.refs_0_ = f32[512,256]{1,0:T(8,128)S(1)} collective-permute-done((f32[512,256]{1,0:T(8,128)S(1)}, f32[512,256]{1,0:T(8,128)S(1)}, u32[]{:S(2)}, u32[]{:S(2)}) %collective-permute-start.16) | collective-permute-done | bytes 524320 | tf_op jit(solution)/shard_map/ppermute | solution.py:395
  154.3 2.5 %shard_map.72.refs_6_.refs_4_ = f32[256,1536]{1,0:T(8,128)S(1)} custom-call(f32[512,256]{1,0:T(8,128)S(1)} %collective-permute-done.16.refs_0_, bf16[512,1536]{1,0:T(8,128)(2,1)S(1)} %get-tuple-element.118.refs_1_.refs_5_.refs_3_, bf16[512,1536]{1,0:T(8,128)(2,1)S(1)} %get-tuple-element.119.refs_2_.refs_6_.refs_4_, f32[256,1536]{1,0:T(8,128)S(1)} %shard_map.71.refs_3_), custom_call_target="tpu_custom_call" | custom-call | flops 1207959552 | bytes 2097152 | tf_op jit(solution)/shard_map/pallas_call | solution.py:196
  156.8 2.3 %shard_map.73 = (f32[768,256]{1,0:T(8,128)S(1)}, bf16[2,256,512]{2,1,0:T(8,128)(2,1)S(1)}, bf16[2,256,512]{2,1,0:T(8,128)(2,1)S(1)}) custom-call(s32[1]{0:T(128)} %bitcast.2.plane_ref.planes_ref, f32[512,256]{1,0:T(8,128)S(1)} %collective-permute-done.14.refs_0_, f32[512,256]{1,0:T(8,128)S(1)} %collective-permute-done.15.refs_1_, ...), custom_call_target="tpu_custom_call" | custom-call | flops 1207959552 | bytes 1835008 | tf_op jit(solution)/shard_map/pallas_call | solution.py:236
  159.1 3.3 %collective-permute-start.18 = (f32[768,256]{1,0:T(8,128)S(1)}, f32[768,256]{1,0:T(8,128)S(1)}, u32[]{:S(2)}, u32[]{:S(2)}) collective-permute-start(f32[768,256]{1,0:T(8,128)S(1)} %get-tuple-element.152), channel_id=1, source_target_pairs={{0,32},{32,0},{1,33},{33,1},{2,34},{34,2},{3,35},{35,3},{4,36},{36... | collective-permute-start | bytes 2359304 | tf_op jit(solution)/shard_map/ppermute | solution.py:368
  167.7 6.5 %shard_map.75.inner_ref = f32[768,256]{1,0:T(8,128)S(1)} custom-call(f32[8,768]{1,0:T(8,128)S(1)} %maximum_maximum_fusion.table_ref, f32[768,256]{1,0:T(8,128)S(1)} %shard_map.65.refs_0_.own_ref, f32[768,256]{1,0:T(8,128)S(1)} %collective-permute-done.10.refs_1_.refs_0_.twin_ref), custom_call_target="tpu_custom_call" | custom-call | flops 3623878656 | bytes 3145728 | tf_op jit(solution)/shard_map/pallas_call | solution.py:305
  174.3 11.0 %collective-permute-done.20 = f32[768,256]{1,0:T(8,128)S(1)} collective-permute-done((f32[768,256]{1,0:T(8,128)S(1)}, f32[768,256]{1,0:T(8,128)S(1)}, u32[]{:S(2)}, u32[]{:S(2)}) %collective-permute-start.20) | collective-permute-done | bytes 786464 | tf_op jit(solution)/shard_map/ppermute | solution.py:368
  (70 shorter events, 27.8 us)
Async XLA Ops:
  0.1 7.9 %copy-start = (f32[2048,1536]{1,0:T(8,128)S(1)}, f32[2048,1536]{1,0:T(8,128)}, u32[]{:S(2)}) copy-start(f32[2048,1536]{1,0:T(8,128)} %s_ref.7) | copy-start | bytes 37748740
  5.1 10.4 %collective-permute-start = (f32[512,256]{1,0:T(8,128)S(1)}, f32[512,256]{1,0:T(8,128)S(1)}, u32[]{:S(2)}, u32[]{:S(2)}) collective-permute-start(f32[512,256]{1,0:T(8,128)S(1)} %get-tuple-element.98), channel_id=1, source_target_pairs={{0,2},{32,40},{1,3},{33,41},{2,0},{34,42},{3,1},{35,43},{4,6},{36,... | collective-permute-start | bytes 1572872 | tf_op jit(solution)/shard_map/ppermute | solution.py:395
  9.4 11.3 %collective-permute-start.1 = (f32[512,256]{1,0:T(8,128)S(1)}, f32[512,256]{1,0:T(8,128)S(1)}, u32[]{:S(2)}, u32[]{:S(2)}) collective-permute-start(f32[512,256]{1,0:T(8,128)S(1)} %get-tuple-element.90), channel_id=1, source_target_pairs={{0,1},{32,36},{1,2},{33,37},{2,3},{34,38},{3,0},{35,39},{4,5},{36,... | collective-permute-start | bytes 1572872 | tf_op jit(solution)/shard_map/ppermute | solution.py:395
  11.2 3.9 %copy-start.4 = (s32[1536]{0:T(1024)S(1)}, s32[1536]{0:T(1024)}, u32[]{:S(2)}) copy-start(s32[1536]{0:T(1024)} %param.9) | copy-start | bytes 18436
  11.2 4.0 %copy-start.3 = (s32[4,768]{1,0:T(4,128)S(1)}, s32[4,768]{1,0:T(4,128)}, u32[]{:S(2)}) copy-start(s32[4,768]{1,0:T(4,128)} %param.8) | copy-start | bytes 36868
  11.3 4.1 %copy-start.2 = (f32[1536,256]{1,0:T(8,128)S(1)}, f32[1536,256]{1,0:T(8,128)}, u32[]{:S(2)}) copy-start(f32[1536,256]{1,0:T(8,128)} %x_ref.1) | copy-start | bytes 4718596
  11.3 9.5 %collective-permute-start.2 = (f32[512,256]{1,0:T(8,128)S(1)}, f32[512,256]{1,0:T(8,128)S(1)}, u32[]{:S(2)}, u32[]{:S(2)}) collective-permute-start(f32[512,256]{1,0:T(8,128)S(1)} %get-tuple-element.93), channel_id=1, source_target_pairs={{0,3},{32,44},{1,0},{33,45},{2,1},{34,46},{3,2},{35,47},{4,7},{36,... | collective-permute-start | bytes 1572872 | tf_op jit(solution)/shard_map/ppermute | solution.py:395
  20.8 12.7 %copy-start.1 = (f32[2048,256]{1,0:T(8,128)S(1)}, f32[2048,256]{1,0:T(8,128)}, u32[]{:S(2)}) copy-start(f32[2048,256]{1,0:T(8,128)} %observed_ref.3) | copy-start | bytes 6291460
  44.1 17.0 %collective-permute-start.6 = (f32[768,256]{1,0:T(8,128)S(1)}, f32[768,256]{1,0:T(8,128)S(1)}, u32[]{:S(2)}, u32[]{:S(2)}) collective-permute-start(f32[768,256]{1,0:T(8,128)S(1)} %get-tuple-element.130.own_ref), channel_id=1, source_target_pairs={{47,63},{16,0},{111,127},{80,64}} | collective-permute-start | bytes 2359304 | tf_op jit(solution)/shard_map/ppermute | solution.py:374
  44.8 13.8 %collective-permute-start.5 = (f32[512,256]{1,0:T(8,128)S(1)}, f32[512,256]{1,0:T(8,128)S(1)}, u32[]{:S(2)}, u32[]{:S(2)}) collective-permute-start(f32[512,256]{1,0:T(8,128)S(1)} %bitcast.15), channel_id=1, source_target_pairs={{0,1},{32,36},{1,2},{33,37},{2,3},{34,38},{3,0},{35,39},{4,5},{36,... | collective-permute-start | bytes 1572872 | tf_op jit(solution)/shard_map/ppermute | solution.py:395
  48.9 14.7 %collective-permute-start.3 = (f32[512,256]{1,0:T(8,128)S(1)}, f32[512,256]{1,0:T(8,128)S(1)}, u32[]{:S(2)}, u32[]{:S(2)}) collective-permute-start(f32[512,256]{1,0:T(8,128)S(1)} %bitcast.16), channel_id=1, source_target_pairs={{0,3},{32,44},{1,0},{33,45},{2,1},{34,46},{3,2},{35,47},{4,7},{36,... | collective-permute-start | bytes 1572872 | tf_op jit(solution)/shard_map/ppermute | solution.py:395
  51.8 13.6 %collective-permute-start.4 = (f32[512,256]{1,0:T(8,128)S(1)}, f32[512,256]{1,0:T(8,128)S(1)}, u32[]{:S(2)}, u32[]{:S(2)}) collective-permute-start(f32[512,256]{1,0:T(8,128)S(1)} %bitcast.17), channel_id=1, source_target_pairs={{0,2},{32,40},{1,3},{33,41},{2,0},{34,42},{3,1},{35,43},{4,6},{36,... | collective-permute-start | bytes 1572872 | tf_op jit(solution)/shard_map/ppermute | solution.py:395
  67.7 6.6 %collective-permute-start.7 = (f32[768,256]{1,0:T(8,128)S(1)}, f32[768,256]{1,0:T(8,128)S(1)}, u32[]{:S(2)}, u32[]{:S(2)}) collective-permute-start(f32[768,256]{1,0:T(8,128)S(1)} %get-tuple-element.126), channel_id=1, source_target_pairs={{0,32},{32,0},{1,33},{33,1},{2,34},{34,2},{3,35},{35,3},{4,36},{36... | collective-permute-start | bytes 2359304 | tf_op jit(solution)/shard_map/ppermute | solution.py:368
  74.4 20.5 %collective-permute-start.9 = (f32[768,256]{1,0:T(8,128)S(1)}, f32[768,256]{1,0:T(8,128)S(1)}, u32[]{:S(2)}, u32[]{:S(2)}) collective-permute-start(f32[768,256]{1,0:T(8,128)S(1)} %add.78), channel_id=1, source_target_pairs={{0,64},{64,0},{1,65},{65,1},{2,66},{66,2},{3,67},{67,3},{4,68},{68... | collective-permute-start | bytes 2359304 | tf_op jit(solution)/shard_map/ppermute | solution.py:368
  75.5 19.7 %collective-permute-start.8 = (f32[768,256]{1,0:T(8,128)S(1)}, f32[768,256]{1,0:T(8,128)S(1)}, u32[]{:S(2)}, u32[]{:S(2)}) collective-permute-start(f32[768,256]{1,0:T(8,128)S(1)} %broadcast_select_fusion.1), channel_id=1, source_target_pairs={{32,1},{33,2},{34,3},{35,4},{36,5},{37,6},{38,7},{39,8},{40,9},{41... | collective-permute-start | bytes 2359304 | tf_op jit(solution)/shard_map/ppermute | solution.py:382
  95.7 3.1 %collective-permute-start.10 = (f32[768,256]{1,0:T(8,128)S(1)}, f32[768,256]{1,0:T(8,128)S(1)}, u32[]{:S(2)}, u32[]{:S(2)}) collective-permute-start(f32[768,256]{1,0:T(8,128)S(1)} %shard_map.65.refs_0_.own_ref), channel_id=1, source_target_pairs={{0,32},{32,0},{1,33},{33,1},{2,34},{34,2},{3,35},{35,3},{4,36},{36... | collective-permute-start | bytes 2359304 | tf_op jit(solution)/shard_map/ppermute | solution.py:368
  99.6 10.0 %collective-permute-start.11 = (f32[512,256]{1,0:T(8,128)S(1)}, f32[512,256]{1,0:T(8,128)S(1)}, u32[]{:S(2)}, u32[]{:S(2)}) collective-permute-start(f32[512,256]{1,0:T(8,128)S(1)} %shard_map.68), channel_id=1, source_target_pairs={{0,2},{32,40},{1,3},{33,41},{2,0},{34,42},{3,1},{35,43},{4,6},{36,... | collective-permute-start | bytes 1572872 | tf_op jit(solution)/shard_map/ppermute | solution.py:395
  101.1 14.0 %collective-permute-start.12 = (f32[512,256]{1,0:T(8,128)S(1)}, f32[512,256]{1,0:T(8,128)S(1)}, u32[]{:S(2)}, u32[]{:S(2)}) collective-permute-start(f32[512,256]{1,0:T(8,128)S(1)} %get-tuple-element.137), channel_id=1, source_target_pairs={{0,1},{32,36},{1,2},{33,37},{2,3},{34,38},{3,0},{35,39},{4,5},{36,... | collective-permute-start | bytes 1572872 | tf_op jit(solution)/shard_map/ppermute | solution.py:395
  101.2 14.0 %collective-permute-start.13 = (f32[512,256]{1,0:T(8,128)S(1)}, f32[512,256]{1,0:T(8,128)S(1)}, u32[]{:S(2)}, u32[]{:S(2)}) collective-permute-start(f32[512,256]{1,0:T(8,128)S(1)} %get-tuple-element.138), channel_id=1, source_target_pairs={{0,3},{32,44},{1,0},{33,45},{2,1},{34,46},{3,2},{35,47},{4,7},{36,... | collective-permute-start | bytes 1572872 | tf_op jit(solution)/shard_map/ppermute | solution.py:395
  138.3 18.4 %collective-permute-start.17 = (f32[768,256]{1,0:T(8,128)S(1)}, f32[768,256]{1,0:T(8,128)S(1)}, u32[]{:S(2)}, u32[]{:S(2)}) collective-permute-start(f32[768,256]{1,0:T(8,128)S(1)} %shard_map.65.refs_0_.own_ref), channel_id=1, source_target_pairs={{47,63},{16,0},{111,127},{80,64}} | collective-permute-start | bytes 2359304 | tf_op jit(solution)/shard_map/ppermute | solution.py:374
  139.1 15.2 %collective-permute-start.16 = (f32[512,256]{1,0:T(8,128)S(1)}, f32[512,256]{1,0:T(8,128)S(1)}, u32[]{:S(2)}, u32[]{:S(2)}) collective-permute-start(f32[512,256]{1,0:T(8,128)S(1)} %bitcast.11), channel_id=1, source_target_pairs={{0,1},{32,36},{1,2},{33,37},{2,3},{34,38},{3,0},{35,39},{4,5},{36,... | collective-permute-start | bytes 1572872 | tf_op jit(solution)/shard_map/ppermute | solution.py:395
  139.1 17.6 %collective-permute-start.14 = (f32[512,256]{1,0:T(8,128)S(1)}, f32[512,256]{1,0:T(8,128)S(1)}, u32[]{:S(2)}, u32[]{:S(2)}) collective-permute-start(f32[512,256]{1,0:T(8,128)S(1)} %bitcast.12), channel_id=1, source_target_pairs={{0,3},{32,44},{1,0},{33,45},{2,1},{34,46},{3,2},{35,47},{4,7},{36,... | collective-permute-start | bytes 1572872 | tf_op jit(solution)/shard_map/ppermute | solution.py:395
  141.8 15.0 %collective-permute-start.15 = (f32[512,256]{1,0:T(8,128)S(1)}, f32[512,256]{1,0:T(8,128)S(1)}, u32[]{:S(2)}, u32[]{:S(2)}) collective-permute-start(f32[512,256]{1,0:T(8,128)S(1)} %bitcast.13), channel_id=1, source_target_pairs={{0,2},{32,40},{1,3},{33,41},{2,0},{34,42},{3,1},{35,43},{4,6},{36,... | collective-permute-start | bytes 1572872 | tf_op jit(solution)/shard_map/ppermute | solution.py:395
  159.1 5.4 %collective-permute-start.18 = (f32[768,256]{1,0:T(8,128)S(1)}, f32[768,256]{1,0:T(8,128)S(1)}, u32[]{:S(2)}, u32[]{:S(2)}) collective-permute-start(f32[768,256]{1,0:T(8,128)S(1)} %get-tuple-element.152), channel_id=1, source_target_pairs={{0,32},{32,0},{1,33},{33,1},{2,34},{34,2},{3,35},{35,3},{4,36},{36... | collective-permute-start | bytes 2359304 | tf_op jit(solution)/shard_map/ppermute | solution.py:368
  164.6 20.7 %collective-permute-start.20 = (f32[768,256]{1,0:T(8,128)S(1)}, f32[768,256]{1,0:T(8,128)S(1)}, u32[]{:S(2)}, u32[]{:S(2)}) collective-permute-start(f32[768,256]{1,0:T(8,128)S(1)} %add.83), channel_id=1, source_target_pairs={{0,64},{64,0},{1,65},{65,1},{2,66},{66,2},{3,67},{67,3},{4,68},{68... | collective-permute-start | bytes 2359304 | tf_op jit(solution)/shard_map/ppermute | solution.py:368
  165.8 19.7 %collective-permute-start.19 = (f32[768,256]{1,0:T(8,128)S(1)}, f32[768,256]{1,0:T(8,128)S(1)}, u32[]{:S(2)}, u32[]{:S(2)}) collective-permute-start(f32[768,256]{1,0:T(8,128)S(1)} %broadcast_select_fusion), channel_id=1, source_target_pairs={{32,1},{33,2},{34,3},{35,4},{36,5},{37,6},{38,7},{39,8},{40,9},{41... | collective-permute-start | bytes 2359304 | tf_op jit(solution)/shard_map/ppermute | solution.py:382
  186.1 3.0 %collective-permute-start.21 = (f32[768,256]{1,0:T(8,128)S(1)}, f32[768,256]{1,0:T(8,128)S(1)}, u32[]{:S(2)}, u32[]{:S(2)}) collective-permute-start(f32[768,256]{1,0:T(8,128)S(1)} %shard_map.76.value_ref), channel_id=1, source_target_pairs={{0,32},{32,0},{1,33},{33,1},{2,34},{34,2},{3,35},{35,3},{4,36},{36... | collective-permute-start | bytes 2359304 | tf_op jit(solution)/shard_map/ppermute | solution.py:368
